TPU v7x, 128 devices: a whole 4x4x4 slice. The times are simulated.
128 devices in a mesh: req: 16 (over y, z), head: 8 (over x, core).
Axes of the slice: x: 4, y: 4, z: 4, core: 2. Of those that a mesh axis runs over, the one named last changes fastest.
Arguments:
- queries: bfloat16 [1536, 128, 576], P('req', 'head'), may hold values from -16 to 16
- out_grad: bfloat16 [1536, 128, 512], P('req', 'head'), may hold values from -96 to 96
- latents: bfloat16 [256, 128, 576], P('req', 'head'), may hold values from -4 to 4
- list_blocks: int32 [16, 16], replicated, may hold values from 0 to 255, as said below
- list_counts: int32 [16], replicated, may hold values from 8 to 16
- valid_tokens: int32 [256], replicated, may hold values from 32 to 128
Outputs:
- attended: bfloat16 [1536, 128, 512], P('req', 'head')
- query_grad: bfloat16 [1536, 128, 576], P('req', 'head')
- latent_grad: float32 [256, 128, 576], P('req', 'head')
Inputs may be any that keep to these rules, and one draw needn't show every extreme that they name: `list_blocks`: each row holds 16 distinct block numbers. Group g reads its first list_counts[g] entries, and among them at most 2 are owned by one req index, the owner of block b being b // 16; some group reaches 2 in every draw.
All inputs are finite; a program needn't handle non-finite values.
Results may differ from a plain program's by a relative error of at most 0.017.
Values may be sent and summed in bfloat16 or wider, within the bound.
No kernel may reach another device: no remote copies, remote signals or barrier semaphores. Data moves between devices by JAX's collectives and lax.ppermute only.
A program may use at most 64 MiB of HBM per device.

v0:
```python
import jax
import jax.numpy as jnp
from jax import lax
from jax.sharding import PartitionSpec as P

LAT = 512
ROPE = 64
BLOCK = 128
MAXL = 16
CAP = 2


softmax_scale = 192.0 ** (-0.5)


def laid_out(parts, dim):
    parts = jnp.moveaxis(parts, 0, dim)
    lengths = parts.shape
    return parts.reshape(*lengths[:dim], lengths[dim] * lengths[dim + 1], *lengths[dim + 2 :])


def from_everyone(x, axis):
    devices = lax.axis_size(axis)
    return lax.all_to_all(jnp.broadcast_to(x[None], (devices, *x.shape)), axis, 0, 0, tiled=True)


def gather_directly(x, axis, dim):
    return laid_out(from_everyone(x, axis), dim)


def cut_along(x, dim, devices):
    lengths = x.shape
    parts = x.reshape(*lengths[:dim], devices, lengths[dim] // devices, *lengths[dim + 1 :])
    return jnp.moveaxis(parts, dim, 0)


def sent_and_summed(x, axis, dim):
    devices = lax.axis_size(axis)
    parts = lax.all_to_all(cut_along(x, dim, devices), axis, 0, 0, tiled=True)
    return jnp.sum(parts.astype(jnp.float32), axis=0)


def attend(query_rows, cotangent, key_rows, live_keys):
    scores = jnp.dot(query_rows, key_rows.T, preferred_element_type=jnp.float32) * softmax_scale
    scores = jnp.where(live_keys[None, :], scores, -jnp.inf)
    row_max = jnp.max(scores, axis=1, keepdims=True)
    exponent = jnp.exp(scores - row_max)
    row_sum = jnp.sum(exponent, axis=1, keepdims=True)
    weights = (exponent / row_sum).astype(jnp.bfloat16)
    values = key_rows[:, :LAT]
    output = jnp.dot(weights, values, preferred_element_type=jnp.float32).astype(jnp.bfloat16)
    weight_grads = jnp.dot(cotangent, values.T, preferred_element_type=jnp.float32)
    row_dot = jnp.sum(
        cotangent.astype(jnp.float32) * output.astype(jnp.float32), axis=1, keepdims=True
    )
    score_grads = (weights.astype(jnp.float32) * (weight_grads - row_dot) * softmax_scale).astype(
        jnp.bfloat16
    )
    query_grad = jnp.dot(score_grads, key_rows, preferred_element_type=jnp.float32).astype(
        jnp.bfloat16
    )
    key_grads = jnp.dot(score_grads.T, query_rows, preferred_element_type=jnp.float32)
    value_grads = jnp.dot(weights.T, cotangent, preferred_element_type=jnp.float32)
    key_grads = key_grads + jnp.pad(value_grads, ((0, 0), (0, ROPE)))
    return (output, query_grad, key_grads)


def per_device(queries, out_grad, latents, list_blocks, list_counts, valid_tokens):
    req_count = lax.axis_size("req")
    my_index = lax.axis_index("req")
    blk_owned = latents.shape[0]
    share_len = latents.shape[1]
    wide_len = latents.shape[2]
    slot_total = req_count * CAP
    owner_of = list_blocks // blk_owned
    local_of = list_blocks - owner_of * blk_owned
    entry_pos = jnp.arange(MAXL, dtype=jnp.int32)
    live_entry = entry_pos[None, :] < list_counts[:, None]
    earlier = (
        (owner_of[:, :, None] == owner_of[:, None, :])
        & live_entry[:, None, :]
        & (entry_pos[None, None, :] < entry_pos[None, :, None])
    )
    entry_rank = jnp.sum(earlier.astype(jnp.int32), axis=2)
    slot_of = owner_of * CAP + entry_rank
    owned_here = live_entry & (owner_of == my_index)
    chosen = (
        owned_here[:, :, None, None]
        & (entry_rank[:, :, None, None] == jnp.arange(CAP, dtype=jnp.int32)[None, None, :, None])
        & (
            local_of[:, :, None, None]
            == jnp.arange(blk_owned, dtype=jnp.int32)[None, None, None, :]
        )
    )
    send_pick = jnp.sum(chosen.astype(jnp.float32), axis=1).reshape(slot_total, blk_owned)
    my_slot = lax.dynamic_index_in_dim(slot_of, my_index, 0, keepdims=False)
    my_live = lax.dynamic_index_in_dim(live_entry, my_index, 0, keepdims=False)
    my_blocks = lax.dynamic_index_in_dim(list_blocks, my_index, 0, keepdims=False)
    gather_pick = (
        my_live[:, None] & (my_slot[:, None] == jnp.arange(slot_total, dtype=jnp.int32)[None, :])
    ).astype(jnp.float32)
    block_ids = jnp.arange(valid_tokens.shape[0], dtype=jnp.int32)
    my_valid = jnp.sum(
        jnp.where(my_blocks[:, None] == block_ids[None, :], valid_tokens[None, :], 0), axis=1
    )
    token_pos = jnp.arange(BLOCK, dtype=jnp.int32)
    live_keys = (my_live[:, None] & (token_pos[None, :] < my_valid[:, None])).reshape(-1)
    send_bf = send_pick.astype(jnp.bfloat16)
    pick_bf = gather_pick.astype(jnp.bfloat16)
    outgoing = jnp.dot(send_bf, latents.reshape(blk_owned, -1), preferred_element_type=jnp.float32)
    outgoing = outgoing.astype(jnp.bfloat16).reshape(req_count, CAP, share_len, wide_len)
    arrived = lax.all_to_all(outgoing, "req", split_axis=0, concat_axis=0, tiled=True)
    piece_rows = jnp.dot(
        pick_bf, arrived.reshape(slot_total, -1), preferred_element_type=jnp.float32
    )
    piece_rows = piece_rows.astype(jnp.bfloat16).reshape(MAXL, share_len, wide_len)
    listed = gather_directly(piece_rows, "head", 1)
    query_count = queries.shape[0]
    head_count = queries.shape[1]
    output, query_grad, key_grads = attend(
        queries.reshape(-1, wide_len),
        out_grad.reshape(-1, LAT),
        listed.reshape(MAXL * BLOCK, wide_len),
        live_keys,
    )
    attended = output.reshape(query_count, head_count, LAT)
    query_grad = query_grad.reshape(query_count, head_count, wide_len)
    list_grads = key_grads.reshape(MAXL, BLOCK, wide_len)
    head_shares = sent_and_summed(list_grads.astype(jnp.bfloat16), "head", 1)
    slot_grads = jnp.dot(
        gather_pick.T,
        head_shares.reshape(MAXL, -1),
        precision=lax.Precision.HIGHEST,
        preferred_element_type=jnp.float32,
    )
    returned = lax.all_to_all(
        slot_grads.reshape(req_count, CAP, share_len, wide_len).astype(jnp.bfloat16),
        "req",
        split_axis=0,
        concat_axis=0,
        tiled=True,
    ).astype(jnp.float32)
    owned_grads = jnp.dot(
        send_pick.T,
        returned.reshape(slot_total, -1),
        precision=lax.Precision.HIGHEST,
        preferred_element_type=jnp.float32,
    )
    latent_grad = owned_grads.reshape(blk_owned, share_len, wide_len)
    return (attended, query_grad, latent_grad)


def solution(mesh):
    in_specs = (
        P("req", "head", None),
        P("req", "head", None),
        P("req", "head", None),
        P(),
        P(),
        P(),
    )
    out_specs = (P("req", "head", None), P("req", "head", None), P("req", "head", None))
    return jax.shard_map(
        per_device, mesh=mesh, in_specs=in_specs, out_specs=out_specs, check_vma=False
    )
```

profile of v0, /device:TPU:0, one launch (start us, length us, event | category | flops | bytes accessed | tf_op | source)
XLA Modules:
  0.0 173.6 jit_solution(5804208840301592318)
XLA Ops:
  0.6 0.0 copy-start
  0.6 0.8 add_select_fusion
  1.5 0.1 iota_compare_fusion
  1.6 0.8 iota_compare_fusion.5
  2.4 0.4 convert_reduce_fusion.2
  2.9 0.2 convert_reduce_fusion.1
  3.0 1.3 reshape.163
  4.3 0.3 convolution_convert_fusion
  4.6 1.4 reshape.164
  6.0 8.2 %all-to-all-start = ((bf16[16,2,16,576]{3,2,1,0:T(8,128)(2,1)}), bf16[16,2,16,576]{3,2,1,0:T(8,128)(2,1)S(1)}, u32[]{:S(2)}, u32[]{:S(2)}) async-start(bf16[16,2,16,576]{3,2,1,0:T(8,128)(2,1)} %reshape.164), calls=%async_computation | async-start | bytes 1310720 | tf_op jit(solution)/shard_map/all_to_all | solution.py:112
  14.2 12.9 %all-to-all-done = bf16[16,2,16,576]{3,2,1,0:T(8,128)(2,1)S(1)} async-done(((bf16[16,2,16,576]{3,2,1,0:T(8,128)(2,1)}), bf16[16,2,16,576]{3,2,1,0:T(8,128)(2,1)S(1)}, u32[]{:S(2)}, u32[]{:S(2)}) %all-to-all-start) | async-done | bytes 589856 | tf_op jit(solution)/shard_map/all_to_all | solution.py:112
  27.0 0.5 reshape.165
  27.6 0.3 convolution_convert_fusion.1
  27.9 0.3 broadcast_in_dim.27
  28.2 0.0 copy-start.3
  28.2 1.7 %broadcast_in_dim.28 = bf16[8,16,16,576]{3,2,1,0:T(8,128)(2,1)} broadcast(bf16[16,16,576]{2,1,0:T(8,128)(2,1)S(1)} %broadcast_in_dim.27), dimensions={1,2,3} | broadcast | bytes 2654208 | tf_op jit(solution)/shard_map/broadcast_in_dim | solution.py:24
  29.9 4.6 %all-to-all-start.1 = ((bf16[8,16,16,576]{3,2,1,0:T(8,128)(2,1)}), bf16[8,16,16,576]{3,2,1,0:T(8,128)(2,1)}, u32[]{:S(2)}, u32[]{:S(2)}) async-start(bf16[8,16,16,576]{3,2,1,0:T(8,128)(2,1)} %broadcast_in_dim.28), calls=%async_computation.1 | async-start | bytes 5242880 | tf_op jit(solution)/shard_map/all_to_all | solution.py:24
  34.5 0.7 fusion.21
  35.2 0.0 copy-done.3
  35.2 0.2 select_reduce_fusion
  35.4 0.1 fusion.15
  35.5 31.7 %all-to-all-done.1 = bf16[8,16,16,576]{3,2,1,0:T(8,128)(2,1)} async-done(((bf16[8,16,16,576]{3,2,1,0:T(8,128)(2,1)}), bf16[8,16,16,576]{3,2,1,0:T(8,128)(2,1)}, u32[]{:S(2)}, u32[]{:S(2)}) %all-to-all-start.1) | async-done | bytes 2359328 | tf_op jit(solution)/shard_map/all_to_all | solution.py:24
  67.1 2.1 %copy.27 = bf16[16,8,16,576]{3,2,1,0:T(8,128)(2,1)S(1)} copy(bf16[16,8,16,576]{3,2,0,1:T(8,128)(2,1)} %bitcast.5) | data formatting | bytes 4718592 | tf_op jit(solution)/shard_map/transpose | solution.py:17
  69.2 0.0 copy-start.1
  69.2 0.0 copy-done
  69.2 5.5 %fusion = (f32[1536]{0:T(1024)S(1)}, f32[2048,1536]{1,0:T(8,128)S(1)}) fusion(pred[2048]{0:T(1024)(128)(4,1)S(1)} %fusion.15, bf16[2048,576]{1,0:T(8,128)(2,1)S(1)} %bitcast.57, bf16[1536,576]{1,0:T(8,128)(2,1)S(1)} %bitcast.54), kind=kOutput, calls=%fused_computation.4 | convolution fusion | flops 3633314304 | bytes 16719872 | tf_op jit(solution)/shard_map/dot_general | solution.py:44
  74.8 3.3 %fusion.1 = f32[1536]{0:T(1024)S(1)} fusion(f32[2048,1536]{1,0:T(8,128)S(1)} %get-tuple-element.20, f32[1536]{0:T(1024)S(1)} %get-tuple-element.19, pred[2048]{0:T(1024)(128)(4,1)S(1)} %fusion.15), kind=kLoop, calls=%fused_computation.7 | loop fusion | flops 12581376 | bytes 12597248 | tf_op jit(solution)/shard_map/reduce_sum | solution.py:48
  78.1 0.0 copy-start.4
  78.1 3.5 %divide_convert_fusion = bf16[2048,1536]{1,0:T(8,128)(2,1)S(1)} fusion(f32[2048,1536]{1,0:T(8,128)S(1)} %get-tuple-element.20, f32[1536]{0:T(1024)S(1)} %fusion.1, f32[1536]{0:T(1024)S(1)} %get-tuple-element.19, pred[2048]{0:T(1024)(128)(4,1)S(1)} %fusion.15), kind=kLoop, calls=%fused_computation.1 | loop fusion | flops 15728640 | bytes 18888704 | tf_op jit(solution)/shard_map/convert_element_type | solution.py:49
  81.7 0.0 copy-done.1
  81.7 0.0 copy-done.4
  81.7 4.7 %multiply_reduce_fusion = (f32[1536]{0:T(1024)S(1)}, bf16[1536,512]{1,0:T(8,128)(2,1)}) fusion(bf16[96,16,512]{2,1,0:T(8,128)(2,1)S(1)} %copy-done.4, bf16[2048,1536]{1,0:T(8,128)(2,1)S(1)} %divide_convert_fusion, bf16[2048,576]{1,0:T(8,128)(2,1)S(1)} %bitcast.58), kind=kOutput, calls=%fused_computation.10 | convolution fusion | flops 3225156096 | bytes 11540480 | tf_op jit(solution)/shard_map/dot_general | solution.py:51
  86.3 0.0 copy-start.2
  86.3 0.0 copy-start.5
  86.3 5.1 %fusion.25 = f32[2048,512]{0,1:T(8,128)} fusion(bf16[2048,1536]{1,0:T(8,128)(2,1)S(1)} %divide_convert_fusion, bf16[1536,512]{1,0:T(8,128)(2,1)S(1)} %bitcast.66), kind=kOutput, calls=%fused_computation.60 | convolution fusion | flops 3221225472 | bytes 12058624 | tf_op jit(solution)/shard_map/dot_general | solution.py:63
  91.4 0.0 copy-done.2
  91.4 0.0 copy-done.5
  91.4 4.1 %multiply_convert_fusion = bf16[2048,1536]{1,0:T(8,128)(2,1)S(1)} fusion(bf16[2048,1536]{1,0:T(8,128)(2,1)S(1)} %divide_convert_fusion, bf16[1536,512]{1,0:T(8,128)(2,1)S(1)} %bitcast.67, f32[1536]{0:T(1024)S(1)} %get-tuple-element.21, bf16[2048,576]{1,0:T(8,128)(2,1)S(1)} %bitcast.60), kind=kOutput, calls=%fused_computation | convolution fusion | flops 3236954112 | bytes 16261120 | tf_op jit(solution)/shard_map/dot_general | solution.py:52
  95.6 0.0 copy-start.6
  95.6 2.6 %copy-done.6 = bf16[2048,1536]{1,0:T(8,128)(2,1)} copy-done((bf16[2048,1536]{1,0:T(8,128)(2,1)}, bf16[2048,1536]{1,0:T(8,128)(2,1)S(1)}, u32[]{:S(2)}) %copy-start.6) | copy-done | bytes 6291480
  98.2 6.8 %add_convert_fusion = bf16[2048,576]{0,1:T(8,128)(2,1)} fusion(f32[2048,512]{0,1:T(8,128)} %fusion.25, bf16[2048,1536]{1,0:T(8,128)(2,1)S(1)} %multiply_convert_fusion, bf16[1536,576]{1,0:T(8,128)(2,1)S(1)} %bitcast.55), kind=kOutput, calls=%fused_computation.9 | convolution fusion | flops 3626237952 | bytes 14614528 | tf_op jit(solution)/shard_map/dot_general | solution.py:62
  105.0 4.4 %copy.29 = bf16[2048,576]{1,0:T(8,128)(2,1)} copy(bf16[2048,576]{0,1:T(8,128)(2,1)} %add_convert_fusion) | data formatting | bytes 4718592 | tf_op jit(solution)/shard_map/convert_element_type | solution.py:129
  109.4 3.6 %copy.30 = bf16[8,16,16,576]{3,2,1,0:T(8,128)(2,1)} copy(bf16[8,16,16,576]{3,2,0,1:T(8,128)(2,1)} %bitcast.56) | data formatting | bytes 4718592 | tf_op jit(solution)/shard_map/transpose | solution.py:34
  112.9 4.4 %all-to-all-start.2 = ((bf16[8,16,16,576]{3,2,1,0:T(8,128)(2,1)}), bf16[8,16,16,576]{3,2,1,0:T(8,128)(2,1)}, u32[]{:S(2)}, u32[]{:S(2)}) async-start(bf16[8,16,16,576]{3,2,1,0:T(8,128)(2,1)} %copy.30), calls=%async_computation.2 | async-start | bytes 5242880 | tf_op jit(solution)/shard_map/all_to_all | solution.py:39
  117.4 32.8 %all-to-all-done.2 = bf16[8,16,16,576]{3,2,1,0:T(8,128)(2,1)} async-done(((bf16[8,16,16,576]{3,2,1,0:T(8,128)(2,1)}), bf16[8,16,16,576]{3,2,1,0:T(8,128)(2,1)}, u32[]{:S(2)}, u32[]{:S(2)}) %all-to-all-start.2) | async-done | bytes 2359328 | tf_op jit(solution)/shard_map/all_to_all | solution.py:39
  150.2 2.2 %convert_reduce_fusion = f32[16,16,576]{2,1,0:T(8,128)S(1)} fusion(bf16[8,16,16,576]{3,2,1,0:T(8,128)(2,1)} %all-to-all-done.2), kind=kLoop, calls=%fused_computation.8 | loop fusion | flops 2211840 | bytes 2949120 | tf_op jit(solution)/shard_map/reduce_sum | solution.py:40
  152.4 0.2 reshape.171
  152.6 0.2 dot_general.47
  152.8 0.8 convolution_convert_fusion.4
  153.6 1.0 copy.32
  154.6 3.9 %all-to-all-start.3 = ((bf16[16,2,16,576]{3,2,1,0:T(8,128)(2,1)}), bf16[16,2,16,576]{3,2,1,0:T(8,128)(2,1)S(1)}, u32[]{:S(2)}, u32[]{:S(2)}) async-start(bf16[16,2,16,576]{3,2,1,0:T(8,128)(2,1)} %copy.32), calls=%async_computation.3 | async-start | bytes 1310720 | tf_op jit(solution)/shard_map/all_to_all | solution.py:136
  158.4 8.7 %convolution_convert_fusion.2 = bf16[1536,576]{0,1:T(8,128)(2,1)} fusion(bf16[2048,1536]{1,0:T(8,128)(2,1)} %copy-done.6, bf16[2048,576]{1,0:T(8,128)(2,1)} %bitcast.59), kind=kOutput, calls=%fused_computation.11 | convolution fusion | flops 3624763392 | bytes 10420224 | tf_op jit(solution)/shard_map/dot_general | solution.py:59
  167.1 3.9 %copy.28 = bf16[1536,576]{1,0:T(8,128)(2,1)} copy(bf16[1536,576]{0,1:T(8,128)(2,1)} %convolution_convert_fusion.2) | data formatting | bytes 3538944 | tf_op jit(solution)/shard_map/convert_element_type | solution.py:59
  171.0 0.0 all-to-all-done.3
  171.0 0.5 reshape.172
  171.6 0.5 dot_general.50
  172.1 0.5 fusion.5
  172.6 1.0 copy.35
  (5 shorter events, 0.1 us)
Async XLA Ops:
  0.6 68.6 %copy-start = (bf16[96,16,576]{2,1,0:T(8,128)(2,1)S(1)}, bf16[96,16,576]{2,1,0:T(8,128)(2,1)}, u32[]{:S(2)}) copy-start(bf16[96,16,576]{2,1,0:T(8,128)(2,1)} %param.6) | copy-start | bytes 5308420
  6.0 21.1 %all-to-all-start = ((bf16[16,2,16,576]{3,2,1,0:T(8,128)(2,1)}), bf16[16,2,16,576]{3,2,1,0:T(8,128)(2,1)S(1)}, u32[]{:S(2)}, u32[]{:S(2)}) async-start(bf16[16,2,16,576]{3,2,1,0:T(8,128)(2,1)} %reshape.164), calls=%async_computation | async-start | bytes 1310720 | tf_op jit(solution)/shard_map/all_to_all | solution.py:112
  28.2 7.0 %copy-start.3 = (s32[256]{0:T(256)S(1)}, s32[256]{0:T(256)}, u32[]{:S(2)}) copy-start(s32[256]{0:T(256)} %param.11) | copy-start | bytes 3076
  29.9 37.2 %all-to-all-start.1 = ((bf16[8,16,16,576]{3,2,1,0:T(8,128)(2,1)}), bf16[8,16,16,576]{3,2,1,0:T(8,128)(2,1)}, u32[]{:S(2)}, u32[]{:S(2)}) async-start(bf16[8,16,16,576]{3,2,1,0:T(8,128)(2,1)} %broadcast_in_dim.28), calls=%async_computation.1 | async-start | bytes 5242880 | tf_op jit(solution)/shard_map/all_to_all | solution.py:24
  69.2 12.5 %copy-start.1 = (bf16[16,8,16,576]{3,2,1,0:T(8,128)(2,1)}, bf16[16,8,16,576]{3,2,1,0:T(8,128)(2,1)S(1)}, u32[]{:S(2)}) copy-start(bf16[16,8,16,576]{3,2,1,0:T(8,128)(2,1)S(1)} %copy.27) | copy-start | bytes 7077892
  78.1 3.6 %copy-start.4 = (bf16[96,16,512]{2,1,0:T(8,128)(2,1)S(1)}, bf16[96,16,512]{2,1,0:T(8,128)(2,1)}, u32[]{:S(2)}) copy-start(bf16[96,16,512]{2,1,0:T(8,128)(2,1)} %param.7) | copy-start | bytes 4718596
  86.3 5.1 %copy-start.2 = (bf16[16,8,16,576]{3,2,1,0:T(8,128)(2,1)S(1)}, bf16[16,8,16,576]{3,2,1,0:T(8,128)(2,1)}, u32[]{:S(2)}) copy-start(bf16[16,8,16,576]{3,2,1,0:T(8,128)(2,1)} %copy-done.1) | copy-start | bytes 7077892
  86.3 5.1 %copy-start.5 = (bf16[96,16,512]{2,1,0:T(8,128)(2,1)S(1)}, bf16[96,16,512]{2,1,0:T(8,128)(2,1)}, u32[]{:S(2)}) copy-start(bf16[96,16,512]{2,1,0:T(8,128)(2,1)} %param.7) | copy-start | bytes 4718596
  95.6 2.6 %copy-start.6 = (bf16[2048,1536]{1,0:T(8,128)(2,1)}, bf16[2048,1536]{1,0:T(8,128)(2,1)S(1)}, u32[]{:S(2)}) copy-start(bf16[2048,1536]{1,0:T(8,128)(2,1)S(1)} %multiply_convert_fusion) | copy-start | bytes 18874372
  112.9 37.2 %all-to-all-start.2 = ((bf16[8,16,16,576]{3,2,1,0:T(8,128)(2,1)}), bf16[8,16,16,576]{3,2,1,0:T(8,128)(2,1)}, u32[]{:S(2)}, u32[]{:S(2)}) async-start(bf16[8,16,16,576]{3,2,1,0:T(8,128)(2,1)} %copy.30), calls=%async_computation.2 | async-start | bytes 5242880 | tf_op jit(solution)/shard_map/all_to_all | solution.py:39
  154.6 16.4 %all-to-all-start.3 = ((bf16[16,2,16,576]{3,2,1,0:T(8,128)(2,1)}), bf16[16,2,16,576]{3,2,1,0:T(8,128)(2,1)S(1)}, u32[]{:S(2)}, u32[]{:S(2)}) async-start(bf16[16,2,16,576]{3,2,1,0:T(8,128)(2,1)} %copy.32), calls=%async_computation.3 | async-start | bytes 1310720 | tf_op jit(solution)/shard_map/all_to_all | solution.py:136
where the time goes:
time: 175 us; the launch traced here: 174 us
  waiting for transfers between devices  77.3 us (44%)
  matrix products  36.7 us (21%)
  local copies, waits for them, and re-layouts  26 us (15%)
  starting transfers between devices  21 us (12%)
  other arithmetic  11.7 us (7%)
    all_to_all x1, waiting for transfers between devices, sent_and_summed(): parts = lax.all_to_all(cut_along(x, dim, devices), axis, 0, 0, tiled=True)  32.8 us
    all_to_all x1, waiting for transfers between devices, from_everyone(): lax.all_to_all(jnp.broadcast_to(x[None], (devices, *x.shape)), axis, 0, 0...  31.7 us
    all_to_all x1, waiting for transfers between devices, per_device(): lax.all_to_all(outgoing, 'req', split_axis=0, concat_axis=0, tiled=True)  12.9 us
    dot_general x1, matrix products, attend(): jnp.dot(score_grads, key_rows, preferred_element_type=jnp.float32)  8.68 us
    all_to_all x1, starting transfers between devices, per_device(): lax.all_to_all(outgoing, 'req', split_axis=0, concat_axis=0, tiled=True)  8.16 us
    dot_general x1, matrix products, attend(): jnp.dot(score_grads.T, query_rows, preferred_element_type=jnp.float32)  6.77 us
    dot_general x1, matrix products, attend(): jnp.dot(query_rows, key_rows.T, preferred_element_type=jnp.float32)  5.54 us
    dot_general x1, matrix products, attend(): jnp.dot(weights.T, cotangent, preferred_element_type=jnp.float32)  5.06 us
  transfers between devices with their start and end apart: 4, of which 3 were waited for; matrix products, arithmetic and copies ran while one was open for 8% of the time, Pallas kernels for 0%

commit v1 on v0

v1 whole, which is shorter than its diff:
```python
import functools
import math

import jax
import jax.numpy as jnp
from jax import lax
from jax.experimental import pallas as pl
from jax.experimental.pallas import tpu as pltpu
from jax.sharding import PartitionSpec as P

LAT = 512
WIDE = 576
BLOCK = 128
MAXL = 16
CAP = 2
BIG = -1e30
SCALE = 192.0 ** (-0.5)
EXPC = SCALE * math.log2(math.e)
NT = (((1,), (1,)), ((), ()))
NN = (((1,), (0,)), ((), ()))
f32 = jnp.float32
bf16 = jnp.bfloat16


def dot(a, b, dims=NN):
    return lax.dot_general(a, b, dims, preferred_element_type=f32)


def whole(shape):
    rank = len(shape)
    return pl.BlockSpec(shape, lambda *_: (0,) * rank)


def pick_body(lists, counts, me, lat_ref, out_ref):
    own = me[0]

    def group(g, carry):
        def entry(j, rank):
            block = lists[g, j]
            mine = (block // MAXL) == own

            @pl.when(mine)
            def _():
                out_ref[g * CAP + jnp.minimum(rank, CAP - 1)] = lat_ref[lax.rem(block, MAXL)]

            return rank + mine.astype(jnp.int32)

        lax.fori_loop(0, counts[g], entry, jnp.int32(0))
        return carry

    lax.fori_loop(0, 16, group, 0)


def slots_of(lists, counts, me, seen, visit):
    own = me[0]

    def clear(o, carry):
        seen[o] = 0
        return carry

    lax.fori_loop(0, 16, clear, 0)

    def entry(j, carry):
        owner = lists[own, j] // MAXL
        rank = seen[owner]
        seen[owner] = rank + 1
        visit(j, owner * CAP + jnp.minimum(rank, CAP - 1))
        return carry

    lax.fori_loop(0, counts[own], entry, 0)


def take_body(lists, counts, me, arrived_ref, out_ref, seen):
    def visit(j, slot):
        out_ref[j] = arrived_ref[slot]

    slots_of(lists, counts, me, seen, visit)

    def blank(j, carry):
        out_ref[j] = jnp.zeros(out_ref.shape[1:], out_ref.dtype)
        return carry

    lax.fori_loop(counts[me[0]], MAXL, blank, 0)


def put_body(lists, counts, me, a_ref, b_ref, c_ref, d_ref, out_ref, seen):
    def visit(j, slot):
        total = a_ref[j].astype(f32) + b_ref[j].astype(f32)
        total = total + c_ref[j].astype(f32) + d_ref[j].astype(f32)
        out_ref[slot] = total.astype(out_ref.dtype)

    slots_of(lists, counts, me, seen, visit)


def gather_body(lists, counts, me, arrived_ref, out_ref):
    own = me[0]
    out_ref[...] = jnp.zeros(out_ref.shape, out_ref.dtype)

    def group(g, carry):
        def entry(j, rank):
            block = lists[g, j]
            mine = (block // MAXL) == own

            @pl.when(mine)
            def _():
                at = lax.rem(block, MAXL)
                out_ref[at] = out_ref[at] + arrived_ref[g * CAP + jnp.minimum(rank, CAP - 1)].astype(f32)

            return rank + mine.astype(jnp.int32)

        lax.fori_loop(0, counts[g], entry, jnp.int32(0))
        return carry

    lax.fori_loop(0, 16, group, 0)


def listed_call(body, out_shape, scalars, *arrays, scratch=()):
    return pl.pallas_call(
        body,
        grid_spec=pltpu.PrefetchScalarGridSpec(
            num_scalar_prefetch=3,
            grid=(1,),
            in_specs=[whole(a.shape) for a in arrays],
            out_specs=whole(out_shape.shape),
            scratch_shapes=list(scratch),
        ),
        out_shape=out_shape,
    )(*scalars, *arrays)


def forward_body(nkeys, first, last, *refs):
    refs = list(refs)
    key_refs = [refs.pop(0) for _ in range(nkeys)]
    bias, q_ref, g_ref = refs[:3]
    refs = refs[3:]
    if not first:
        m_in, l_in, r_in, o_in = refs[:4]
        refs = refs[4:]
    e_out, p_out, m_out, l_out, r_out, o_out, keys = refs

    @pl.when(pl.program_id(0) == 0)
    def _():
        at = 0
        for ref in key_refs:
            keys[at : at + ref.shape[0]] = ref[...]
            at += ref.shape[0]

    rows = q_ref.shape[0]
    scores = dot(q_ref[...], keys[...], NT) + bias[...]
    top = jnp.max(scores, axis=1, keepdims=True)
    if not first:
        m_old = m_in[:, :1]
        top = jnp.maximum(top, m_old)
    expo = jnp.exp2((scores - top) * EXPC)
    values = keys[:, :LAT]
    grads = dot(g_ref[...], values, NT)
    total = jnp.sum(expo, axis=1, keepdims=True)
    rdot = jnp.sum(expo * grads, axis=1, keepdims=True)
    expo = expo.astype(bf16)
    e_out[...] = expo
    p_out[...] = grads.astype(bf16)
    attended = dot(expo, values)
    if not first:
        fade = jnp.exp2((m_old - top) * EXPC)
        total = total + fade * l_in[:, :1]
        rdot = rdot + fade * r_in[:, :1]
        attended = attended + fade * o_in[...]
    if last:
        total = 1.0 / total
        rdot = rdot * total
        attended = attended * total
    m_out[...] = jnp.broadcast_to(top, (rows, 128))
    l_out[...] = jnp.broadcast_to(total, (rows, 128))
    r_out[...] = jnp.broadcast_to(rdot, (rows, 128))
    o_out[...] = attended.astype(o_out.dtype)


def forward(key_parts, bias, q, g, state, last, block=256):
    n = bias.shape[1]
    rows = q.shape[0]
    first = state is None
    by_row = lambda width: pl.BlockSpec((block, width), lambda i: (i, 0))
    in_specs = [whole(k.shape) for k in key_parts] + [whole((1, n)), by_row(WIDE), by_row(LAT)]
    args = [*key_parts, bias, q, g]
    if not first:
        in_specs += [by_row(128)] * 3 + [by_row(LAT)]
        args += list(state)
    stat = jax.ShapeDtypeStruct((rows, 128), f32)
    side = jax.ShapeDtypeStruct((rows, n), bf16)
    out_shape = (side, side, stat, stat, stat, jax.ShapeDtypeStruct((rows, LAT), bf16 if last else f32))
    return pl.pallas_call(
        functools.partial(forward_body, len(key_parts), first, last),
        grid=(rows // block,),
        in_specs=in_specs,
        out_specs=(by_row(n), by_row(n), by_row(128), by_row(128), by_row(128), by_row(LAT)),
        out_shape=out_shape,
        scratch_shapes=[pltpu.VMEM((n, WIDE), bf16)],
        cost_estimate=pl.CostEstimate(
            flops=2 * rows * n * (WIDE + 2 * LAT), transcendentals=rows * n, bytes_accessed=8 * rows * n
        ),
    )(*args)


def backward_body(half, step, qt_ref, gt_ref, e_ref, p_ref, mc_ref, m_ref, l_ref, r_ref, far_out, near_out, s_out, a_sc, r_sc):
    i = pl.program_id(0)
    rows = qt_ref.shape[1]

    @pl.when(i == 0)
    def _():
        a_sc[...] = jnp.exp2((mc_ref[...] - m_ref[...]) * EXPC) * l_ref[...]
        r_sc[...] = r_ref[...]

    width = e_ref.shape[1]
    acc = None
    for at in range(0, rows, step):
        here = slice(at, at + step)
        a = jnp.tile(a_sc[here], (1, width // 128))
        r = jnp.tile(r_sc[here], (1, width // 128))
        weights = (e_ref[here].astype(f32) * a).astype(bf16)
        sg = (weights.astype(f32) * (p_ref[here].astype(f32) - r) * SCALE).astype(bf16)
        s_out[here] = sg
        key_part = dot(qt_ref[:, here], sg)
        value_part = dot(gt_ref[:, here], weights)
        if acc is None:
            acc = [key_part[:LAT] + value_part, key_part[LAT:]]
        else:
            acc = [acc[0] + (key_part[:LAT] + value_part), acc[1] + key_part[LAT:]]
    top = acc[0].T.astype(bf16)
    low = jnp.concatenate([acc[1], jnp.zeros_like(acc[1])], axis=0).T[:, : WIDE - LAT].astype(bf16)

    def write(ref):
        ref[:, :LAT] = top
        ref[:, LAT:] = low

    @pl.when(i < half)
    def _():
        write(far_out)

    @pl.when(i >= half)
    def _():
        write(near_out)


def backward(qt, gt, e, p, mc, m, linv, r, tile=256):
    rows, n = e.shape
    steps = n // tile
    half = steps // 2
    where = lambda i: lax.rem(i + half, steps)
    part = jax.ShapeDtypeStruct((n // 2, WIDE), bf16)
    by_key = pl.BlockSpec((rows, tile), lambda i: (0, where(i)))
    stat = whole((rows, 128))
    return pl.pallas_call(
        functools.partial(backward_body, half, 256),
        grid=(steps,),
        in_specs=[whole(qt.shape), whole(gt.shape), by_key, by_key, stat, stat, stat, stat],
        out_specs=(
            pl.BlockSpec((tile, WIDE), lambda i: (jnp.minimum(i, half - 1), 0)),
            pl.BlockSpec((tile, WIDE), lambda i: (jnp.maximum(i - half, 0), 0)),
            by_key,
        ),
        out_shape=(part, part, jax.ShapeDtypeStruct((rows, n), bf16)),
        scratch_shapes=[pltpu.VMEM((rows, 128), f32)] * 2,
        cost_estimate=pl.CostEstimate(
            flops=2 * rows * n * (WIDE + LAT), transcendentals=0, bytes_accessed=6 * rows * n
        ),
    )(qt, gt, e, p, mc, m, linv, r)


def query_body(counts, *refs):
    refs = list(refs)
    chunks = len(counts)
    s_refs = [refs.pop(0) for _ in range(chunks)]
    k_refs = [[refs.pop(0) for _ in range(c)] for c in counts]
    out_ref, keys = refs

    @pl.when(pl.program_id(0) == 0)
    def _():
        at = 0
        for ref in sum(k_refs, []):
            keys[at : at + ref.shape[0]] = ref[...]
            at += ref.shape[0]

    total = None
    at = 0
    for ref in s_refs:
        n = ref.shape[1]
        piece = dot(ref[...], keys[at : at + n])
        total = piece if total is None else total + piece
        at += n
    out_ref[...] = total.astype(out_ref.dtype)


def query_side(sgs, parts, block=256):
    rows = sgs[0].shape[0]
    n = sum(s.shape[1] for s in sgs)
    flat = sum(parts, [])
    return pl.pallas_call(
        functools.partial(query_body, [len(p) for p in parts]),
        grid=(rows // block,),
        in_specs=[pl.BlockSpec((block, s.shape[1]), lambda i: (i, 0)) for s in sgs] + [whole(k.shape) for k in flat],
        out_specs=pl.BlockSpec((block, WIDE), lambda i: (i, 0)),
        out_shape=jax.ShapeDtypeStruct((rows, WIDE), bf16),
        scratch_shapes=[pltpu.VMEM((n, WIDE), bf16)],
        cost_estimate=pl.CostEstimate(flops=2 * rows * n * WIDE, transcendentals=0, bytes_accessed=2 * rows * n),
    )(*sgs, *flat)


def per_device(queries, out_grad, latents, list_blocks, list_counts, valid_tokens):
    me = lax.axis_index("req")
    head = lax.axis_index("head")
    chip, core = head // 2, head % 2
    tokens = latents.shape[1]
    shift = lambda d: [(x * 2 + c, ((x + d) % 4) * 2 + c) for x in range(4) for c in range(2)]
    right, left, sibling = shift(1), shift(-1), [(h, h ^ 1) for h in range(8)]
    send = lambda a, perm: lax.ppermute(a, "head", perm)
    scalars = (list_blocks, list_counts, me.reshape(1).astype(jnp.int32))

    slots = jax.ShapeDtypeStruct((16 * CAP, tokens, WIDE), bf16)
    outgoing = listed_call(pick_body, slots, scalars, latents)
    arrived = lax.all_to_all(outgoing.reshape(16, CAP, tokens, WIDE), "req", 0, 0, tiled=True)
    share = listed_call(
        take_body,
        jax.ShapeDtypeStruct((MAXL, tokens, WIDE), bf16),
        scalars,
        arrived.reshape(slots.shape),
        scratch=[pltpu.SMEM((16,), jnp.int32)],
    ).reshape(MAXL * tokens, WIDE)

    my_blocks = lax.dynamic_index_in_dim(list_blocks, me, 0, keepdims=False)
    my_count = lax.dynamic_index_in_dim(list_counts, me, 0, keepdims=False)
    ids = jnp.arange(valid_tokens.shape[0], dtype=jnp.int32)
    filled = jnp.sum(jnp.where(my_blocks[:, None] == ids[None, :], valid_tokens[None, :], 0), axis=1)
    filled = jnp.where(jnp.arange(MAXL, dtype=jnp.int32) < my_count, filled, 0)
    filled = jnp.repeat(filled, tokens)
    offset = jnp.tile(jnp.arange(tokens, dtype=jnp.int32), MAXL)

    def bias_of(places):
        rows = [jnp.where(place * tokens + offset < filled, 0.0, BIG) for place in places]
        return jnp.concatenate(rows).astype(f32)[None, :]

    at = lambda d, c: ((chip + d) % 4) * 2 + c
    other = 1 - core
    bias0 = bias_of([at(0, core), at(0, other)])
    bias1 = bias_of([at(3, core), at(1, core), at(3, other), at(1, other)])
    bias2 = bias_of([at(2, core), at(2, other)])

    q = queries.reshape(-1, WIDE)
    g = out_grad.reshape(-1, LAT)
    qt = q.T
    gt = g.T

    keep = MAXL * tokens // 2
    r1 = send(share, right)
    l1 = send(share, left)
    s0 = send(share, sibling)
    r2 = send(r1[:keep], right)
    l2 = send(l1[keep:], left)
    s1 = send(r1, sibling)
    s2 = send(l1, sibling)
    s3 = send(r2, sibling)
    s4 = send(l2, sibling)
    parts0, parts1, parts2 = [share, s0], [r1, l1, s1, s2], [r2, l2, s3, s4]

    e0, p0, m0, *rest = forward(parts0, bias0, q, g, None, False)
    e1, p1, m1, *rest = forward(parts1, bias1, q, g, (m0, *rest), False)
    e2, p2, m2, linv, rdot, attended = forward(parts2, bias2, q, g, (m1, *rest), True)

    back = functools.partial(backward, qt, gt)
    add = lambda a, b: (a.astype(f32) + b.astype(f32)).astype(bf16)
    far, near, sg2 = back(e2, p2, m2, m2, linv, rdot)
    two = add(near, send(far, sibling))
    from_left = send(two[:keep], right)
    from_right = send(two[keep:], left)
    far, near, sg1 = back(e1, p1, m1, m2, linv, rdot)
    one = add(near, send(far, sibling))
    size = 2 * keep
    to_left = jnp.concatenate([one[:keep], add(one[keep:size], from_right)])
    to_right = jnp.concatenate([add(one[size : size + keep], from_left), one[size + keep :]])
    got_left = send(to_right, right)
    got_right = send(to_left, left)
    far, near, sg0 = back(e0, p0, m0, m2, linv, rdot)
    mate = send(far, sibling)
    fold = lambda a: a.reshape(MAXL, tokens, WIDE)
    slot_grads = listed_call(
        put_body,
        slots,
        scalars,
        fold(near),
        fold(mate),
        fold(got_left),
        fold(got_right),
        scratch=[pltpu.SMEM((16,), jnp.int32)],
    )
    returned = lax.all_to_all(slot_grads.reshape(16, CAP, tokens, WIDE), "req", 0, 0, tiled=True)
    query_grad = query_side([sg2, sg1, sg0], [parts2, parts1, parts0])
    latent_grad = listed_call(
        gather_body, jax.ShapeDtypeStruct((16, tokens, WIDE), f32), scalars, returned.reshape(slots.shape)
    )
    return (attended.reshape(out_grad.shape), query_grad.reshape(queries.shape), latent_grad)


def solution(mesh):
    in_specs = (
        P("req", "head", None),
        P("req", "head", None),
        P("req", "head", None),
        P(),
        P(),
        P(),
    )
    out_specs = (P("req", "head", None), P("req", "head", None), P("req", "head", None))
    return jax.shard_map(
        per_device, mesh=mesh, in_specs=in_specs, out_specs=out_specs, check_vma=False
    )
```

time: 175 us -> 160 us (0.914)
  Pallas kernels: 0 us -> 85.5 us
  waiting for transfers between devices: 77.3 us -> 26 us
  matrix products: 36.7 us -> 0 us
  local copies, waits for them, and re-layouts: 26 us -> 16.4 us
  other arithmetic: 11.7 us -> 3.09 us
  starting transfers between devices: 21 us -> 26.9 us
    pallas_call x0 -> x11, Pallas kernels: none -> 85.5 us  [the longest x3 30 us: forward(): pl.pallas_call(functools.partial(forward_body, len(key_parts), first, las...]
    all_to_all x4 -> x2, waiting for transfers between devices: 77.3 us -> 12.2 us  [the longest x1 10.7 us: per_device(): lax.all_to_all(outgoing.reshape(16, CAP, tokens, WIDE), 'req', 0, 0, tile...]
    dot_general x10 -> x0, matrix products: 36.7 us -> none  [the longest x1 8.68 us: attend(): jnp.dot(score_grads, key_rows, preferred_element_type=jnp.float32)]
    ppermute x0 -> x16, starting transfers between devices: none -> 15.1 us  [per_device(): send = lambda a, perm: lax.ppermute(a, 'head', perm)]
    ppermute x0 -> x16, waiting for transfers between devices: none -> 13.8 us  [per_device(): send = lambda a, perm: lax.ppermute(a, 'head', perm)]
    all_to_all x4 -> x2, starting transfers between devices: 21 us -> 11.7 us  [the longest x1 8.15 us: per_device(): lax.all_to_all(outgoing.reshape(16, CAP, tokens, WIDE), 'req', 0, 0, tile...]
    convert_element_type x3 -> x0, local copies, waits for them, and re-layouts: 9.24 us -> none  [the longest x1 4.41 us: per_device(): head_shares = sent_and_summed(list_grads.astype(jnp.bfloat16), 'head', 1)]
    reduce_sum x5 -> x1, other arithmetic: 6.3 us -> 0.18 us  [per_device(): jnp.sum(jnp.where(my_blocks[:, None] == ids[None, :], valid_tokens[None,...]
  transfers between devices with their start and end apart: 4 -> 18, of which waited for: 3 -> 5; matrix products, arithmetic and copies ran while one was open for 8% -> 9% of each run, Pallas kernels for 0% -> 30%
where the time goes in v1:
time: 160 us; the launch traced here: 159 us
  Pallas kernels  85.5 us (53%)
  starting transfers between devices  26.9 us (17%)
  waiting for transfers between devices  26 us (16%)
  local copies, waits for them, and re-layouts  16.4 us (10%)
  other arithmetic  3.09 us (2%)
    pallas_call x3, Pallas kernels, forward(): pl.pallas_call(functools.partial(forward_body, len(key_parts), first, las...  30 us
    pallas_call x3, Pallas kernels, backward(): pl.pallas_call(functools.partial(backward_body, half, 256), grid=(steps,)...  25 us
    pallas_call x4, Pallas kernels, listed_call(): pl.pallas_call(body, grid_spec=pltpu.PrefetchScalarGridSpec(num_scalar_pr...  20.7 us
    ppermute x16, starting transfers between devices, per_device(): send = lambda a, perm: lax.ppermute(a, 'head', perm)  15.1 us
    ppermute x16, waiting for transfers between devices, per_device(): send = lambda a, perm: lax.ppermute(a, 'head', perm)  13.8 us
    all_to_all x1, waiting for transfers between devices, per_device(): lax.all_to_all(outgoing.reshape(16, CAP, tokens, WIDE), 'req', 0, 0, tile...  10.7 us
    pallas_call x1, Pallas kernels, query_side(): pl.pallas_call(functools.partial(query_body, [len(p) for p in parts]), gr...  9.87 us
    all_to_all x1, starting transfers between devices, per_device(): lax.all_to_all(outgoing.reshape(16, CAP, tokens, WIDE), 'req', 0, 0, tile...  8.15 us
  transfers between devices with their start and end apart: 18, of which 5 were waited for; matrix products, arithmetic and copies ran while one was open for 9% of the time, Pallas kernels for 30%

profile of v1, /device:TPU:0, one launch (start us, length us, event | category | flops | bytes accessed | tf_op | source)
XLA Modules:
  0.0 158.9 jit_solution(16769999272490372939)
XLA Ops:
  0.7 7.0 %shard_map.85 = bf16[32,16,576]{2,1,0:T(8,128)(2,1)} custom-call(s32[16,16]{1,0:T(8,128)} %lists.7, s32[16]{0:T(128)} %counts.7, s32[1]{0:T(128)} %bitcast.me, bf16[16,16,576]{2,1,0:T(8,128)(2,1)} %lat_ref.1), custom_call_target="tpu_custom_call" | custom-call | tf_op jit(solution)/shard_map/pallas_call | solution.py:118
  7.6 8.1 %all-to-all-start = ((bf16[16,2,16,576]{3,2,1,0:T(8,128)(2,1)}), bf16[16,2,16,576]{3,2,1,0:T(8,128)(2,1)S(1)}, u32[]{:S(2)}, u32[]{:S(2)}) async-start(bf16[16,2,16,576]{3,2,1,0:T(8,128)(2,1)} %bitcast.38), calls=%async_computation | async-start | bytes 1310720 | tf_op jit(solution)/shard_map/all_to_all | solution.py:320
  15.9 0.6 dynamic_slice.8
  16.5 0.7 dynamic-slice_bitcast_fusion
  17.2 0.2 select_reduce_fusion
  17.4 0.7 compare_select_fusion
  18.0 10.7 %all-to-all-done = bf16[16,2,16,576]{3,2,1,0:T(8,128)(2,1)S(1)} async-done(((bf16[16,2,16,576]{3,2,1,0:T(8,128)(2,1)}), bf16[16,2,16,576]{3,2,1,0:T(8,128)(2,1)S(1)}, u32[]{:S(2)}, u32[]{:S(2)}) %all-to-all-start) | async-done | bytes 589856 | tf_op jit(solution)/shard_map/all_to_all | solution.py:320
  28.7 0.8 copy-done.2
  29.5 2.8 %shard_map.86 = bf16[16,16,576]{2,1,0:T(8,128)(2,1)} custom-call(s32[16,16]{1,0:T(8,128)} %lists.7, s32[16]{0:T(128)} %counts.7, s32[1]{0:T(128)} %bitcast.me, bf16[32,16,576]{2,1,0:T(8,128)(2,1)} %bitcast.37), custom_call_target="tpu_custom_call" | custom-call | tf_op jit(solution)/shard_map/pallas_call | solution.py:118
  32.4 1.5 collective-permute-start
  33.9 1.7 %collective-permute-start.2 = (bf16[256,576]{1,0:T(8,128)(2,1)}, bf16[256,576]{1,0:T(8,128)(2,1)}, u32[]{:S(2)}, u32[]{:S(2)}) collective-permute-start(bf16[256,576]{1,0:T(8,128)(2,1)} %bitcast.41), channel_id=1, source_target_pairs={{0,6},{1,7},{2,0},{3,1},{4,2},{5,3},{6,4},{7,5},{8,14},{9,15},{10,... | collective-permute-start | bytes 884744 | tf_op jit(solution)/shard_map/ppermute | solution.py:315
  35.7 0.1 select_n.120
  35.8 0.1 select_n.122
  35.8 0.7 select_n.110
  36.5 0.7 select_n.113
  37.2 0.6 select_n.115
  37.8 0.6 select_n.117
  38.5 0.1 select_n.105
  38.5 0.1 select_n.107
  38.6 2.2 %copy.23 = bf16[1536,576]{0,1:T(8,128)(2,1)} copy(bf16[1536,576]{1,0:T(8,128)(2,1)S(1)} %bitcast.31) | data formatting | bytes 3538944 | tf_op jit(solution)/shard_map/reshape | solution.py:347
  40.9 1.6 copy.24
  42.5 0.6 pad_maximum_fusion.4
  43.1 0.6 pad_maximum_fusion.2
  43.7 0.5 collective-permute-start.6
  44.2 0.1 collective-permute-start.7
  44.3 0.6 pad_maximum_fusion.3
  44.9 0.9 slice.32
  45.8 0.3 collective-permute-start.1
  46.2 0.9 slice.33
  47.1 3.0 %collective-permute-start.3 = (bf16[128,576]{1,0:T(8,128)(2,1)S(1)}, bf16[128,576]{1,0:T(8,128)(2,1)S(1)}, u32[]{:S(2)}, u32[]{:S(2)}) collective-permute-start(bf16[128,576]{1,0:T(8,128)(2,1)S(1)} %slice.33), channel_id=1, source_target_pairs={{0,6},{1,7},{2,0},{3,1},{4,2},{5,3},{6,4},{7,5},{8,14},{9,15},{10,... | collective-permute-start | bytes 442376 | tf_op jit(solution)/shard_map/ppermute | solution.py:315
  50.1 0.7 copy-done.20
  50.9 8.0 %shard_map.87 = (bf16[1536,512]{1,0:T(8,128)(2,1)}, bf16[1536,512]{1,0:T(8,128)(2,1)}, f32[1536,128]{1,0:T(8,128)}, f32[1536,128]{1,0:T(8,128)}, f32[1536,128]{1,0:T(8,128)}, /*index=5*/f32[1536,512]{1,0:T(8,128)}) custom-call(bf16[256,576]{1,0:T(8,128)(2,1)} %bitcast.42, bf16[256,576]{1,0:T(8,128)(2,1)} %copy-done.20, f32[1,512]{1,0:T(1,128)} %bitcast.51, ...), custom_call_target="tpu_custom_call" | custom-call | flops 2516582400 | bytes 6291456 | tf_op jit(solution)/shard_map/pallas_call | solution.py:191
  58.9 0.1 collective-permute-start.4
  59.0 0.5 collective-permute-start.5
  59.5 0.8 copy-done.21
  60.3 0.1 copy-done.22
  60.4 12.6 %shard_map.88 = (bf16[1536,1024]{1,0:T(8,128)(2,1)}, bf16[1536,1024]{1,0:T(8,128)(2,1)}, f32[1536,128]{1,0:T(8,128)}, f32[1536,128]{1,0:T(8,128)}, f32[1536,128]{1,0:T(8,128)}, /*index=5*/f32[1536,512]{1,0:T(8,128)}) custom-call(bf16[256,576]{1,0:T(8,128)(2,1)} %collective-permute-done.refs_0_.refs_7_, ...), custom_call_target="tpu_custom_call" | custom-call | flops 5033164800 | bytes 12582912 | tf_op jit(solution)/shard_map/pallas_call | solution.py:191
  73.1 0.7 copy-done.12
  73.8 9.4 %shard_map.89 = (bf16[1536,512]{1,0:T(8,128)(2,1)}, bf16[1536,512]{1,0:T(8,128)(2,1)}, f32[1536,128]{1,0:T(8,128)}, f32[1536,128]{1,0:T(8,128)}, f32[1536,128]{1,0:T(8,128)}, /*index=5*/bf16[1536,512]{1,0:T(8,128)(2,1)}) custom-call(bf16[128,576]{1,0:T(8,128)(2,1)} %copy-done.10, bf16[128,576]{1,0:T(8,128)(2,1)} %copy-done.11, bf16[128,576]{1,0:T(8,128)(2,1)} %copy-done.12, ...), custom_call_target="tpu_custom_call" | custom-call | flops 2516582400 | bytes 6291456 | tf_op jit(solution)/shard_map/pallas_call | solution.py:191
  83.2 7.6 %shard_map.90 = (bf16[256,576]{1,0:T(8,128)(2,1)}, bf16[256,576]{1,0:T(8,128)(2,1)}, bf16[1536,512]{1,0:T(8,128)(2,1)}) custom-call(bf16[576,1536]{1,0:T(8,128)(2,1)} %bitcast.22, bf16[512,1536]{1,0:T(8,128)(2,1)} %bitcast.25, bf16[1536,512]{1,0:T(8,128)(2,1)} %get-tuple-element.39.e_ref, bf16[1536,512]{1,0:T(8,128)(2,1)} %get-tuple-element.40.p_ref, ...), custom_call_target="tpu_custom_call" | custom-call | flops 1711276032 | bytes 4718592 | tf_op jit(solution)/shard_map/pallas_call | solution.py:252
  90.8 0.1 collective-permute-start.11
  90.9 10.2 %shard_map.91 = (bf16[512,576]{1,0:T(8,128)(2,1)}, bf16[512,576]{1,0:T(8,128)(2,1)}, bf16[1536,1024]{1,0:T(8,128)(2,1)}) custom-call(bf16[576,1536]{1,0:T(8,128)(2,1)} %bitcast.23, bf16[512,1536]{1,0:T(8,128)(2,1)} %bitcast.26, bf16[1536,1024]{1,0:T(8,128)(2,1)} %get-tuple-element.45.e_ref, bf16[1536,1024]{1,0:T(8,128)(2,1)} %get-tuple-element.46.p_ref, ...), custom_call_target="tpu_custom_call" | custom-call | flops 3422552064 | bytes 9437184 | tf_op jit(solution)/shard_map/pallas_call | solution.py:252
  101.1 1.3 copy.25
  102.4 0.7 collective-permute-start.10
  103.1 7.2 %shard_map.92 = (bf16[256,576]{1,0:T(8,128)(2,1)}, bf16[256,576]{1,0:T(8,128)(2,1)}, bf16[1536,512]{1,0:T(8,128)(2,1)}) custom-call(bf16[576,1536]{1,0:T(8,128)(2,1)} %bitcast.24, bf16[512,1536]{1,0:T(8,128)(2,1)} %bitcast.27, bf16[1536,512]{1,0:T(8,128)(2,1)} %get-tuple-element.48.e_ref, bf16[1536,512]{1,0:T(8,128)(2,1)} %get-tuple-element.49.p_ref, ...), custom_call_target="tpu_custom_call" | custom-call | flops 1711276032 | bytes 4718592 | tf_op jit(solution)/shard_map/pallas_call | solution.py:252
  110.3 0.2 collective-permute-start.9
  110.5 0.1 add_convert_fusion.1
  110.6 0.1 collective-permute-start.12
  110.7 3.2 %collective-permute-start.14 = (bf16[128,576]{1,0:T(8,128)(2,1)S(1)}, bf16[128,576]{1,0:T(8,128)(2,1)S(1)}, u32[]{:S(2)}, u32[]{:S(2)}) collective-permute-start(bf16[128,576]{1,0:T(8,128)(2,1)S(1)} %get-tuple-element.61), channel_id=1, source_target_pairs={{0,6},{1,7},{2,0},{3,1},{4,2},{5,3},{6,4},{7,5},{8,14},{9,15},{10,... | collective-permute-start | bytes 442376 | tf_op jit(solution)/shard_map/ppermute | solution.py:315
  113.9 0.3 copy.26
  114.2 0.2 add_convert_fusion
  114.4 4.0 %collective-permute-done.12 = bf16[128,576]{1,0:T(8,128)(2,1)S(1)} collective-permute-done((bf16[128,576]{1,0:T(8,128)(2,1)S(1)}, bf16[128,576]{1,0:T(8,128)(2,1)S(1)}, u32[]{:S(2)}, u32[]{:S(2)}) %collective-permute-start.12) | collective-permute-done | bytes 147488 | tf_op jit(solution)/shard_map/ppermute | solution.py:315
  118.4 0.1 add_convert_fusion.2
  118.5 3.0 %collective-permute-start.15 = (bf16[256,576]{1,0:T(8,128)(2,1)S(1)}, bf16[256,576]{1,0:T(8,128)(2,1)S(1)}, u32[]{:S(2)}, u32[]{:S(2)}) collective-permute-start(bf16[256,576]{1,0:T(8,128)(2,1)S(1)} %pad_maximum_fusion.1), channel_id=1, source_target_pairs={{0,6},{1,7},{2,0},{3,1},{4,2},{5,3},{6,4},{7,5},{8,14},{9,15},{10,... | collective-permute-start | bytes 884744 | tf_op jit(solution)/shard_map/ppermute | solution.py:315
  121.6 0.1 collective-permute-start.13
  121.7 6.3 %collective-permute-done.15 = bf16[256,576]{1,0:T(8,128)(2,1)S(1)} collective-permute-done((bf16[256,576]{1,0:T(8,128)(2,1)S(1)}, bf16[256,576]{1,0:T(8,128)(2,1)S(1)}, u32[]{:S(2)}, u32[]{:S(2)}) %collective-permute-start.15) | collective-permute-done | bytes 294944 | tf_op jit(solution)/shard_map/ppermute | solution.py:315
  127.9 3.5 %collective-permute-done.13 = bf16[256,576]{1,0:T(8,128)(2,1)S(1)} collective-permute-done((bf16[256,576]{1,0:T(8,128)(2,1)S(1)}, bf16[256,576]{1,0:T(8,128)(2,1)S(1)}, u32[]{:S(2)}, u32[]{:S(2)}) %collective-permute-start.13) | collective-permute-done | bytes 294944 | tf_op jit(solution)/shard_map/ppermute | solution.py:315
  131.4 0.7 copy-done.8
  132.2 3.2 %shard_map.94 = bf16[32,16,576]{2,1,0:T(8,128)(2,1)} custom-call(s32[16,16]{1,0:T(8,128)} %lists.7, s32[16]{0:T(128)} %counts.7, s32[1]{0:T(128)} %bitcast.me, bf16[16,16,576]{2,1,0:T(8,128)(2,1)} %bitcast.45, bf16[16,16,576]{2,1,0:T(8,128)(2,1)} %bitcast.46, bf16[16,16,576]{2,1,0:T(8,128)(2,1)} %bitcast.48, bf16[16,16,576]{2,1,0:T(8,128)(2,1)} %bitcast.47), custom_call_target="tpu_custom_call" | custom-call | tf_op jit(solution)/shard_map/pallas_call | solution.py:118
  135.3 3.6 %all-to-all-start.1 = ((bf16[16,2,16,576]{3,2,1,0:T(8,128)(2,1)}), bf16[16,2,16,576]{3,2,1,0:T(8,128)(2,1)S(1)}, u32[]{:S(2)}, u32[]{:S(2)}) async-start(bf16[16,2,16,576]{3,2,1,0:T(8,128)(2,1)} %bitcast.36), calls=%async_computation.1 | async-start | bytes 1310720 | tf_op jit(solution)/shard_map/all_to_all | solution.py:394
  138.9 9.9 %shard_map.93 = bf16[1536,576]{1,0:T(8,128)(2,1)} custom-call(bf16[1536,512]{1,0:T(8,128)(2,1)} %get-tuple-element.44.refs_0_, bf16[1536,1024]{1,0:T(8,128)(2,1)} %get-tuple-element.47.refs_1_, bf16[1536,512]{1,0:T(8,128)(2,1)} %get-tuple-element.50.refs_2_, bf16[128,576]{1,0:T(8,128)(2,1)} %copy-done.10, bf16[128,576]{1,0:T(8,128)(2,1)} %copy-done.11, ...), custom_call_target="tpu_custom_call" | custom-call | flops 3623878656 | bytes 6291456 | tf_op jit(solution)/shard_map/pallas_call | solution.py:297
  148.8 1.6 all-to-all-done.1
  150.3 0.9 copy-done.3
  151.2 7.7 %shard_map.95 = f32[16,16,576]{2,1,0:T(8,128)} custom-call(s32[16,16]{1,0:T(8,128)} %lists.7, s32[16]{0:T(128)} %counts.7, s32[1]{0:T(128)} %bitcast.me, bf16[32,16,576]{2,1,0:T(8,128)(2,1)} %bitcast.39), custom_call_target="tpu_custom_call" | custom-call | tf_op jit(solution)/shard_map/pallas_call | solution.py:118
  (58 shorter events, 0.4 us)
Async XLA Ops:
  0.6 15.3 %copy-start.14 = (s32[16]{0:T(128)S(1)}, s32[16]{0:T(128)}, u32[]{:S(2)}) copy-start(s32[16]{0:T(128)} %counts.7) | copy-start | bytes 196
  0.6 16.5 %copy-start.19 = (s32[256]{0:T(256)S(1)}, s32[256]{0:T(256)}, u32[]{:S(2)}) copy-start(s32[256]{0:T(256)} %param.11) | copy-start | bytes 3076
  7.6 31.0 %copy-start = (bf16[96,16,576]{2,1,0:T(8,128)(2,1)S(1)}, bf16[96,16,576]{2,1,0:T(8,128)(2,1)}, u32[]{:S(2)}) copy-start(bf16[96,16,576]{2,1,0:T(8,128)(2,1)} %param.6) | copy-start | bytes 5308420
  7.6 21.1 %all-to-all-start = ((bf16[16,2,16,576]{3,2,1,0:T(8,128)(2,1)}), bf16[16,2,16,576]{3,2,1,0:T(8,128)(2,1)S(1)}, u32[]{:S(2)}, u32[]{:S(2)}) async-start(bf16[16,2,16,576]{3,2,1,0:T(8,128)(2,1)} %bitcast.38), calls=%async_computation | async-start | bytes 1310720 | tf_op jit(solution)/shard_map/all_to_all | solution.py:320
  28.7 0.8 copy-start.2
  32.4 11.3 %collective-permute-start = (bf16[256,576]{1,0:T(8,128)(2,1)}, bf16[256,576]{1,0:T(8,128)(2,1)}, u32[]{:S(2)}, u32[]{:S(2)}) collective-permute-start(bf16[256,576]{1,0:T(8,128)(2,1)} %bitcast.40), channel_id=1, source_target_pairs={{0,2},{1,3},{2,4},{3,5},{4,6},{5,7},{6,0},{7,1},{8,10},{9,11},{10,... | collective-permute-start | bytes 884744 | tf_op jit(solution)/shard_map/ppermute | solution.py:315
  33.9 10.3 %collective-permute-start.2 = (bf16[256,576]{1,0:T(8,128)(2,1)}, bf16[256,576]{1,0:T(8,128)(2,1)}, u32[]{:S(2)}, u32[]{:S(2)}) collective-permute-start(bf16[256,576]{1,0:T(8,128)(2,1)} %bitcast.41), channel_id=1, source_target_pairs={{0,6},{1,7},{2,0},{3,1},{4,2},{5,3},{6,4},{7,5},{8,14},{9,15},{10,... | collective-permute-start | bytes 884744 | tf_op jit(solution)/shard_map/ppermute | solution.py:315
  38.6 2.2 %copy-start.1 = (bf16[96,16,512]{2,1,0:T(8,128)(2,1)S(1)}, bf16[96,16,512]{2,1,0:T(8,128)(2,1)}, u32[]{:S(2)}) copy-start(bf16[96,16,512]{2,1,0:T(8,128)(2,1)} %param.7) | copy-start | bytes 4718596
  40.9 1.6 %copy-start.5 = (bf16[16,16,576]{2,1,0:T(8,128)(2,1)S(1)}, bf16[16,16,576]{2,1,0:T(8,128)(2,1)}, u32[]{:S(2)}) copy-start(bf16[16,16,576]{2,1,0:T(8,128)(2,1)} %shard_map.86) | copy-start | bytes 884740
  40.9 2.2 %copy-start.15 = (f32[256]{0:T(256)S(1)}, f32[256]{0:T(256)}, u32[]{:S(2)}) copy-start(f32[256]{0:T(256)} %select_n.110) | copy-start | bytes 3076
  40.9 2.2 %copy-start.16 = (f32[256]{0:T(256)S(1)}, f32[256]{0:T(256)}, u32[]{:S(2)}) copy-start(f32[256]{0:T(256)} %select_n.113) | copy-start | bytes 3076
  40.9 2.2 %copy-start.17 = (f32[256]{0:T(256)S(1)}, f32[256]{0:T(256)}, u32[]{:S(2)}) copy-start(f32[256]{0:T(256)} %select_n.115) | copy-start | bytes 3076
  40.9 2.2 %copy-start.18 = (f32[256]{0:T(256)S(1)}, f32[256]{0:T(256)}, u32[]{:S(2)}) copy-start(f32[256]{0:T(256)} %select_n.117) | copy-start | bytes 3076
  42.5 7.7 %collective-permute-start.8 = (bf16[256,576]{1,0:T(8,128)(2,1)S(1)}, bf16[256,576]{1,0:T(8,128)(2,1)S(1)}, u32[]{:S(2)}, u32[]{:S(2)}) collective-permute-start(bf16[256,576]{1,0:T(8,128)(2,1)S(1)} %bitcast.44), channel_id=1, source_target_pairs={{0,1},{1,0},{2,3},{3,2},{4,5},{5,4},{6,7},{7,6},{8,9},{9,8},{10,11... | collective-permute-start | bytes 884744 | tf_op jit(solution)/shard_map/ppermute | solution.py:315
  43.7 15.8 %collective-permute-start.6 = (bf16[256,576]{1,0:T(8,128)(2,1)}, bf16[256,576]{1,0:T(8,128)(2,1)S(1)}, u32[]{:S(2)}, u32[]{:S(2)}) collective-permute-start(bf16[256,576]{1,0:T(8,128)(2,1)} %collective-permute-done.refs_0_.refs_7_), channel_id=1, source_target_pairs={{0,1},{1,0},{2,3},{3,2},{4,5},{5,4},{6,7},{7,6},{8,9},{9,8},{10,11... | collective-permute-start | bytes 884744 | tf_op jit(solution)/shard_map/ppermute | solution.py:315
  44.2 15.3 %collective-permute-start.7 = (bf16[256,576]{1,0:T(8,128)(2,1)}, bf16[256,576]{1,0:T(8,128)(2,1)S(1)}, u32[]{:S(2)}, u32[]{:S(2)}) collective-permute-start(bf16[256,576]{1,0:T(8,128)(2,1)} %collective-permute-done.2.refs_1_.refs_8_), channel_id=1, source_target_pairs={{0,1},{1,0},{2,3},{3,2},{4,5},{5,4},{6,7},{7,6},{8,9},{9,8},{10,11... | collective-permute-start | bytes 884744 | tf_op jit(solution)/shard_map/ppermute | solution.py:315
  45.8 13.1 %collective-permute-start.1 = (bf16[128,576]{1,0:T(8,128)(2,1)S(1)}, bf16[128,576]{1,0:T(8,128)(2,1)S(1)}, u32[]{:S(2)}, u32[]{:S(2)}) collective-permute-start(bf16[128,576]{1,0:T(8,128)(2,1)S(1)} %slice.32), channel_id=1, source_target_pairs={{0,2},{1,3},{2,4},{3,5},{4,6},{5,7},{6,0},{7,1},{8,10},{9,11},{10,... | collective-permute-start | bytes 442376 | tf_op jit(solution)/shard_map/ppermute | solution.py:315
  47.1 11.9 %collective-permute-start.3 = (bf16[128,576]{1,0:T(8,128)(2,1)S(1)}, bf16[128,576]{1,0:T(8,128)(2,1)S(1)}, u32[]{:S(2)}, u32[]{:S(2)}) collective-permute-start(bf16[128,576]{1,0:T(8,128)(2,1)S(1)} %slice.33), channel_id=1, source_target_pairs={{0,6},{1,7},{2,0},{3,1},{4,2},{5,3},{6,4},{7,5},{8,14},{9,15},{10,... | collective-permute-start | bytes 442376 | tf_op jit(solution)/shard_map/ppermute | solution.py:315
  50.1 0.7 copy-start.20
  58.9 14.1 %copy-start.10 = (bf16[128,576]{1,0:T(8,128)(2,1)}, bf16[128,576]{1,0:T(8,128)(2,1)S(1)}, u32[]{:S(2)}) copy-start(bf16[128,576]{1,0:T(8,128)(2,1)S(1)} %collective-permute-done.1.refs_0_.refs_3_) | copy-start | bytes 442372
  58.9 14.2 %collective-permute-start.4 = (bf16[128,576]{1,0:T(8,128)(2,1)S(1)}, bf16[128,576]{1,0:T(8,128)(2,1)S(1)}, u32[]{:S(2)}, u32[]{:S(2)}) collective-permute-start(bf16[128,576]{1,0:T(8,128)(2,1)S(1)} %collective-permute-done.1.refs_0_.refs_3_), channel_id=1, source_target_pairs={{0,1},{1,0},{2,3},{3,2},{4,5},{5,4},{6,7},{7,6},{8,9},{9,8},{10,11... | collective-permute-start | bytes 442376 | tf_op jit(solution)/shard_map/ppermute | solution.py:315
  59.0 14.0 %copy-start.11 = (bf16[128,576]{1,0:T(8,128)(2,1)}, bf16[128,576]{1,0:T(8,128)(2,1)S(1)}, u32[]{:S(2)}) copy-start(bf16[128,576]{1,0:T(8,128)(2,1)S(1)} %collective-permute-done.3.refs_1_.refs_4_) | copy-start | bytes 442372
  59.0 14.1 %collective-permute-start.5 = (bf16[128,576]{1,0:T(8,128)(2,1)S(1)}, bf16[128,576]{1,0:T(8,128)(2,1)S(1)}, u32[]{:S(2)}, u32[]{:S(2)}) collective-permute-start(bf16[128,576]{1,0:T(8,128)(2,1)S(1)} %collective-permute-done.3.refs_1_.refs_4_), channel_id=1, source_target_pairs={{0,1},{1,0},{2,3},{3,2},{4,5},{5,4},{6,7},{7,6},{8,9},{9,8},{10,11... | collective-permute-start | bytes 442376 | tf_op jit(solution)/shard_map/ppermute | solution.py:315
  59.5 0.8 copy-start.21
  59.5 0.9 copy-start.22
  73.1 0.7 copy-start.12
  73.1 0.7 copy-start.13
  90.8 19.6 %collective-permute-start.11 = (bf16[256,576]{1,0:T(8,128)(2,1)}, bf16[256,576]{1,0:T(8,128)(2,1)S(1)}, u32[]{:S(2)}, u32[]{:S(2)}) collective-permute-start(bf16[256,576]{1,0:T(8,128)(2,1)} %get-tuple-element.56), channel_id=1, source_target_pairs={{0,1},{1,0},{2,3},{3,2},{4,5},{5,4},{6,7},{7,6},{8,9},{9,8},{10,11... | collective-permute-start | bytes 884744 | tf_op jit(solution)/shard_map/ppermute | solution.py:315
  102.4 11.5 %collective-permute-start.10 = (bf16[512,576]{0,1:T(8,128)(2,1)S(1)}, bf16[512,576]{0,1:T(8,128)(2,1)S(1)}, u32[]{:S(2)}, u32[]{:S(2)}) collective-permute-start(bf16[512,576]{0,1:T(8,128)(2,1)S(1)} %copy.25), channel_id=1, source_target_pairs={{0,1},{1,0},{2,3},{3,2},{4,5},{5,4},{6,7},{7,6},{8,9},{9,8},{10,11... | collective-permute-start | bytes 1769480 | tf_op jit(solution)/shard_map/ppermute | solution.py:315
  103.1 7.4 %copy-start.9 = (bf16[256,576]{1,0:T(8,128)(2,1)S(1)}, bf16[256,576]{1,0:T(8,128)(2,1)}, u32[]{:S(2)}) copy-start(bf16[256,576]{1,0:T(8,128)(2,1)} %get-tuple-element.55) | copy-start | bytes 884740
  110.3 3.9 %copy-start.4 = (bf16[512,576]{1,0:T(8,128)(2,1)S(1)}, bf16[512,576]{1,0:T(8,128)(2,1)}, u32[]{:S(2)}) copy-start(bf16[512,576]{1,0:T(8,128)(2,1)} %get-tuple-element.53) | copy-start | bytes 1769476
  110.3 11.4 %collective-permute-start.9 = (bf16[256,576]{1,0:T(8,128)(2,1)}, bf16[256,576]{1,0:T(8,128)(2,1)S(1)}, u32[]{:S(2)}, u32[]{:S(2)}) collective-permute-start(bf16[256,576]{1,0:T(8,128)(2,1)} %get-tuple-element.52), channel_id=1, source_target_pairs={{0,1},{1,0},{2,3},{3,2},{4,5},{5,4},{6,7},{7,6},{8,9},{9,8},{10,11... | collective-permute-start | bytes 884744 | tf_op jit(solution)/shard_map/ppermute | solution.py:315
  110.6 7.8 %collective-permute-start.12 = (bf16[128,576]{1,0:T(8,128)(2,1)S(1)}, bf16[128,576]{1,0:T(8,128)(2,1)S(1)}, u32[]{:S(2)}, u32[]{:S(2)}) collective-permute-start(bf16[128,576]{1,0:T(8,128)(2,1)S(1)} %get-tuple-element.62), channel_id=1, source_target_pairs={{0,2},{1,3},{2,4},{3,5},{4,6},{5,7},{6,0},{7,1},{8,10},{9,11},{10,... | collective-permute-start | bytes 442376 | tf_op jit(solution)/shard_map/ppermute | solution.py:315
  110.7 7.7 %collective-permute-start.14 = (bf16[128,576]{1,0:T(8,128)(2,1)S(1)}, bf16[128,576]{1,0:T(8,128)(2,1)S(1)}, u32[]{:S(2)}, u32[]{:S(2)}) collective-permute-start(bf16[128,576]{1,0:T(8,128)(2,1)S(1)} %get-tuple-element.61), channel_id=1, source_target_pairs={{0,6},{1,7},{2,0},{3,1},{4,2},{5,3},{6,4},{7,5},{8,14},{9,15},{10,... | collective-permute-start | bytes 442376 | tf_op jit(solution)/shard_map/ppermute | solution.py:315
  118.5 9.4 %collective-permute-start.15 = (bf16[256,576]{1,0:T(8,128)(2,1)S(1)}, bf16[256,576]{1,0:T(8,128)(2,1)S(1)}, u32[]{:S(2)}, u32[]{:S(2)}) collective-permute-start(bf16[256,576]{1,0:T(8,128)(2,1)S(1)} %pad_maximum_fusion.1), channel_id=1, source_target_pairs={{0,6},{1,7},{2,0},{3,1},{4,2},{5,3},{6,4},{7,5},{8,14},{9,15},{10,... | collective-permute-start | bytes 884744 | tf_op jit(solution)/shard_map/ppermute | solution.py:315
  121.6 9.9 %collective-permute-start.13 = (bf16[256,576]{1,0:T(8,128)(2,1)S(1)}, bf16[256,576]{1,0:T(8,128)(2,1)S(1)}, u32[]{:S(2)}, u32[]{:S(2)}) collective-permute-start(bf16[256,576]{1,0:T(8,128)(2,1)S(1)} %pad_maximum_fusion), channel_id=1, source_target_pairs={{0,2},{1,3},{2,4},{3,5},{4,6},{5,7},{6,0},{7,1},{8,10},{9,11},{10,... | collective-permute-start | bytes 884744 | tf_op jit(solution)/shard_map/ppermute | solution.py:315
  121.6 9.8 %copy-start.6 = (bf16[256,576]{1,0:T(8,128)(2,1)}, bf16[256,576]{1,0:T(8,128)(2,1)S(1)}, u32[]{:S(2)}) copy-start(bf16[256,576]{1,0:T(8,128)(2,1)S(1)} %collective-permute-done.9) | copy-start | bytes 884740
  127.9 3.5 %copy-start.7 = (bf16[256,576]{1,0:T(8,128)(2,1)}, bf16[256,576]{1,0:T(8,128)(2,1)S(1)}, u32[]{:S(2)}) copy-start(bf16[256,576]{1,0:T(8,128)(2,1)S(1)} %collective-permute-done.15) | copy-start | bytes 884740
  131.4 0.7 copy-start.8
  135.3 15.0 %all-to-all-start.1 = ((bf16[16,2,16,576]{3,2,1,0:T(8,128)(2,1)}), bf16[16,2,16,576]{3,2,1,0:T(8,128)(2,1)S(1)}, u32[]{:S(2)}, u32[]{:S(2)}) async-start(bf16[16,2,16,576]{3,2,1,0:T(8,128)(2,1)} %bitcast.36), calls=%async_computation.1 | async-start | bytes 1310720 | tf_op jit(solution)/shard_map/all_to_all | solution.py:394
  150.3 0.9 copy-start.3

commit v2 on v1

v2 whole, which is shorter than its diff:
```python
import functools
import math

import jax
import jax.numpy as jnp
from jax import lax
from jax.experimental import pallas as pl
from jax.experimental.pallas import tpu as pltpu
from jax.sharding import PartitionSpec as P

LAT = 512
WIDE = 576
BLOCK = 128
MAXL = 16
CAP = 2
BIG = -1e30
SCALE = 192.0 ** (-0.5)
EXPC = SCALE * math.log2(math.e)
NT = (((1,), (1,)), ((), ()))
NN = (((1,), (0,)), ((), ()))
f32 = jnp.float32
bf16 = jnp.bfloat16


def dot(a, b, dims=NN):
    return lax.dot_general(a, b, dims, preferred_element_type=f32)


def whole(shape):
    rank = len(shape)
    return pl.BlockSpec(shape, lambda *_: (0,) * rank)


def pick_body(lists, counts, me, lat_ref, out_ref):
    own = me[0]

    def group(g, carry):
        def entry(j, rank):
            block = lists[g, j]
            mine = (block // MAXL) == own

            @pl.when(mine)
            def _():
                out_ref[g * CAP + jnp.minimum(rank, CAP - 1)] = lat_ref[lax.rem(block, MAXL)]

            return rank + mine.astype(jnp.int32)

        lax.fori_loop(0, counts[g], entry, jnp.int32(0))
        return carry

    lax.fori_loop(0, 16, group, 0)


def slots_of(lists, counts, me, seen, visit):
    own = me[0]

    def clear(o, carry):
        seen[o] = 0
        return carry

    lax.fori_loop(0, 16, clear, 0)

    def entry(j, carry):
        owner = lists[own, j] // MAXL
        rank = seen[owner]
        seen[owner] = rank + 1
        visit(j, owner * CAP + jnp.minimum(rank, CAP - 1))
        return carry

    lax.fori_loop(0, counts[own], entry, 0)


def take_body(lists, counts, me, arrived_ref, out_ref, seen):
    def visit(j, slot):
        out_ref[j] = arrived_ref[slot]

    slots_of(lists, counts, me, seen, visit)

    def blank(j, carry):
        out_ref[j] = jnp.zeros(out_ref.shape[1:], out_ref.dtype)
        return carry

    lax.fori_loop(counts[me[0]], MAXL, blank, 0)


def put_body(lists, counts, me, a_ref, b_ref, c_ref, d_ref, out_ref, seen):
    def visit(j, slot):
        total = a_ref[j].astype(f32) + b_ref[j].astype(f32)
        total = total + c_ref[j].astype(f32) + d_ref[j].astype(f32)
        out_ref[slot] = total.astype(out_ref.dtype)

    slots_of(lists, counts, me, seen, visit)


def gather_body(lists, counts, me, arrived_ref, out_ref):
    own = me[0]
    out_ref[...] = jnp.zeros(out_ref.shape, out_ref.dtype)

    def group(g, carry):
        def entry(j, rank):
            block = lists[g, j]
            mine = (block // MAXL) == own

            @pl.when(mine)
            def _():
                at = lax.rem(block, MAXL)
                out_ref[at] = out_ref[at] + arrived_ref[g * CAP + jnp.minimum(rank, CAP - 1)].astype(f32)

            return rank + mine.astype(jnp.int32)

        lax.fori_loop(0, counts[g], entry, jnp.int32(0))
        return carry

    lax.fori_loop(0, 16, group, 0)


def on_chip(*arrays):
    return [pltpu.with_memory_space_constraint(a, pltpu.VMEM) for a in arrays]


def call(body, out_shape, scalars, *arrays, scratch=(), limit=24, cost=None):
    single = not isinstance(out_shape, tuple)
    outs = [pltpu.VMEM(o.shape, o.dtype) for o in ((out_shape,) if single else out_shape)]
    vmem = pl.BlockSpec(memory_space=pltpu.VMEM)
    return pl.pallas_call(
        body,
        in_specs=[pl.BlockSpec(memory_space=pltpu.SMEM)] * len(scalars) + [vmem] * len(arrays),
        out_specs=vmem if single else tuple(vmem for _ in outs),
        out_shape=outs[0] if single else tuple(outs),
        scratch_shapes=list(scratch),
        cost_estimate=cost,
        compiler_params=pltpu.CompilerParams(vmem_limit_bytes=limit * 1024 * 1024),
    )(*scalars, *on_chip(*arrays))


def load_keys(key_refs, keys):
    at = 0
    for ref in key_refs:
        keys[at : at + ref.shape[0]] = ref[...]
        at += ref.shape[0]


def forward_body(nkeys, first, last, block, *refs):
    refs = list(refs)
    key_refs = [refs.pop(0) for _ in range(nkeys)]
    bias, q_ref, g_ref = refs[:3]
    refs = refs[3:]
    if not first:
        m_in, l_in, r_in, o_in = refs[:4]
        refs = refs[4:]
    e_out, p_out, m_out, l_out, r_out, o_out, keys = refs
    load_keys(key_refs, keys)

    def rows(i, carry):
        here = pl.ds(pl.multiple_of(i * block, block), block)
        scores = dot(q_ref[here], keys[...], NT) + bias[...]
        top = jnp.max(scores, axis=1, keepdims=True)
        if not first:
            m_old = m_in[here, :1]
            top = jnp.maximum(top, m_old)
        expo = jnp.exp2((scores - top) * EXPC)
        values = keys[:, :LAT]
        grads = dot(g_ref[here], values, NT)
        total = jnp.sum(expo, axis=1, keepdims=True)
        rdot = jnp.sum(expo * grads, axis=1, keepdims=True)
        expo = expo.astype(bf16)
        e_out[here] = expo
        p_out[here] = grads.astype(bf16)
        attended = dot(expo, values)
        if not first:
            fade = jnp.exp2((m_old - top) * EXPC)
            total = total + fade * l_in[here, :1]
            rdot = rdot + fade * r_in[here, :1]
            attended = attended + fade * o_in[here]
        if last:
            total = 1.0 / total
            rdot = rdot * total
            attended = attended * total
        m_out[here] = jnp.broadcast_to(top, (block, 128))
        l_out[here] = jnp.broadcast_to(total, (block, 128))
        r_out[here] = jnp.broadcast_to(rdot, (block, 128))
        o_out[here] = attended.astype(o_out.dtype)
        return carry

    lax.fori_loop(0, q_ref.shape[0] // block, rows, 0)


def forward(key_parts, bias, q, g, state, last, block=256):
    n = bias.shape[1]
    rows = q.shape[0]
    first = state is None
    stat = jax.ShapeDtypeStruct((rows, 128), f32)
    side = jax.ShapeDtypeStruct((rows, n), bf16)
    return call(
        functools.partial(forward_body, len(key_parts), first, last, block),
        (side, side, stat, stat, stat, jax.ShapeDtypeStruct((rows, LAT), bf16 if last else f32)),
        (),
        *key_parts,
        bias,
        q,
        g,
        *(() if first else state),
        scratch=[pltpu.VMEM((n, WIDE), bf16)],
        cost=pl.CostEstimate(
            flops=2 * rows * n * (WIDE + 2 * LAT), transcendentals=rows * n, bytes_accessed=8 * rows * n
        ),
    )


def backward_body(step, tile, qt_ref, gt_ref, e_ref, p_ref, mc_ref, m_ref, l_ref, r_ref, far_out, near_out, s_out, a_sc):
    rows = qt_ref.shape[1]
    n = e_ref.shape[1]
    half = n // 2
    a_sc[...] = jnp.exp2((mc_ref[...] - m_ref[...]) * EXPC) * l_ref[...]
    for start in range(0, n, tile):
        cols = slice((start + half) % n, (start + half) % n + tile)
        acc = None
        for at in range(0, rows, step):
            here = slice(at, at + step)
            a = jnp.tile(a_sc[here], (1, tile // 128))
            r = jnp.tile(r_ref[here], (1, tile // 128))
            weights = (e_ref[here, cols].astype(f32) * a).astype(bf16)
            sg = (weights.astype(f32) * (p_ref[here, cols].astype(f32) - r) * SCALE).astype(bf16)
            s_out[here, cols] = sg
            key_part = dot(qt_ref[:, here], sg)
            value_part = dot(gt_ref[:, here], weights)
            if acc is None:
                acc = [key_part[:LAT] + value_part, key_part[LAT:]]
            else:
                acc = [acc[0] + (key_part[:LAT] + value_part), acc[1] + key_part[LAT:]]
        top = acc[0].T.astype(bf16)
        low = jnp.concatenate([acc[1], jnp.zeros_like(acc[1])], axis=0).T[:, : WIDE - LAT].astype(bf16)
        ref = far_out if start < half else near_out
        put = slice(start % half, start % half + tile)
        ref[put, :LAT] = top
        ref[put, LAT:] = low


def backward(qt, gt, e, p, mc, m, linv, r, tile=256, step=256):
    rows, n = e.shape
    part = jax.ShapeDtypeStruct((n // 2, WIDE), bf16)
    return call(
        functools.partial(backward_body, step, tile),
        (part, part, jax.ShapeDtypeStruct((rows, n), bf16)),
        (),
        qt,
        gt,
        e,
        p,
        mc,
        m,
        linv,
        r,
        scratch=[pltpu.VMEM((rows, 128), f32)],
        cost=pl.CostEstimate(flops=2 * rows * n * (WIDE + LAT), transcendentals=0, bytes_accessed=6 * rows * n),
    )


def query_body(counts, block, *refs):
    refs = list(refs)
    chunks = len(counts)
    s_refs = [refs.pop(0) for _ in range(chunks)]
    k_refs = [refs.pop(0) for _ in range(sum(counts))]
    out_ref, keys = refs
    load_keys(k_refs, keys)

    def rows(i, carry):
        here = pl.ds(pl.multiple_of(i * block, block), block)
        total = None
        at = 0
        for ref in s_refs:
            n = ref.shape[1]
            piece = dot(ref[here], keys[at : at + n])
            total = piece if total is None else total + piece
            at += n
        out_ref[here] = total.astype(out_ref.dtype)
        return carry

    lax.fori_loop(0, out_ref.shape[0] // block, rows, 0)


def query_side(sgs, parts, block=256):
    rows = sgs[0].shape[0]
    n = sum(s.shape[1] for s in sgs)
    return call(
        functools.partial(query_body, [len(p) for p in parts], block),
        jax.ShapeDtypeStruct((rows, WIDE), bf16),
        (),
        *sgs,
        *sum(parts, []),
        scratch=[pltpu.VMEM((n, WIDE), bf16)],
        cost=pl.CostEstimate(flops=2 * rows * n * WIDE, transcendentals=0, bytes_accessed=2 * rows * n),
    )


def per_device(queries, out_grad, latents, list_blocks, list_counts, valid_tokens):
    me = lax.axis_index("req")
    head = lax.axis_index("head")
    chip, core = head // 2, head % 2
    tokens = latents.shape[1]
    shift = lambda d: [(x * 2 + c, ((x + d) % 4) * 2 + c) for x in range(4) for c in range(2)]
    right, left, sibling = shift(1), shift(-1), [(h, h ^ 1) for h in range(8)]
    send = lambda a, perm: lax.ppermute(a, "head", perm)
    scalars = (list_blocks, list_counts, me.reshape(1).astype(jnp.int32))

    slots = jax.ShapeDtypeStruct((16 * CAP, tokens, WIDE), bf16)
    outgoing = call(pick_body, slots, scalars, latents)
    arrived = lax.all_to_all(outgoing.reshape(16, CAP, tokens, WIDE), "req", 0, 0, tiled=True)
    share = call(
        take_body,
        jax.ShapeDtypeStruct((MAXL, tokens, WIDE), bf16),
        scalars,
        arrived.reshape(slots.shape),
        scratch=[pltpu.SMEM((16,), jnp.int32)],
    ).reshape(MAXL * tokens, WIDE)

    my_blocks = lax.dynamic_index_in_dim(list_blocks, me, 0, keepdims=False)
    my_count = lax.dynamic_index_in_dim(list_counts, me, 0, keepdims=False)
    ids = jnp.arange(valid_tokens.shape[0], dtype=jnp.int32)
    filled = jnp.sum(jnp.where(my_blocks[:, None] == ids[None, :], valid_tokens[None, :], 0), axis=1)
    filled = jnp.where(jnp.arange(MAXL, dtype=jnp.int32) < my_count, filled, 0)
    filled = jnp.repeat(filled, tokens)
    offset = jnp.tile(jnp.arange(tokens, dtype=jnp.int32), MAXL)

    def bias_of(places):
        rows = [jnp.where(place * tokens + offset < filled, 0.0, BIG) for place in places]
        return jnp.concatenate(rows).astype(f32)[None, :]

    at = lambda d, c: ((chip + d) % 4) * 2 + c
    other = 1 - core
    bias0 = bias_of([at(0, core), at(0, other)])
    bias1 = bias_of([at(3, core), at(1, core), at(3, other), at(1, other)])
    bias2 = bias_of([at(2, core), at(2, other)])

    q = queries.reshape(-1, WIDE)
    g = out_grad.reshape(-1, LAT)
    qt = q.T
    gt = g.T

    keep = MAXL * tokens // 2
    r1 = send(share, right)
    l1 = send(share, left)
    s0 = send(share, sibling)
    r2 = send(r1[:keep], right)
    l2 = send(l1[keep:], left)
    s1 = send(r1, sibling)
    s2 = send(l1, sibling)
    s3 = send(r2, sibling)
    s4 = send(l2, sibling)
    parts0, parts1, parts2 = [share, s0], [r1, l1, s1, s2], [r2, l2, s3, s4]

    e0, p0, m0, *rest = forward(parts0, bias0, q, g, None, False)
    e1, p1, m1, *rest = forward(parts1, bias1, q, g, (m0, *rest), False)
    e2, p2, m2, linv, rdot, attended = forward(parts2, bias2, q, g, (m1, *rest), True)

    back = functools.partial(backward, qt, gt)
    add = lambda a, b: (a.astype(f32) + b.astype(f32)).astype(bf16)
    far, near, sg2 = back(e2, p2, m2, m2, linv, rdot)
    two = add(near, send(far, sibling))
    from_left = send(two[:keep], right)
    from_right = send(two[keep:], left)
    far, near, sg1 = back(e1, p1, m1, m2, linv, rdot)
    one = add(near, send(far, sibling))
    size = 2 * keep
    to_left = jnp.concatenate([one[:keep], add(one[keep:size], from_right)])
    to_right = jnp.concatenate([add(one[size : size + keep], from_left), one[size + keep :]])
    got_left = send(to_right, right)
    got_right = send(to_left, left)
    far, near, sg0 = back(e0, p0, m0, m2, linv, rdot)
    mate = send(far, sibling)
    fold = lambda a: a.reshape(MAXL, tokens, WIDE)
    slot_grads = call(
        put_body,
        slots,
        scalars,
        fold(near),
        fold(mate),
        fold(got_left),
        fold(got_right),
        scratch=[pltpu.SMEM((16,), jnp.int32)],
    )
    returned = lax.all_to_all(slot_grads.reshape(16, CAP, tokens, WIDE), "req", 0, 0, tiled=True)
    query_grad = query_side([sg2, sg1, sg0], [parts2, parts1, parts0])
    latent_grad = call(
        gather_body, jax.ShapeDtypeStruct((16, tokens, WIDE), f32), scalars, returned.reshape(slots.shape)
    )
    return (attended.reshape(out_grad.shape), query_grad.reshape(queries.shape), latent_grad)


def solution(mesh):
    in_specs = (
        P("req", "head", None),
        P("req", "head", None),
        P("req", "head", None),
        P(),
        P(),
        P(),
    )
    out_specs = (P("req", "head", None), P("req", "head", None), P("req", "head", None))
    return jax.shard_map(
        per_device, mesh=mesh, in_specs=in_specs, out_specs=out_specs, check_vma=False
    )
```

time: 160 us -> 154 us (0.963)
  Pallas kernels: 85.5 us -> 52.8 us
  local copies, waits for them, and re-layouts: 16.4 us -> 43.6 us
    pallas_call x11, Pallas kernels: 85.5 us -> 52.8 us  [call(): pl.pallas_call(body, in_specs=[pl.BlockSpec(memory_space=pltpu.SMEM)] * l...]
    unnamed x46 -> x101, local copies, waits for them, and re-layouts: 4.86 us -> 31.9 us
    select_n x8, local copies, waits for them, and re-layouts: 2.94 us -> 0.64 us  [bias_of(): jnp.where(place * tokens + offset < filled, 0.0, BIG)]
    convert_element_type x3, other arithmetic: 0.32 us -> 2.39 us  [per_device(): add = lambda a, b: (a.astype(f32) + b.astype(f32)).astype(bf16)]
    concatenate x3, other arithmetic: 1.8 us -> 0.02 us  [bias_of(): return jnp.concatenate(rows).astype(f32)[None, :]]
  transfers between devices with their start and end apart: 18 -> 18, of which waited for: 5 -> 5; matrix products, arithmetic and copies ran while one was open for 9% -> 11% of each run, Pallas kernels for 30% -> 20%
where the time goes in v2:
time: 154 us; the launch traced here: 153 us
  Pallas kernels  52.8 us (34%)
  local copies, waits for them, and re-layouts  43.6 us (28%)
  starting transfers between devices  26.3 us (17%)
  waiting for transfers between devices  25.5 us (17%)
  other arithmetic  3.39 us (2%)
    pallas_call x11, Pallas kernels, call(): pl.pallas_call(body, in_specs=[pl.BlockSpec(memory_space=pltpu.SMEM)] * l...  52.8 us
    unnamed x101, local copies, waits for them, and re-layouts  31.9 us
    ppermute x16, starting transfers between devices, per_device(): send = lambda a, perm: lax.ppermute(a, 'head', perm)  14.3 us
    ppermute x16, waiting for transfers between devices, per_device(): send = lambda a, perm: lax.ppermute(a, 'head', perm)  14.1 us
    all_to_all x1, waiting for transfers between devices, per_device(): lax.all_to_all(outgoing.reshape(16, CAP, tokens, WIDE), 'req', 0, 0, tile...  11.4 us
    all_to_all x1, starting transfers between devices, per_device(): lax.all_to_all(outgoing.reshape(16, CAP, tokens, WIDE), 'req', 0, 0, tile...  8.16 us
    all_to_all x1, starting transfers between devices, per_device(): lax.all_to_all(slot_grads.reshape(16, CAP, tokens, WIDE), 'req', 0, 0, ti...  3.91 us
  transfers between devices with their start and end apart: 18, of which 5 were waited for; matrix products, arithmetic and copies ran while one was open for 11% of the time, Pallas kernels for 20%

profile of v2, /device:TPU:0, one launch (start us, length us, event | category | flops | bytes accessed | tf_op | source)
XLA Modules:
  0.0 152.7 jit_solution(17338513116614482285)
XLA Ops:
  0.7 1.0 copy-done.21
  1.6 0.7 copy-done.32
  2.3 0.7 copy-done.34
  3.0 5.9 %shard_map.85 = bf16[32,16,576]{2,1,0:T(8,128)(2,1)} custom-call(s32[16,16]{1,0:T(8,128)S(1)} %copy-done.32, s32[16]{0:T(128)S(1)} %copy-done.34, s32[1]{0:T(128)} %bitcast.me, bf16[16,16,576]{2,1,0:T(8,128)(2,1)S(1)} %copy-done.21), custom_call_target="tpu_custom_call" | custom-call | tf_op jit(solution)/shard_map/pallas_call | solution.py:125
  8.9 8.2 %all-to-all-start = ((bf16[16,2,16,576]{3,2,1,0:T(8,128)(2,1)}), bf16[16,2,16,576]{3,2,1,0:T(8,128)(2,1)S(1)}, u32[]{:S(2)}, u32[]{:S(2)}) async-start(bf16[16,2,16,576]{3,2,1,0:T(8,128)(2,1)} %bitcast.1), calls=%async_computation | async-start | bytes 1310720 | tf_op jit(solution)/shard_map/all_to_all | solution.py:308
  17.1 0.6 dynamic_slice.8
  17.9 0.7 compare_select_fusion
  18.6 11.4 %all-to-all-done = bf16[16,2,16,576]{3,2,1,0:T(8,128)(2,1)S(1)} async-done(((bf16[16,2,16,576]{3,2,1,0:T(8,128)(2,1)}), bf16[16,2,16,576]{3,2,1,0:T(8,128)(2,1)S(1)}, u32[]{:S(2)}, u32[]{:S(2)}) %all-to-all-start) | async-done | bytes 589856 | tf_op jit(solution)/shard_map/all_to_all | solution.py:308
  29.9 1.7 %shard_map.86 = bf16[16,16,576]{2,1,0:T(8,128)(2,1)} custom-call(s32[16,16]{1,0:T(8,128)S(1)} %copy-done.33, s32[16]{0:T(128)S(1)} %copy-done.35, s32[1]{0:T(128)} %bitcast.me, bf16[32,16,576]{2,1,0:T(8,128)(2,1)S(1)} %bitcast.38), custom_call_target="tpu_custom_call" | custom-call | tf_op jit(solution)/shard_map/pallas_call | solution.py:125
  31.7 1.5 collective-permute-start
  33.2 1.7 %collective-permute-start.2 = (bf16[256,576]{1,0:T(8,128)(2,1)}, bf16[256,576]{1,0:T(8,128)(2,1)}, u32[]{:S(2)}, u32[]{:S(2)}) collective-permute-start(bf16[256,576]{1,0:T(8,128)(2,1)} %bitcast.3.refs_0_.refs_11_), channel_id=1, source_target_pairs={{0,6},{1,7},{2,0},{3,1},{4,2},{5,3},{6,4},{7,5},{8,14},{9,15},{10,... | collective-permute-start | bytes 884744 | tf_op jit(solution)/shard_map/ppermute | solution.py:303
  35.6 2.8 %copy.23 = bf16[1536,576]{0,1:T(8,128)(2,1)S(1)} copy(bf16[1536,576]{1,0:T(8,128)(2,1)} %bitcast.30) | data formatting | bytes 3538944 | tf_op jit(solution)/shard_map/reshape | solution.py:335
  38.4 1.6 %copy.24 = bf16[1536,512]{0,1:T(8,128)(2,1)} copy(bf16[1536,512]{1,0:T(8,128)(2,1)S(1)} %bitcast.34) | data formatting | bytes 3145728 | tf_op jit(solution)/shard_map/reshape | solution.py:336
  40.0 1.0 collective-permute-done.refs_0_.refs_7_
  41.0 0.5 collective-permute-start.7
  41.6 0.9 slice.32
  42.5 1.1 collective-permute-start.1
  43.5 0.9 slice.33
  44.5 2.3 %collective-permute-start.3 = (bf16[128,576]{1,0:T(8,128)(2,1)S(1)}, bf16[128,576]{1,0:T(8,128)(2,1)S(1)}, u32[]{:S(2)}, u32[]{:S(2)}) collective-permute-start(bf16[128,576]{1,0:T(8,128)(2,1)S(1)} %slice.33), channel_id=1, source_target_pairs={{0,6},{1,7},{2,0},{3,1},{4,2},{5,3},{6,4},{7,5},{8,14},{9,15},{10,... | collective-permute-start | bytes 442376 | tf_op jit(solution)/shard_map/ppermute | solution.py:303
  46.8 1.7 %copy-done.4 = bf16[96,16,576]{2,1,0:T(8,128)(2,1)S(1)} copy-done((bf16[96,16,576]{2,1,0:T(8,128)(2,1)S(1)}, bf16[96,16,576]{2,1,0:T(8,128)(2,1)}, u32[]{:S(2)}) %copy-start.4) | copy-done | bytes 1769496
  48.5 5.4 %shard_map.87 = (bf16[1536,512]{1,0:T(8,128)(2,1)S(1)}, bf16[1536,512]{1,0:T(8,128)(2,1)S(1)}, f32[1536,128]{1,0:T(8,128)S(1)}, f32[1536,128]{1,0:T(8,128)S(1)},...) custom-call(bf16[256,576]{1,0:T(8,128)(2,1)} %bitcast.3.refs_0_.refs_11_, ...), custom_call_target="tpu_custom_call" | custom-call | flops 2516582400 | bytes 6291456 | tf_op jit(solution)/shard_map/pallas_call | solution.py:125
  53.9 1.2 copy-done.12
  55.7 10.5 %shard_map.88 = (bf16[1536,1024]{1,0:T(8,128)(2,1)S(1)}, bf16[1536,1024]{1,0:T(8,128)(2,1)S(1)}, f32[1536,128]{1,0:T(8,128)S(1)}, f32[1536,128]{1,0:T(8,128)S(1)...) custom-call(bf16[256,576]{1,0:T(8,128)(2,1)} %collective-permute-done.refs_0_.refs_7_, ...), custom_call_target="tpu_custom_call" | custom-call | flops 5033164800 | bytes 12582912 | tf_op jit(solution)/shard_map/pallas_call | solution.py:125
  66.3 5.3 %shard_map.89 = (bf16[1536,512]{1,0:T(8,128)(2,1)S(1)}, bf16[1536,512]{1,0:T(8,128)(2,1)S(1)}, f32[1536,128]{1,0:T(8,128)S(1)}, f32[1536,128]{1,0:T(8,128)S(1)},...) custom-call(bf16[128,576]{1,0:T(8,128)(2,1)S(1)} %collective-permute-done.1.refs_0_.refs_3_, ...), custom_call_target="tpu_custom_call" | custom-call | flops 2516582400 | bytes 6291456 | tf_op jit(solution)/shard_map/pallas_call | solution.py:125
  71.6 2.9 %shard_map.90 = (bf16[256,576]{1,0:T(8,128)(2,1)}, bf16[256,576]{1,0:T(8,128)(2,1)S(1)}, bf16[1536,512]{1,0:T(8,128)(2,1)S(1)}) custom-call(bf16[576,1536]{1,0:T(8,128)(2,1)S(1)} %bitcast.24, bf16[512,1536]{1,0:T(8,128)(2,1)S(1)} %bitcast.27, bf16[1536,512]{1,0:T(8,128)(2,1)S(1)} %get-tuple-element.39.e_ref, bf16[1536,512]{1,0:T(8,128)(2,1)S(1)} %get-tuple-element.40.p_ref, ...), custom_call_target="tpu_custom_call" | custom-call | flops 1711276032 | bytes 4718592 | tf_op jit(solution)/shard_map/pallas_call | solution.py:125
  74.5 0.7 copy-done.24
  75.2 1.1 copy-done.38
  76.4 3.9 %shard_map.91 = (bf16[512,576]{1,0:T(8,128)(2,1)S(1)}, bf16[512,576]{1,0:T(8,128)(2,1)S(1)}, bf16[1536,1024]{1,0:T(8,128)(2,1)S(1)}) custom-call(bf16[576,1536]{1,0:T(8,128)(2,1)S(1)} %bitcast.25, bf16[512,1536]{1,0:T(8,128)(2,1)S(1)} %bitcast.28, bf16[1536,1024]{1,0:T(8,128)(2,1)S(1)} %get-tuple-element.45.e_ref, ...), custom_call_target="tpu_custom_call" | custom-call | flops 3422552064 | bytes 9437184 | tf_op jit(solution)/shard_map/pallas_call | solution.py:125
  80.3 0.8 copy-done.18
  81.1 0.8 copy-done.19
  82.0 1.6 %copy-done.36 = bf16[1536,1024]{1,0:T(8,128)(2,1)} copy-done((bf16[1536,1024]{1,0:T(8,128)(2,1)}, bf16[1536,1024]{1,0:T(8,128)(2,1)S(1)}, u32[]{:S(2)}) %copy-start.36) | copy-done | bytes 3145752
  83.6 2.1 %copy.25 = bf16[512,576]{0,1:T(8,128)(2,1)} copy(bf16[512,576]{1,0:T(8,128)(2,1)} %copy-done.18) | data formatting | bytes 1179648 | tf_op jit(solution)/shard_map/pallas_call | solution.py:125
  86.2 1.4 copy-done.1
  87.6 1.1 copy-done.3
  88.8 1.1 copy-done.7
  89.9 1.1 copy-done.9
  91.0 1.4 copy-done.13
  92.4 1.4 copy-done.15
  93.8 1.1 copy-done.17
  95.0 2.9 %shard_map.92 = (bf16[256,576]{1,0:T(8,128)(2,1)}, bf16[256,576]{1,0:T(8,128)(2,1)S(1)}, bf16[1536,512]{1,0:T(8,128)(2,1)S(1)}) custom-call(bf16[576,1536]{1,0:T(8,128)(2,1)S(1)} %bitcast.26, bf16[512,1536]{1,0:T(8,128)(2,1)S(1)} %bitcast.29, bf16[1536,512]{1,0:T(8,128)(2,1)S(1)} %copy-done.13, bf16[1536,512]{1,0:T(8,128)(2,1)S(1)} %copy-done.15, ...), custom_call_target="tpu_custom_call" | custom-call | flops 1711276032 | bytes 4718592 | tf_op jit(solution)/shard_map/pallas_call | solution.py:125
  97.9 0.7 copy-done.22
  98.6 1.1 copy-done.40
  99.7 1.1 add_convert_fusion.1
  100.9 0.7 fusion.9
  101.6 3.2 %collective-permute-start.14 = (bf16[128,576]{1,0:T(8,128)(2,1)S(1)}, bf16[128,576]{1,0:T(8,128)(2,1)}, u32[]{:S(2)}, u32[]{:S(2)}) collective-permute-start(bf16[128,576]{1,0:T(8,128)(2,1)S(1)} %get-tuple-element.61), channel_id=1, source_target_pairs={{0,6},{1,7},{2,0},{3,1},{4,2},{5,3},{6,4},{7,5},{8,14},{9,15},{10,... | collective-permute-start | bytes 442376 | tf_op jit(solution)/shard_map/ppermute | solution.py:303
  104.8 1.4 copy.26
  106.4 3.2 %collective-permute-done.12 = bf16[128,576]{1,0:T(8,128)(2,1)} collective-permute-done((bf16[128,576]{1,0:T(8,128)(2,1)}, bf16[128,576]{1,0:T(8,128)(2,1)}, u32[]{:S(2)}, u32[]{:S(2)}) %collective-permute-start.12) | collective-permute-done | bytes 147488 | tf_op jit(solution)/shard_map/ppermute | solution.py:303
  109.6 1.1 add_convert_fusion.2
  110.8 2.8 %collective-permute-start.15 = (bf16[256,576]{1,0:T(8,128)(2,1)S(1)}, bf16[256,576]{1,0:T(8,128)(2,1)S(1)}, u32[]{:S(2)}, u32[]{:S(2)}) collective-permute-start(bf16[256,576]{1,0:T(8,128)(2,1)S(1)} %pad_maximum_fusion.1), channel_id=1, source_target_pairs={{0,6},{1,7},{2,0},{3,1},{4,2},{5,3},{6,4},{7,5},{8,14},{9,15},{10,... | collective-permute-start | bytes 884744 | tf_op jit(solution)/shard_map/ppermute | solution.py:303
  113.7 6.3 %collective-permute-done.15 = bf16[256,576]{1,0:T(8,128)(2,1)S(1)} collective-permute-done((bf16[256,576]{1,0:T(8,128)(2,1)S(1)}, bf16[256,576]{1,0:T(8,128)(2,1)S(1)}, u32[]{:S(2)}, u32[]{:S(2)}) %collective-permute-start.15) | collective-permute-done | bytes 294944 | tf_op jit(solution)/shard_map/ppermute | solution.py:303
  120.0 3.5 %collective-permute-done.13 = bf16[256,576]{1,0:T(8,128)(2,1)S(1)} collective-permute-done((bf16[256,576]{1,0:T(8,128)(2,1)S(1)}, bf16[256,576]{1,0:T(8,128)(2,1)S(1)}, u32[]{:S(2)}, u32[]{:S(2)}) %collective-permute-start.13) | collective-permute-done | bytes 294944 | tf_op jit(solution)/shard_map/ppermute | solution.py:303
  123.5 1.8 %shard_map.94 = bf16[32,16,576]{2,1,0:T(8,128)(2,1)} custom-call(s32[16,16]{1,0:T(8,128)S(1)} %copy-done.33, s32[16]{0:T(128)S(1)} %copy-done.35, s32[1]{0:T(128)} %bitcast.me, bf16[16,16,576]{2,1,0:T(8,128)(2,1)S(1)} %bitcast.40, bf16[16,16,576]{2,1,0:T(8,128)(2,1)S(1)} %bitcast.41, bf16[16,16,576]{2,1,0:T(8,128)(2,1)S(1)} %bitcast.43, ...), custom_call_target="tpu_custom_call" | custom-call | tf_op jit(solution)/shard_map/pallas_call | solution.py:125
  125.4 3.9 %all-to-all-start.1 = ((bf16[16,2,16,576]{3,2,1,0:T(8,128)(2,1)}), bf16[16,2,16,576]{3,2,1,0:T(8,128)(2,1)S(1)}, u32[]{:S(2)}, u32[]{:S(2)}) async-start(bf16[16,2,16,576]{3,2,1,0:T(8,128)(2,1)} %bitcast.19), calls=%async_computation.1 | async-start | bytes 1310720 | tf_op jit(solution)/shard_map/all_to_all | solution.py:382
  129.3 1.9 %copy-done.37 = bf16[1536,1024]{1,0:T(8,128)(2,1)S(1)} copy-done((bf16[1536,1024]{1,0:T(8,128)(2,1)S(1)}, bf16[1536,1024]{1,0:T(8,128)(2,1)}, u32[]{:S(2)}) %copy-start.37) | copy-done | bytes 3145752
  131.2 1.4 copy-done.39
  132.6 1.4 copy-done.41
  134.0 1.0 copy-done.43
  135.0 1.0 copy-done.45
  136.0 1.0 copy-done.47
  136.9 7.4 %shard_map.93 = bf16[1536,576]{1,0:T(8,128)(2,1)S(1)} custom-call(bf16[1536,512]{1,0:T(8,128)(2,1)S(1)} %copy-done.39, bf16[1536,1024]{1,0:T(8,128)(2,1)S(1)} %copy-done.37, bf16[1536,512]{1,0:T(8,128)(2,1)S(1)} %copy-done.41, bf16[128,576]{1,0:T(8,128)(2,1)S(1)} %collective-permute-done.1.refs_0_.refs_3_, bf16[128,576]{1,0:T(8,128)(2,1)S(1)} %copy-done.27, ...), custom_call_target="tpu_custom_call" | custom-call | flops 3623878656 | bytes 6291456 | tf_op jit(solution)/shard_map/pallas_call | solution.py:125
  144.3 1.3 copy.28
  145.6 1.1 copy.27
  146.7 5.1 %shard_map.95 = f32[16,16,576]{2,1,0:T(8,128)S(1)} custom-call(s32[16,16]{1,0:T(8,128)S(1)} %copy-done.33, s32[16]{0:T(128)S(1)} %copy-done.35, s32[1]{0:T(128)} %bitcast.me, bf16[32,16,576]{2,1,0:T(8,128)(2,1)S(1)} %bitcast.39), custom_call_target="tpu_custom_call" | custom-call | tf_op jit(solution)/shard_map/pallas_call | solution.py:125
  151.9 0.8 copy.29
  (113 shorter events, 2.5 us)
Async XLA Ops:
  0.6 17.1 %copy-start.33 = (s32[16,16]{1,0:T(8,128)S(1)}, s32[16,16]{1,0:T(8,128)}, u32[]{:S(2)}) copy-start(s32[16,16]{1,0:T(8,128)} %lists.7) | copy-start | bytes 3076
  0.6 16.5 %copy-start.35 = (s32[16]{0:T(128)S(1)}, s32[16]{0:T(128)}, u32[]{:S(2)}) copy-start(s32[16]{0:T(128)} %counts.7) | copy-start | bytes 196
  0.7 1.0 copy-start.21
  3.0 14.7 %copy-start.48 = (s32[256]{0:T(256)S(1)}, s32[256]{0:T(256)}, u32[]{:S(2)}) copy-start(s32[256]{0:T(256)} %param.11) | copy-start | bytes 3076
  8.9 21.1 %all-to-all-start = ((bf16[16,2,16,576]{3,2,1,0:T(8,128)(2,1)}), bf16[16,2,16,576]{3,2,1,0:T(8,128)(2,1)S(1)}, u32[]{:S(2)}, u32[]{:S(2)}) async-start(bf16[16,2,16,576]{3,2,1,0:T(8,128)(2,1)} %bitcast.1), calls=%async_computation | async-start | bytes 1310720 | tf_op jit(solution)/shard_map/all_to_all | solution.py:308
  31.7 9.4 %collective-permute-start = (bf16[256,576]{1,0:T(8,128)(2,1)}, bf16[256,576]{1,0:T(8,128)(2,1)}, u32[]{:S(2)}, u32[]{:S(2)}) collective-permute-start(bf16[256,576]{1,0:T(8,128)(2,1)} %bitcast.3.refs_0_.refs_11_), channel_id=1, source_target_pairs={{0,2},{1,3},{2,4},{3,5},{4,6},{5,7},{6,0},{7,1},{8,10},{9,11},{10,... | collective-permute-start | bytes 884744 | tf_op jit(solution)/shard_map/ppermute | solution.py:303
  33.2 7.9 %collective-permute-start.2 = (bf16[256,576]{1,0:T(8,128)(2,1)}, bf16[256,576]{1,0:T(8,128)(2,1)}, u32[]{:S(2)}, u32[]{:S(2)}) collective-permute-start(bf16[256,576]{1,0:T(8,128)(2,1)} %bitcast.3.refs_0_.refs_11_), channel_id=1, source_target_pairs={{0,6},{1,7},{2,0},{3,1},{4,2},{5,3},{6,4},{7,5},{8,14},{9,15},{10,... | collective-permute-start | bytes 884744 | tf_op jit(solution)/shard_map/ppermute | solution.py:303
  35.6 2.8 %copy-start.10 = (bf16[96,16,512]{2,1,0:T(8,128)(2,1)S(1)}, bf16[96,16,512]{2,1,0:T(8,128)(2,1)}, u32[]{:S(2)}) copy-start(bf16[96,16,512]{2,1,0:T(8,128)(2,1)} %param.7) | copy-start | bytes 4718596
  40.0 6.8 %collective-permute-start.8 = (bf16[256,576]{1,0:T(8,128)(2,1)}, bf16[256,576]{1,0:T(8,128)(2,1)S(1)}, u32[]{:S(2)}, u32[]{:S(2)}) collective-permute-start(bf16[256,576]{1,0:T(8,128)(2,1)} %bitcast.3.refs_0_.refs_11_), channel_id=1, source_target_pairs={{0,1},{1,0},{2,3},{3,2},{4,5},{5,4},{6,7},{7,6},{8,9},{9,8},{10,11... | collective-permute-start | bytes 884744 | tf_op jit(solution)/shard_map/ppermute | solution.py:303
  41.0 14.6 %collective-permute-start.6 = (bf16[256,576]{1,0:T(8,128)(2,1)}, bf16[256,576]{1,0:T(8,128)(2,1)S(1)}, u32[]{:S(2)}, u32[]{:S(2)}) collective-permute-start(bf16[256,576]{1,0:T(8,128)(2,1)} %collective-permute-done.refs_0_.refs_7_), channel_id=1, source_target_pairs={{0,1},{1,0},{2,3},{3,2},{4,5},{5,4},{6,7},{7,6},{8,9},{9,8},{10,11... | collective-permute-start | bytes 884744 | tf_op jit(solution)/shard_map/ppermute | solution.py:303
  41.0 14.6 %collective-permute-start.7 = (bf16[256,576]{1,0:T(8,128)(2,1)}, bf16[256,576]{1,0:T(8,128)(2,1)S(1)}, u32[]{:S(2)}, u32[]{:S(2)}) collective-permute-start(bf16[256,576]{1,0:T(8,128)(2,1)} %collective-permute-done.2.refs_1_.refs_8_), channel_id=1, source_target_pairs={{0,1},{1,0},{2,3},{3,2},{4,5},{5,4},{6,7},{7,6},{8,9},{9,8},{10,11... | collective-permute-start | bytes 884744 | tf_op jit(solution)/shard_map/ppermute | solution.py:303
  42.5 12.6 %collective-permute-start.1 = (bf16[128,576]{1,0:T(8,128)(2,1)S(1)}, bf16[128,576]{1,0:T(8,128)(2,1)S(1)}, u32[]{:S(2)}, u32[]{:S(2)}) collective-permute-start(bf16[128,576]{1,0:T(8,128)(2,1)S(1)} %slice.32), channel_id=1, source_target_pairs={{0,2},{1,3},{2,4},{3,5},{4,6},{5,7},{6,0},{7,1},{8,10},{9,11},{10,... | collective-permute-start | bytes 442376 | tf_op jit(solution)/shard_map/ppermute | solution.py:303
  44.5 10.6 %collective-permute-start.3 = (bf16[128,576]{1,0:T(8,128)(2,1)S(1)}, bf16[128,576]{1,0:T(8,128)(2,1)S(1)}, u32[]{:S(2)}, u32[]{:S(2)}) collective-permute-start(bf16[128,576]{1,0:T(8,128)(2,1)S(1)} %slice.33), channel_id=1, source_target_pairs={{0,6},{1,7},{2,0},{3,1},{4,2},{5,3},{6,4},{7,5},{8,14},{9,15},{10,... | collective-permute-start | bytes 442376 | tf_op jit(solution)/shard_map/ppermute | solution.py:303
  46.8 7.1 %copy-start.42 = (bf16[256,576]{1,0:T(8,128)(2,1)}, bf16[256,576]{1,0:T(8,128)(2,1)S(1)}, u32[]{:S(2)}) copy-start(bf16[256,576]{1,0:T(8,128)(2,1)S(1)} %collective-permute-done.8.refs_1_.refs_12_) | copy-start | bytes 884740
  46.8 1.7 %copy-start.4 = (bf16[96,16,576]{2,1,0:T(8,128)(2,1)S(1)}, bf16[96,16,576]{2,1,0:T(8,128)(2,1)}, u32[]{:S(2)}) copy-start(bf16[96,16,576]{2,1,0:T(8,128)(2,1)} %param.6) | copy-start | bytes 5308420
  48.5 7.2 %copy-start.5 = (bf16[96,16,576]{2,1,0:T(8,128)(2,1)S(1)}, bf16[96,16,576]{2,1,0:T(8,128)(2,1)}, u32[]{:S(2)}) copy-start(bf16[96,16,576]{2,1,0:T(8,128)(2,1)} %param.6) | copy-start | bytes 5308420
  53.9 1.2 copy-start.12
  55.1 11.1 %copy-start.14 = (bf16[1536,512]{1,0:T(8,128)(2,1)}, bf16[1536,512]{1,0:T(8,128)(2,1)S(1)}, u32[]{:S(2)}) copy-start(bf16[1536,512]{1,0:T(8,128)(2,1)S(1)} %get-tuple-element.49.p_ref) | copy-start | bytes 4718596
  55.1 11.1 %copy-start.16 = (f32[1536,128]{1,0:T(8,128)}, f32[1536,128]{1,0:T(8,128)S(1)}, u32[]{:S(2)}) copy-start(f32[1536,128]{1,0:T(8,128)S(1)} %get-tuple-element.30.refs_7_.mc_ref) | copy-start | bytes 2359300
  55.1 11.1 %collective-permute-start.4 = (bf16[128,576]{1,0:T(8,128)(2,1)S(1)}, bf16[128,576]{1,0:T(8,128)(2,1)S(1)}, u32[]{:S(2)}, u32[]{:S(2)}) collective-permute-start(bf16[128,576]{1,0:T(8,128)(2,1)S(1)} %collective-permute-done.1.refs_0_.refs_3_), channel_id=1, source_target_pairs={{0,1},{1,0},{2,3},{3,2},{4,5},{5,4},{6,7},{7,6},{8,9},{9,8},{10,11... | collective-permute-start | bytes 442376 | tf_op jit(solution)/shard_map/ppermute | solution.py:303
  55.1 11.1 %copy-start.26 = (bf16[128,576]{1,0:T(8,128)(2,1)}, bf16[128,576]{1,0:T(8,128)(2,1)S(1)}, u32[]{:S(2)}) copy-start(bf16[128,576]{1,0:T(8,128)(2,1)S(1)} %collective-permute-done.3.refs_1_.refs_4_) | copy-start | bytes 442372
  55.1 11.1 %collective-permute-start.5 = (bf16[128,576]{1,0:T(8,128)(2,1)S(1)}, bf16[128,576]{1,0:T(8,128)(2,1)S(1)}, u32[]{:S(2)}, u32[]{:S(2)}) collective-permute-start(bf16[128,576]{1,0:T(8,128)(2,1)S(1)} %collective-permute-done.3.refs_1_.refs_4_), channel_id=1, source_target_pairs={{0,1},{1,0},{2,3},{3,2},{4,5},{5,4},{6,7},{7,6},{8,9},{9,8},{10,11... | collective-permute-start | bytes 442376 | tf_op jit(solution)/shard_map/ppermute | solution.py:303
  55.6 10.5 %copy-start.44 = (bf16[256,576]{1,0:T(8,128)(2,1)}, bf16[256,576]{1,0:T(8,128)(2,1)S(1)}, u32[]{:S(2)}) copy-start(bf16[256,576]{1,0:T(8,128)(2,1)S(1)} %collective-permute-done.6.refs_2_.refs_9_) | copy-start | bytes 884740
  55.6 10.5 %copy-start.46 = (bf16[256,576]{1,0:T(8,128)(2,1)}, bf16[256,576]{1,0:T(8,128)(2,1)S(1)}, u32[]{:S(2)}) copy-start(bf16[256,576]{1,0:T(8,128)(2,1)S(1)} %collective-permute-done.7.refs_3_.refs_10_) | copy-start | bytes 884740
  55.6 10.6 %copy-start.11 = (bf16[96,16,512]{2,1,0:T(8,128)(2,1)S(1)}, bf16[96,16,512]{2,1,0:T(8,128)(2,1)}, u32[]{:S(2)}) copy-start(bf16[96,16,512]{2,1,0:T(8,128)(2,1)} %param.7) | copy-start | bytes 4718596
  66.2 5.4 %copy-start.28 = (bf16[128,576]{1,0:T(8,128)(2,1)}, bf16[128,576]{1,0:T(8,128)(2,1)S(1)}, u32[]{:S(2)}) copy-start(bf16[128,576]{1,0:T(8,128)(2,1)S(1)} %collective-permute-done.4.refs_2_.refs_5_) | copy-start | bytes 442372
  66.2 5.3 %copy-start.30 = (bf16[128,576]{1,0:T(8,128)(2,1)}, bf16[128,576]{1,0:T(8,128)(2,1)S(1)}, u32[]{:S(2)}) copy-start(bf16[128,576]{1,0:T(8,128)(2,1)S(1)} %collective-permute-done.5.refs_3_.refs_6_) | copy-start | bytes 442372
  66.2 5.4 %copy-start = (bf16[1536,512]{0,1:T(8,128)(2,1)S(1)}, bf16[1536,512]{0,1:T(8,128)(2,1)}, u32[]{:S(2)}) copy-start(bf16[1536,512]{0,1:T(8,128)(2,1)} %copy.24) | copy-start | bytes 4718596
  71.6 4.8 %copy-start.2 = (f32[1536,128]{1,0:T(8,128)}, f32[1536,128]{1,0:T(8,128)S(1)}, u32[]{:S(2)}) copy-start(f32[1536,128]{1,0:T(8,128)S(1)} %get-tuple-element.41.mc_ref.m_ref) | copy-start | bytes 2359300
  71.6 4.8 %copy-start.6 = (f32[1536,128]{1,0:T(8,128)}, f32[1536,128]{1,0:T(8,128)S(1)}, u32[]{:S(2)}) copy-start(f32[1536,128]{1,0:T(8,128)S(1)} %get-tuple-element.42.l_ref) | copy-start | bytes 2359300
  71.6 4.8 %copy-start.8 = (f32[1536,128]{1,0:T(8,128)}, f32[1536,128]{1,0:T(8,128)S(1)}, u32[]{:S(2)}) copy-start(f32[1536,128]{1,0:T(8,128)S(1)} %get-tuple-element.43.r_ref) | copy-start | bytes 2359300
  74.5 0.7 copy-start.24
  75.2 1.1 copy-start.38
  76.3 23.4 %collective-permute-start.11 = (bf16[256,576]{1,0:T(8,128)(2,1)}, bf16[256,576]{1,0:T(8,128)(2,1)}, u32[]{:S(2)}, u32[]{:S(2)}) collective-permute-start(bf16[256,576]{1,0:T(8,128)(2,1)} %get-tuple-element.56), channel_id=1, source_target_pairs={{0,1},{1,0},{2,3},{3,2},{4,5},{5,4},{6,7},{7,6},{8,9},{9,8},{10,11... | collective-permute-start | bytes 884744 | tf_op jit(solution)/shard_map/ppermute | solution.py:303
  80.3 0.8 copy-start.18
  81.1 0.8 copy-start.19
  82.0 1.6 %copy-start.36 = (bf16[1536,1024]{1,0:T(8,128)(2,1)}, bf16[1536,1024]{1,0:T(8,128)(2,1)S(1)}, u32[]{:S(2)}) copy-start(bf16[1536,1024]{1,0:T(8,128)(2,1)S(1)} %get-tuple-element.47.refs_1_) | copy-start | bytes 9437188
  85.7 19.1 %collective-permute-start.10 = (bf16[512,576]{0,1:T(8,128)(2,1)}, bf16[512,576]{0,1:T(8,128)(2,1)}, u32[]{:S(2)}, u32[]{:S(2)}) collective-permute-start(bf16[512,576]{0,1:T(8,128)(2,1)} %copy.25), channel_id=1, source_target_pairs={{0,1},{1,0},{2,3},{3,2},{4,5},{5,4},{6,7},{7,6},{8,9},{9,8},{10,11... | collective-permute-start | bytes 1769480 | tf_op jit(solution)/shard_map/ppermute | solution.py:303
  86.2 1.4 copy-start.1
  87.6 1.1 copy-start.3
  88.8 1.1 copy-start.7
  89.9 1.1 copy-start.9
  91.0 1.4 copy-start.13
  92.4 1.4 copy-start.15
  93.8 1.1 copy-start.17
  95.0 4.8 %copy-start.25 = (bf16[256,576]{1,0:T(8,128)(2,1)S(1)}, bf16[256,576]{1,0:T(8,128)(2,1)}, u32[]{:S(2)}) copy-start(bf16[256,576]{1,0:T(8,128)(2,1)} %copy-done.24) | copy-start | bytes 884740
  98.6 1.1 copy-start.40
  99.7 6.5 %copy-start.20 = (bf16[512,576]{1,0:T(8,128)(2,1)S(1)}, bf16[512,576]{1,0:T(8,128)(2,1)}, u32[]{:S(2)}) copy-start(bf16[512,576]{1,0:T(8,128)(2,1)} %copy-done.19) | copy-start | bytes 1769476
  99.7 14.0 %collective-permute-start.9 = (bf16[256,576]{1,0:T(8,128)(2,1)}, bf16[256,576]{1,0:T(8,128)(2,1)S(1)}, u32[]{:S(2)}, u32[]{:S(2)}) collective-permute-start(bf16[256,576]{1,0:T(8,128)(2,1)} %get-tuple-element.52), channel_id=1, source_target_pairs={{0,1},{1,0},{2,3},{3,2},{4,5},{5,4},{6,7},{7,6},{8,9},{9,8},{10,11... | collective-permute-start | bytes 884744 | tf_op jit(solution)/shard_map/ppermute | solution.py:303
  101.6 8.1 %collective-permute-start.12 = (bf16[128,576]{1,0:T(8,128)(2,1)}, bf16[128,576]{1,0:T(8,128)(2,1)}, u32[]{:S(2)}, u32[]{:S(2)}) collective-permute-start(bf16[128,576]{1,0:T(8,128)(2,1)} %get-tuple-element.62), channel_id=1, source_target_pairs={{0,2},{1,3},{2,4},{3,5},{4,6},{5,7},{6,0},{7,1},{8,10},{9,11},{10,... | collective-permute-start | bytes 442376 | tf_op jit(solution)/shard_map/ppermute | solution.py:303
  101.6 8.1 %collective-permute-start.14 = (bf16[128,576]{1,0:T(8,128)(2,1)S(1)}, bf16[128,576]{1,0:T(8,128)(2,1)}, u32[]{:S(2)}, u32[]{:S(2)}) collective-permute-start(bf16[128,576]{1,0:T(8,128)(2,1)S(1)} %get-tuple-element.61), channel_id=1, source_target_pairs={{0,6},{1,7},{2,0},{3,1},{4,2},{5,3},{6,4},{7,5},{8,14},{9,15},{10,... | collective-permute-start | bytes 442376 | tf_op jit(solution)/shard_map/ppermute | solution.py:303
  106.4 17.2 %copy-start.23 = (bf16[256,576]{1,0:T(8,128)(2,1)S(1)}, bf16[256,576]{1,0:T(8,128)(2,1)}, u32[]{:S(2)}) copy-start(bf16[256,576]{1,0:T(8,128)(2,1)} %copy-done.22) | copy-start | bytes 884740
  110.8 9.3 %collective-permute-start.15 = (bf16[256,576]{1,0:T(8,128)(2,1)S(1)}, bf16[256,576]{1,0:T(8,128)(2,1)S(1)}, u32[]{:S(2)}, u32[]{:S(2)}) collective-permute-start(bf16[256,576]{1,0:T(8,128)(2,1)S(1)} %pad_maximum_fusion.1), channel_id=1, source_target_pairs={{0,6},{1,7},{2,0},{3,1},{4,2},{5,3},{6,4},{7,5},{8,14},{9,15},{10,... | collective-permute-start | bytes 884744 | tf_op jit(solution)/shard_map/ppermute | solution.py:303
  113.6 9.9 %collective-permute-start.13 = (bf16[256,576]{1,0:T(8,128)(2,1)S(1)}, bf16[256,576]{1,0:T(8,128)(2,1)S(1)}, u32[]{:S(2)}, u32[]{:S(2)}) collective-permute-start(bf16[256,576]{1,0:T(8,128)(2,1)S(1)} %pad_maximum_fusion), channel_id=1, source_target_pairs={{0,2},{1,3},{2,4},{3,5},{4,6},{5,7},{6,0},{7,1},{8,10},{9,11},{10,... | collective-permute-start | bytes 884744 | tf_op jit(solution)/shard_map/ppermute | solution.py:303
  123.5 5.7 %copy-start.27 = (bf16[128,576]{1,0:T(8,128)(2,1)S(1)}, bf16[128,576]{1,0:T(8,128)(2,1)}, u32[]{:S(2)}) copy-start(bf16[128,576]{1,0:T(8,128)(2,1)} %copy-done.26) | copy-start | bytes 442372
  123.5 5.7 %copy-start.29 = (bf16[128,576]{1,0:T(8,128)(2,1)S(1)}, bf16[128,576]{1,0:T(8,128)(2,1)}, u32[]{:S(2)}) copy-start(bf16[128,576]{1,0:T(8,128)(2,1)} %copy-done.28) | copy-start | bytes 442372
  123.5 5.8 %copy-start.31 = (bf16[128,576]{1,0:T(8,128)(2,1)S(1)}, bf16[128,576]{1,0:T(8,128)(2,1)}, u32[]{:S(2)}) copy-start(bf16[128,576]{1,0:T(8,128)(2,1)} %copy-done.30) | copy-start | bytes 442372
  125.4 21.4 %all-to-all-start.1 = ((bf16[16,2,16,576]{3,2,1,0:T(8,128)(2,1)}), bf16[16,2,16,576]{3,2,1,0:T(8,128)(2,1)S(1)}, u32[]{:S(2)}, u32[]{:S(2)}) async-start(bf16[16,2,16,576]{3,2,1,0:T(8,128)(2,1)} %bitcast.19), calls=%async_computation.1 | async-start | bytes 1310720 | tf_op jit(solution)/shard_map/all_to_all | solution.py:382
  129.3 1.9 %copy-start.37 = (bf16[1536,1024]{1,0:T(8,128)(2,1)S(1)}, bf16[1536,1024]{1,0:T(8,128)(2,1)}, u32[]{:S(2)}) copy-start(bf16[1536,1024]{1,0:T(8,128)(2,1)} %copy-done.36) | copy-start | bytes 9437188
  131.2 1.4 copy-start.39
  132.6 1.4 copy-start.41
  134.0 1.0 copy-start.43
  135.0 1.0 copy-start.45
  136.0 1.0 copy-start.47
  (3 other events, 2.1 us)

commit v3 on v2

v3 whole, which is shorter than its diff:
```python
import functools
import math

import jax
import jax.numpy as jnp
from jax import lax
from jax.experimental import pallas as pl
from jax.experimental.pallas import tpu as pltpu
from jax.sharding import PartitionSpec as P

LAT = 512
WIDE = 576
BLOCK = 128
MAXL = 16
CAP = 2
BIG = -1e30
SLOTS = 16 * CAP
SCALE = 192.0 ** (-0.5)
EXPC = SCALE * math.log2(math.e)
NT = (((1,), (1,)), ((), ()))
NN = (((1,), (0,)), ((), ()))
f32 = jnp.float32
bf16 = jnp.bfloat16


def dot(a, b, dims=NN):
    return lax.dot_general(a, b, dims, preferred_element_type=f32)


def owner_table(lists, counts, own, table, empty):
    def group(g, carry):
        table[g * CAP] = empty
        table[g * CAP + 1] = empty
        rank = jnp.int32(0)
        for j in range(MAXL):
            block = lists[g, j]
            mine = ((block >> 4) == own) & (j < counts[g])
            table[jnp.where(mine, g * CAP + rank, SLOTS)] = block & 15
            rank = jnp.where(mine, jnp.minimum(rank + 1, CAP - 1), rank)
        return carry

    lax.fori_loop(0, 16, group, 0)


def slot_table(lists, counts, own, table, seen):
    for o in range(16):
        seen[o] = 0
    for j in range(MAXL):
        owner = lists[own, j] >> 4
        rank = seen[owner]
        seen[owner] = jnp.minimum(rank + 1, CAP - 1)
        table[j] = owner * CAP + rank


def pick_body(lists, counts, me, lat_ref, out_ref, table, sems):
    owner_table(lists, counts, me[0], table, 0)
    copies = [pltpu.make_async_copy(lat_ref.at[table[s]], out_ref.at[s], sems.at[s]) for s in range(SLOTS)]
    for copy in copies:
        copy.start()
    for copy in copies:
        copy.wait()


def gather_body(lists, counts, me, arrived_ref, out_ref, table, held, total, sems, sems_out):
    step = SLOTS // 4
    parts = [slice(i * step, i * step + step) for i in range(4)]
    copies = [pltpu.make_async_copy(arrived_ref.at[p], held.at[p], sems.at[i]) for i, p in enumerate(parts)]
    for copy in copies:
        copy.start()
    owner_table(lists, counts, me[0], table, 16)
    total[...] = jnp.zeros(total.shape, total.dtype)
    for s in range(SLOTS):
        if s % step == 0:
            copies[s // step].wait()
        total[table[s]] = total[table[s]] + held[s].astype(f32)
    copies = [pltpu.make_async_copy(total.at[4 * i : 4 * i + 4], out_ref.at[4 * i : 4 * i + 4], sems_out.at[i]) for i in range(4)]
    for copy in copies:
        copy.start()
    for copy in copies:
        copy.wait()


def take_body(lists, counts, me, arrived_ref, out_ref, table, seen, sems):
    slot_table(lists, counts, me[0], table, seen)
    count = counts[me[0]]

    def copy(j):
        return pltpu.make_async_copy(arrived_ref.at[table[j]], out_ref.at[j * 16 : j * 16 + 16], sems.at[j])

    for j in range(MAXL):
        live = j < count

        @pl.when(live)
        def _():
            copy(j).start()

        @pl.when(jnp.logical_not(live))
        def _():
            out_ref[j * 16 : j * 16 + 16] = jnp.zeros((16, WIDE), bf16)

    for j in range(MAXL):

        @pl.when(j < count)
        def _():
            copy(j).wait()


def put_body(lists, counts, me, a_ref, b_ref, c_ref, d_ref, out_ref, table, seen, held, sems):
    slot_table(lists, counts, me[0], table, seen)
    count = counts[me[0]]

    def copy(j):
        return pltpu.make_async_copy(held.at[j * 16 : j * 16 + 16], out_ref.at[table[j]], sems.at[j])

    for j in range(MAXL):
        here = slice(j * 16, j * 16 + 16)
        total = a_ref[here].astype(f32) + b_ref[here].astype(f32)
        total = total + (c_ref[here].astype(f32) + d_ref[here].astype(f32))
        held[here] = total.astype(bf16)

        @pl.when(j < count)
        def _():
            copy(j).start()

    for j in range(MAXL):

        @pl.when(j < count)
        def _():
            copy(j).wait()


def turn_body(q_ref, g_ref, qt_ref, gt_ref):
    rows = qt_ref.shape[1]
    for at in range(0, rows, 256):
        here = slice(at, at + 256)
        part = slice(at // 16, at // 16 + 16)
        q = q_ref[part].reshape(256, WIDE)
        qt_ref[:LAT, here] = q[:, :LAT].T
        rope = jnp.concatenate([q[:, LAT:], q[:, LAT:]], axis=1)
        qt_ref[LAT:, here] = rope.T[: WIDE - LAT]
        gt_ref[:, here] = g_ref[part].reshape(256, LAT).T


def two_body(near_ref, far_ref, low_ref, high_ref):
    half = low_ref.shape[0]
    total = near_ref[...].astype(f32) + far_ref[...].astype(f32)
    low_ref[...] = total[:half].astype(bf16)
    high_ref[...] = total[half:].astype(bf16)


def one_body(near_ref, far_ref, low_ref, high_ref, left_ref, right_ref):
    size = left_ref.shape[0]
    half = size // 2
    total = near_ref[...].astype(f32) + far_ref[...].astype(f32)
    left_ref[:half] = total[:half].astype(bf16)
    left_ref[half:] = (total[half:size] + high_ref[...].astype(f32)).astype(bf16)
    right_ref[:half] = (total[size : size + half] + low_ref[...].astype(f32)).astype(bf16)
    right_ref[half:] = total[size + half :].astype(bf16)


ONCHIP = pl.BlockSpec(memory_space=pltpu.VMEM)
INPLACE = pl.BlockSpec(memory_space=pltpu.HBM)


def call(body, outs, scalars, arrays, scratch=(), direct_in=(), direct=(), alias=None):
    args = [
        pltpu.with_memory_space_constraint(a, pltpu.HBM if i in direct_in else pltpu.VMEM)
        for i, a in enumerate(arrays)
    ]
    scalars = [pltpu.with_memory_space_constraint(a, pltpu.HBM) for a in scalars]
    shapes = [(pltpu.HBM if i in direct else pltpu.VMEM)(o.shape, o.dtype) for i, o in enumerate(outs)]
    return pl.pallas_call(
        body,
        in_specs=[pl.BlockSpec(memory_space=pltpu.SMEM)] * len(scalars)
        + [INPLACE if i in direct_in else ONCHIP for i in range(len(arrays))],
        out_specs=tuple(INPLACE if i in direct else ONCHIP for i in range(len(outs))),
        out_shape=tuple(shapes),
        scratch_shapes=list(scratch),
        input_output_aliases=alias or {},
        compiler_params=pltpu.CompilerParams(vmem_limit_bytes=16 * 1024 * 1024),
    )(*scalars, *args)


M_COL, L_COL, R_COL = (0, 1, 2), 3, 4


def forward_body(nkeys, chunk, off, n, block, *refs):
    refs = list(refs)
    first, last = chunk == 0, chunk == 2
    key_refs = [refs.pop(0) for _ in range(nkeys)]
    bias, q_ref, g_ref = refs[:3]
    refs = refs[3:]
    if not first:
        _, _, _, st_in, o_in = refs[:5]
        refs = refs[5:]
    if last:
        qt_in, gt_in = refs[:2]
        refs = refs[2:]
    e_out, p_out, k_out, st_out, o_out = refs[:5]
    refs = refs[5:]
    steps = q_ref.shape[0] * 16 // block
    if last:
        qt_out, gt_out, held, sems, sems_t = refs
        turned = [
            pltpu.make_async_copy(qt_in, qt_out, sems_t.at[0]),
            pltpu.make_async_copy(gt_in, gt_out, sems_t.at[1]),
        ]
        for copy in turned:
            copy.start()

        def leave(i):
            part = pl.ds(i * (block // 16), block // 16)
            return pltpu.make_async_copy(held.at[part], o_out.at[part], sems.at[i])

    at = off
    for ref in key_refs:
        k_out[at : at + ref.shape[0]] = ref[...]
        at += ref.shape[0]
    mine = slice(off, off + n)

    def rows(i, carry):
        here = pl.ds(pl.multiple_of(i * block, block), block)
        part = pl.ds(i * (block // 16), block // 16)
        scores = dot(q_ref[part].reshape(block, WIDE), k_out[mine], NT) + bias[...]
        top = jnp.max(scores, axis=1, keepdims=True)
        if not first:
            m_old = st_in[here, chunk - 1 : chunk]
            l_old = st_in[here, L_COL : L_COL + 1]
            r_old = st_in[here, R_COL : R_COL + 1]
            top = jnp.maximum(top, m_old)
        expo = jnp.exp2((scores - top) * EXPC)
        values = k_out[mine, :LAT]
        grads = dot(g_ref[part].reshape(block, LAT), values, NT)
        total = jnp.sum(expo, axis=1, keepdims=True)
        rdot = jnp.sum(expo * grads, axis=1, keepdims=True)
        expo = expo.astype(bf16)
        e_out[here, mine] = expo
        p_out[here, mine] = grads.astype(bf16)
        attended = dot(expo, values)
        if not first:
            fade = jnp.exp2((m_old - top) * EXPC)
            total = total + fade * l_old
            rdot = rdot + fade * r_old
            attended = attended + fade * o_in[here]
        if last:
            total = 1.0 / total
            rdot = rdot * total
            attended = attended * total
        st_out[here, chunk : chunk + 1] = top
        st_out[here, L_COL : L_COL + 1] = total
        st_out[here, R_COL : R_COL + 1] = rdot
        if last:
            held[part] = attended.astype(bf16).reshape(block // 16, 16, LAT)
            leave(i).start()
        else:
            o_out[here] = attended
        return carry

    lax.fori_loop(0, steps, rows, 0)
    if last:
        for i in range(steps):
            leave(i).wait()
        for copy in turned:
            copy.wait()


def forward(chunk, off, n, total_keys, key_parts, bias, q, g, state=(), turned=(), block=256):
    rows = q.shape[0] * 16
    last = chunk == 2
    side = jax.ShapeDtypeStruct((rows, total_keys), bf16)
    outs = [
        side,
        side,
        jax.ShapeDtypeStruct((total_keys, WIDE), bf16),
        jax.ShapeDtypeStruct((rows, 128), f32),
        jax.ShapeDtypeStruct(g.shape, bf16) if last else jax.ShapeDtypeStruct((rows, LAT), f32),
    ]
    scratch = []
    if last:
        outs += [jax.ShapeDtypeStruct(t.shape, t.dtype) for t in turned]
        scratch = [pltpu.VMEM(g.shape, bf16), pltpu.SemaphoreType.DMA((rows // block,)), pltpu.SemaphoreType.DMA((2,))]
    arrays = [*key_parts, bias, q, g, *state, *turned]
    start = len(key_parts) + 3
    return call(
        functools.partial(forward_body, len(key_parts), chunk, off, n, block),
        outs,
        (),
        arrays,
        scratch=scratch,
        direct_in=range(len(arrays) - len(turned), len(arrays)),
        direct=(4,) if last else (),
        alias={start + i: i for i in range((4 if last else 5) if state else 0)},
    )


def backward_body(chunk, off, n, step, tile, qt_ref, gt_ref, e_ref, p_ref, st_ref, k_ref, far_out, near_out, s_out, k_out, a_sc, r_sc):
    rows = qt_ref.shape[1]
    half = n // 2
    st = st_ref[...]
    a = jnp.exp2((st[:, chunk : chunk + 1] - st[:, 2:3]) * EXPC) * st[:, L_COL : L_COL + 1]
    a_sc[...] = jnp.broadcast_to(a, (rows, 128))
    r_sc[...] = jnp.broadcast_to(st[:, R_COL : R_COL + 1], (rows, 128))
    for start in range(0, n, tile):
        cols = slice(off + (start + half) % n, off + (start + half) % n + tile)
        acc = None
        for at in range(0, rows, step):
            here = slice(at, at + step)
            a = jnp.tile(a_sc[here], (1, tile // 128))
            r = jnp.tile(r_sc[here], (1, tile // 128))
            weights = (e_ref[here, cols].astype(f32) * a).astype(bf16)
            sg = (weights.astype(f32) * (p_ref[here, cols].astype(f32) - r) * SCALE).astype(bf16)
            s_out[here, cols] = sg
            key_part = dot(qt_ref[:, here], sg)
            value_part = dot(gt_ref[:, here], weights)
            if acc is None:
                acc = [key_part[:LAT] + value_part, key_part[LAT:]]
            else:
                acc = [acc[0] + (key_part[:LAT] + value_part), acc[1] + key_part[LAT:]]
        top = acc[0].T.astype(bf16)
        low = jnp.concatenate([acc[1], jnp.zeros_like(acc[1])], axis=0).T[:, : WIDE - LAT].astype(bf16)
        ref = far_out if start < half else near_out
        put = slice(start % half, start % half + tile)
        ref[put, :LAT] = top
        ref[put, LAT:] = low


def backward(chunk, off, n, qt, gt, e, p, st, k, tile=256, step=256):
    rows = e.shape[0]
    part = jax.ShapeDtypeStruct((n // 2, WIDE), bf16)
    return call(
        functools.partial(backward_body, chunk, off, n, step, tile),
        (part, part, jax.ShapeDtypeStruct(p.shape, bf16), jax.ShapeDtypeStruct(k.shape, bf16)),
        (),
        (qt, gt, e, p, st, k),
        scratch=[pltpu.VMEM((rows, 128), f32)] * 2,
        alias={3: 2, 5: 3},
    )


def query_body(block, s_ref, k_ref, out_ref, held, sems):
    steps = out_ref.shape[0] * 16 // block

    def leave(i):
        part = pl.ds(i * (block // 16), block // 16)
        return pltpu.make_async_copy(held.at[part], out_ref.at[part], sems.at[i])

    def rows(i, carry):
        here = pl.ds(pl.multiple_of(i * block, block), block)
        part = pl.ds(i * (block // 16), block // 16)
        held[part] = dot(s_ref[here], k_ref[...]).astype(bf16).reshape(block // 16, 16, WIDE)
        leave(i).start()
        return carry

    lax.fori_loop(0, steps, rows, 0)
    for i in range(steps):
        leave(i).wait()


def query_side(s, k, block=256):
    rows = s.shape[0]
    shape = (rows // 16, 16, WIDE)
    return call(
        functools.partial(query_body, block),
        (jax.ShapeDtypeStruct(shape, bf16),),
        (),
        (s, k),
        scratch=[pltpu.VMEM(shape, bf16), pltpu.SemaphoreType.DMA((rows // block,))],
        direct=(0,),
    )[0]


def per_device(queries, out_grad, latents, list_blocks, list_counts, valid_tokens):
    me = lax.axis_index("req")
    head = lax.axis_index("head")
    chip, core = head // 2, head % 2
    tokens = latents.shape[1]
    shift = lambda d: [(x * 2 + c, ((x + d) % 4) * 2 + c) for x in range(4) for c in range(2)]
    right, left, sibling = shift(1), shift(-1), [(h, h ^ 1) for h in range(8)]
    send = lambda a, perm: lax.ppermute(a, "head", perm)
    scalars = (list_blocks, list_counts, me.reshape(1).astype(jnp.int32))

    smem = lambda n: pltpu.SMEM((n,), jnp.int32)
    slots = jax.ShapeDtypeStruct((SLOTS, tokens, WIDE), bf16)
    keys = MAXL * tokens
    share_of = lambda n: jax.ShapeDtypeStruct((n, WIDE), bf16)

    dma = lambda n: pltpu.SemaphoreType.DMA((n,))
    (outgoing,) = call(
        pick_body, (slots,), scalars, (latents,), scratch=[smem(SLOTS + 1), dma(SLOTS)], direct_in=(0,), direct=(0,)
    )
    arrived = lax.all_to_all(outgoing.reshape(16, CAP, tokens, WIDE), "req", 0, 0, tiled=True)

    my_blocks = lax.dynamic_index_in_dim(list_blocks, me, 0, keepdims=False)
    my_count = lax.dynamic_index_in_dim(list_counts, me, 0, keepdims=False)
    ids = jnp.arange(valid_tokens.shape[0], dtype=jnp.int32)
    filled = jnp.sum(jnp.where(my_blocks[:, None] == ids[None, :], valid_tokens[None, :], 0), axis=1)
    filled = jnp.where(jnp.arange(MAXL, dtype=jnp.int32) < my_count, filled, 0)
    filled = jnp.repeat(filled, tokens)[None, :]
    offset = jnp.tile(jnp.arange(tokens, dtype=jnp.int32), MAXL)[None, :]
    at = lambda d, c: ((chip + d) % 4) * 2 + c
    other = 1 - core
    places = [at(0, core), at(0, other), at(3, core), at(1, core), at(3, other), at(1, other), at(2, core), at(2, other)]
    first_token = jnp.stack(places)[:, None] * tokens
    bias = jnp.where(first_token + offset < filled, 0.0, BIG).astype(f32)
    bias0, bias1, bias2 = [bias[i:j].reshape(1, -1) for i, j in ((0, 2), (2, 6), (6, 8))]

    flat = lambda a: jax.ShapeDtypeStruct((a.shape[2], a.shape[0] * a.shape[1]), bf16)
    qt, gt = call(turn_body, (flat(queries), flat(out_grad)), (), (queries, out_grad))
    arrived, qt, gt, bias0, bias1, bias2 = lax.optimization_barrier((arrived, qt, gt, bias0, bias1, bias2))

    (share,) = call(
        take_body,
        (share_of(keys),),
        scalars,
        (arrived.reshape(slots.shape),),
        scratch=[smem(MAXL), smem(16), dma(MAXL)],
        direct_in=(0,),
    )

    after = lambda a, *others: lax.optimization_barrier((a, *others))[0]
    q, g = queries, out_grad
    every = 8 * keys
    r1 = send(share, right)
    l1 = send(share, left)
    s0 = send(share, sibling)
    state = forward(0, 0, 2 * keys, every, [share, s0], bias0, q, g)
    r1 = after(r1, state[3])
    l1 = after(l1, state[3])
    r2 = send(r1, right)
    s1 = send(r1, sibling)
    s2 = send(l1, sibling)
    state = forward(1, 2 * keys, 4 * keys, every, [r1, l1, s1, s2], bias1, q, g, state)
    r2 = after(r2, state[3])
    s3 = send(r2, sibling)
    e, p, k, st, attended, qt, gt = forward(2, 6 * keys, 2 * keys, every, [r2, s3], bias2, q, g, state, (qt, gt))

    fold = lambda a: a.reshape(-1, tokens, WIDE)
    unfold = lambda a: a.reshape(-1, WIDE)
    far2, near2, p, k = backward(2, 6 * keys, 2 * keys, qt, gt, e, p, st, k)
    mate2 = send(far2, sibling)
    far1, near1, p, k = backward(1, 2 * keys, 4 * keys, qt, gt, e, p, st, k)
    mate1 = unfold(send(fold(far1), sibling))
    low, high = call(two_body, (share_of(keys // 2),) * 2, (), (after(near2, near1), mate2))
    from_left = send(low, right)
    from_right = send(high, left)
    far0, near0, p, k = backward(0, 0, 2 * keys, qt, gt, e, p, after(st, low), k)
    mate0 = send(far0, sibling)
    to_left, to_right = call(
        one_body, (share_of(keys),) * 2, (), (after(near1, near0), mate1, from_left, from_right)
    )
    got_left = send(to_right, right)
    got_right = send(to_left, left)
    query_grad = query_side(p, after(k, to_left))
    near0 = after(near0, query_grad)
    (slot_grads,) = call(
        put_body,
        (slots,),
        scalars,
        (near0, mate0, got_left, got_right),
        scratch=[smem(MAXL), smem(16), pltpu.VMEM((keys, WIDE), bf16), dma(MAXL)],
        direct=(0,),
    )
    returned = lax.all_to_all(slot_grads.reshape(16, CAP, tokens, WIDE), "req", 0, 0, tiled=True)
    (latent_grad,) = call(
        gather_body,
        (jax.ShapeDtypeStruct((16, tokens, WIDE), f32),),
        scalars,
        (returned.reshape(slots.shape),),
        scratch=[
            smem(SLOTS + 1),
            pltpu.VMEM((SLOTS, tokens, WIDE), bf16),
            pltpu.VMEM((17, tokens, WIDE), f32),
            dma(4),
            dma(4),
        ],
        direct_in=(0,),
        direct=(0,),
    )
    return (attended, query_grad, latent_grad)


def solution(mesh):
    in_specs = (
        P("req", "head", None),
        P("req", "head", None),
        P("req", "head", None),
        P(),
        P(),
        P(),
    )
    out_specs = (P("req", "head", None), P("req", "head", None), P("req", "head", None))
    return jax.shard_map(
        per_device, mesh=mesh, in_specs=in_specs, out_specs=out_specs, check_vma=False
    )
```

time: 154 us -> 130 us (0.84)
  local copies, waits for them, and re-layouts: 43.6 us -> 6.07 us
  blocking collectives: 0 us -> 15.9 us
  Pallas kernels: 52.8 us -> 67 us
  starting transfers between devices: 26.3 us -> 17.7 us
  waiting for transfers between devices: 25.5 us -> 19.9 us
  other arithmetic: 3.39 us -> 1.59 us
    unnamed x101 -> x15, local copies, waits for them, and re-layouts: 31.9 us -> 3.81 us
    all_to_all x0 -> x1, blocking collectives: none -> 15.9 us  [per_device(): lax.all_to_all(slot_grads.reshape(16, CAP, tokens, WIDE), 'req', 0, 0, ti...]
    pallas_call x11 -> x14, Pallas kernels: 52.8 us -> 67 us  [call(): pl.pallas_call(body, in_specs=[pl.BlockSpec(memory_space=pltpu.SMEM)] * l...]
    all_to_all x1, waiting for transfers between devices: 11.4 us -> 3.73 us  [per_device(): lax.all_to_all(outgoing.reshape(16, CAP, tokens, WIDE), 'req', 0, 0, tile...]
    ppermute x16 -> x14, starting transfers between devices: 14.3 us -> 9.5 us  [per_device(): send = lambda a, perm: lax.ppermute(a, 'head', perm)]
    reshape x2 -> x0, local copies, waits for them, and re-layouts: 4.35 us -> none  [the longest x1 2.78 us: per_device(): q = queries.reshape(-1, WIDE)]
    all_to_all x1 -> x0, starting transfers between devices: 3.91 us -> none  [per_device(): lax.all_to_all(slot_grads.reshape(16, CAP, tokens, WIDE), 'req', 0, 0, ti...]
    slice x4 -> x0, local copies, waits for them, and re-layouts: 2.59 us -> none  [the longest x1 0.93 us: per_device(): r2 = send(r1[:keep], right)]
  transfers between devices with their start and end apart: 18 -> 15, of which waited for: 5 -> 10; matrix products, arithmetic and copies ran while one was open for 11% -> 3% of each run, Pallas kernels for 20% -> 19%
where the time goes in v3:
time: 130 us; the launch traced here: 129 us
  Pallas kernels  67 us (52%)
  waiting for transfers between devices  19.9 us (15%)
  starting transfers between devices  17.7 us (14%)
  blocking collectives  15.9 us (12%)
  local copies, waits for them, and re-layouts  6.07 us (5%)
  other arithmetic  1.59 us (1%)
    pallas_call x14, Pallas kernels, call(): pl.pallas_call(body, in_specs=[pl.BlockSpec(memory_space=pltpu.SMEM)] * l...  67 us
    ppermute x14, waiting for transfers between devices, per_device(): send = lambda a, perm: lax.ppermute(a, 'head', perm)  16.1 us
    all_to_all x1, blocking collectives, per_device(): lax.all_to_all(slot_grads.reshape(16, CAP, tokens, WIDE), 'req', 0, 0, ti...  15.9 us
    ppermute x14, starting transfers between devices, per_device(): send = lambda a, perm: lax.ppermute(a, 'head', perm)  9.5 us
    all_to_all x1, starting transfers between devices, per_device(): lax.all_to_all(outgoing.reshape(16, CAP, tokens, WIDE), 'req', 0, 0, tile...  8.22 us
    unnamed x15, local copies, waits for them, and re-layouts  3.81 us
    all_to_all x1, waiting for transfers between devices, per_device(): lax.all_to_all(outgoing.reshape(16, CAP, tokens, WIDE), 'req', 0, 0, tile...  3.73 us
  transfers between devices with their start and end apart: 15, of which 10 were waited for; matrix products, arithmetic and copies ran while one was open for 3% of the time, Pallas kernels for 19%

profile of v3, /device:TPU:0, one launch (start us, length us, event | category | flops | bytes accessed | tf_op | source)
XLA Modules:
  0.0 129.3 jit_solution(11601268329363660124)
XLA Ops:
  0.6 0.0 copy-start
  0.6 23.2 %shard_map.85 = bf16[32,16,576]{2,1,0:T(8,128)(2,1)} custom-call(s32[16,16]{1,0:T(8,128)} %lists.7, s32[16]{0:T(128)} %counts.7, s32[1]{0:T(128)} %bitcast.me, bf16[16,16,576]{2,1,0:T(8,128)(2,1)} %lat_ref.1), custom_call_target="tpu_custom_call" | custom-call | tf_op jit(solution)/shard_map/pallas_call | solution.py:172
  23.8 8.2 %all-to-all-start = ((bf16[16,2,16,576]{3,2,1,0:T(8,128)(2,1)}), bf16[16,2,16,576]{3,2,1,0:T(8,128)(2,1)}, u32[]{:S(2)}, u32[]{:S(2)}) async-start(bf16[16,2,16,576]{3,2,1,0:T(8,128)(2,1)} %bitcast.36), calls=%async_computation | async-start | bytes 1310720 | tf_op jit(solution)/shard_map/all_to_all | solution.py:391
  32.1 1.2 dynamic_slice.8
  33.4 0.7 dynamic-slice_bitcast_fusion
  34.1 0.1 stack.35
  34.2 0.9 select_reduce_fusion
  35.0 0.7 compare_select_fusion
  35.7 0.1 broadcast_in_dim.34
  35.8 0.1 lt.60
  35.8 0.1 add.95
  35.9 0.1 fusion
  36.0 0.0 copy-done
  36.1 0.0 copy-start.1
  36.1 1.4 %copy-done.1 = bf16[96,16,512]{2,1,0:T(8,128)(2,1)S(1)} copy-done((bf16[96,16,512]{2,1,0:T(8,128)(2,1)S(1)}, bf16[96,16,512]{2,1,0:T(8,128)(2,1)}, u32[]{:S(2)}) %copy-start.1) | copy-done | bytes 1572888
  37.5 0.0 copy-start.2
  37.5 1.4 %shard_map.86 = (bf16[576,1536]{1,0:T(8,128)(2,1)S(1)}, bf16[512,1536]{1,0:T(8,128)(2,1)S(1)}) custom-call(bf16[96,16,576]{2,1,0:T(8,128)(2,1)S(1)} %copy-done, bf16[96,16,512]{2,1,0:T(8,128)(2,1)S(1)} %copy-done.1), custom_call_target="tpu_custom_call" | custom-call | tf_op jit(solution)/shard_map/pallas_call | solution.py:172
  38.9 0.0 copy-start.3
  38.9 1.2 copy-done.3
  40.1 0.0 copy-start.4
  40.1 1.2 copy-done.4
  41.3 3.7 %all-to-all-done = bf16[16,2,16,576]{3,2,1,0:T(8,128)(2,1)} async-done(((bf16[16,2,16,576]{3,2,1,0:T(8,128)(2,1)}), bf16[16,2,16,576]{3,2,1,0:T(8,128)(2,1)}, u32[]{:S(2)}, u32[]{:S(2)}) %all-to-all-start) | async-done | bytes 589856 | tf_op jit(solution)/shard_map/all_to_all | solution.py:391
  45.0 1.9 %shard_map.87.refs_0_ = bf16[256,576]{1,0:T(8,128)(2,1)S(1)} custom-call(s32[16,16]{1,0:T(8,128)} %lists.7, s32[16]{0:T(128)} %counts.7, s32[1]{0:T(128)} %bitcast.me, bf16[32,16,576]{2,1,0:T(8,128)(2,1)} %bitcast.12.arrived_ref), custom_call_target="tpu_custom_call" | custom-call | tf_op jit(solution)/shard_map/pallas_call | solution.py:172
  46.9 0.1 collective-permute-start.1
  47.0 2.8 %collective-permute-start.3 = (bf16[256,576]{1,0:T(8,128)(2,1)S(1)}, bf16[256,576]{1,0:T(8,128)(2,1)S(1)}, u32[]{:S(2)}, u32[]{:S(2)}) collective-permute-start(bf16[256,576]{1,0:T(8,128)(2,1)S(1)} %shard_map.87.refs_0_), channel_id=1, source_target_pairs={{0,6},{1,7},{2,0},{3,1},{4,2},{5,3},{6,4},{7,5},{8,14},{9,15},{10,... | collective-permute-start | bytes 884744 | tf_op jit(solution)/shard_map/ppermute | solution.py:379
  49.9 0.0 collective-permute-start
  49.9 0.0 collective-permute-done.1.refs_1_
  49.9 0.0 copy-done.2
  49.9 4.3 %shard_map.88 = (bf16[1536,2048]{1,0:T(8,128)(2,1)S(1)}, bf16[1536,2048]{1,0:T(8,128)(2,1)S(1)}, bf16[2048,576]{1,0:T(8,128)(2,1)S(1)}, f32[1536,128]{1,0:T(8,128)S(1)}, f32[1536,512]{1,0:T(8,128)S(1)}) custom-call(bf16[256,576]{1,0:T(8,128)(2,1)S(1)} %shard_map.87.refs_0_, bf16[256,576]{1,0:T(8,128)(2,1)S(1)} %collective-permute-done.1.refs_1_, ...), custom_call_target="tpu_custom_call" | custom-call | tf_op jit(solution)/shard_map/pallas_call | solution.py:172
  54.2 3.2 %collective-permute-done.3.refs_1_ = bf16[256,576]{1,0:T(8,128)(2,1)S(1)} collective-permute-done((bf16[256,576]{1,0:T(8,128)(2,1)S(1)}, bf16[256,576]{1,0:T(8,128)(2,1)S(1)}, u32[]{:S(2)}, u32[]{:S(2)}) %collective-permute-start.3) | collective-permute-done | bytes 294944 | tf_op jit(solution)/shard_map/ppermute | solution.py:379
  57.4 3.4 %collective-permute-done.refs_0_ = bf16[256,576]{1,0:T(8,128)(2,1)S(1)} collective-permute-done((bf16[256,576]{1,0:T(8,128)(2,1)S(1)}, bf16[256,576]{1,0:T(8,128)(2,1)S(1)}, u32[]{:S(2)}, u32[]{:S(2)}) %collective-permute-start) | collective-permute-done | bytes 294944 | tf_op jit(solution)/shard_map/ppermute | solution.py:379
  60.8 0.0 collective-permute-start.4
  60.8 0.5 collective-permute-start.5
  61.3 0.0 collective-permute-start.2
  61.3 1.1 collective-permute-done.4.refs_2_
  62.5 0.5 collective-permute-done.5.refs_3_
  62.9 8.8 %shard_map.89 = (bf16[1536,2048]{1,0:T(8,128)(2,1)S(1)}, bf16[1536,2048]{1,0:T(8,128)(2,1)S(1)}, bf16[2048,576]{1,0:T(8,128)(2,1)S(1)}, f32[1536,128]{1,0:T(8,128)S(1)}, f32[1536,512]{1,0:T(8,128)S(1)}) custom-call(bf16[256,576]{1,0:T(8,128)(2,1)S(1)} %collective-permute-done.refs_0_, ...), custom_call_target="tpu_custom_call", output_to_operand_aliasing={{0}: (7, {}), {1}: (8, {}), {2}: (9, {}), {3}: (10, {}), {4... | custom-call | tf_op jit(solution)/shard_map/pallas_call | solution.py:172
  71.8 0.4 collective-permute-done.2.refs_0_
  72.2 0.0 collective-permute-start.6
  72.2 1.6 %collective-permute-done.6.refs_1_ = bf16[256,576]{1,0:T(8,128)(2,1)S(1)} collective-permute-done((bf16[256,576]{1,0:T(8,128)(2,1)S(1)}, bf16[256,576]{1,0:T(8,128)(2,1)S(1)}, u32[]{:S(2)}, u32[]{:S(2)}) %collective-permute-start.6) | collective-permute-done | bytes 294944 | tf_op jit(solution)/shard_map/ppermute | solution.py:379
  73.8 6.2 %shard_map.90 = (bf16[1536,2048]{1,0:T(8,128)(2,1)S(1)}, bf16[1536,2048]{1,0:T(8,128)(2,1)S(1)}, bf16[2048,576]{1,0:T(8,128)(2,1)S(1)}, f32[1536,128]{1,0:T(8,12...) custom-call(bf16[256,576]{1,0:T(8,128)(2,1)S(1)} %collective-permute, ...), custom_call_target="tpu_custom_call", output_to_operand_aliasing={{0}: (5, {}), {1}: (6, {}), {2}: (7, {}), {3}: (8, {})} | custom-call | tf_op jit(solution)/shard_map/pallas_call | solution.py:172
  80.0 2.7 %shard_map.91 = (bf16[256,576]{1,0:T(8,128)(2,1)S(1)}, bf16[256,576]{1,0:T(8,128)(2,1)S(1)}, bf16[1536,2048]{1,0:T(8,128)(2,1)S(1)}, bf16[2048,576]{1,0:T(8,128)(2,1)S(1)}) custom-call(bf16[576,1536]{1,0:T(8,128)(2,1)S(1)} %get-tuple-element.74.qt_ref, bf16[512,1536]{1,0:T(8,128)(2,1)S(1)} %get-tuple-element.75.gt_ref, ...), custom_call_target="tpu_custom_call", output_to_operand_aliasing={{2}: (3, {}), {3}: (5, {})} | custom-call | tf_op jit(solution)/shard_map/pallas_call | solution.py:172
  82.6 4.3 %shard_map.92 = (bf16[512,576]{1,0:T(8,128)(2,1)S(1)}, bf16[512,576]{1,0:T(8,128)(2,1)S(1)}, bf16[1536,2048]{1,0:T(8,128)(2,1)S(1)}, bf16[2048,576]{1,0:T(8,128)(2,1)S(1)}) custom-call(bf16[576,1536]{1,0:T(8,128)(2,1)S(1)} %get-tuple-element.74.qt_ref, bf16[512,1536]{1,0:T(8,128)(2,1)S(1)} %get-tuple-element.75.gt_ref, ...), custom_call_target="tpu_custom_call", output_to_operand_aliasing={{2}: (3, {}), {3}: (5, {})} | custom-call | tf_op jit(solution)/shard_map/pallas_call | solution.py:172
  86.9 0.2 collective-permute-start.8
  87.1 0.4 collective-permute-start.7
  87.5 2.1 %collective-permute-done.7.far_ref = bf16[256,576]{1,0:T(8,128)(2,1)S(1)} collective-permute-done((bf16[256,576]{1,0:T(8,128)(2,1)S(1)}, bf16[256,576]{1,0:T(8,128)(2,1)S(1)}, u32[]{:S(2)}, u32[]{:S(2)}) %collective-permute-start.7) | collective-permute-done | bytes 294944 | tf_op jit(solution)/shard_map/ppermute | solution.py:379
  89.6 0.1 shard_map.93
  89.6 1.6 %collective-permute-start.10 = (bf16[128,576]{1,0:T(8,128)(2,1)S(1)}, bf16[128,576]{1,0:T(8,128)(2,1)S(1)}, u32[]{:S(2)}, u32[]{:S(2)}) collective-permute-start(bf16[128,576]{1,0:T(8,128)(2,1)S(1)} %get-tuple-element.95), channel_id=1, source_target_pairs={{0,6},{1,7},{2,0},{3,1},{4,2},{5,3},{6,4},{7,5},{8,14},{9,15},{10,... | collective-permute-start | bytes 442376 | tf_op jit(solution)/shard_map/ppermute | solution.py:379
  91.2 0.5 collective-permute-start.9
  91.7 2.7 %shard_map.94 = (bf16[256,576]{1,0:T(8,128)(2,1)S(1)}, bf16[256,576]{1,0:T(8,128)(2,1)S(1)}, bf16[1536,2048]{1,0:T(8,128)(2,1)S(1)}, bf16[2048,576]{1,0:T(8,128)(2,1)S(1)}) custom-call(bf16[576,1536]{1,0:T(8,128)(2,1)S(1)} %get-tuple-element.74.qt_ref, bf16[512,1536]{1,0:T(8,128)(2,1)S(1)} %get-tuple-element.75.gt_ref, ...), custom_call_target="tpu_custom_call", output_to_operand_aliasing={{2}: (3, {}), {3}: (5, {})} | custom-call | tf_op jit(solution)/shard_map/pallas_call | solution.py:172
  94.5 0.1 collective-permute-start.11
  94.6 1.4 %collective-permute-done.10.high_ref = bf16[128,576]{1,0:T(8,128)(2,1)S(1)} collective-permute-done((bf16[128,576]{1,0:T(8,128)(2,1)S(1)}, bf16[128,576]{1,0:T(8,128)(2,1)S(1)}, u32[]{:S(2)}, u32[]{:S(2)}) %collective-permute-start.10) | collective-permute-done | bytes 147488 | tf_op jit(solution)/shard_map/ppermute | solution.py:379
  96.0 2.4 %collective-permute-done.9.low_ref = bf16[128,576]{1,0:T(8,128)(2,1)S(1)} collective-permute-done((bf16[128,576]{1,0:T(8,128)(2,1)S(1)}, bf16[128,576]{1,0:T(8,128)(2,1)S(1)}, u32[]{:S(2)}, u32[]{:S(2)}) %collective-permute-start.9) | collective-permute-done | bytes 147488 | tf_op jit(solution)/shard_map/ppermute | solution.py:379
  98.4 0.0 collective-permute-done.8
  98.4 0.2 shard_map.95
  98.6 0.1 collective-permute-start.12
  98.7 3.2 %collective-permute-start.13 = (bf16[256,576]{1,0:T(8,128)(2,1)S(1)}, bf16[256,576]{1,0:T(8,128)(2,1)S(1)}, u32[]{:S(2)}, u32[]{:S(2)}) collective-permute-start(bf16[256,576]{1,0:T(8,128)(2,1)S(1)} %get-tuple-element.96), channel_id=1, source_target_pairs={{0,6},{1,7},{2,0},{3,1},{4,2},{5,3},{6,4},{7,5},{8,14},{9,15},{10,... | collective-permute-start | bytes 884744 | tf_op jit(solution)/shard_map/ppermute | solution.py:379
  101.9 6.7 %shard_map.96 = bf16[96,16,576]{2,1,0:T(8,128)(2,1)} custom-call(bf16[1536,2048]{1,0:T(8,128)(2,1)S(1)} %get-tuple-element.90.s_ref, bf16[2048,576]{1,0:T(8,128)(2,1)S(1)} %get-tuple-element.97.k_ref), custom_call_target="tpu_custom_call" | custom-call | tf_op jit(solution)/shard_map/pallas_call | solution.py:172
  108.6 0.0 collective-permute-done.11.b_ref
  108.6 0.0 collective-permute-done.12.c_ref
  108.6 0.0 collective-permute-done.13.d_ref
  108.6 1.7 %shard_map.97 = bf16[32,16,576]{2,1,0:T(8,128)(2,1)} custom-call(s32[16,16]{1,0:T(8,128)} %lists.7, s32[16]{0:T(128)} %counts.7, s32[1]{0:T(128)} %bitcast.me, bf16[256,576]{1,0:T(8,128)(2,1)S(1)} %get-tuple-element.98.a_ref, bf16[256,576]{1,0:T(8,128)(2,1)S(1)} %collective-permute-done.11.b_ref, bf16[256,576]{1,0:T(8,128)(2,1)S(1)} %collective-permute-done.12.c_ref, ...), custom_call_target="tpu_custom_call" | custom-call | tf_op jit(solution)/shard_map/pallas_call | solution.py:172
  110.3 15.9 %all_to_all.10 = bf16[16,2,16,576]{3,2,1,0:T(8,128)(2,1)} all-to-all(bf16[16,2,16,576]{3,2,1,0:T(8,128)(2,1)} %bitcast.35), channel_id=1, replica_groups=mesh['req'=16,'head'=8] {'req'}, dimensions={0} | all-to-all | bytes 1179648 | tf_op jit(solution)/shard_map/all_to_all | solution.py:463
  126.2 2.9 %shard_map.98 = f32[16,16,576]{2,1,0:T(8,128)} custom-call(s32[16,16]{1,0:T(8,128)} %lists.7, s32[16]{0:T(128)} %counts.7, s32[1]{0:T(128)} %bitcast.me, bf16[32,16,576]{2,1,0:T(8,128)(2,1)} %bitcast.37), custom_call_target="tpu_custom_call" | custom-call | tf_op jit(solution)/shard_map/pallas_call | solution.py:172
  (7 shorter events, 0.0 us)
Async XLA Ops:
  0.6 35.4 %copy-start = (bf16[96,16,576]{2,1,0:T(8,128)(2,1)S(1)}, bf16[96,16,576]{2,1,0:T(8,128)(2,1)}, u32[]{:S(2)}) copy-start(bf16[96,16,576]{2,1,0:T(8,128)(2,1)} %refs_3_.3) | copy-start | bytes 5308420
  23.8 21.2 %all-to-all-start = ((bf16[16,2,16,576]{3,2,1,0:T(8,128)(2,1)}), bf16[16,2,16,576]{3,2,1,0:T(8,128)(2,1)}, u32[]{:S(2)}, u32[]{:S(2)}) async-start(bf16[16,2,16,576]{3,2,1,0:T(8,128)(2,1)} %bitcast.36), calls=%async_computation | async-start | bytes 1310720 | tf_op jit(solution)/shard_map/all_to_all | solution.py:391
  36.1 1.4 %copy-start.1 = (bf16[96,16,512]{2,1,0:T(8,128)(2,1)S(1)}, bf16[96,16,512]{2,1,0:T(8,128)(2,1)}, u32[]{:S(2)}) copy-start(bf16[96,16,512]{2,1,0:T(8,128)(2,1)} %refs_4_.3) | copy-start | bytes 4718596
  37.5 12.4 %copy-start.2 = (bf16[96,16,512]{2,1,0:T(8,128)(2,1)S(1)}, bf16[96,16,512]{2,1,0:T(8,128)(2,1)}, u32[]{:S(2)}) copy-start(bf16[96,16,512]{2,1,0:T(8,128)(2,1)} %refs_4_.3) | copy-start | bytes 4718596
  38.9 1.2 copy-start.3
  40.1 1.2 copy-start.4
  46.9 2.9 %collective-permute-start.1 = (bf16[256,576]{1,0:T(8,128)(2,1)S(1)}, bf16[256,576]{1,0:T(8,128)(2,1)S(1)}, u32[]{:S(2)}, u32[]{:S(2)}) collective-permute-start(bf16[256,576]{1,0:T(8,128)(2,1)S(1)} %shard_map.87.refs_0_), channel_id=1, source_target_pairs={{0,1},{1,0},{2,3},{3,2},{4,5},{5,4},{6,7},{7,6},{8,9},{9,8},{10,11... | collective-permute-start | bytes 884744 | tf_op jit(solution)/shard_map/ppermute | solution.py:379
  47.0 10.4 %collective-permute-start.3 = (bf16[256,576]{1,0:T(8,128)(2,1)S(1)}, bf16[256,576]{1,0:T(8,128)(2,1)S(1)}, u32[]{:S(2)}, u32[]{:S(2)}) collective-permute-start(bf16[256,576]{1,0:T(8,128)(2,1)S(1)} %shard_map.87.refs_0_), channel_id=1, source_target_pairs={{0,6},{1,7},{2,0},{3,1},{4,2},{5,3},{6,4},{7,5},{8,14},{9,15},{10,... | collective-permute-start | bytes 884744 | tf_op jit(solution)/shard_map/ppermute | solution.py:379
  49.9 11.0 %collective-permute-start = (bf16[256,576]{1,0:T(8,128)(2,1)S(1)}, bf16[256,576]{1,0:T(8,128)(2,1)S(1)}, u32[]{:S(2)}, u32[]{:S(2)}) collective-permute-start(bf16[256,576]{1,0:T(8,128)(2,1)S(1)} %shard_map.87.refs_0_), channel_id=1, source_target_pairs={{0,2},{1,3},{2,4},{3,5},{4,6},{5,7},{6,0},{7,1},{8,10},{9,11},{10,... | collective-permute-start | bytes 884744 | tf_op jit(solution)/shard_map/ppermute | solution.py:379
  60.8 1.6 %collective-permute-start.4 = (bf16[256,576]{1,0:T(8,128)(2,1)S(1)}, bf16[256,576]{1,0:T(8,128)(2,1)S(1)}, u32[]{:S(2)}, u32[]{:S(2)}) collective-permute-start(bf16[256,576]{1,0:T(8,128)(2,1)S(1)} %collective-permute-done.refs_0_), channel_id=1, source_target_pairs={{0,1},{1,0},{2,3},{3,2},{4,5},{5,4},{6,7},{7,6},{8,9},{9,8},{10,11... | collective-permute-start | bytes 884744 | tf_op jit(solution)/shard_map/ppermute | solution.py:379
  60.8 2.1 %collective-permute-start.5 = (bf16[256,576]{1,0:T(8,128)(2,1)S(1)}, bf16[256,576]{1,0:T(8,128)(2,1)S(1)}, u32[]{:S(2)}, u32[]{:S(2)}) collective-permute-start(bf16[256,576]{1,0:T(8,128)(2,1)S(1)} %collective-permute-done.3.refs_1_), channel_id=1, source_target_pairs={{0,1},{1,0},{2,3},{3,2},{4,5},{5,4},{6,7},{7,6},{8,9},{9,8},{10,11... | collective-permute-start | bytes 884744 | tf_op jit(solution)/shard_map/ppermute | solution.py:379
  61.3 10.8 %collective-permute-start.2 = (bf16[256,576]{1,0:T(8,128)(2,1)S(1)}, bf16[256,576]{1,0:T(8,128)(2,1)S(1)}, u32[]{:S(2)}, u32[]{:S(2)}) collective-permute-start(bf16[256,576]{1,0:T(8,128)(2,1)S(1)} %collective-permute-done.refs_0_), channel_id=1, source_target_pairs={{0,2},{1,3},{2,4},{3,5},{4,6},{5,7},{6,0},{7,1},{8,10},{9,11},{10,... | collective-permute-start | bytes 884744 | tf_op jit(solution)/shard_map/ppermute | solution.py:379
  72.2 1.6 %collective-permute-start.6 = (bf16[256,576]{1,0:T(8,128)(2,1)S(1)}, bf16[256,576]{1,0:T(8,128)(2,1)S(1)}, u32[]{:S(2)}, u32[]{:S(2)}) collective-permute-start(bf16[256,576]{1,0:T(8,128)(2,1)S(1)} %collective-permute-done.2.refs_0_), channel_id=1, source_target_pairs={{0,1},{1,0},{2,3},{3,2},{4,5},{5,4},{6,7},{7,6},{8,9},{9,8},{10,11... | collective-permute-start | bytes 884744 | tf_op jit(solution)/shard_map/ppermute | solution.py:379
  86.9 11.5 %collective-permute-start.8 = (bf16[32,16,576]{2,1,0:T(8,128)(2,1)S(1)}, bf16[32,16,576]{2,1,0:T(8,128)(2,1)S(1)}, u32[]{:S(2)}, u32[]{:S(2)}) collective-permute-start(bf16[32,16,576]{2,1,0:T(8,128)(2,1)S(1)} %bitcast.34), channel_id=1, source_target_pairs={{0,1},{1,0},{2,3},{3,2},{4,5},{5,4},{6,7},{7,6},{8,9},{9,8},{10,11... | collective-permute-start | bytes 1769480 | tf_op jit(solution)/shard_map/ppermute | solution.py:379
  87.1 2.4 %collective-permute-start.7 = (bf16[256,576]{1,0:T(8,128)(2,1)S(1)}, bf16[256,576]{1,0:T(8,128)(2,1)S(1)}, u32[]{:S(2)}, u32[]{:S(2)}) collective-permute-start(bf16[256,576]{1,0:T(8,128)(2,1)S(1)} %get-tuple-element.86), channel_id=1, source_target_pairs={{0,1},{1,0},{2,3},{3,2},{4,5},{5,4},{6,7},{7,6},{8,9},{9,8},{10,11... | collective-permute-start | bytes 884744 | tf_op jit(solution)/shard_map/ppermute | solution.py:379
  89.6 6.3 %collective-permute-start.10 = (bf16[128,576]{1,0:T(8,128)(2,1)S(1)}, bf16[128,576]{1,0:T(8,128)(2,1)S(1)}, u32[]{:S(2)}, u32[]{:S(2)}) collective-permute-start(bf16[128,576]{1,0:T(8,128)(2,1)S(1)} %get-tuple-element.95), channel_id=1, source_target_pairs={{0,6},{1,7},{2,0},{3,1},{4,2},{5,3},{6,4},{7,5},{8,14},{9,15},{10,... | collective-permute-start | bytes 442376 | tf_op jit(solution)/shard_map/ppermute | solution.py:379
  91.2 7.2 %collective-permute-start.9 = (bf16[128,576]{1,0:T(8,128)(2,1)S(1)}, bf16[128,576]{1,0:T(8,128)(2,1)S(1)}, u32[]{:S(2)}, u32[]{:S(2)}) collective-permute-start(bf16[128,576]{1,0:T(8,128)(2,1)S(1)} %get-tuple-element.87), channel_id=1, source_target_pairs={{0,2},{1,3},{2,4},{3,5},{4,6},{5,7},{6,0},{7,1},{8,10},{9,11},{10,... | collective-permute-start | bytes 442376 | tf_op jit(solution)/shard_map/ppermute | solution.py:379
  94.5 14.1 %collective-permute-start.11 = (bf16[256,576]{1,0:T(8,128)(2,1)S(1)}, bf16[256,576]{1,0:T(8,128)(2,1)S(1)}, u32[]{:S(2)}, u32[]{:S(2)}) collective-permute-start(bf16[256,576]{1,0:T(8,128)(2,1)S(1)} %get-tuple-element.99), channel_id=1, source_target_pairs={{0,1},{1,0},{2,3},{3,2},{4,5},{5,4},{6,7},{7,6},{8,9},{9,8},{10,11... | collective-permute-start | bytes 884744 | tf_op jit(solution)/shard_map/ppermute | solution.py:379
  98.6 10.0 %collective-permute-start.12 = (bf16[256,576]{1,0:T(8,128)(2,1)S(1)}, bf16[256,576]{1,0:T(8,128)(2,1)S(1)}, u32[]{:S(2)}, u32[]{:S(2)}) collective-permute-start(bf16[256,576]{1,0:T(8,128)(2,1)S(1)} %get-tuple-element.100), channel_id=1, source_target_pairs={{0,2},{1,3},{2,4},{3,5},{4,6},{5,7},{6,0},{7,1},{8,10},{9,11},{10,... | collective-permute-start | bytes 884744 | tf_op jit(solution)/shard_map/ppermute | solution.py:379
  98.7 9.9 %collective-permute-start.13 = (bf16[256,576]{1,0:T(8,128)(2,1)S(1)}, bf16[256,576]{1,0:T(8,128)(2,1)S(1)}, u32[]{:S(2)}, u32[]{:S(2)}) collective-permute-start(bf16[256,576]{1,0:T(8,128)(2,1)S(1)} %get-tuple-element.96), channel_id=1, source_target_pairs={{0,6},{1,7},{2,0},{3,1},{4,2},{5,3},{6,4},{7,5},{8,14},{9,15},{10,... | collective-permute-start | bytes 884744 | tf_op jit(solution)/shard_map/ppermute | solution.py:379

commit v4 on v3

--- a/solution.py
+++ b/solution.py
@@ -52,11 +52,18 @@
         table[j] = owner * CAP + rank
 
 
-def pick_body(lists, counts, me, lat_ref, out_ref, table, sems):
+def pick_body(lists, counts, me, lat_ref, out_ref, table, lat, held, sem, sems):
+    load = pltpu.make_async_copy(lat_ref, lat, sem.at[0])
+    load.start()
     owner_table(lists, counts, me[0], table, 0)
-    copies = [pltpu.make_async_copy(lat_ref.at[table[s]], out_ref.at[s], sems.at[s]) for s in range(SLOTS)]
-    for copy in copies:
-        copy.start()
+    load.wait()
+    step = SLOTS // 4
+    parts = [slice(i * step, i * step + step) for i in range(4)]
+    copies = [pltpu.make_async_copy(held.at[p], out_ref.at[p], sems.at[i]) for i, p in enumerate(parts)]
+    for s in range(SLOTS):
+        held[s] = lat[table[s]]
+        if s % step == step - 1:
+            copies[s // step].start()
     for copy in copies:
         copy.wait()
 
@@ -162,7 +169,7 @@
 INPLACE = pl.BlockSpec(memory_space=pltpu.HBM)
 
 
-def call(body, outs, scalars, arrays, scratch=(), direct_in=(), direct=(), alias=None):
+def call(body, outs, scalars, arrays, scratch=(), direct_in=(), direct=(), alias=None, flops=None):
     args = [
         pltpu.with_memory_space_constraint(a, pltpu.HBM if i in direct_in else pltpu.VMEM)
         for i, a in enumerate(arrays)
@@ -177,6 +184,7 @@
         out_shape=tuple(shapes),
         scratch_shapes=list(scratch),
         input_output_aliases=alias or {},
+        cost_estimate=flops and pl.CostEstimate(flops=flops, transcendentals=0, bytes_accessed=0),
         compiler_params=pltpu.CompilerParams(vmem_limit_bytes=16 * 1024 * 1024),
     )(*scalars, *args)
 
@@ -290,6 +298,7 @@
         direct_in=range(len(arrays) - len(turned), len(arrays)),
         direct=(4,) if last else (),
         alias={start + i: i for i in range((4 if last else 5) if state else 0)},
+        flops=2 * rows * n * (WIDE + 2 * LAT),
     )
 
 
@@ -334,6 +343,7 @@
         (qt, gt, e, p, st, k),
         scratch=[pltpu.VMEM((rows, 128), f32)] * 2,
         alias={3: 2, 5: 3},
+        flops=2 * rows * n * (WIDE + LAT),
     )
 
 
@@ -366,6 +376,7 @@
         (s, k),
         scratch=[pltpu.VMEM(shape, bf16), pltpu.SemaphoreType.DMA((rows // block,))],
         direct=(0,),
+        flops=2 * rows * k.shape[0] * WIDE,
     )[0]
 
 
@@ -386,7 +397,19 @@
 
     dma = lambda n: pltpu.SemaphoreType.DMA((n,))
     (outgoing,) = call(
-        pick_body, (slots,), scalars, (latents,), scratch=[smem(SLOTS + 1), dma(SLOTS)], direct_in=(0,), direct=(0,)
+        pick_body,
+        (slots,),
+        scalars,
+        (latents,),
+        scratch=[
+            smem(SLOTS + 1),
+            pltpu.VMEM(latents.shape, bf16),
+            pltpu.VMEM((SLOTS, tokens, WIDE), bf16),
+            dma(1),
+            dma(4),
+        ],
+        direct_in=(0,),
+        direct=(0,),
     )
     arrived = lax.all_to_all(outgoing.reshape(16, CAP, tokens, WIDE), "req", 0, 0, tiled=True)
 

time: 130 us -> 110 us (0.85)
  Pallas kernels: 67 us -> 46.7 us
    pallas_call x14, Pallas kernels: 67 us -> 46.7 us  [call(): pl.pallas_call(body, in_specs=[pl.BlockSpec(memory_space=pltpu.SMEM)] * l...]
  transfers between devices with their start and end apart: 15 -> 15, of which waited for: 10 -> 11; matrix products, arithmetic and copies ran while one was open for 3% -> 4% of each run, Pallas kernels for 19% -> 22%
where the time goes in v4:
time: 110 us
  Pallas kernels  46.7 us (42%)
  waiting for transfers between devices  20.3 us (18%)
  starting transfers between devices  18.7 us (17%)
  blocking collectives  15.3 us (14%)
  local copies, waits for them, and re-layouts  6.07 us (6%)
  other arithmetic  1.59 us (1%)
    pallas_call x14, Pallas kernels, call(): pl.pallas_call(body, in_specs=[pl.BlockSpec(memory_space=pltpu.SMEM)] * l...  46.7 us
    ppermute x14, waiting for transfers between devices, per_device(): send = lambda a, perm: lax.ppermute(a, 'head', perm)  16.5 us
    all_to_all x1, blocking collectives, per_device(): lax.all_to_all(slot_grads.reshape(16, CAP, tokens, WIDE), 'req', 0, 0, ti...  15.3 us
    ppermute x14, starting transfers between devices, per_device(): send = lambda a, perm: lax.ppermute(a, 'head', perm)  10.4 us
    all_to_all x1, starting transfers between devices, per_device(): lax.all_to_all(outgoing.reshape(16, CAP, tokens, WIDE), 'req', 0, 0, tile...  8.22 us
    unnamed x15, local copies, waits for them, and re-layouts  3.81 us
    all_to_all x1, waiting for transfers between devices, per_device(): lax.all_to_all(outgoing.reshape(16, CAP, tokens, WIDE), 'req', 0, 0, tile...  3.73 us
  transfers between devices with their start and end apart: 15, of which 11 were waited for; matrix products, arithmetic and copies ran while one was open for 4% of the time, Pallas kernels for 22%

profile of v4, /device:TPU:0, one launch (start us, length us, event | category | flops | bytes accessed | tf_op | source)
XLA Modules:
  0.0 109.7 jit_solution(11171148578500138122)
XLA Ops:
  0.6 0.0 copy-start
  0.6 2.8 %shard_map.85 = bf16[32,16,576]{2,1,0:T(8,128)(2,1)} custom-call(s32[16,16]{1,0:T(8,128)} %lists.7, s32[16]{0:T(128)} %counts.7, s32[1]{0:T(128)} %bitcast.me, bf16[16,16,576]{2,1,0:T(8,128)(2,1)} %lat_ref.1), custom_call_target="tpu_custom_call" | custom-call | tf_op jit(solution)/shard_map/pallas_call | solution.py:179
  3.4 8.2 %all-to-all-start = ((bf16[16,2,16,576]{3,2,1,0:T(8,128)(2,1)}), bf16[16,2,16,576]{3,2,1,0:T(8,128)(2,1)}, u32[]{:S(2)}, u32[]{:S(2)}) async-start(bf16[16,2,16,576]{3,2,1,0:T(8,128)(2,1)} %bitcast.36), calls=%async_computation | async-start | bytes 1310720 | tf_op jit(solution)/shard_map/all_to_all | solution.py:414
  11.8 1.2 %dynamic_slice.8 = s32[1]{0:T(128)} dynamic-slice(s32[16]{0:T(128)} %counts.7, s32[]{:T(128)S(6)} %select_n.59), dynamic_slice_sizes={1} | dynamic-slice | bytes 12 | tf_op jit(solution)/shard_map/jit(dynamic_index_in_dim)/dynamic_slice | solution.py:417
  13.0 0.7 dynamic-slice_bitcast_fusion
  13.7 0.1 stack.35
  13.8 0.9 select_reduce_fusion
  14.7 0.7 compare_select_fusion
  15.3 0.1 broadcast_in_dim.34
  15.4 0.1 lt.60
  15.5 0.1 add.95
  15.5 0.1 fusion
  15.7 0.0 copy-done
  15.7 0.0 copy-start.1
  15.7 1.4 %copy-done.1 = bf16[96,16,512]{2,1,0:T(8,128)(2,1)S(1)} copy-done((bf16[96,16,512]{2,1,0:T(8,128)(2,1)S(1)}, bf16[96,16,512]{2,1,0:T(8,128)(2,1)}, u32[]{:S(2)}) %copy-start.1) | copy-done | bytes 1572888
  17.1 0.0 copy-start.2
  17.1 1.4 %shard_map.86 = (bf16[576,1536]{1,0:T(8,128)(2,1)S(1)}, bf16[512,1536]{1,0:T(8,128)(2,1)S(1)}) custom-call(bf16[96,16,576]{2,1,0:T(8,128)(2,1)S(1)} %copy-done, bf16[96,16,512]{2,1,0:T(8,128)(2,1)S(1)} %copy-done.1), custom_call_target="tpu_custom_call" | custom-call | tf_op jit(solution)/shard_map/pallas_call | solution.py:179
  18.5 0.0 copy-start.3
  18.5 1.2 %copy-done.3 = bf16[576,1536]{1,0:T(8,128)(2,1)} copy-done((bf16[576,1536]{1,0:T(8,128)(2,1)}, bf16[576,1536]{1,0:T(8,128)(2,1)S(1)}, u32[]{:S(2)}) %copy-start.3) | copy-done | bytes 1769496
  19.7 0.0 copy-start.4
  19.7 1.2 %copy-done.4 = bf16[512,1536]{1,0:T(8,128)(2,1)} copy-done((bf16[512,1536]{1,0:T(8,128)(2,1)}, bf16[512,1536]{1,0:T(8,128)(2,1)S(1)}, u32[]{:S(2)}) %copy-start.4) | copy-done | bytes 1572888
  20.9 3.7 %all-to-all-done = bf16[16,2,16,576]{3,2,1,0:T(8,128)(2,1)} async-done(((bf16[16,2,16,576]{3,2,1,0:T(8,128)(2,1)}), bf16[16,2,16,576]{3,2,1,0:T(8,128)(2,1)}, u32[]{:S(2)}, u32[]{:S(2)}) %all-to-all-start) | async-done | bytes 589856 | tf_op jit(solution)/shard_map/all_to_all | solution.py:414
  24.6 1.9 %shard_map.87.refs_0_ = bf16[256,576]{1,0:T(8,128)(2,1)S(1)} custom-call(s32[16,16]{1,0:T(8,128)} %lists.7, s32[16]{0:T(128)} %counts.7, s32[1]{0:T(128)} %bitcast.me, bf16[32,16,576]{2,1,0:T(8,128)(2,1)} %bitcast.12.arrived_ref), custom_call_target="tpu_custom_call" | custom-call | tf_op jit(solution)/shard_map/pallas_call | solution.py:179
  26.6 0.1 collective-permute-start.1
  26.7 2.8 %collective-permute-start.3 = (bf16[256,576]{1,0:T(8,128)(2,1)S(1)}, bf16[256,576]{1,0:T(8,128)(2,1)S(1)}, u32[]{:S(2)}, u32[]{:S(2)}) collective-permute-start(bf16[256,576]{1,0:T(8,128)(2,1)S(1)} %shard_map.87.refs_0_), channel_id=1, source_target_pairs={{0,6},{1,7},{2,0},{3,1},{4,2},{5,3},{6,4},{7,5},{8,14},{9,15},{10,... | collective-permute-start | bytes 884744 | tf_op jit(solution)/shard_map/ppermute | solution.py:390
  29.5 0.0 collective-permute-start
  29.5 0.0 collective-permute-done.1.refs_1_
  29.5 0.0 copy-done.2
  29.5 4.3 %shard_map.88 = (bf16[1536,2048]{1,0:T(8,128)(2,1)S(1)}, bf16[1536,2048]{1,0:T(8,128)(2,1)S(1)}, bf16[2048,576]{1,0:T(8,128)(2,1)S(1)}, f32[1536,128]{1,0:T(8,128)S(1)}, f32[1536,512]{1,0:T(8,128)S(1)}) custom-call(bf16[256,576]{1,0:T(8,128)(2,1)S(1)} %shard_map.87.refs_0_, bf16[256,576]{1,0:T(8,128)(2,1)S(1)} %collective-permute-done.1.refs_1_, ...), custom_call_target="tpu_custom_call" | custom-call | flops 2516582400 | tf_op jit(solution)/shard_map/pallas_call | solution.py:179
  33.8 3.2 %collective-permute-done.3.refs_1_ = bf16[256,576]{1,0:T(8,128)(2,1)S(1)} collective-permute-done((bf16[256,576]{1,0:T(8,128)(2,1)S(1)}, bf16[256,576]{1,0:T(8,128)(2,1)S(1)}, u32[]{:S(2)}, u32[]{:S(2)}) %collective-permute-start.3) | collective-permute-done | bytes 294944 | tf_op jit(solution)/shard_map/ppermute | solution.py:390
  37.1 3.4 %collective-permute-done.refs_0_ = bf16[256,576]{1,0:T(8,128)(2,1)S(1)} collective-permute-done((bf16[256,576]{1,0:T(8,128)(2,1)S(1)}, bf16[256,576]{1,0:T(8,128)(2,1)S(1)}, u32[]{:S(2)}, u32[]{:S(2)}) %collective-permute-start) | collective-permute-done | bytes 294944 | tf_op jit(solution)/shard_map/ppermute | solution.py:390
  40.5 0.0 collective-permute-start.4
  40.5 0.5 collective-permute-start.5
  41.0 0.0 collective-permute-start.2
  41.0 1.1 %collective-permute-done.4.refs_2_ = bf16[256,576]{1,0:T(8,128)(2,1)S(1)} collective-permute-done((bf16[256,576]{1,0:T(8,128)(2,1)S(1)}, bf16[256,576]{1,0:T(8,128)(2,1)S(1)}, u32[]{:S(2)}, u32[]{:S(2)}) %collective-permute-start.4) | collective-permute-done | bytes 294944 | tf_op jit(solution)/shard_map/ppermute | solution.py:390
  42.1 0.5 collective-permute-done.5.refs_3_
  42.6 8.8 %shard_map.89 = (bf16[1536,2048]{1,0:T(8,128)(2,1)S(1)}, bf16[1536,2048]{1,0:T(8,128)(2,1)S(1)}, bf16[2048,576]{1,0:T(8,128)(2,1)S(1)}, f32[1536,128]{1,0:T(8,128)S(1)}, f32[1536,512]{1,0:T(8,128)S(1)}) custom-call(bf16[256,576]{1,0:T(8,128)(2,1)S(1)} %collective-permute-done.refs_0_, ...), custom_call_target="tpu_custom_call", output_to_operand_aliasing={{0}: (7, {}), {1}: (8, {}), {2}: (9, {}), {3}: (10, {}), {4... | custom-call | flops 5033164800 | tf_op jit(solution)/shard_map/pallas_call | solution.py:179
  51.4 0.4 collective-permute-done.2.refs_0_
  51.8 0.0 collective-permute-start.6
  51.8 1.6 %collective-permute-done.6.refs_1_ = bf16[256,576]{1,0:T(8,128)(2,1)S(1)} collective-permute-done((bf16[256,576]{1,0:T(8,128)(2,1)S(1)}, bf16[256,576]{1,0:T(8,128)(2,1)S(1)}, u32[]{:S(2)}, u32[]{:S(2)}) %collective-permute-start.6) | collective-permute-done | bytes 294944 | tf_op jit(solution)/shard_map/ppermute | solution.py:390
  53.4 6.2 %shard_map.90 = (bf16[1536,2048]{1,0:T(8,128)(2,1)S(1)}, bf16[1536,2048]{1,0:T(8,128)(2,1)S(1)}, bf16[2048,576]{1,0:T(8,128)(2,1)S(1)}, f32[1536,128]{1,0:T(8,12...) custom-call(bf16[256,576]{1,0:T(8,128)(2,1)S(1)} %collective-permute, ...), custom_call_target="tpu_custom_call", output_to_operand_aliasing={{0}: (5, {}), {1}: (6, {}), {2}: (7, {}), {3}: (8, {})} | custom-call | flops 2516582400 | tf_op jit(solution)/shard_map/pallas_call | solution.py:179
  59.6 2.7 %shard_map.91 = (bf16[256,576]{1,0:T(8,128)(2,1)S(1)}, bf16[256,576]{1,0:T(8,128)(2,1)S(1)}, bf16[1536,2048]{1,0:T(8,128)(2,1)S(1)}, bf16[2048,576]{1,0:T(8,128)(2,1)S(1)}) custom-call(bf16[576,1536]{1,0:T(8,128)(2,1)S(1)} %get-tuple-element.74.qt_ref, bf16[512,1536]{1,0:T(8,128)(2,1)S(1)} %get-tuple-element.75.gt_ref, ...), custom_call_target="tpu_custom_call", output_to_operand_aliasing={{2}: (3, {}), {3}: (5, {})} | custom-call | flops 1711276032 | tf_op jit(solution)/shard_map/pallas_call | solution.py:179
  62.3 4.3 %shard_map.92 = (bf16[512,576]{1,0:T(8,128)(2,1)S(1)}, bf16[512,576]{1,0:T(8,128)(2,1)S(1)}, bf16[1536,2048]{1,0:T(8,128)(2,1)S(1)}, bf16[2048,576]{1,0:T(8,128)(2,1)S(1)}) custom-call(bf16[576,1536]{1,0:T(8,128)(2,1)S(1)} %get-tuple-element.74.qt_ref, bf16[512,1536]{1,0:T(8,128)(2,1)S(1)} %get-tuple-element.75.gt_ref, ...), custom_call_target="tpu_custom_call", output_to_operand_aliasing={{2}: (3, {}), {3}: (5, {})} | custom-call | flops 3422552064 | tf_op jit(solution)/shard_map/pallas_call | solution.py:179
  66.6 0.2 collective-permute-start.8
  66.8 0.4 collective-permute-start.7
  67.1 2.1 %collective-permute-done.7.far_ref = bf16[256,576]{1,0:T(8,128)(2,1)S(1)} collective-permute-done((bf16[256,576]{1,0:T(8,128)(2,1)S(1)}, bf16[256,576]{1,0:T(8,128)(2,1)S(1)}, u32[]{:S(2)}, u32[]{:S(2)}) %collective-permute-start.7) | collective-permute-done | bytes 294944 | tf_op jit(solution)/shard_map/ppermute | solution.py:390
  69.2 0.1 shard_map.93
  69.3 0.1 collective-permute-start.9
  69.4 3.2 %collective-permute-start.10 = (bf16[128,576]{1,0:T(8,128)(2,1)S(1)}, bf16[128,576]{1,0:T(8,128)(2,1)S(1)}, u32[]{:S(2)}, u32[]{:S(2)}) collective-permute-start(bf16[128,576]{1,0:T(8,128)(2,1)S(1)} %get-tuple-element.95), channel_id=1, source_target_pairs={{0,6},{1,7},{2,0},{3,1},{4,2},{5,3},{6,4},{7,5},{8,14},{9,15},{10,... | collective-permute-start | bytes 442376 | tf_op jit(solution)/shard_map/ppermute | solution.py:390
  72.6 2.8 %shard_map.94 = (bf16[256,576]{1,0:T(8,128)(2,1)S(1)}, bf16[256,576]{1,0:T(8,128)(2,1)S(1)}, bf16[1536,2048]{1,0:T(8,128)(2,1)S(1)}, bf16[2048,576]{1,0:T(8,128)(2,1)S(1)}) custom-call(bf16[576,1536]{1,0:T(8,128)(2,1)S(1)} %get-tuple-element.74.qt_ref, bf16[512,1536]{1,0:T(8,128)(2,1)S(1)} %get-tuple-element.75.gt_ref, ...), custom_call_target="tpu_custom_call", output_to_operand_aliasing={{2}: (3, {}), {3}: (5, {})} | custom-call | flops 1711276032 | tf_op jit(solution)/shard_map/pallas_call | solution.py:179
  75.4 0.1 collective-permute-start.11
  75.5 0.6 collective-permute-done.10.high_ref
  76.1 0.7 collective-permute-done.9.low_ref
  76.8 0.0 collective-permute-done.8
  76.8 0.2 shard_map.95
  77.0 3.0 %collective-permute-start.13 = (bf16[256,576]{1,0:T(8,128)(2,1)S(1)}, bf16[256,576]{1,0:T(8,128)(2,1)S(1)}, u32[]{:S(2)}, u32[]{:S(2)}) collective-permute-start(bf16[256,576]{1,0:T(8,128)(2,1)S(1)} %get-tuple-element.96), channel_id=1, source_target_pairs={{0,6},{1,7},{2,0},{3,1},{4,2},{5,3},{6,4},{7,5},{8,14},{9,15},{10,... | collective-permute-start | bytes 884744 | tf_op jit(solution)/shard_map/ppermute | solution.py:390
  80.0 0.0 collective-permute-start.12
  80.0 6.7 %shard_map.96 = bf16[96,16,576]{2,1,0:T(8,128)(2,1)} custom-call(bf16[1536,2048]{1,0:T(8,128)(2,1)S(1)} %get-tuple-element.90.s_ref, bf16[2048,576]{1,0:T(8,128)(2,1)S(1)} %get-tuple-element.97.k_ref), custom_call_target="tpu_custom_call" | custom-call | flops 3623878656 | tf_op jit(solution)/shard_map/pallas_call | solution.py:179
  86.7 0.0 collective-permute-done.11.b_ref
  86.7 2.8 %collective-permute-done.12.c_ref = bf16[256,576]{1,0:T(8,128)(2,1)S(1)} collective-permute-done((bf16[256,576]{1,0:T(8,128)(2,1)S(1)}, bf16[256,576]{1,0:T(8,128)(2,1)S(1)}, u32[]{:S(2)}, u32[]{:S(2)}) %collective-permute-start.12) | collective-permute-done | bytes 294944 | tf_op jit(solution)/shard_map/ppermute | solution.py:390
  89.6 0.0 collective-permute-done.13.d_ref
  89.6 1.7 %shard_map.97 = bf16[32,16,576]{2,1,0:T(8,128)(2,1)} custom-call(s32[16,16]{1,0:T(8,128)} %lists.7, s32[16]{0:T(128)} %counts.7, s32[1]{0:T(128)} %bitcast.me, bf16[256,576]{1,0:T(8,128)(2,1)S(1)} %get-tuple-element.98.a_ref, bf16[256,576]{1,0:T(8,128)(2,1)S(1)} %collective-permute-done.11.b_ref, bf16[256,576]{1,0:T(8,128)(2,1)S(1)} %collective-permute-done.12.c_ref, ...), custom_call_target="tpu_custom_call" | custom-call | tf_op jit(solution)/shard_map/pallas_call | solution.py:179
  91.3 15.3 %all_to_all.10 = bf16[16,2,16,576]{3,2,1,0:T(8,128)(2,1)} all-to-all(bf16[16,2,16,576]{3,2,1,0:T(8,128)(2,1)} %bitcast.35), channel_id=1, replica_groups=mesh['req'=16,'head'=8] {'req'}, dimensions={0} | all-to-all | bytes 1179648 | tf_op jit(solution)/shard_map/all_to_all | solution.py:486
  106.6 2.9 %shard_map.98 = f32[16,16,576]{2,1,0:T(8,128)} custom-call(s32[16,16]{1,0:T(8,128)} %lists.7, s32[16]{0:T(128)} %counts.7, s32[1]{0:T(128)} %bitcast.me, bf16[32,16,576]{2,1,0:T(8,128)(2,1)} %bitcast.37), custom_call_target="tpu_custom_call" | custom-call | tf_op jit(solution)/shard_map/pallas_call | solution.py:179
  (7 shorter events, 0.0 us)
Async XLA Ops:
  0.6 15.0 %copy-start = (bf16[96,16,576]{2,1,0:T(8,128)(2,1)S(1)}, bf16[96,16,576]{2,1,0:T(8,128)(2,1)}, u32[]{:S(2)}) copy-start(bf16[96,16,576]{2,1,0:T(8,128)(2,1)} %refs_3_.3) | copy-start | bytes 5308420
  3.4 21.2 %all-to-all-start = ((bf16[16,2,16,576]{3,2,1,0:T(8,128)(2,1)}), bf16[16,2,16,576]{3,2,1,0:T(8,128)(2,1)}, u32[]{:S(2)}, u32[]{:S(2)}) async-start(bf16[16,2,16,576]{3,2,1,0:T(8,128)(2,1)} %bitcast.36), calls=%async_computation | async-start | bytes 1310720 | tf_op jit(solution)/shard_map/all_to_all | solution.py:414
  15.7 1.4 %copy-start.1 = (bf16[96,16,512]{2,1,0:T(8,128)(2,1)S(1)}, bf16[96,16,512]{2,1,0:T(8,128)(2,1)}, u32[]{:S(2)}) copy-start(bf16[96,16,512]{2,1,0:T(8,128)(2,1)} %refs_4_.3) | copy-start | bytes 4718596
  17.1 12.4 %copy-start.2 = (bf16[96,16,512]{2,1,0:T(8,128)(2,1)S(1)}, bf16[96,16,512]{2,1,0:T(8,128)(2,1)}, u32[]{:S(2)}) copy-start(bf16[96,16,512]{2,1,0:T(8,128)(2,1)} %refs_4_.3) | copy-start | bytes 4718596
  18.5 1.2 %copy-start.3 = (bf16[576,1536]{1,0:T(8,128)(2,1)}, bf16[576,1536]{1,0:T(8,128)(2,1)S(1)}, u32[]{:S(2)}) copy-start(bf16[576,1536]{1,0:T(8,128)(2,1)S(1)} %get-tuple-element.71.refs_10_) | copy-start | bytes 5308420
  19.7 1.2 %copy-start.4 = (bf16[512,1536]{1,0:T(8,128)(2,1)}, bf16[512,1536]{1,0:T(8,128)(2,1)S(1)}, u32[]{:S(2)}) copy-start(bf16[512,1536]{1,0:T(8,128)(2,1)S(1)} %get-tuple-element.72.refs_11_) | copy-start | bytes 4718596
  26.6 2.9 %collective-permute-start.1 = (bf16[256,576]{1,0:T(8,128)(2,1)S(1)}, bf16[256,576]{1,0:T(8,128)(2,1)S(1)}, u32[]{:S(2)}, u32[]{:S(2)}) collective-permute-start(bf16[256,576]{1,0:T(8,128)(2,1)S(1)} %shard_map.87.refs_0_), channel_id=1, source_target_pairs={{0,1},{1,0},{2,3},{3,2},{4,5},{5,4},{6,7},{7,6},{8,9},{9,8},{10,11... | collective-permute-start | bytes 884744 | tf_op jit(solution)/shard_map/ppermute | solution.py:390
  26.7 10.4 %collective-permute-start.3 = (bf16[256,576]{1,0:T(8,128)(2,1)S(1)}, bf16[256,576]{1,0:T(8,128)(2,1)S(1)}, u32[]{:S(2)}, u32[]{:S(2)}) collective-permute-start(bf16[256,576]{1,0:T(8,128)(2,1)S(1)} %shard_map.87.refs_0_), channel_id=1, source_target_pairs={{0,6},{1,7},{2,0},{3,1},{4,2},{5,3},{6,4},{7,5},{8,14},{9,15},{10,... | collective-permute-start | bytes 884744 | tf_op jit(solution)/shard_map/ppermute | solution.py:390
  29.5 11.0 %collective-permute-start = (bf16[256,576]{1,0:T(8,128)(2,1)S(1)}, bf16[256,576]{1,0:T(8,128)(2,1)S(1)}, u32[]{:S(2)}, u32[]{:S(2)}) collective-permute-start(bf16[256,576]{1,0:T(8,128)(2,1)S(1)} %shard_map.87.refs_0_), channel_id=1, source_target_pairs={{0,2},{1,3},{2,4},{3,5},{4,6},{5,7},{6,0},{7,1},{8,10},{9,11},{10,... | collective-permute-start | bytes 884744 | tf_op jit(solution)/shard_map/ppermute | solution.py:390
  40.5 1.6 %collective-permute-start.4 = (bf16[256,576]{1,0:T(8,128)(2,1)S(1)}, bf16[256,576]{1,0:T(8,128)(2,1)S(1)}, u32[]{:S(2)}, u32[]{:S(2)}) collective-permute-start(bf16[256,576]{1,0:T(8,128)(2,1)S(1)} %collective-permute-done.refs_0_), channel_id=1, source_target_pairs={{0,1},{1,0},{2,3},{3,2},{4,5},{5,4},{6,7},{7,6},{8,9},{9,8},{10,11... | collective-permute-start | bytes 884744 | tf_op jit(solution)/shard_map/ppermute | solution.py:390
  40.5 2.1 %collective-permute-start.5 = (bf16[256,576]{1,0:T(8,128)(2,1)S(1)}, bf16[256,576]{1,0:T(8,128)(2,1)S(1)}, u32[]{:S(2)}, u32[]{:S(2)}) collective-permute-start(bf16[256,576]{1,0:T(8,128)(2,1)S(1)} %collective-permute-done.3.refs_1_), channel_id=1, source_target_pairs={{0,1},{1,0},{2,3},{3,2},{4,5},{5,4},{6,7},{7,6},{8,9},{9,8},{10,11... | collective-permute-start | bytes 884744 | tf_op jit(solution)/shard_map/ppermute | solution.py:390
  41.0 10.8 %collective-permute-start.2 = (bf16[256,576]{1,0:T(8,128)(2,1)S(1)}, bf16[256,576]{1,0:T(8,128)(2,1)S(1)}, u32[]{:S(2)}, u32[]{:S(2)}) collective-permute-start(bf16[256,576]{1,0:T(8,128)(2,1)S(1)} %collective-permute-done.refs_0_), channel_id=1, source_target_pairs={{0,2},{1,3},{2,4},{3,5},{4,6},{5,7},{6,0},{7,1},{8,10},{9,11},{10,... | collective-permute-start | bytes 884744 | tf_op jit(solution)/shard_map/ppermute | solution.py:390
  51.8 1.6 %collective-permute-start.6 = (bf16[256,576]{1,0:T(8,128)(2,1)S(1)}, bf16[256,576]{1,0:T(8,128)(2,1)S(1)}, u32[]{:S(2)}, u32[]{:S(2)}) collective-permute-start(bf16[256,576]{1,0:T(8,128)(2,1)S(1)} %collective-permute-done.2.refs_0_), channel_id=1, source_target_pairs={{0,1},{1,0},{2,3},{3,2},{4,5},{5,4},{6,7},{7,6},{8,9},{9,8},{10,11... | collective-permute-start | bytes 884744 | tf_op jit(solution)/shard_map/ppermute | solution.py:390
  66.6 10.3 %collective-permute-start.8 = (bf16[32,16,576]{2,1,0:T(8,128)(2,1)S(1)}, bf16[32,16,576]{2,1,0:T(8,128)(2,1)S(1)}, u32[]{:S(2)}, u32[]{:S(2)}) collective-permute-start(bf16[32,16,576]{2,1,0:T(8,128)(2,1)S(1)} %bitcast.34), channel_id=1, source_target_pairs={{0,1},{1,0},{2,3},{3,2},{4,5},{5,4},{6,7},{7,6},{8,9},{9,8},{10,11... | collective-permute-start | bytes 1769480 | tf_op jit(solution)/shard_map/ppermute | solution.py:390
  66.8 2.4 %collective-permute-start.7 = (bf16[256,576]{1,0:T(8,128)(2,1)S(1)}, bf16[256,576]{1,0:T(8,128)(2,1)S(1)}, u32[]{:S(2)}, u32[]{:S(2)}) collective-permute-start(bf16[256,576]{1,0:T(8,128)(2,1)S(1)} %get-tuple-element.86), channel_id=1, source_target_pairs={{0,1},{1,0},{2,3},{3,2},{4,5},{5,4},{6,7},{7,6},{8,9},{9,8},{10,11... | collective-permute-start | bytes 884744 | tf_op jit(solution)/shard_map/ppermute | solution.py:390
  69.3 7.5 %collective-permute-start.9 = (bf16[128,576]{1,0:T(8,128)(2,1)S(1)}, bf16[128,576]{1,0:T(8,128)(2,1)S(1)}, u32[]{:S(2)}, u32[]{:S(2)}) collective-permute-start(bf16[128,576]{1,0:T(8,128)(2,1)S(1)} %get-tuple-element.87), channel_id=1, source_target_pairs={{0,2},{1,3},{2,4},{3,5},{4,6},{5,7},{6,0},{7,1},{8,10},{9,11},{10,... | collective-permute-start | bytes 442376 | tf_op jit(solution)/shard_map/ppermute | solution.py:390
  69.4 6.7 %collective-permute-start.10 = (bf16[128,576]{1,0:T(8,128)(2,1)S(1)}, bf16[128,576]{1,0:T(8,128)(2,1)S(1)}, u32[]{:S(2)}, u32[]{:S(2)}) collective-permute-start(bf16[128,576]{1,0:T(8,128)(2,1)S(1)} %get-tuple-element.95), channel_id=1, source_target_pairs={{0,6},{1,7},{2,0},{3,1},{4,2},{5,3},{6,4},{7,5},{8,14},{9,15},{10,... | collective-permute-start | bytes 442376 | tf_op jit(solution)/shard_map/ppermute | solution.py:390
  75.4 11.4 %collective-permute-start.11 = (bf16[256,576]{1,0:T(8,128)(2,1)S(1)}, bf16[256,576]{1,0:T(8,128)(2,1)S(1)}, u32[]{:S(2)}, u32[]{:S(2)}) collective-permute-start(bf16[256,576]{1,0:T(8,128)(2,1)S(1)} %get-tuple-element.99), channel_id=1, source_target_pairs={{0,1},{1,0},{2,3},{3,2},{4,5},{5,4},{6,7},{7,6},{8,9},{9,8},{10,11... | collective-permute-start | bytes 884744 | tf_op jit(solution)/shard_map/ppermute | solution.py:390
  77.0 12.6 %collective-permute-start.13 = (bf16[256,576]{1,0:T(8,128)(2,1)S(1)}, bf16[256,576]{1,0:T(8,128)(2,1)S(1)}, u32[]{:S(2)}, u32[]{:S(2)}) collective-permute-start(bf16[256,576]{1,0:T(8,128)(2,1)S(1)} %get-tuple-element.96), channel_id=1, source_target_pairs={{0,6},{1,7},{2,0},{3,1},{4,2},{5,3},{6,4},{7,5},{8,14},{9,15},{10,... | collective-permute-start | bytes 884744 | tf_op jit(solution)/shard_map/ppermute | solution.py:390
  80.0 9.5 %collective-permute-start.12 = (bf16[256,576]{1,0:T(8,128)(2,1)S(1)}, bf16[256,576]{1,0:T(8,128)(2,1)S(1)}, u32[]{:S(2)}, u32[]{:S(2)}) collective-permute-start(bf16[256,576]{1,0:T(8,128)(2,1)S(1)} %get-tuple-element.100), channel_id=1, source_target_pairs={{0,2},{1,3},{2,4},{3,5},{4,6},{5,7},{6,0},{7,1},{8,10},{9,11},{10,... | collective-permute-start | bytes 884744 | tf_op jit(solution)/shard_map/ppermute | solution.py:390

commit v5 on v4

--- a/solution.py
+++ b/solution.py
@@ -8,9 +8,9 @@
 from jax.experimental.pallas import tpu as pltpu
 from jax.sharding import PartitionSpec as P
 
+
 LAT = 512
 WIDE = 576
-BLOCK = 128
 MAXL = 16
 CAP = 2
 BIG = -1e30
@@ -42,7 +42,7 @@
     lax.fori_loop(0, 16, group, 0)
 
 
-def slot_table(lists, counts, own, table, seen):
+def slot_table(lists, own, table, seen):
     for o in range(16):
         seen[o] = 0
     for j in range(MAXL):
@@ -88,7 +88,7 @@
 
 
 def take_body(lists, counts, me, arrived_ref, out_ref, table, seen, sems):
-    slot_table(lists, counts, me[0], table, seen)
+    slot_table(lists, me[0], table, seen)
     count = counts[me[0]]
 
     def copy(j):
@@ -113,7 +113,7 @@
 
 
 def put_body(lists, counts, me, a_ref, b_ref, c_ref, d_ref, out_ref, table, seen, held, sems):
-    slot_table(lists, counts, me[0], table, seen)
+    slot_table(lists, me[0], table, seen)
     count = counts[me[0]]
 
     def copy(j):
@@ -169,9 +169,11 @@
 INPLACE = pl.BlockSpec(memory_space=pltpu.HBM)
 
 
-def call(body, outs, scalars, arrays, scratch=(), direct_in=(), direct=(), alias=None, flops=None):
+def call(body, outs, scalars, arrays, scratch=(), direct_in=(), direct=(), alias=None, flops=None, anywhere=()):
     args = [
-        pltpu.with_memory_space_constraint(a, pltpu.HBM if i in direct_in else pltpu.VMEM)
+        a
+        if i in anywhere
+        else pltpu.with_memory_space_constraint(a, pltpu.HBM if i in direct_in else pltpu.VMEM)
         for i, a in enumerate(arrays)
     ]
     scalars = [pltpu.with_memory_space_constraint(a, pltpu.HBM) for a in scalars]
@@ -179,7 +181,10 @@
     return pl.pallas_call(
         body,
         in_specs=[pl.BlockSpec(memory_space=pltpu.SMEM)] * len(scalars)
-        + [INPLACE if i in direct_in else ONCHIP for i in range(len(arrays))],
+        + [
+            pl.BlockSpec(memory_space=pl.ANY) if i in anywhere else INPLACE if i in direct_in else ONCHIP
+            for i in range(len(arrays))
+        ],
         out_specs=tuple(INPLACE if i in direct else ONCHIP for i in range(len(outs))),
         out_shape=tuple(shapes),
         scratch_shapes=list(scratch),
@@ -189,37 +194,24 @@
     )(*scalars, *args)
 
 
-M_COL, L_COL, R_COL = (0, 1, 2), 3, 4
-
-
 def forward_body(nkeys, chunk, off, n, block, *refs):
     refs = list(refs)
-    first, last = chunk == 0, chunk == 2
+    last = chunk == 2
     key_refs = [refs.pop(0) for _ in range(nkeys)]
     bias, q_ref, g_ref = refs[:3]
-    refs = refs[3:]
-    if not first:
-        _, _, _, st_in, o_in = refs[:5]
-        refs = refs[5:]
+    refs = refs[3 + (4 if chunk else 0) :]
+    turned = []
     if last:
-        qt_in, gt_in = refs[:2]
-        refs = refs[2:]
-    e_out, p_out, k_out, st_out, o_out = refs[:5]
-    refs = refs[5:]
-    steps = q_ref.shape[0] * 16 // block
+        (qt_in, gt_in), refs = refs[:2], refs[2:]
+    (e_out, p_out, k_out, st_out), refs = refs[:4], refs[4:]
     if last:
-        qt_out, gt_out, held, sems, sems_t = refs
+        qt_out, gt_out, sems = refs
         turned = [
-            pltpu.make_async_copy(qt_in, qt_out, sems_t.at[0]),
-            pltpu.make_async_copy(gt_in, gt_out, sems_t.at[1]),
+            pltpu.make_async_copy(qt_in, qt_out, sems.at[0]),
+            pltpu.make_async_copy(gt_in, gt_out, sems.at[1]),
         ]
-        for copy in turned:
-            copy.start()
-
-        def leave(i):
-            part = pl.ds(i * (block // 16), block // 16)
-            return pltpu.make_async_copy(held.at[part], o_out.at[part], sems.at[i])
-
+    for copy in turned:
+        copy.start()
     at = off
     for ref in key_refs:
         k_out[at : at + ref.shape[0]] = ref[...]
@@ -231,62 +223,26 @@
         part = pl.ds(i * (block // 16), block // 16)
         scores = dot(q_ref[part].reshape(block, WIDE), k_out[mine], NT) + bias[...]
         top = jnp.max(scores, axis=1, keepdims=True)
-        if not first:
-            m_old = st_in[here, chunk - 1 : chunk]
-            l_old = st_in[here, L_COL : L_COL + 1]
-            r_old = st_in[here, R_COL : R_COL + 1]
-            top = jnp.maximum(top, m_old)
         expo = jnp.exp2((scores - top) * EXPC)
-        values = k_out[mine, :LAT]
-        grads = dot(g_ref[part].reshape(block, LAT), values, NT)
-        total = jnp.sum(expo, axis=1, keepdims=True)
-        rdot = jnp.sum(expo * grads, axis=1, keepdims=True)
-        expo = expo.astype(bf16)
-        e_out[here, mine] = expo
+        grads = dot(g_ref[part].reshape(block, LAT), k_out[mine, :LAT], NT)
+        e_out[here, mine] = expo.astype(bf16)
         p_out[here, mine] = grads.astype(bf16)
-        attended = dot(expo, values)
-        if not first:
-            fade = jnp.exp2((m_old - top) * EXPC)
-            total = total + fade * l_old
-            rdot = rdot + fade * r_old
-            attended = attended + fade * o_in[here]
-        if last:
-            total = 1.0 / total
-            rdot = rdot * total
-            attended = attended * total
-        st_out[here, chunk : chunk + 1] = top
-        st_out[here, L_COL : L_COL + 1] = total
-        st_out[here, R_COL : R_COL + 1] = rdot
-        if last:
-            held[part] = attended.astype(bf16).reshape(block // 16, 16, LAT)
-            leave(i).start()
-        else:
-            o_out[here] = attended
+        wide = lambda x: jnp.broadcast_to(x, (block, 128))
+        st_out[chunk, here] = wide(top)
+        st_out[3 + chunk, here] = wide(jnp.sum(expo, axis=1, keepdims=True))
+        st_out[6 + chunk, here] = wide(jnp.sum(expo * grads, axis=1, keepdims=True))
         return carry
 
-    lax.fori_loop(0, steps, rows, 0)
-    if last:
-        for i in range(steps):
-            leave(i).wait()
-        for copy in turned:
-            copy.wait()
-
-
-def forward(chunk, off, n, total_keys, key_parts, bias, q, g, state=(), turned=(), block=256):
+    lax.fori_loop(0, q_ref.shape[0] * 16 // block, rows, 0)
+    for copy in turned:
+        copy.wait()
+
+
+def forward(chunk, off, n, total_keys, key_parts, bias, q, g, state=(), turned=(), block=768):
     rows = q.shape[0] * 16
-    last = chunk == 2
     side = jax.ShapeDtypeStruct((rows, total_keys), bf16)
-    outs = [
-        side,
-        side,
-        jax.ShapeDtypeStruct((total_keys, WIDE), bf16),
-        jax.ShapeDtypeStruct((rows, 128), f32),
-        jax.ShapeDtypeStruct(g.shape, bf16) if last else jax.ShapeDtypeStruct((rows, LAT), f32),
-    ]
-    scratch = []
-    if last:
-        outs += [jax.ShapeDtypeStruct(t.shape, t.dtype) for t in turned]
-        scratch = [pltpu.VMEM(g.shape, bf16), pltpu.SemaphoreType.DMA((rows // block,)), pltpu.SemaphoreType.DMA((2,))]
+    outs = [side, side, jax.ShapeDtypeStruct((total_keys, WIDE), bf16), jax.ShapeDtypeStruct((9, rows, 128), f32)]
+    outs += [jax.ShapeDtypeStruct(t.shape, t.dtype) for t in turned]
     arrays = [*key_parts, bias, q, g, *state, *turned]
     start = len(key_parts) + 3
     return call(
@@ -294,88 +250,209 @@
         outs,
         (),
         arrays,
-        scratch=scratch,
+        scratch=[pltpu.SemaphoreType.DMA((2,))] if turned else [],
         direct_in=range(len(arrays) - len(turned), len(arrays)),
-        direct=(4,) if last else (),
-        alias={start + i: i for i in range((4 if last else 5) if state else 0)},
-        flops=2 * rows * n * (WIDE + 2 * LAT),
-    )
-
-
-def backward_body(chunk, off, n, step, tile, qt_ref, gt_ref, e_ref, p_ref, st_ref, k_ref, far_out, near_out, s_out, k_out, a_sc, r_sc):
+        alias={start + i: i for i in range(len(state))},
+        flops=2 * rows * n * (WIDE + LAT),
+    )
+
+
+def backward_body(chunk, off, n, early, step, tile, *refs):
+    refs = list(refs)
+    lead, final = chunk == 2, chunk == 0
+    qt_ref, gt_ref, e_ref, p_ref, row_ref, k_ref = refs[:6]
+    far_out, near_out, e_out, p_out, row_out, _, s_out = refs[6:13]
+    held, sems = refs[-2:]
     rows = qt_ref.shape[1]
     half = n // 2
-    st = st_ref[...]
-    a = jnp.exp2((st[:, chunk : chunk + 1] - st[:, 2:3]) * EXPC) * st[:, L_COL : L_COL + 1]
-    a_sc[...] = jnp.broadcast_to(a, (rows, 128))
-    r_sc[...] = jnp.broadcast_to(st[:, R_COL : R_COL + 1], (rows, 128))
+    if final:
+        kept, sem = refs[13], refs[14]
+        save = pltpu.make_async_copy(k_ref, kept, sem.at[0])
+        save.start()
+    if lead:
+        for at in range(0, rows, step):
+            here = slice(at, at + step)
+            col = lambda c: row_ref[c, here]
+            top = jnp.maximum(jnp.maximum(col(0), col(1)), col(2))
+            fade = [jnp.exp2((col(c) - top) * EXPC) for c in range(3)]
+            total = fade[0] * col(3) + fade[1] * col(4) + fade[2] * col(5)
+            rdot = fade[0] * col(6) + fade[1] * col(7) + fade[2] * col(8)
+            total = 1.0 / total
+            for c in range(3):
+                row_out[c, here] = fade[c] * total
+            row_out[3, here] = rdot * total
+    copies = []
     for start in range(0, n, tile):
-        cols = slice(off + (start + half) % n, off + (start + half) % n + tile)
+        local = slice((start + half) % n, (start + half) % n + tile)
+        cols = slice(off + local.start, off + local.stop)
         acc = None
         for at in range(0, rows, step):
             here = slice(at, at + step)
-            a = jnp.tile(a_sc[here], (1, tile // 128))
-            r = jnp.tile(r_sc[here], (1, tile // 128))
+            a = jnp.tile(row_out[chunk, here], (1, tile // 128))
+            r = jnp.tile(row_out[3, here], (1, tile // 128))
             weights = (e_ref[here, cols].astype(f32) * a).astype(bf16)
             sg = (weights.astype(f32) * (p_ref[here, cols].astype(f32) - r) * SCALE).astype(bf16)
-            s_out[here, cols] = sg
+            e_out[here, cols] = weights
+            if at < early:
+                p_out[here, cols] = sg
+            else:
+                held[local.start // tile, at - early : at - early + step] = sg
             key_part = dot(qt_ref[:, here], sg)
             value_part = dot(gt_ref[:, here], weights)
             if acc is None:
                 acc = [key_part[:LAT] + value_part, key_part[LAT:]]
             else:
                 acc = [acc[0] + (key_part[:LAT] + value_part), acc[1] + key_part[LAT:]]
+        spot = local.start // tile
+        copy = pltpu.make_async_copy(held.at[spot], s_out.at[spot], sems.at[spot])
+        copy.start()
+        copies.append(copy)
         top = acc[0].T.astype(bf16)
         low = jnp.concatenate([acc[1], jnp.zeros_like(acc[1])], axis=0).T[:, : WIDE - LAT].astype(bf16)
         ref = far_out if start < half else near_out
         put = slice(start % half, start % half + tile)
         ref[put, :LAT] = top
         ref[put, LAT:] = low
-
-
-def backward(chunk, off, n, qt, gt, e, p, st, k, tile=256, step=256):
+    for copy in copies:
+        copy.wait()
+    if final:
+        save.wait()
+
+
+def backward(chunk, off, n, early, qt, gt, e, p, row, k, tile=256, step=256):
     rows = e.shape[0]
+    lead, final = chunk == 2, chunk == 0
+    like = lambda a: jax.ShapeDtypeStruct(a.shape, a.dtype)
     part = jax.ShapeDtypeStruct((n // 2, WIDE), bf16)
+    merged = jax.ShapeDtypeStruct((4, rows, 128), f32) if lead else like(row)
+    late = (n // tile, rows - early, tile)
+    outs = [part, part, like(e), like(p), merged, like(k), jax.ShapeDtypeStruct(late, bf16)]
+    alias = {2: 2, 3: 3, 5: 5}
+    scratch = [pltpu.VMEM(late, bf16), pltpu.SemaphoreType.DMA((n // tile,))]
+    direct = (6,)
+    if not lead:
+        alias[4] = 4
+    if final:
+        outs.append(like(k))
+        direct = (6, 7)
+        scratch = [pltpu.SemaphoreType.DMA((1,)), *scratch]
     return call(
-        functools.partial(backward_body, chunk, off, n, step, tile),
-        (part, part, jax.ShapeDtypeStruct(p.shape, bf16), jax.ShapeDtypeStruct(k.shape, bf16)),
+        functools.partial(backward_body, chunk, off, n, early, step, tile),
+        outs,
         (),
-        (qt, gt, e, p, st, k),
-        scratch=[pltpu.VMEM((rows, 128), f32)] * 2,
-        alias={3: 2, 5: 3},
+        (qt, gt, e, p, row, k),
+        scratch=scratch,
+        alias=alias,
+        direct=direct,
         flops=2 * rows * n * (WIDE + LAT),
     )
 
 
-def query_body(block, s_ref, k_ref, out_ref, held, sems):
-    steps = out_ref.shape[0] * 16 // block
-
-    def leave(i):
+def leaving(held, out_ref, sems, block):
+    def copy(i):
         part = pl.ds(i * (block // 16), block // 16)
         return pltpu.make_async_copy(held.at[part], out_ref.at[part], sems.at[i])
+
+    return copy
+
+
+def value_body(block, early, w_ref, s_ref, k_ref, out_ref, q_ref, held, held_q, sems, sems_q):
+    steps = out_ref.shape[0] * 16 // block
+    leave = leaving(held, out_ref, sems, block)
+    leave_q = leaving(held_q, q_ref, sems_q, block)
+    for i in range(early // block):
+        here = slice(i * block, i * block + block)
+        part = slice(i * (block // 16), (i + 1) * (block // 16))
+        held_q[part] = dot(s_ref[here], k_ref[...]).astype(bf16).reshape(block // 16, 16, WIDE)
+        leave_q(i).start()
 
     def rows(i, carry):
         here = pl.ds(pl.multiple_of(i * block, block), block)
         part = pl.ds(i * (block // 16), block // 16)
-        held[part] = dot(s_ref[here], k_ref[...]).astype(bf16).reshape(block // 16, 16, WIDE)
+        held[part] = dot(w_ref[here], k_ref[:, :LAT]).astype(bf16).reshape(block // 16, 16, LAT)
         leave(i).start()
         return carry
 
     lax.fori_loop(0, steps, rows, 0)
+    for i in range(early // block):
+        leave_q(i).wait()
     for i in range(steps):
         leave(i).wait()
 
 
-def query_side(s, k, block=256):
-    rows = s.shape[0]
-    shape = (rows // 16, 16, WIDE)
+def value_side(w, s, k, early, block=512):
+    rows = w.shape[0]
+    shape = (rows // 16, 16, LAT)
+    dma = lambda n: pltpu.SemaphoreType.DMA((n,))
     return call(
-        functools.partial(query_body, block),
-        (jax.ShapeDtypeStruct(shape, bf16),),
+        functools.partial(value_body, block, early),
+        (jax.ShapeDtypeStruct(shape, bf16), jax.ShapeDtypeStruct((rows // 16, 16, WIDE), bf16)),
         (),
-        (s, k),
-        scratch=[pltpu.VMEM(shape, bf16), pltpu.SemaphoreType.DMA((rows // block,))],
+        (w, s, k),
+        scratch=[
+            pltpu.VMEM(shape, bf16),
+            pltpu.VMEM((early // 16, 16, WIDE), bf16),
+            dma(rows // block),
+            dma(early // block),
+        ],
+        direct=(0, 1),
+        flops=2 * k.shape[0] * (rows * LAT + early * WIDE),
+    )
+
+
+def query_body(offs, early, block, *refs):
+    s_refs, (k_ref, _, out_ref, s_v, k_v, held, sems_k, sems_s, sems) = refs[: len(offs)], refs[len(offs) :]
+    steps = s_v.shape[1] // block
+    load_k = pltpu.make_async_copy(k_ref, k_v, sems_k.at[0])
+    load_k.start()
+    loads = []
+    for i in range(steps):
+        here = slice(i * block, i * block + block)
+        loads.append(
+            [
+                pltpu.make_async_copy(ref.at[t, here], s_v.at[off + t, here], sems_s.at[i * s_v.shape[0] + off + t])
+                for ref, off in zip(s_refs, offs)
+                for t in range(ref.shape[0])
+            ]
+        )
+        for copy in loads[-1]:
+            copy.start()
+    load_k.wait()
+    leave = []
+    for i in range(steps):
+        for copy in loads[i]:
+            copy.wait()
+        here = slice(i * block, i * block + block)
+        part = slice(i * (block // 16), (i + 1) * (block // 16))
+        to = slice(early // 16 + part.start, early // 16 + part.stop)
+        sg = jnp.concatenate([s_v[t, here] for t in range(s_v.shape[0])], axis=1)
+        held[part] = dot(sg, k_v[...]).astype(bf16).reshape(block // 16, 16, WIDE)
+        leave.append(pltpu.make_async_copy(held.at[part], out_ref.at[to], sems.at[i]))
+        leave[-1].start()
+    for copy in leave:
+        copy.wait()
+
+
+def query_side(sgs, offs, early, k, out, block=512):
+    tile, rows = sgs[0].shape[2], sgs[0].shape[1]
+    dma = lambda n: pltpu.SemaphoreType.DMA((n,))
+    steps, tiles = rows // block, k.shape[0] // tile
+    return call(
+        functools.partial(query_body, [off // tile for off in offs], early, block),
+        (jax.ShapeDtypeStruct(out.shape, bf16),),
+        (),
+        (*sgs, k, out),
+        scratch=[
+            pltpu.VMEM((tiles, rows, tile), bf16),
+            pltpu.VMEM(k.shape, bf16),
+            pltpu.VMEM((rows // 16, 16, WIDE), bf16),
+            dma(1),
+            dma(steps * tiles),
+            dma(steps),
+        ],
+        direct_in=range(len(sgs) + 2),
         direct=(0,),
+        alias={len(sgs) + 1: 0},
         flops=2 * rows * k.shape[0] * WIDE,
     )[0]
 
@@ -455,26 +532,29 @@
     state = forward(1, 2 * keys, 4 * keys, every, [r1, l1, s1, s2], bias1, q, g, state)
     r2 = after(r2, state[3])
     s3 = send(r2, sibling)
-    e, p, k, st, attended, qt, gt = forward(2, 6 * keys, 2 * keys, every, [r2, s3], bias2, q, g, state, (qt, gt))
+    e, p, k, row, qt, gt = forward(2, 6 * keys, 2 * keys, every, [r2, s3], bias2, q, g, state, (qt, gt))
 
     fold = lambda a: a.reshape(-1, tokens, WIDE)
     unfold = lambda a: a.reshape(-1, WIDE)
-    far2, near2, p, k = backward(2, 6 * keys, 2 * keys, qt, gt, e, p, st, k)
+    early = 512
+    far2, near2, e, p, row, k, sg2 = backward(2, 6 * keys, 2 * keys, early, qt, gt, e, p, row, k)
     mate2 = send(far2, sibling)
-    far1, near1, p, k = backward(1, 2 * keys, 4 * keys, qt, gt, e, p, st, k)
+    far1, near1, e, p, row, k, sg1 = backward(1, 2 * keys, 4 * keys, early, qt, gt, e, p, row, k)
     mate1 = unfold(send(fold(far1), sibling))
     low, high = call(two_body, (share_of(keys // 2),) * 2, (), (after(near2, near1), mate2))
     from_left = send(low, right)
     from_right = send(high, left)
-    far0, near0, p, k = backward(0, 0, 2 * keys, qt, gt, e, p, after(st, low), k)
+    far0, near0, e, p, row, k, sg0, k_saved = backward(
+        0, 0, 2 * keys, early, qt, gt, e, p, after(row, low), k
+    )
     mate0 = send(far0, sibling)
     to_left, to_right = call(
         one_body, (share_of(keys),) * 2, (), (after(near1, near0), mate1, from_left, from_right)
     )
     got_left = send(to_right, right)
     got_right = send(to_left, left)
-    query_grad = query_side(p, after(k, to_left))
-    near0 = after(near0, query_grad)
+    attended, query_grad = value_side(e, p, after(k, to_left), early)
+    near0 = after(near0, attended)
     (slot_grads,) = call(
         put_body,
         (slots,),
@@ -483,6 +563,8 @@
         scratch=[smem(MAXL), smem(16), pltpu.VMEM((keys, WIDE), bf16), dma(MAXL)],
         direct=(0,),
     )
+    k_saved = after(k_saved, slot_grads)
+    query_grad = query_side((sg2, sg1, sg0), (6 * keys, 2 * keys, 0), early, k_saved, query_grad)
     returned = lax.all_to_all(slot_grads.reshape(16, CAP, tokens, WIDE), "req", 0, 0, tiled=True)
     (latent_grad,) = call(
         gather_body,
@@ -496,7 +578,7 @@
             dma(4),
             dma(4),
         ],
-        direct_in=(0,),
+        anywhere=(0,),
         direct=(0,),
     )
     return (attended, query_grad, latent_grad)
@@ -512,6 +594,4 @@
         P(),
     )
     out_specs = (P("req", "head", None), P("req", "head", None), P("req", "head", None))
-    return jax.shard_map(
-        per_device, mesh=mesh, in_specs=in_specs, out_specs=out_specs, check_vma=False
-    )
+    return jax.shard_map(per_device, mesh=mesh, in_specs=in_specs, out_specs=out_specs, check_vma=False)

time: 110 us -> 109 us (level)
  blocking collectives: 15.3 us -> 0 us
  waiting for transfers between devices: 20.3 us -> 27.7 us
  starting transfers between devices: 18.7 us -> 22.3 us
  Pallas kernels: 46.7 us -> 49.7 us
    all_to_all x1 -> x0, blocking collectives: 15.3 us -> none  [per_device(): lax.all_to_all(slot_grads.reshape(16, CAP, tokens, WIDE), 'req', 0, 0, ti...]
    ppermute x14, waiting for transfers between devices: 16.5 us -> 21.4 us  [per_device(): send = lambda a, perm: lax.ppermute(a, 'head', perm)]
    all_to_all x0 -> x1, starting transfers between devices: none -> 3.61 us  [per_device(): lax.all_to_all(slot_grads.reshape(16, CAP, tokens, WIDE), 'req', 0, 0, ti...]
    pallas_call x14 -> x15, Pallas kernels: 46.7 us -> 49.7 us  [call(): pl.pallas_call(body, in_specs=[pl.BlockSpec(memory_space=pltpu.SMEM)] * l...]
    all_to_all x0 -> x1, waiting for transfers between devices: none -> 2.53 us  [per_device(): lax.all_to_all(slot_grads.reshape(16, CAP, tokens, WIDE), 'req', 0, 0, ti...]
  transfers between devices with their start and end apart: 15 -> 16, of which waited for: 11 -> 12; matrix products, arithmetic and copies ran while one was open for 4% -> 4% of each run, Pallas kernels for 22% -> 26%
where the time goes in v5:
time: 109 us; the launch traced here: 108 us
  Pallas kernels  49.7 us (46%)
  waiting for transfers between devices  27.7 us (25%)
  starting transfers between devices  22.3 us (20%)
  local copies, waits for them, and re-layouts  6.04 us (6%)
  other arithmetic  1.59 us (1%)
  between operations  1.13 us (1%)
    pallas_call x15, Pallas kernels, call(): pl.pallas_call(body, in_specs=[pl.BlockSpec(memory_space=pltpu.SMEM)] * l...  49.7 us
    ppermute x14, waiting for transfers between devices, per_device(): send = lambda a, perm: lax.ppermute(a, 'head', perm)  21.4 us
    ppermute x14, starting transfers between devices, per_device(): send = lambda a, perm: lax.ppermute(a, 'head', perm)  10.4 us
    all_to_all x1, starting transfers between devices, per_device(): lax.all_to_all(outgoing.reshape(16, CAP, tokens, WIDE), 'req', 0, 0, tile...  8.22 us
    unnamed x15, local copies, waits for them, and re-layouts  3.78 us
    all_to_all x1, waiting for transfers between devices, per_device(): lax.all_to_all(outgoing.reshape(16, CAP, tokens, WIDE), 'req', 0, 0, tile...  3.76 us
    all_to_all x1, starting transfers between devices, per_device(): lax.all_to_all(slot_grads.reshape(16, CAP, tokens, WIDE), 'req', 0, 0, ti...  3.61 us
    all_to_all x1, waiting for transfers between devices, per_device(): lax.all_to_all(slot_grads.reshape(16, CAP, tokens, WIDE), 'req', 0, 0, ti...  2.53 us
  transfers between devices with their start and end apart: 16, of which 12 were waited for; matrix products, arithmetic and copies ran while one was open for 4% of the time, Pallas kernels for 26%

profile of v5, /device:TPU:0, one launch (start us, length us, event | category | flops | bytes accessed | tf_op | source)
XLA Modules:
  0.0 108.4 jit_solution(10366793072935752552)
XLA Ops:
  0.6 0.0 copy-start
  0.6 2.8 %shard_map.85 = bf16[32,16,576]{2,1,0:T(8,128)(2,1)} custom-call(s32[16,16]{1,0:T(8,128)} %lists.7, s32[16]{0:T(128)} %counts.7, s32[1]{0:T(128)} %bitcast.me, bf16[16,16,576]{2,1,0:T(8,128)(2,1)} %lat_ref.1), custom_call_target="tpu_custom_call" | custom-call | tf_op jit(solution)/shard_map/pallas_call | solution.py:181
  3.4 8.2 %all-to-all-start = ((bf16[16,2,16,576]{3,2,1,0:T(8,128)(2,1)}), bf16[16,2,16,576]{3,2,1,0:T(8,128)(2,1)}, u32[]{:S(2)}, u32[]{:S(2)}) async-start(bf16[16,2,16,576]{3,2,1,0:T(8,128)(2,1)} %bitcast.37), calls=%async_computation | async-start | bytes 1310720 | tf_op jit(solution)/shard_map/all_to_all | solution.py:491
  11.8 1.2 %dynamic_slice.8 = s32[1]{0:T(128)} dynamic-slice(s32[16]{0:T(128)} %counts.7, s32[]{:T(128)S(6)} %select_n.59), dynamic_slice_sizes={1} | dynamic-slice | bytes 12 | tf_op jit(solution)/shard_map/jit(dynamic_index_in_dim)/dynamic_slice | solution.py:494
  13.0 0.7 dynamic-slice_bitcast_fusion
  13.7 0.1 stack.35
  13.8 0.9 select_reduce_fusion
  14.7 0.7 compare_select_fusion
  15.3 0.1 broadcast_in_dim.34
  15.4 0.1 lt.60
  15.5 0.1 add.95
  15.6 0.1 fusion
  15.7 0.0 copy-done
  15.7 0.0 copy-start.1
  15.7 1.4 %copy-done.1 = bf16[96,16,512]{2,1,0:T(8,128)(2,1)S(1)} copy-done((bf16[96,16,512]{2,1,0:T(8,128)(2,1)S(1)}, bf16[96,16,512]{2,1,0:T(8,128)(2,1)}, u32[]{:S(2)}) %copy-start.1) | copy-done | bytes 1572888
  17.1 1.4 %shard_map.86 = (bf16[576,1536]{1,0:T(8,128)(2,1)S(1)}, bf16[512,1536]{1,0:T(8,128)(2,1)S(1)}) custom-call(bf16[96,16,576]{2,1,0:T(8,128)(2,1)S(1)} %copy-done, bf16[96,16,512]{2,1,0:T(8,128)(2,1)S(1)} %copy-done.1), custom_call_target="tpu_custom_call" | custom-call | tf_op jit(solution)/shard_map/pallas_call | solution.py:181
  18.5 0.0 copy-start.3
  18.5 1.2 %copy-done.3 = bf16[576,1536]{1,0:T(8,128)(2,1)} copy-done((bf16[576,1536]{1,0:T(8,128)(2,1)}, bf16[576,1536]{1,0:T(8,128)(2,1)S(1)}, u32[]{:S(2)}) %copy-start.3) | copy-done | bytes 1769496
  19.7 1.1 %copy-done.4 = bf16[512,1536]{1,0:T(8,128)(2,1)} copy-done((bf16[512,1536]{1,0:T(8,128)(2,1)}, bf16[512,1536]{1,0:T(8,128)(2,1)S(1)}, u32[]{:S(2)}) %copy-start.4) | copy-done | bytes 1572888
  20.9 3.8 %all-to-all-done = bf16[16,2,16,576]{3,2,1,0:T(8,128)(2,1)} async-done(((bf16[16,2,16,576]{3,2,1,0:T(8,128)(2,1)}), bf16[16,2,16,576]{3,2,1,0:T(8,128)(2,1)}, u32[]{:S(2)}, u32[]{:S(2)}) %all-to-all-start) | async-done | bytes 589856 | tf_op jit(solution)/shard_map/all_to_all | solution.py:491
  24.6 1.9 %shard_map.87.refs_0_ = bf16[256,576]{1,0:T(8,128)(2,1)S(1)} custom-call(s32[16,16]{1,0:T(8,128)} %lists.7, s32[16]{0:T(128)} %counts.7, s32[1]{0:T(128)} %bitcast.me, bf16[32,16,576]{2,1,0:T(8,128)(2,1)} %bitcast.12.arrived_ref), custom_call_target="tpu_custom_call" | custom-call | tf_op jit(solution)/shard_map/pallas_call | solution.py:181
  26.6 0.1 collective-permute-start.1
  26.7 2.8 %collective-permute-start.3 = (bf16[256,576]{1,0:T(8,128)(2,1)S(1)}, bf16[256,576]{1,0:T(8,128)(2,1)S(1)}, u32[]{:S(2)}, u32[]{:S(2)}) collective-permute-start(bf16[256,576]{1,0:T(8,128)(2,1)S(1)} %shard_map.87.refs_0_), channel_id=1, source_target_pairs={{0,6},{1,7},{2,0},{3,1},{4,2},{5,3},{6,4},{7,5},{8,14},{9,15},{10,... | collective-permute-start | bytes 884744 | tf_op jit(solution)/shard_map/ppermute | solution.py:467
  29.5 0.0 collective-permute-start
  29.5 0.0 collective-permute-done.1.refs_1_
  29.5 0.0 copy-done.2
  29.5 2.8 %shard_map.88 = (bf16[1536,2048]{1,0:T(8,128)(2,1)S(1)}, bf16[1536,2048]{1,0:T(8,128)(2,1)S(1)}, bf16[2048,576]{1,0:T(8,128)(2,1)S(1)}, f32[9,1536,128]{2,1,0:T(8,128)S(1)}) custom-call(bf16[256,576]{1,0:T(8,128)(2,1)S(1)} %shard_map.87.refs_0_, bf16[256,576]{1,0:T(8,128)(2,1)S(1)} %collective-permute-done.1.refs_1_, f32[1,512]{1,0:T(1,128)S(1)} %bitcast.34, ...), custom_call_target="tpu_custom_call" | custom-call | flops 1711276032 | tf_op jit(solution)/shard_map/pallas_call | solution.py:181
  32.3 4.7 %collective-permute-done.3.refs_1_ = bf16[256,576]{1,0:T(8,128)(2,1)S(1)} collective-permute-done((bf16[256,576]{1,0:T(8,128)(2,1)S(1)}, bf16[256,576]{1,0:T(8,128)(2,1)S(1)}, u32[]{:S(2)}, u32[]{:S(2)}) %collective-permute-start.3) | collective-permute-done | bytes 294944 | tf_op jit(solution)/shard_map/ppermute | solution.py:467
  37.1 3.4 %collective-permute-done.refs_0_ = bf16[256,576]{1,0:T(8,128)(2,1)S(1)} collective-permute-done((bf16[256,576]{1,0:T(8,128)(2,1)S(1)}, bf16[256,576]{1,0:T(8,128)(2,1)S(1)}, u32[]{:S(2)}, u32[]{:S(2)}) %collective-permute-start) | collective-permute-done | bytes 294944 | tf_op jit(solution)/shard_map/ppermute | solution.py:467
  40.5 0.0 collective-permute-start.4
  40.5 0.5 collective-permute-start.5
  41.0 0.0 collective-permute-start.2
  41.0 1.1 %collective-permute-done.4.refs_2_ = bf16[256,576]{1,0:T(8,128)(2,1)S(1)} collective-permute-done((bf16[256,576]{1,0:T(8,128)(2,1)S(1)}, bf16[256,576]{1,0:T(8,128)(2,1)S(1)}, u32[]{:S(2)}, u32[]{:S(2)}) %collective-permute-start.4) | collective-permute-done | bytes 294944 | tf_op jit(solution)/shard_map/ppermute | solution.py:467
  42.1 0.5 collective-permute-done.5.refs_3_
  42.6 5.6 %shard_map.89 = (bf16[1536,2048]{1,0:T(8,128)(2,1)S(1)}, bf16[1536,2048]{1,0:T(8,128)(2,1)S(1)}, bf16[2048,576]{1,0:T(8,128)(2,1)S(1)}, f32[9,1536,128]{2,1,0:T(8,128)S(1)}) custom-call(bf16[256,576]{1,0:T(8,128)(2,1)S(1)} %collective-permute-done.refs_0_, ...), custom_call_target="tpu_custom_call", output_to_operand_aliasing={{0}: (7, {}), {1}: (8, {}), {2}: (9, {}), {3}: (10, {})} | custom-call | flops 3422552064 | tf_op jit(solution)/shard_map/pallas_call | solution.py:181
  48.2 3.6 %collective-permute-done.2.refs_0_ = bf16[256,576]{1,0:T(8,128)(2,1)S(1)} collective-permute-done((bf16[256,576]{1,0:T(8,128)(2,1)S(1)}, bf16[256,576]{1,0:T(8,128)(2,1)S(1)}, u32[]{:S(2)}, u32[]{:S(2)}) %collective-permute-start.2) | collective-permute-done | bytes 294944 | tf_op jit(solution)/shard_map/ppermute | solution.py:467
  51.8 0.0 collective-permute-start.6
  51.8 1.6 %collective-permute-done.6.refs_1_ = bf16[256,576]{1,0:T(8,128)(2,1)S(1)} collective-permute-done((bf16[256,576]{1,0:T(8,128)(2,1)S(1)}, bf16[256,576]{1,0:T(8,128)(2,1)S(1)}, u32[]{:S(2)}, u32[]{:S(2)}) %collective-permute-start.6) | collective-permute-done | bytes 294944 | tf_op jit(solution)/shard_map/ppermute | solution.py:467
  53.4 2.8 %shard_map.90 = (bf16[1536,2048]{1,0:T(8,128)(2,1)S(1)}, bf16[1536,2048]{1,0:T(8,128)(2,1)S(1)}, bf16[2048,576]{1,0:T(8,128)(2,1)S(1)}, f32[9,1536,128]{2,1,0:T(...) custom-call(bf16[256,576]{1,0:T(8,128)(2,1)S(1)} %collective-permute, ...), custom_call_target="tpu_custom_call", output_to_operand_aliasing={{0}: (5, {}), {1}: (6, {}), {2}: (7, {}), {3}: (8, {})} | custom-call | flops 1711276032 | tf_op jit(solution)/shard_map/pallas_call | solution.py:181
  56.3 3.6 %shard_map.91 = (bf16[256,576]{1,0:T(8,128)(2,1)S(1)}, bf16[256,576]{1,0:T(8,128)(2,1)S(1)}, bf16[1536,2048]{1,0:T(8,128)(2,1)S(1)}, bf16[1536,2048]{1,0:T(8,128...) custom-call(bf16[576,1536]{1,0:T(8,128)(2,1)S(1)} %get-tuple-element, ...), custom_call_target="tpu_custom_call", output_to_operand_aliasing={{2}: (2, {}), {3}: (3, {}), {5}: (5, {})} | custom-call | flops 1711276032 | tf_op jit(solution)/shard_map/pallas_call | solution.py:181
  59.9 5.1 %shard_map.92 = (bf16[512,576]{1,0:T(8,128)(2,1)S(1)}, bf16[512,576]{1,0:T(8,128)(2,1)S(1)}, bf16[1536,2048]{1,0:T(8,128)(2,1)S(1)}, bf16[1536,2048]{1,0:T(8,128...) custom-call(bf16[576,1536]{1,0:T(8,128)(2,1)S(1)} %get-tuple-element, ...), custom_call_target="tpu_custom_call", output_to_operand_aliasing={{2}: (2, {}), {3}: (3, {}), {5}: (5, {}), {4}: (4, {})} | custom-call | flops 3422552064 | tf_op jit(solution)/shard_map/pallas_call | solution.py:181
  65.0 0.2 collective-permute-start.8
  65.2 0.4 collective-permute-start.7
  65.6 2.1 %collective-permute-done.7.far_ref = bf16[256,576]{1,0:T(8,128)(2,1)S(1)} collective-permute-done((bf16[256,576]{1,0:T(8,128)(2,1)S(1)}, bf16[256,576]{1,0:T(8,128)(2,1)S(1)}, u32[]{:S(2)}, u32[]{:S(2)}) %collective-permute-start.7) | collective-permute-done | bytes 294944 | tf_op jit(solution)/shard_map/ppermute | solution.py:467
  67.7 0.1 shard_map.93
  67.8 0.1 collective-permute-start.9
  67.8 3.2 %collective-permute-start.10 = (bf16[128,576]{1,0:T(8,128)(2,1)S(1)}, bf16[128,576]{1,0:T(8,128)(2,1)S(1)}, u32[]{:S(2)}, u32[]{:S(2)}) collective-permute-start(bf16[128,576]{1,0:T(8,128)(2,1)S(1)} %get-tuple-element.106), channel_id=1, source_target_pairs={{0,6},{1,7},{2,0},{3,1},{4,2},{5,3},{6,4},{7,5},{8,14},{9,15},{10,... | collective-permute-start | bytes 442376 | tf_op jit(solution)/shard_map/ppermute | solution.py:467
  71.1 2.9 %shard_map.94 = (bf16[256,576]{1,0:T(8,128)(2,1)S(1)}, bf16[256,576]{1,0:T(8,128)(2,1)S(1)}, bf16[1536,2048]{1,0:T(8,128)(2,1)S(1)}, bf16[1536,2048]{1,0:T(8,128...) custom-call(bf16[576,1536]{1,0:T(8,128)(2,1)S(1)} %get-tuple-element, ...), custom_call_target="tpu_custom_call", output_to_operand_aliasing={{2}: (2, {}), {3}: (3, {}), {5}: (5, {}), {4}: (4, {})} | custom-call | flops 1711276032 | tf_op jit(solution)/shard_map/pallas_call | solution.py:181
  74.0 0.1 collective-permute-start.11
  74.1 0.4 collective-permute-done.10.high_ref
  74.5 0.7 collective-permute-done.9.low_ref
  75.3 0.0 collective-permute-done.8
  75.3 0.2 shard_map.95
  75.5 3.0 %collective-permute-start.13 = (bf16[256,576]{1,0:T(8,128)(2,1)S(1)}, bf16[256,576]{1,0:T(8,128)(2,1)S(1)}, u32[]{:S(2)}, u32[]{:S(2)}) collective-permute-start(bf16[256,576]{1,0:T(8,128)(2,1)S(1)} %get-tuple-element.107), channel_id=1, source_target_pairs={{0,6},{1,7},{2,0},{3,1},{4,2},{5,3},{6,4},{7,5},{8,14},{9,15},{10,... | collective-permute-start | bytes 884744 | tf_op jit(solution)/shard_map/ppermute | solution.py:467
  78.5 0.0 collective-permute-start.12
  78.5 6.4 %shard_map.96 = (bf16[96,16,512]{2,1,0:T(8,128)(2,1)}, bf16[96,16,576]{2,1,0:T(8,128)(2,1)}) custom-call(bf16[1536,2048]{1,0:T(8,128)(2,1)S(1)} %get-tuple-element.100.w_ref, bf16[1536,2048]{1,0:T(8,128)(2,1)S(1)} %get-tuple-element.101.s_ref, bf16[2048,576]{1,0:T(8,128)(2,1)S(1)} %get-tuple-element.108.k_ref), custom_call_target="tpu_custom_call" | custom-call | flops 4429185024 | tf_op jit(solution)/shard_map/pallas_call | solution.py:181
  84.9 0.0 collective-permute-done.11.b_ref
  84.9 3.2 %collective-permute-done.12.c_ref = bf16[256,576]{1,0:T(8,128)(2,1)S(1)} collective-permute-done((bf16[256,576]{1,0:T(8,128)(2,1)S(1)}, bf16[256,576]{1,0:T(8,128)(2,1)S(1)}, u32[]{:S(2)}, u32[]{:S(2)}) %collective-permute-start.12) | collective-permute-done | bytes 294944 | tf_op jit(solution)/shard_map/ppermute | solution.py:467
  88.1 0.0 collective-permute-done.13.d_ref
  88.1 1.7 %shard_map.97 = bf16[32,16,576]{2,1,0:T(8,128)(2,1)} custom-call(s32[16,16]{1,0:T(8,128)} %lists.7, s32[16]{0:T(128)} %counts.7, s32[1]{0:T(128)} %bitcast.me, bf16[256,576]{1,0:T(8,128)(2,1)S(1)} %get-tuple-element.114.a_ref, bf16[256,576]{1,0:T(8,128)(2,1)S(1)} %collective-permute-done.11.b_ref, bf16[256,576]{1,0:T(8,128)(2,1)S(1)} %collective-permute-done.12.c_ref, ...), custom_call_target="tpu_custom_call" | custom-call | tf_op jit(solution)/shard_map/pallas_call | solution.py:181
  89.7 3.6 %all-to-all-start.1 = ((bf16[16,2,16,576]{3,2,1,0:T(8,128)(2,1)}), bf16[16,2,16,576]{3,2,1,0:T(8,128)(2,1)S(1)}, u32[]{:S(2)}, u32[]{:S(2)}) async-start(bf16[16,2,16,576]{3,2,1,0:T(8,128)(2,1)} %bitcast.36), calls=%async_computation.1 | async-start | bytes 1310720 | tf_op jit(solution)/shard_map/all_to_all | solution.py:568
  93.4 8.6 %shard_map.98 = bf16[96,16,576]{2,1,0:T(8,128)(2,1)} custom-call(bf16[2,1024,256]{2,1,0:T(8,128)(2,1)} %get-tuple-element.110.refs_0_, bf16[4,1024,256]{2,1,0:T(8,128)(2,1)} %get-tuple-element.111.refs_1_, bf16[2,1024,256]{2,1,0:T(8,128)(2,1)} %get-tuple-element.112.refs_2_, ...), custom_call_target="tpu_custom_call", output_to_operand_aliasing={{}: (4, {})} | custom-call | flops 2415919104 | tf_op jit(solution)/shard_map/pallas_call | solution.py:181
  102.0 2.5 %all-to-all-done.1 = bf16[16,2,16,576]{3,2,1,0:T(8,128)(2,1)S(1)} async-done(((bf16[16,2,16,576]{3,2,1,0:T(8,128)(2,1)}), bf16[16,2,16,576]{3,2,1,0:T(8,128)(2,1)S(1)}, u32[]{:S(2)}, u32[]{:S(2)}) %all-to-all-start.1) | async-done | bytes 589856 | tf_op jit(solution)/shard_map/all_to_all | solution.py:568
  104.5 3.7 %shard_map.99 = f32[16,16,576]{2,1,0:T(8,128)} custom-call(s32[16,16]{1,0:T(8,128)} %lists.7, s32[16]{0:T(128)} %counts.7, s32[1]{0:T(128)} %bitcast.me, bf16[32,16,576]{2,1,0:T(8,128)(2,1)S(1)} %bitcast.30), custom_call_target="tpu_custom_call" | custom-call | tf_op jit(solution)/shard_map/pallas_call | solution.py:181
  (9 shorter events, 0.0 us)
Async XLA Ops:
  0.6 15.0 %copy-start = (bf16[96,16,576]{2,1,0:T(8,128)(2,1)S(1)}, bf16[96,16,576]{2,1,0:T(8,128)(2,1)}, u32[]{:S(2)}) copy-start(bf16[96,16,576]{2,1,0:T(8,128)(2,1)} %refs_3_.3) | copy-start | bytes 5308420
  3.4 21.2 %all-to-all-start = ((bf16[16,2,16,576]{3,2,1,0:T(8,128)(2,1)}), bf16[16,2,16,576]{3,2,1,0:T(8,128)(2,1)}, u32[]{:S(2)}, u32[]{:S(2)}) async-start(bf16[16,2,16,576]{3,2,1,0:T(8,128)(2,1)} %bitcast.37), calls=%async_computation | async-start | bytes 1310720 | tf_op jit(solution)/shard_map/all_to_all | solution.py:491
  15.7 1.4 %copy-start.1 = (bf16[96,16,512]{2,1,0:T(8,128)(2,1)S(1)}, bf16[96,16,512]{2,1,0:T(8,128)(2,1)}, u32[]{:S(2)}) copy-start(bf16[96,16,512]{2,1,0:T(8,128)(2,1)} %refs_4_.3) | copy-start | bytes 4718596
  17.1 12.4 %copy-start.2 = (bf16[96,16,512]{2,1,0:T(8,128)(2,1)S(1)}, bf16[96,16,512]{2,1,0:T(8,128)(2,1)}, u32[]{:S(2)}) copy-start(bf16[96,16,512]{2,1,0:T(8,128)(2,1)} %refs_4_.3) | copy-start | bytes 4718596
  18.5 1.2 %copy-start.3 = (bf16[576,1536]{1,0:T(8,128)(2,1)}, bf16[576,1536]{1,0:T(8,128)(2,1)S(1)}, u32[]{:S(2)}) copy-start(bf16[576,1536]{1,0:T(8,128)(2,1)S(1)} %get-tuple-element.78.refs_9_) | copy-start | bytes 5308420
  19.7 1.1 %copy-start.4 = (bf16[512,1536]{1,0:T(8,128)(2,1)}, bf16[512,1536]{1,0:T(8,128)(2,1)S(1)}, u32[]{:S(2)}) copy-start(bf16[512,1536]{1,0:T(8,128)(2,1)S(1)} %get-tuple-element.79.refs_10_) | copy-start | bytes 4718596
  26.6 2.9 %collective-permute-start.1 = (bf16[256,576]{1,0:T(8,128)(2,1)S(1)}, bf16[256,576]{1,0:T(8,128)(2,1)S(1)}, u32[]{:S(2)}, u32[]{:S(2)}) collective-permute-start(bf16[256,576]{1,0:T(8,128)(2,1)S(1)} %shard_map.87.refs_0_), channel_id=1, source_target_pairs={{0,1},{1,0},{2,3},{3,2},{4,5},{5,4},{6,7},{7,6},{8,9},{9,8},{10,11... | collective-permute-start | bytes 884744 | tf_op jit(solution)/shard_map/ppermute | solution.py:467
  26.7 10.4 %collective-permute-start.3 = (bf16[256,576]{1,0:T(8,128)(2,1)S(1)}, bf16[256,576]{1,0:T(8,128)(2,1)S(1)}, u32[]{:S(2)}, u32[]{:S(2)}) collective-permute-start(bf16[256,576]{1,0:T(8,128)(2,1)S(1)} %shard_map.87.refs_0_), channel_id=1, source_target_pairs={{0,6},{1,7},{2,0},{3,1},{4,2},{5,3},{6,4},{7,5},{8,14},{9,15},{10,... | collective-permute-start | bytes 884744 | tf_op jit(solution)/shard_map/ppermute | solution.py:467
  29.5 11.0 %collective-permute-start = (bf16[256,576]{1,0:T(8,128)(2,1)S(1)}, bf16[256,576]{1,0:T(8,128)(2,1)S(1)}, u32[]{:S(2)}, u32[]{:S(2)}) collective-permute-start(bf16[256,576]{1,0:T(8,128)(2,1)S(1)} %shard_map.87.refs_0_), channel_id=1, source_target_pairs={{0,2},{1,3},{2,4},{3,5},{4,6},{5,7},{6,0},{7,1},{8,10},{9,11},{10,... | collective-permute-start | bytes 884744 | tf_op jit(solution)/shard_map/ppermute | solution.py:467
  40.5 1.6 %collective-permute-start.4 = (bf16[256,576]{1,0:T(8,128)(2,1)S(1)}, bf16[256,576]{1,0:T(8,128)(2,1)S(1)}, u32[]{:S(2)}, u32[]{:S(2)}) collective-permute-start(bf16[256,576]{1,0:T(8,128)(2,1)S(1)} %collective-permute-done.refs_0_), channel_id=1, source_target_pairs={{0,1},{1,0},{2,3},{3,2},{4,5},{5,4},{6,7},{7,6},{8,9},{9,8},{10,11... | collective-permute-start | bytes 884744 | tf_op jit(solution)/shard_map/ppermute | solution.py:467
  40.5 2.1 %collective-permute-start.5 = (bf16[256,576]{1,0:T(8,128)(2,1)S(1)}, bf16[256,576]{1,0:T(8,128)(2,1)S(1)}, u32[]{:S(2)}, u32[]{:S(2)}) collective-permute-start(bf16[256,576]{1,0:T(8,128)(2,1)S(1)} %collective-permute-done.3.refs_1_), channel_id=1, source_target_pairs={{0,1},{1,0},{2,3},{3,2},{4,5},{5,4},{6,7},{7,6},{8,9},{9,8},{10,11... | collective-permute-start | bytes 884744 | tf_op jit(solution)/shard_map/ppermute | solution.py:467
  41.0 10.8 %collective-permute-start.2 = (bf16[256,576]{1,0:T(8,128)(2,1)S(1)}, bf16[256,576]{1,0:T(8,128)(2,1)S(1)}, u32[]{:S(2)}, u32[]{:S(2)}) collective-permute-start(bf16[256,576]{1,0:T(8,128)(2,1)S(1)} %collective-permute-done.refs_0_), channel_id=1, source_target_pairs={{0,2},{1,3},{2,4},{3,5},{4,6},{5,7},{6,0},{7,1},{8,10},{9,11},{10,... | collective-permute-start | bytes 884744 | tf_op jit(solution)/shard_map/ppermute | solution.py:467
  51.8 1.6 %collective-permute-start.6 = (bf16[256,576]{1,0:T(8,128)(2,1)S(1)}, bf16[256,576]{1,0:T(8,128)(2,1)S(1)}, u32[]{:S(2)}, u32[]{:S(2)}) collective-permute-start(bf16[256,576]{1,0:T(8,128)(2,1)S(1)} %collective-permute-done.2.refs_0_), channel_id=1, source_target_pairs={{0,1},{1,0},{2,3},{3,2},{4,5},{5,4},{6,7},{7,6},{8,9},{9,8},{10,11... | collective-permute-start | bytes 884744 | tf_op jit(solution)/shard_map/ppermute | solution.py:467
  65.0 10.3 %collective-permute-start.8 = (bf16[32,16,576]{2,1,0:T(8,128)(2,1)S(1)}, bf16[32,16,576]{2,1,0:T(8,128)(2,1)S(1)}, u32[]{:S(2)}, u32[]{:S(2)}) collective-permute-start(bf16[32,16,576]{2,1,0:T(8,128)(2,1)S(1)} %bitcast.35), channel_id=1, source_target_pairs={{0,1},{1,0},{2,3},{3,2},{4,5},{5,4},{6,7},{7,6},{8,9},{9,8},{10,11... | collective-permute-start | bytes 1769480 | tf_op jit(solution)/shard_map/ppermute | solution.py:467
  65.2 2.4 %collective-permute-start.7 = (bf16[256,576]{1,0:T(8,128)(2,1)S(1)}, bf16[256,576]{1,0:T(8,128)(2,1)S(1)}, u32[]{:S(2)}, u32[]{:S(2)}) collective-permute-start(bf16[256,576]{1,0:T(8,128)(2,1)S(1)} %get-tuple-element.96), channel_id=1, source_target_pairs={{0,1},{1,0},{2,3},{3,2},{4,5},{5,4},{6,7},{7,6},{8,9},{9,8},{10,11... | collective-permute-start | bytes 884744 | tf_op jit(solution)/shard_map/ppermute | solution.py:467
  67.8 7.5 %collective-permute-start.9 = (bf16[128,576]{1,0:T(8,128)(2,1)S(1)}, bf16[128,576]{1,0:T(8,128)(2,1)S(1)}, u32[]{:S(2)}, u32[]{:S(2)}) collective-permute-start(bf16[128,576]{1,0:T(8,128)(2,1)S(1)} %get-tuple-element.97), channel_id=1, source_target_pairs={{0,2},{1,3},{2,4},{3,5},{4,6},{5,7},{6,0},{7,1},{8,10},{9,11},{10,... | collective-permute-start | bytes 442376 | tf_op jit(solution)/shard_map/ppermute | solution.py:467
  67.8 6.7 %collective-permute-start.10 = (bf16[128,576]{1,0:T(8,128)(2,1)S(1)}, bf16[128,576]{1,0:T(8,128)(2,1)S(1)}, u32[]{:S(2)}, u32[]{:S(2)}) collective-permute-start(bf16[128,576]{1,0:T(8,128)(2,1)S(1)} %get-tuple-element.106), channel_id=1, source_target_pairs={{0,6},{1,7},{2,0},{3,1},{4,2},{5,3},{6,4},{7,5},{8,14},{9,15},{10,... | collective-permute-start | bytes 442376 | tf_op jit(solution)/shard_map/ppermute | solution.py:467
  74.0 10.9 %collective-permute-start.11 = (bf16[256,576]{1,0:T(8,128)(2,1)S(1)}, bf16[256,576]{1,0:T(8,128)(2,1)S(1)}, u32[]{:S(2)}, u32[]{:S(2)}) collective-permute-start(bf16[256,576]{1,0:T(8,128)(2,1)S(1)} %get-tuple-element.115), channel_id=1, source_target_pairs={{0,1},{1,0},{2,3},{3,2},{4,5},{5,4},{6,7},{7,6},{8,9},{9,8},{10,11... | collective-permute-start | bytes 884744 | tf_op jit(solution)/shard_map/ppermute | solution.py:467
  75.5 12.6 %collective-permute-start.13 = (bf16[256,576]{1,0:T(8,128)(2,1)S(1)}, bf16[256,576]{1,0:T(8,128)(2,1)S(1)}, u32[]{:S(2)}, u32[]{:S(2)}) collective-permute-start(bf16[256,576]{1,0:T(8,128)(2,1)S(1)} %get-tuple-element.107), channel_id=1, source_target_pairs={{0,6},{1,7},{2,0},{3,1},{4,2},{5,3},{6,4},{7,5},{8,14},{9,15},{10,... | collective-permute-start | bytes 884744 | tf_op jit(solution)/shard_map/ppermute | solution.py:467
  78.5 9.5 %collective-permute-start.12 = (bf16[256,576]{1,0:T(8,128)(2,1)S(1)}, bf16[256,576]{1,0:T(8,128)(2,1)S(1)}, u32[]{:S(2)}, u32[]{:S(2)}) collective-permute-start(bf16[256,576]{1,0:T(8,128)(2,1)S(1)} %get-tuple-element.116), channel_id=1, source_target_pairs={{0,2},{1,3},{2,4},{3,5},{4,6},{5,7},{6,0},{7,1},{8,10},{9,11},{10,... | collective-permute-start | bytes 884744 | tf_op jit(solution)/shard_map/ppermute | solution.py:467
  89.7 14.8 %all-to-all-start.1 = ((bf16[16,2,16,576]{3,2,1,0:T(8,128)(2,1)}), bf16[16,2,16,576]{3,2,1,0:T(8,128)(2,1)S(1)}, u32[]{:S(2)}, u32[]{:S(2)}) async-start(bf16[16,2,16,576]{3,2,1,0:T(8,128)(2,1)} %bitcast.36), calls=%async_computation.1 | async-start | bytes 1310720 | tf_op jit(solution)/shard_map/all_to_all | solution.py:568

commit v6 on v5

--- a/solution.py
+++ b/solution.py
@@ -55,61 +55,44 @@
 def pick_body(lists, counts, me, lat_ref, out_ref, table, lat, held, sem, sems):
     load = pltpu.make_async_copy(lat_ref, lat, sem.at[0])
     load.start()
-    owner_table(lists, counts, me[0], table, 0)
+    owner_table(lists, counts, me[0], table, 16)
     load.wait()
     step = SLOTS // 4
     parts = [slice(i * step, i * step + step) for i in range(4)]
     copies = [pltpu.make_async_copy(held.at[p], out_ref.at[p], sems.at[i]) for i, p in enumerate(parts)]
     for s in range(SLOTS):
-        held[s] = lat[table[s]]
+        held[s] = lat[table[s] & 15]
         if s % step == step - 1:
             copies[s // step].start()
     for copy in copies:
         copy.wait()
 
 
-def gather_body(lists, counts, me, arrived_ref, out_ref, table, held, total, sems, sems_out):
-    step = SLOTS // 4
-    parts = [slice(i * step, i * step + step) for i in range(4)]
-    copies = [pltpu.make_async_copy(arrived_ref.at[p], held.at[p], sems.at[i]) for i, p in enumerate(parts)]
-    for copy in copies:
-        copy.start()
-    owner_table(lists, counts, me[0], table, 16)
+def gather_body(table, arrived_ref, out_ref, total, sems):
     total[...] = jnp.zeros(total.shape, total.dtype)
     for s in range(SLOTS):
-        if s % step == 0:
-            copies[s // step].wait()
-        total[table[s]] = total[table[s]] + held[s].astype(f32)
-    copies = [pltpu.make_async_copy(total.at[4 * i : 4 * i + 4], out_ref.at[4 * i : 4 * i + 4], sems_out.at[i]) for i in range(4)]
+        total[table[s]] = total[table[s]] + arrived_ref[s].astype(f32)
+    parts = [slice(i * 4, i * 4 + 4) for i in range(4)]
+    copies = [pltpu.make_async_copy(total.at[p], out_ref.at[p], sems.at[i]) for i, p in enumerate(parts)]
     for copy in copies:
         copy.start()
     for copy in copies:
         copy.wait()
 
 
-def take_body(lists, counts, me, arrived_ref, out_ref, table, seen, sems):
+def take_body(lists, counts, me, arrived_ref, out_ref, table, seen):
     slot_table(lists, me[0], table, seen)
     count = counts[me[0]]
-
-    def copy(j):
-        return pltpu.make_async_copy(arrived_ref.at[table[j]], out_ref.at[j * 16 : j * 16 + 16], sems.at[j])
-
     for j in range(MAXL):
         live = j < count
 
         @pl.when(live)
         def _():
-            copy(j).start()
+            out_ref[j * 16 : j * 16 + 16] = arrived_ref[table[j]]
 
         @pl.when(jnp.logical_not(live))
         def _():
             out_ref[j * 16 : j * 16 + 16] = jnp.zeros((16, WIDE), bf16)
-
-    for j in range(MAXL):
-
-        @pl.when(j < count)
-        def _():
-            copy(j).wait()
 
 
 def put_body(lists, counts, me, a_ref, b_ref, c_ref, d_ref, out_ref, table, seen, held, sems):
@@ -169,23 +152,22 @@
 INPLACE = pl.BlockSpec(memory_space=pltpu.HBM)
 
 
-def call(body, outs, scalars, arrays, scratch=(), direct_in=(), direct=(), alias=None, flops=None, anywhere=()):
+def call(body, outs, scalars, arrays, scratch=(), direct_in=(), direct=(), alias=None, flops=None, smem_out=()):
     args = [
-        a
-        if i in anywhere
-        else pltpu.with_memory_space_constraint(a, pltpu.HBM if i in direct_in else pltpu.VMEM)
+        pltpu.with_memory_space_constraint(a, pltpu.HBM if i in direct_in else pltpu.VMEM)
         for i, a in enumerate(arrays)
     ]
     scalars = [pltpu.with_memory_space_constraint(a, pltpu.HBM) for a in scalars]
-    shapes = [(pltpu.HBM if i in direct else pltpu.VMEM)(o.shape, o.dtype) for i, o in enumerate(outs)]
+    shapes = [
+        o if i in smem_out else (pltpu.HBM if i in direct else pltpu.VMEM)(o.shape, o.dtype)
+        for i, o in enumerate(outs)
+    ]
+    small = pl.BlockSpec(memory_space=pltpu.SMEM)
     return pl.pallas_call(
         body,
-        in_specs=[pl.BlockSpec(memory_space=pltpu.SMEM)] * len(scalars)
-        + [
-            pl.BlockSpec(memory_space=pl.ANY) if i in anywhere else INPLACE if i in direct_in else ONCHIP
-            for i in range(len(arrays))
-        ],
-        out_specs=tuple(INPLACE if i in direct else ONCHIP for i in range(len(outs))),
+        in_specs=[small] * len(scalars)
+        + [INPLACE if i in direct_in else ONCHIP for i in range(len(arrays))],
+        out_specs=tuple(small if i in smem_out else INPLACE if i in direct else ONCHIP for i in range(len(outs))),
         out_shape=tuple(shapes),
         scratch_shapes=list(scratch),
         input_output_aliases=alias or {},
@@ -257,16 +239,15 @@
     )
 
 
-def backward_body(chunk, off, n, early, step, tile, *refs):
+def backward_body(chunk, offs, n, lead, final, early, step, tile, *refs):
     refs = list(refs)
-    lead, final = chunk == 2, chunk == 0
     qt_ref, gt_ref, e_ref, p_ref, row_ref, k_ref = refs[:6]
-    far_out, near_out, e_out, p_out, row_out, _, s_out = refs[6:13]
+    parts, refs = refs[6 : 6 + len(offs)], refs[6 + len(offs) :]
+    e_out, p_out, row_out, _, s_out = refs[:5]
     held, sems = refs[-2:]
     rows = qt_ref.shape[1]
-    half = n // 2
     if final:
-        kept, sem = refs[13], refs[14]
+        kept, sem = refs[5], refs[6]
         save = pltpu.make_async_copy(k_ref, kept, sem.at[0])
         save.start()
     if lead:
@@ -282,69 +263,65 @@
                 row_out[c, here] = fade[c] * total
             row_out[3, here] = rdot * total
     copies = []
-    for start in range(0, n, tile):
-        local = slice((start + half) % n, (start + half) % n + tile)
-        cols = slice(off + local.start, off + local.stop)
-        acc = None
-        for at in range(0, rows, step):
-            here = slice(at, at + step)
-            a = jnp.tile(row_out[chunk, here], (1, tile // 128))
-            r = jnp.tile(row_out[3, here], (1, tile // 128))
-            weights = (e_ref[here, cols].astype(f32) * a).astype(bf16)
-            sg = (weights.astype(f32) * (p_ref[here, cols].astype(f32) - r) * SCALE).astype(bf16)
-            e_out[here, cols] = weights
-            if at < early:
-                p_out[here, cols] = sg
-            else:
-                held[local.start // tile, at - early : at - early + step] = sg
-            key_part = dot(qt_ref[:, here], sg)
-            value_part = dot(gt_ref[:, here], weights)
-            if acc is None:
-                acc = [key_part[:LAT] + value_part, key_part[LAT:]]
-            else:
-                acc = [acc[0] + (key_part[:LAT] + value_part), acc[1] + key_part[LAT:]]
-        spot = local.start // tile
-        copy = pltpu.make_async_copy(held.at[spot], s_out.at[spot], sems.at[spot])
-        copy.start()
-        copies.append(copy)
-        top = acc[0].T.astype(bf16)
-        low = jnp.concatenate([acc[1], jnp.zeros_like(acc[1])], axis=0).T[:, : WIDE - LAT].astype(bf16)
-        ref = far_out if start < half else near_out
-        put = slice(start % half, start % half + tile)
-        ref[put, :LAT] = top
-        ref[put, LAT:] = low
+    for ref, off in zip(parts, offs):
+        for start in range(0, n, tile):
+            cols = slice(off + start, off + start + tile)
+            spot = len(copies)
+            acc = None
+            for at in range(0, rows, step):
+                here = slice(at, at + step)
+                a = jnp.tile(row_out[chunk, here], (1, tile // 128))
+                r = jnp.tile(row_out[3, here], (1, tile // 128))
+                weights = (e_ref[here, cols].astype(f32) * a).astype(bf16)
+                sg = (weights.astype(f32) * (p_ref[here, cols].astype(f32) - r) * SCALE).astype(bf16)
+                e_out[here, cols] = weights
+                if at < early:
+                    p_out[here, cols] = sg
+                else:
+                    held[spot, at - early : at - early + step] = sg
+                key_part = dot(qt_ref[:, here], sg)
+                value_part = dot(gt_ref[:, here], weights)
+                if acc is None:
+                    acc = [key_part[:LAT] + value_part, key_part[LAT:]]
+                else:
+                    acc = [acc[0] + (key_part[:LAT] + value_part), acc[1] + key_part[LAT:]]
+            copies.append(pltpu.make_async_copy(held.at[spot], s_out.at[spot], sems.at[spot]))
+            copies[-1].start()
+            ref[start : start + tile, :LAT] = acc[0].T.astype(bf16)
+            low = jnp.concatenate([acc[1], jnp.zeros_like(acc[1])], axis=0).T[:, : WIDE - LAT]
+            ref[start : start + tile, LAT:] = low.astype(bf16)
     for copy in copies:
         copy.wait()
     if final:
         save.wait()
 
 
-def backward(chunk, off, n, early, qt, gt, e, p, row, k, tile=256, step=256):
+def backward(chunk, offs, n, early, qt, gt, e, p, row, k, lead=False, final=False, tile=256, step=256):
     rows = e.shape[0]
-    lead, final = chunk == 2, chunk == 0
+    count = len(offs)
     like = lambda a: jax.ShapeDtypeStruct(a.shape, a.dtype)
-    part = jax.ShapeDtypeStruct((n // 2, WIDE), bf16)
+    part = jax.ShapeDtypeStruct((n, WIDE), bf16)
     merged = jax.ShapeDtypeStruct((4, rows, 128), f32) if lead else like(row)
-    late = (n // tile, rows - early, tile)
-    outs = [part, part, like(e), like(p), merged, like(k), jax.ShapeDtypeStruct(late, bf16)]
-    alias = {2: 2, 3: 3, 5: 5}
-    scratch = [pltpu.VMEM(late, bf16), pltpu.SemaphoreType.DMA((n // tile,))]
-    direct = (6,)
+    late = (count * n // tile, rows - early, tile)
+    outs = [part] * count + [like(e), like(p), merged, like(k), jax.ShapeDtypeStruct(late, bf16)]
+    alias = {2: count, 3: count + 1, 5: count + 3}
+    scratch = [pltpu.VMEM(late, bf16), pltpu.SemaphoreType.DMA((late[0],))]
+    direct = (count + 4,)
     if not lead:
-        alias[4] = 4
+        alias[4] = count + 2
     if final:
         outs.append(like(k))
-        direct = (6, 7)
+        direct = (count + 4, count + 5)
         scratch = [pltpu.SemaphoreType.DMA((1,)), *scratch]
     return call(
-        functools.partial(backward_body, chunk, off, n, early, step, tile),
+        functools.partial(backward_body, chunk, offs, n, lead, final, early, step, tile),
         outs,
         (),
         (qt, gt, e, p, row, k),
         scratch=scratch,
         alias=alias,
         direct=direct,
-        flops=2 * rows * n * (WIDE + LAT),
+        flops=2 * rows * n * count * (WIDE + LAT),
     )
 
 
@@ -410,9 +387,9 @@
         here = slice(i * block, i * block + block)
         loads.append(
             [
-                pltpu.make_async_copy(ref.at[t, here], s_v.at[off + t, here], sems_s.at[i * s_v.shape[0] + off + t])
-                for ref, off in zip(s_refs, offs)
-                for t in range(ref.shape[0])
+                pltpu.make_async_copy(ref.at[t, here], s_v.at[spot, here], sems_s.at[i * s_v.shape[0] + spot])
+                for ref, spots in zip(s_refs, offs)
+                for t, spot in enumerate(spots)
             ]
         )
         for copy in loads[-1]:
@@ -438,7 +415,7 @@
     dma = lambda n: pltpu.SemaphoreType.DMA((n,))
     steps, tiles = rows // block, k.shape[0] // tile
     return call(
-        functools.partial(query_body, [off // tile for off in offs], early, block),
+        functools.partial(query_body, [[off // tile for off in o] for o in offs], early, block),
         (jax.ShapeDtypeStruct(out.shape, bf16),),
         (),
         (*sgs, k, out),
@@ -473,13 +450,12 @@
     share_of = lambda n: jax.ShapeDtypeStruct((n, WIDE), bf16)
 
     dma = lambda n: pltpu.SemaphoreType.DMA((n,))
-    (outgoing,) = call(
+    outgoing, owned = call(
         pick_body,
-        (slots,),
+        (slots, jax.ShapeDtypeStruct((SLOTS + 1,), jnp.int32)),
         scalars,
         (latents,),
         scratch=[
-            smem(SLOTS + 1),
             pltpu.VMEM(latents.shape, bf16),
             pltpu.VMEM((SLOTS, tokens, WIDE), bf16),
             dma(1),
@@ -487,6 +463,7 @@
         ],
         direct_in=(0,),
         direct=(0,),
+        smem_out=(1,),
     )
     arrived = lax.all_to_all(outgoing.reshape(16, CAP, tokens, WIDE), "req", 0, 0, tiled=True)
 
@@ -513,8 +490,7 @@
         (share_of(keys),),
         scalars,
         (arrived.reshape(slots.shape),),
-        scratch=[smem(MAXL), smem(16), dma(MAXL)],
-        direct_in=(0,),
+        scratch=[smem(MAXL), smem(16)],
     )
 
     after = lambda a, *others: lax.optimization_barrier((a, *others))[0]
@@ -537,20 +513,18 @@
     fold = lambda a: a.reshape(-1, tokens, WIDE)
     unfold = lambda a: a.reshape(-1, WIDE)
     early = 512
-    far2, near2, e, p, row, k, sg2 = backward(2, 6 * keys, 2 * keys, early, qt, gt, e, p, row, k)
+    back = functools.partial(backward, early=early, qt=qt, gt=gt)
+    far2, near2, e, p, row, k, sg2 = back(2, (7 * keys, 6 * keys), keys, e=e, p=p, row=row, k=k, lead=True)
     mate2 = send(far2, sibling)
-    far1, near1, e, p, row, k, sg1 = backward(1, 2 * keys, 4 * keys, early, qt, gt, e, p, row, k)
-    mate1 = unfold(send(fold(far1), sibling))
-    low, high = call(two_body, (share_of(keys // 2),) * 2, (), (after(near2, near1), mate2))
+    far0, near0, e, p, row, k, sg0, k_saved = back(0, (keys, 0), keys, e=e, p=p, row=row, k=k, final=True)
+    low, high = call(two_body, (share_of(keys // 2),) * 2, (), (after(near2, near0), mate2))
     from_left = send(low, right)
     from_right = send(high, left)
-    far0, near0, e, p, row, k, sg0, k_saved = backward(
-        0, 0, 2 * keys, early, qt, gt, e, p, after(row, low), k
-    )
+    far1, e, p, row, k, sg1f = back(1, (4 * keys,), 2 * keys, e=e, p=p, row=after(row, low), k=k)
+    mate1 = unfold(send(fold(far1), sibling))
+    near1, e, p, row, k, sg1n = back(1, (2 * keys,), 2 * keys, e=e, p=p, row=row, k=k)
     mate0 = send(far0, sibling)
-    to_left, to_right = call(
-        one_body, (share_of(keys),) * 2, (), (after(near1, near0), mate1, from_left, from_right)
-    )
+    to_left, to_right = call(one_body, (share_of(keys),) * 2, (), (near1, mate1, from_left, from_right))
     got_left = send(to_right, right)
     got_right = send(to_left, left)
     attended, query_grad = value_side(e, p, after(k, to_left), early)
@@ -564,21 +538,20 @@
         direct=(0,),
     )
     k_saved = after(k_saved, slot_grads)
-    query_grad = query_side((sg2, sg1, sg0), (6 * keys, 2 * keys, 0), early, k_saved, query_grad)
+    query_grad = query_side(
+        (sg2, sg0, sg1f, sg1n),
+        ((7 * keys, 6 * keys), (keys, 0), (4 * keys, 5 * keys), (2 * keys, 3 * keys)),
+        early,
+        k_saved,
+        query_grad,
+    )
     returned = lax.all_to_all(slot_grads.reshape(16, CAP, tokens, WIDE), "req", 0, 0, tiled=True)
     (latent_grad,) = call(
         gather_body,
         (jax.ShapeDtypeStruct((16, tokens, WIDE), f32),),
-        scalars,
+        (owned,),
         (returned.reshape(slots.shape),),
-        scratch=[
-            smem(SLOTS + 1),
-            pltpu.VMEM((SLOTS, tokens, WIDE), bf16),
-            pltpu.VMEM((17, tokens, WIDE), f32),
-            dma(4),
-            dma(4),
-        ],
-        anywhere=(0,),
+        scratch=[pltpu.VMEM((17, tokens, WIDE), f32), dma(4)],
         direct=(0,),
     )
     return (attended, query_grad, latent_grad)

time: 109 us -> 108 us (level)
  waiting for transfers between devices: 27.7 us -> 24.8 us
  local copies, waits for them, and re-layouts: 6.04 us -> 8.15 us
  starting transfers between devices: 22.3 us -> 23.9 us
  Pallas kernels: 49.7 us -> 48.2 us
    unnamed x15 -> x19, local copies, waits for them, and re-layouts: 3.78 us -> 5.9 us
    pallas_call x15 -> x16, Pallas kernels: 49.7 us -> 48.2 us  [call(): pl.pallas_call(body, in_specs=[small] * len(scalars) + [INPLACE if i in d...]
    all_to_all x1, waiting for transfers between devices: 3.76 us -> 2.23 us  [per_device(): lax.all_to_all(outgoing.reshape(16, CAP, tokens, WIDE), 'req', 0, 0, tile...]
    ppermute x14, waiting for transfers between devices: 21.4 us -> 20.1 us  [per_device(): send = lambda a, perm: lax.ppermute(a, 'head', perm)]
    all_to_all x1, starting transfers between devices: 3.61 us -> 4.9 us  [per_device(): lax.all_to_all(slot_grads.reshape(16, CAP, tokens, WIDE), 'req', 0, 0, ti...]
  transfers between devices with their start and end apart: 16 -> 16, of which waited for: 12 -> 11; matrix products, arithmetic and copies ran while one was open for 4% -> 4% of each run, Pallas kernels for 26% -> 29%
where the time goes in v6:
time: 108 us
  Pallas kernels  48.2 us (45%)
  waiting for transfers between devices  24.8 us (23%)
  starting transfers between devices  23.9 us (22%)
  local copies, waits for them, and re-layouts  8.15 us (8%)
  other arithmetic  1.59 us (1%)
  between operations  1.13 us (1%)
    pallas_call x16, Pallas kernels, call(): pl.pallas_call(body, in_specs=[small] * len(scalars) + [INPLACE if i in d...  48.2 us
    ppermute x14, waiting for transfers between devices, per_device(): send = lambda a, perm: lax.ppermute(a, 'head', perm)  20.1 us
    ppermute x14, starting transfers between devices, per_device(): send = lambda a, perm: lax.ppermute(a, 'head', perm)  10.7 us
    all_to_all x1, starting transfers between devices, per_device(): lax.all_to_all(outgoing.reshape(16, CAP, tokens, WIDE), 'req', 0, 0, tile...  8.34 us
    unnamed x19, local copies, waits for them, and re-layouts  5.9 us
    all_to_all x1, starting transfers between devices, per_device(): lax.all_to_all(slot_grads.reshape(16, CAP, tokens, WIDE), 'req', 0, 0, ti...  4.9 us
    all_to_all x1, waiting for transfers between devices, per_device(): lax.all_to_all(slot_grads.reshape(16, CAP, tokens, WIDE), 'req', 0, 0, ti...  2.53 us
    all_to_all x1, waiting for transfers between devices, per_device(): lax.all_to_all(outgoing.reshape(16, CAP, tokens, WIDE), 'req', 0, 0, tile...  2.23 us
  transfers between devices with their start and end apart: 16, of which 11 were waited for; matrix products, arithmetic and copies ran while one was open for 4% of the time, Pallas kernels for 29%

profile of v6, /device:TPU:0, one launch (start us, length us, event | category | flops | bytes accessed | tf_op | source)
XLA Modules:
  0.0 107.8 jit_solution(5216740416744456039)
XLA Ops:
  0.6 3.3 %shard_map.85 = (bf16[32,16,576]{2,1,0:T(8,128)(2,1)}, s32[33]{0:T(128)S(1)}) custom-call(s32[16,16]{1,0:T(8,128)} %lists.5, s32[16]{0:T(128)} %counts.5, s32[1]{0:T(128)} %bitcast.me, bf16[16,16,576]{2,1,0:T(8,128)(2,1)} %lat_ref.1), custom_call_target="tpu_custom_call" | custom-call | tf_op jit(solution)/shard_map/pallas_call | solution.py:166
  3.9 0.6 copy-done.6
  4.5 8.3 %all-to-all-start = ((bf16[16,2,16,576]{3,2,1,0:T(8,128)(2,1)}), bf16[16,2,16,576]{3,2,1,0:T(8,128)(2,1)}, u32[]{:S(2)}, u32[]{:S(2)}) async-start(bf16[16,2,16,576]{3,2,1,0:T(8,128)(2,1)} %bitcast.37), calls=%async_computation | async-start | bytes 1310720 | tf_op jit(solution)/shard_map/all_to_all | solution.py:468
  12.9 1.2 %dynamic_slice.8 = s32[1]{0:T(128)} dynamic-slice(s32[16]{0:T(128)} %counts.5, s32[]{:T(128)S(6)} %select_n.59), dynamic_slice_sizes={1} | dynamic-slice | bytes 12 | tf_op jit(solution)/shard_map/jit(dynamic_index_in_dim)/dynamic_slice | solution.py:471
  14.2 0.7 dynamic-slice_bitcast_fusion
  14.9 0.1 stack.35
  14.9 0.9 select_reduce_fusion
  15.8 0.7 compare_select_fusion
  16.5 0.1 broadcast_in_dim.34
  16.5 0.1 lt.60
  16.6 0.1 add.95
  16.7 0.1 fusion
  16.8 0.0 copy-start
  16.8 1.5 %copy-done = bf16[96,16,576]{2,1,0:T(8,128)(2,1)S(1)} copy-done((bf16[96,16,576]{2,1,0:T(8,128)(2,1)S(1)}, bf16[96,16,576]{2,1,0:T(8,128)(2,1)}, u32[]{:S(2)}) %copy-start) | copy-done | bytes 1769496
  18.4 1.4 %copy-done.2 = bf16[96,16,512]{2,1,0:T(8,128)(2,1)S(1)} copy-done((bf16[96,16,512]{2,1,0:T(8,128)(2,1)S(1)}, bf16[96,16,512]{2,1,0:T(8,128)(2,1)}, u32[]{:S(2)}) %copy-start.2) | copy-done | bytes 1572888
  19.8 1.4 %shard_map.86 = (bf16[576,1536]{1,0:T(8,128)(2,1)S(1)}, bf16[512,1536]{1,0:T(8,128)(2,1)S(1)}) custom-call(bf16[96,16,576]{2,1,0:T(8,128)(2,1)S(1)} %copy-done, bf16[96,16,512]{2,1,0:T(8,128)(2,1)S(1)} %copy-done.2), custom_call_target="tpu_custom_call" | custom-call | tf_op jit(solution)/shard_map/pallas_call | solution.py:166
  21.2 0.0 copy-start.4
  21.2 1.2 %copy-done.4 = bf16[576,1536]{1,0:T(8,128)(2,1)} copy-done((bf16[576,1536]{1,0:T(8,128)(2,1)}, bf16[576,1536]{1,0:T(8,128)(2,1)S(1)}, u32[]{:S(2)}) %copy-start.4) | copy-done | bytes 1769496
  22.4 1.1 %copy-done.5 = bf16[512,1536]{1,0:T(8,128)(2,1)} copy-done((bf16[512,1536]{1,0:T(8,128)(2,1)}, bf16[512,1536]{1,0:T(8,128)(2,1)S(1)}, u32[]{:S(2)}) %copy-start.5) | copy-done | bytes 1572888
  23.6 2.2 %all-to-all-done = bf16[16,2,16,576]{3,2,1,0:T(8,128)(2,1)} async-done(((bf16[16,2,16,576]{3,2,1,0:T(8,128)(2,1)}), bf16[16,2,16,576]{3,2,1,0:T(8,128)(2,1)}, u32[]{:S(2)}, u32[]{:S(2)}) %all-to-all-start) | async-done | bytes 589856 | tf_op jit(solution)/shard_map/all_to_all | solution.py:468
  25.8 1.4 %shard_map.87.refs_0_ = bf16[256,576]{1,0:T(8,128)(2,1)S(1)} custom-call(s32[16,16]{1,0:T(8,128)} %lists.5, s32[16]{0:T(128)} %counts.5, s32[1]{0:T(128)} %bitcast.me, bf16[32,16,576]{2,1,0:T(8,128)(2,1)} %bitcast.12.arrived_ref), custom_call_target="tpu_custom_call" | custom-call | tf_op jit(solution)/shard_map/pallas_call | solution.py:166
  27.2 0.1 collective-permute-start.1
  27.3 2.8 %collective-permute-start.3 = (bf16[256,576]{1,0:T(8,128)(2,1)S(1)}, bf16[256,576]{1,0:T(8,128)(2,1)S(1)}, u32[]{:S(2)}, u32[]{:S(2)}) collective-permute-start(bf16[256,576]{1,0:T(8,128)(2,1)S(1)} %shard_map.87.refs_0_), channel_id=1, source_target_pairs={{0,6},{1,7},{2,0},{3,1},{4,2},{5,3},{6,4},{7,5},{8,14},{9,15},{10,... | collective-permute-start | bytes 884744 | tf_op jit(solution)/shard_map/ppermute | solution.py:444
  30.1 0.0 collective-permute-start
  30.1 0.0 collective-permute-done.1.refs_1_
  30.1 2.8 %shard_map.88 = (bf16[1536,2048]{1,0:T(8,128)(2,1)S(1)}, bf16[1536,2048]{1,0:T(8,128)(2,1)S(1)}, bf16[2048,576]{1,0:T(8,128)(2,1)S(1)}, f32[9,1536,128]{2,1,0:T(8,128)S(1)}) custom-call(bf16[256,576]{1,0:T(8,128)(2,1)S(1)} %shard_map.87.refs_0_, bf16[256,576]{1,0:T(8,128)(2,1)S(1)} %collective-permute-done.1.refs_1_, f32[1,512]{1,0:T(1,128)S(1)} %bitcast.34, ...), custom_call_target="tpu_custom_call" | custom-call | flops 1711276032 | tf_op jit(solution)/shard_map/pallas_call | solution.py:166
  32.9 4.8 %collective-permute-done.3.refs_1_ = bf16[256,576]{1,0:T(8,128)(2,1)S(1)} collective-permute-done((bf16[256,576]{1,0:T(8,128)(2,1)S(1)}, bf16[256,576]{1,0:T(8,128)(2,1)S(1)}, u32[]{:S(2)}, u32[]{:S(2)}) %collective-permute-start.3) | collective-permute-done | bytes 294944 | tf_op jit(solution)/shard_map/ppermute | solution.py:444
  37.7 3.4 %collective-permute-done.refs_0_ = bf16[256,576]{1,0:T(8,128)(2,1)S(1)} collective-permute-done((bf16[256,576]{1,0:T(8,128)(2,1)S(1)}, bf16[256,576]{1,0:T(8,128)(2,1)S(1)}, u32[]{:S(2)}, u32[]{:S(2)}) %collective-permute-start) | collective-permute-done | bytes 294944 | tf_op jit(solution)/shard_map/ppermute | solution.py:444
  41.1 0.0 collective-permute-start.4
  41.1 0.5 collective-permute-start.5
  41.6 0.0 collective-permute-start.2
  41.6 1.1 %collective-permute-done.4.refs_2_ = bf16[256,576]{1,0:T(8,128)(2,1)S(1)} collective-permute-done((bf16[256,576]{1,0:T(8,128)(2,1)S(1)}, bf16[256,576]{1,0:T(8,128)(2,1)S(1)}, u32[]{:S(2)}, u32[]{:S(2)}) %collective-permute-start.4) | collective-permute-done | bytes 294944 | tf_op jit(solution)/shard_map/ppermute | solution.py:444
  42.7 0.5 collective-permute-done.5.refs_3_
  43.2 5.5 %shard_map.89 = (bf16[1536,2048]{1,0:T(8,128)(2,1)S(1)}, bf16[1536,2048]{1,0:T(8,128)(2,1)S(1)}, bf16[2048,576]{1,0:T(8,128)(2,1)S(1)}, f32[9,1536,128]{2,1,0:T(8,128)S(1)}) custom-call(bf16[256,576]{1,0:T(8,128)(2,1)S(1)} %collective-permute-done.refs_0_, ...), custom_call_target="tpu_custom_call", output_to_operand_aliasing={{0}: (7, {}), {1}: (8, {}), {2}: (9, {}), {3}: (10, {})} | custom-call | flops 3422552064 | tf_op jit(solution)/shard_map/pallas_call | solution.py:166
  48.7 3.7 %collective-permute-done.2.refs_0_ = bf16[256,576]{1,0:T(8,128)(2,1)S(1)} collective-permute-done((bf16[256,576]{1,0:T(8,128)(2,1)S(1)}, bf16[256,576]{1,0:T(8,128)(2,1)S(1)}, u32[]{:S(2)}, u32[]{:S(2)}) %collective-permute-start.2) | collective-permute-done | bytes 294944 | tf_op jit(solution)/shard_map/ppermute | solution.py:444
  52.4 0.0 collective-permute-start.6
  52.4 1.6 %collective-permute-done.6.refs_1_ = bf16[256,576]{1,0:T(8,128)(2,1)S(1)} collective-permute-done((bf16[256,576]{1,0:T(8,128)(2,1)S(1)}, bf16[256,576]{1,0:T(8,128)(2,1)S(1)}, u32[]{:S(2)}, u32[]{:S(2)}) %collective-permute-start.6) | collective-permute-done | bytes 294944 | tf_op jit(solution)/shard_map/ppermute | solution.py:444
  54.0 2.8 %shard_map.90 = (bf16[1536,2048]{1,0:T(8,128)(2,1)S(1)}, bf16[1536,2048]{1,0:T(8,128)(2,1)S(1)}, bf16[2048,576]{1,0:T(8,128)(2,1)S(1)}, f32[9,1536,128]{2,1,0:T(...) custom-call(bf16[256,576]{1,0:T(8,128)(2,1)S(1)} %collective-permute, ...), custom_call_target="tpu_custom_call", output_to_operand_aliasing={{0}: (5, {}), {1}: (6, {}), {2}: (7, {}), {3}: (8, {})} | custom-call | flops 1711276032 | tf_op jit(solution)/shard_map/pallas_call | solution.py:166
  56.8 3.6 %shard_map.91 = (bf16[256,576]{1,0:T(8,128)(2,1)S(1)}, bf16[256,576]{1,0:T(8,128)(2,1)S(1)}, bf16[1536,2048]{1,0:T(8,128)(2,1)S(1)}, bf16[1536,2048]{1,0:T(8,128...) custom-call(bf16[576,1536]{1,0:T(8,128)(2,1)S(1)} %get-tuple-element, ...), custom_call_target="tpu_custom_call", output_to_operand_aliasing={{2}: (2, {}), {3}: (3, {}), {5}: (5, {})} | custom-call | flops 1711276032 | tf_op jit(solution)/shard_map/pallas_call | solution.py:166
  60.4 0.4 collective-permute-start.7
  60.8 3.0 %shard_map.92 = (bf16[256,576]{1,0:T(8,128)(2,1)S(1)}, bf16[256,576]{1,0:T(8,128)(2,1)S(1)}, bf16[1536,2048]{1,0:T(8,128)(2,1)S(1)}, bf16[1536,2048]{1,0:T(8,128...) custom-call(bf16[576,1536]{1,0:T(8,128)(2,1)S(1)} %get-tuple-element, ...), custom_call_target="tpu_custom_call", output_to_operand_aliasing={{2}: (2, {}), {3}: (3, {}), {5}: (5, {}), {4}: (4, {})} | custom-call | flops 1711276032 | tf_op jit(solution)/shard_map/pallas_call | solution.py:166
  63.8 0.0 collective-permute-done.7.far_ref
  63.8 0.1 shard_map.93
  63.9 2.9 %shard_map.94 = (bf16[512,576]{1,0:T(8,128)(2,1)S(1)}, bf16[1536,2048]{1,0:T(8,128)(2,1)S(1)}, bf16[1536,2048]{1,0:T(8,128)(2,1)S(1)}, f32[4,1536,128]{2,1,0:T(8...) custom-call(bf16[576,1536]{1,0:T(8,128)(2,1)S(1)} %get-tuple-element, ...), custom_call_target="tpu_custom_call", output_to_operand_aliasing={{1}: (2, {}), {2}: (3, {}), {4}: (5, {}), {3}: (4, {})} | custom-call | flops 1711276032 | tf_op jit(solution)/shard_map/pallas_call | solution.py:166
  66.8 0.5 collective-permute-start.8
  67.3 0.1 collective-permute-start.11
  67.4 0.0 collective-permute-start.9
  67.4 3.2 %collective-permute-start.10 = (bf16[128,576]{1,0:T(8,128)(2,1)S(1)}, bf16[128,576]{1,0:T(8,128)(2,1)S(1)}, u32[]{:S(2)}, u32[]{:S(2)}) collective-permute-start(bf16[128,576]{1,0:T(8,128)(2,1)S(1)} %get-tuple-element.116), channel_id=1, source_target_pairs={{0,6},{1,7},{2,0},{3,1},{4,2},{5,3},{6,4},{7,5},{8,14},{9,15},{10,... | collective-permute-start | bytes 442376 | tf_op jit(solution)/shard_map/ppermute | solution.py:444
  70.6 2.9 %shard_map.95 = (bf16[512,576]{1,0:T(8,128)(2,1)S(1)}, bf16[1536,2048]{1,0:T(8,128)(2,1)S(1)}, bf16[1536,2048]{1,0:T(8,128)(2,1)S(1)}, f32[4,1536,128]{2,1,0:T(8...) custom-call(bf16[576,1536]{1,0:T(8,128)(2,1)S(1)} %get-tuple-element, ...), custom_call_target="tpu_custom_call", output_to_operand_aliasing={{1}: (2, {}), {2}: (3, {}), {4}: (5, {}), {3}: (4, {})} | custom-call | flops 1711276032 | tf_op jit(solution)/shard_map/pallas_call | solution.py:166
  73.6 0.8 collective-permute-done.10.high_ref
  74.4 0.7 collective-permute-done.9.low_ref
  75.1 0.0 collective-permute-done.8
  75.1 0.2 shard_map.96
  75.3 3.0 %collective-permute-start.13 = (bf16[256,576]{1,0:T(8,128)(2,1)S(1)}, bf16[256,576]{1,0:T(8,128)(2,1)S(1)}, u32[]{:S(2)}, u32[]{:S(2)}) collective-permute-start(bf16[256,576]{1,0:T(8,128)(2,1)S(1)} %get-tuple-element.117), channel_id=1, source_target_pairs={{0,6},{1,7},{2,0},{3,1},{4,2},{5,3},{6,4},{7,5},{8,14},{9,15},{10,... | collective-permute-start | bytes 884744 | tf_op jit(solution)/shard_map/ppermute | solution.py:444
  78.3 0.0 collective-permute-start.12
  78.3 6.4 %shard_map.97 = (bf16[96,16,512]{2,1,0:T(8,128)(2,1)}, bf16[96,16,576]{2,1,0:T(8,128)(2,1)}) custom-call(bf16[1536,2048]{1,0:T(8,128)(2,1)S(1)} %get-tuple-element.111.w_ref, bf16[1536,2048]{1,0:T(8,128)(2,1)S(1)} %get-tuple-element.112.s_ref, bf16[2048,576]{1,0:T(8,128)(2,1)S(1)} %get-tuple-element.118.k_ref), custom_call_target="tpu_custom_call" | custom-call | flops 4429185024 | tf_op jit(solution)/shard_map/pallas_call | solution.py:166
  84.7 0.0 collective-permute-done.11.b_ref
  84.7 3.4 %collective-permute-done.12.c_ref = bf16[256,576]{1,0:T(8,128)(2,1)S(1)} collective-permute-done((bf16[256,576]{1,0:T(8,128)(2,1)S(1)}, bf16[256,576]{1,0:T(8,128)(2,1)S(1)}, u32[]{:S(2)}, u32[]{:S(2)}) %collective-permute-start.12) | collective-permute-done | bytes 294944 | tf_op jit(solution)/shard_map/ppermute | solution.py:444
  88.1 0.0 collective-permute-done.13.d_ref
  88.1 1.7 %shard_map.98 = bf16[32,16,576]{2,1,0:T(8,128)(2,1)} custom-call(s32[16,16]{1,0:T(8,128)} %lists.5, s32[16]{0:T(128)} %counts.5, s32[1]{0:T(128)} %bitcast.me, bf16[256,576]{1,0:T(8,128)(2,1)S(1)} %get-tuple-element.125.a_ref, bf16[256,576]{1,0:T(8,128)(2,1)S(1)} %collective-permute-done.11.b_ref, bf16[256,576]{1,0:T(8,128)(2,1)S(1)} %collective-permute-done.12.c_ref, ...), custom_call_target="tpu_custom_call" | custom-call | tf_op jit(solution)/shard_map/pallas_call | solution.py:166
  89.8 4.9 %all-to-all-start.1 = ((bf16[16,2,16,576]{3,2,1,0:T(8,128)(2,1)}), bf16[16,2,16,576]{3,2,1,0:T(8,128)(2,1)S(1)}, u32[]{:S(2)}, u32[]{:S(2)}) async-start(bf16[16,2,16,576]{3,2,1,0:T(8,128)(2,1)} %bitcast.36), calls=%async_computation.1 | async-start | bytes 1310720 | tf_op jit(solution)/shard_map/all_to_all | solution.py:548
  94.7 8.6 %shard_map.99 = bf16[96,16,576]{2,1,0:T(8,128)(2,1)} custom-call(bf16[2,1024,256]{2,1,0:T(8,128)(2,1)} %get-tuple-element.120.refs_0_, bf16[2,1024,256]{2,1,0:T(8,128)(2,1)} %get-tuple-element.121.refs_1_, bf16[2,1024,256]{2,1,0:T(8,128)(2,1)} %get-tuple-element.122.refs_2_, ...), custom_call_target="tpu_custom_call", output_to_operand_aliasing={{}: (5, {})} | custom-call | flops 2415919104 | tf_op jit(solution)/shard_map/pallas_call | solution.py:166
  103.3 2.5 %all-to-all-done.1 = bf16[16,2,16,576]{3,2,1,0:T(8,128)(2,1)S(1)} async-done(((bf16[16,2,16,576]{3,2,1,0:T(8,128)(2,1)}), bf16[16,2,16,576]{3,2,1,0:T(8,128)(2,1)S(1)}, u32[]{:S(2)}, u32[]{:S(2)}) %all-to-all-start.1) | async-done | bytes 589856 | tf_op jit(solution)/shard_map/all_to_all | solution.py:548
  105.8 1.8 %shard_map.100 = f32[16,16,576]{2,1,0:T(8,128)} custom-call(s32[33]{0:T(128)} %copy-done.6, bf16[32,16,576]{2,1,0:T(8,128)(2,1)S(1)} %bitcast.30), custom_call_target="tpu_custom_call" | custom-call | tf_op jit(solution)/shard_map/pallas_call | solution.py:166
  (14 shorter events, 0.0 us)
Async XLA Ops:
  3.9 0.6 copy-start.6
  4.5 25.6 %copy-start.3 = (bf16[96,16,512]{2,1,0:T(8,128)(2,1)S(1)}, bf16[96,16,512]{2,1,0:T(8,128)(2,1)}, u32[]{:S(2)}) copy-start(bf16[96,16,512]{2,1,0:T(8,128)(2,1)} %refs_4_.3) | copy-start | bytes 4718596
  4.5 21.3 %all-to-all-start = ((bf16[16,2,16,576]{3,2,1,0:T(8,128)(2,1)}), bf16[16,2,16,576]{3,2,1,0:T(8,128)(2,1)}, u32[]{:S(2)}, u32[]{:S(2)}) async-start(bf16[16,2,16,576]{3,2,1,0:T(8,128)(2,1)} %bitcast.37), calls=%async_computation | async-start | bytes 1310720 | tf_op jit(solution)/shard_map/all_to_all | solution.py:468
  16.8 1.5 %copy-start = (bf16[96,16,576]{2,1,0:T(8,128)(2,1)S(1)}, bf16[96,16,576]{2,1,0:T(8,128)(2,1)}, u32[]{:S(2)}) copy-start(bf16[96,16,576]{2,1,0:T(8,128)(2,1)} %refs_3_.3) | copy-start | bytes 5308420
  18.4 1.4 %copy-start.2 = (bf16[96,16,512]{2,1,0:T(8,128)(2,1)S(1)}, bf16[96,16,512]{2,1,0:T(8,128)(2,1)}, u32[]{:S(2)}) copy-start(bf16[96,16,512]{2,1,0:T(8,128)(2,1)} %refs_4_.3) | copy-start | bytes 4718596
  19.8 10.3 %copy-start.1 = (bf16[96,16,576]{2,1,0:T(8,128)(2,1)S(1)}, bf16[96,16,576]{2,1,0:T(8,128)(2,1)}, u32[]{:S(2)}) copy-start(bf16[96,16,576]{2,1,0:T(8,128)(2,1)} %refs_3_.3) | copy-start | bytes 5308420
  21.2 1.2 %copy-start.4 = (bf16[576,1536]{1,0:T(8,128)(2,1)}, bf16[576,1536]{1,0:T(8,128)(2,1)S(1)}, u32[]{:S(2)}) copy-start(bf16[576,1536]{1,0:T(8,128)(2,1)S(1)} %get-tuple-element.85.refs_9_) | copy-start | bytes 5308420
  22.4 1.1 %copy-start.5 = (bf16[512,1536]{1,0:T(8,128)(2,1)}, bf16[512,1536]{1,0:T(8,128)(2,1)S(1)}, u32[]{:S(2)}) copy-start(bf16[512,1536]{1,0:T(8,128)(2,1)S(1)} %get-tuple-element.86.refs_10_) | copy-start | bytes 4718596
  27.2 2.9 %collective-permute-start.1 = (bf16[256,576]{1,0:T(8,128)(2,1)S(1)}, bf16[256,576]{1,0:T(8,128)(2,1)S(1)}, u32[]{:S(2)}, u32[]{:S(2)}) collective-permute-start(bf16[256,576]{1,0:T(8,128)(2,1)S(1)} %shard_map.87.refs_0_), channel_id=1, source_target_pairs={{0,1},{1,0},{2,3},{3,2},{4,5},{5,4},{6,7},{7,6},{8,9},{9,8},{10,11... | collective-permute-start | bytes 884744 | tf_op jit(solution)/shard_map/ppermute | solution.py:444
  27.3 10.4 %collective-permute-start.3 = (bf16[256,576]{1,0:T(8,128)(2,1)S(1)}, bf16[256,576]{1,0:T(8,128)(2,1)S(1)}, u32[]{:S(2)}, u32[]{:S(2)}) collective-permute-start(bf16[256,576]{1,0:T(8,128)(2,1)S(1)} %shard_map.87.refs_0_), channel_id=1, source_target_pairs={{0,6},{1,7},{2,0},{3,1},{4,2},{5,3},{6,4},{7,5},{8,14},{9,15},{10,... | collective-permute-start | bytes 884744 | tf_op jit(solution)/shard_map/ppermute | solution.py:444
  30.1 11.0 %collective-permute-start = (bf16[256,576]{1,0:T(8,128)(2,1)S(1)}, bf16[256,576]{1,0:T(8,128)(2,1)S(1)}, u32[]{:S(2)}, u32[]{:S(2)}) collective-permute-start(bf16[256,576]{1,0:T(8,128)(2,1)S(1)} %shard_map.87.refs_0_), channel_id=1, source_target_pairs={{0,2},{1,3},{2,4},{3,5},{4,6},{5,7},{6,0},{7,1},{8,10},{9,11},{10,... | collective-permute-start | bytes 884744 | tf_op jit(solution)/shard_map/ppermute | solution.py:444
  41.1 1.6 %collective-permute-start.4 = (bf16[256,576]{1,0:T(8,128)(2,1)S(1)}, bf16[256,576]{1,0:T(8,128)(2,1)S(1)}, u32[]{:S(2)}, u32[]{:S(2)}) collective-permute-start(bf16[256,576]{1,0:T(8,128)(2,1)S(1)} %collective-permute-done.refs_0_), channel_id=1, source_target_pairs={{0,1},{1,0},{2,3},{3,2},{4,5},{5,4},{6,7},{7,6},{8,9},{9,8},{10,11... | collective-permute-start | bytes 884744 | tf_op jit(solution)/shard_map/ppermute | solution.py:444
  41.1 2.1 %collective-permute-start.5 = (bf16[256,576]{1,0:T(8,128)(2,1)S(1)}, bf16[256,576]{1,0:T(8,128)(2,1)S(1)}, u32[]{:S(2)}, u32[]{:S(2)}) collective-permute-start(bf16[256,576]{1,0:T(8,128)(2,1)S(1)} %collective-permute-done.3.refs_1_), channel_id=1, source_target_pairs={{0,1},{1,0},{2,3},{3,2},{4,5},{5,4},{6,7},{7,6},{8,9},{9,8},{10,11... | collective-permute-start | bytes 884744 | tf_op jit(solution)/shard_map/ppermute | solution.py:444
  41.6 10.8 %collective-permute-start.2 = (bf16[256,576]{1,0:T(8,128)(2,1)S(1)}, bf16[256,576]{1,0:T(8,128)(2,1)S(1)}, u32[]{:S(2)}, u32[]{:S(2)}) collective-permute-start(bf16[256,576]{1,0:T(8,128)(2,1)S(1)} %collective-permute-done.refs_0_), channel_id=1, source_target_pairs={{0,2},{1,3},{2,4},{3,5},{4,6},{5,7},{6,0},{7,1},{8,10},{9,11},{10,... | collective-permute-start | bytes 884744 | tf_op jit(solution)/shard_map/ppermute | solution.py:444
  52.4 1.6 %collective-permute-start.6 = (bf16[256,576]{1,0:T(8,128)(2,1)S(1)}, bf16[256,576]{1,0:T(8,128)(2,1)S(1)}, u32[]{:S(2)}, u32[]{:S(2)}) collective-permute-start(bf16[256,576]{1,0:T(8,128)(2,1)S(1)} %collective-permute-done.2.refs_0_), channel_id=1, source_target_pairs={{0,1},{1,0},{2,3},{3,2},{4,5},{5,4},{6,7},{7,6},{8,9},{9,8},{10,11... | collective-permute-start | bytes 884744 | tf_op jit(solution)/shard_map/ppermute | solution.py:444
  60.4 3.4 %collective-permute-start.7 = (bf16[256,576]{1,0:T(8,128)(2,1)S(1)}, bf16[256,576]{1,0:T(8,128)(2,1)S(1)}, u32[]{:S(2)}, u32[]{:S(2)}) collective-permute-start(bf16[256,576]{1,0:T(8,128)(2,1)S(1)} %get-tuple-element.103), channel_id=1, source_target_pairs={{0,1},{1,0},{2,3},{3,2},{4,5},{5,4},{6,7},{7,6},{8,9},{9,8},{10,11... | collective-permute-start | bytes 884744 | tf_op jit(solution)/shard_map/ppermute | solution.py:444
  66.8 8.3 %collective-permute-start.8 = (bf16[32,16,576]{2,1,0:T(8,128)(2,1)S(1)}, bf16[32,16,576]{2,1,0:T(8,128)(2,1)S(1)}, u32[]{:S(2)}, u32[]{:S(2)}) collective-permute-start(bf16[32,16,576]{2,1,0:T(8,128)(2,1)S(1)} %bitcast.35), channel_id=1, source_target_pairs={{0,1},{1,0},{2,3},{3,2},{4,5},{5,4},{6,7},{7,6},{8,9},{9,8},{10,11... | collective-permute-start | bytes 1769480 | tf_op jit(solution)/shard_map/ppermute | solution.py:444
  67.3 17.4 %collective-permute-start.11 = (bf16[256,576]{1,0:T(8,128)(2,1)S(1)}, bf16[256,576]{1,0:T(8,128)(2,1)S(1)}, u32[]{:S(2)}, u32[]{:S(2)}) collective-permute-start(bf16[256,576]{1,0:T(8,128)(2,1)S(1)} %get-tuple-element.126), channel_id=1, source_target_pairs={{0,1},{1,0},{2,3},{3,2},{4,5},{5,4},{6,7},{7,6},{8,9},{9,8},{10,11... | collective-permute-start | bytes 884744 | tf_op jit(solution)/shard_map/ppermute | solution.py:444
  67.4 7.7 %collective-permute-start.9 = (bf16[128,576]{1,0:T(8,128)(2,1)S(1)}, bf16[128,576]{1,0:T(8,128)(2,1)S(1)}, u32[]{:S(2)}, u32[]{:S(2)}) collective-permute-start(bf16[128,576]{1,0:T(8,128)(2,1)S(1)} %get-tuple-element.104), channel_id=1, source_target_pairs={{0,2},{1,3},{2,4},{3,5},{4,6},{5,7},{6,0},{7,1},{8,10},{9,11},{10,... | collective-permute-start | bytes 442376 | tf_op jit(solution)/shard_map/ppermute | solution.py:444
  67.4 7.0 %collective-permute-start.10 = (bf16[128,576]{1,0:T(8,128)(2,1)S(1)}, bf16[128,576]{1,0:T(8,128)(2,1)S(1)}, u32[]{:S(2)}, u32[]{:S(2)}) collective-permute-start(bf16[128,576]{1,0:T(8,128)(2,1)S(1)} %get-tuple-element.116), channel_id=1, source_target_pairs={{0,6},{1,7},{2,0},{3,1},{4,2},{5,3},{6,4},{7,5},{8,14},{9,15},{10,... | collective-permute-start | bytes 442376 | tf_op jit(solution)/shard_map/ppermute | solution.py:444
  75.3 12.8 %collective-permute-start.13 = (bf16[256,576]{1,0:T(8,128)(2,1)S(1)}, bf16[256,576]{1,0:T(8,128)(2,1)S(1)}, u32[]{:S(2)}, u32[]{:S(2)}) collective-permute-start(bf16[256,576]{1,0:T(8,128)(2,1)S(1)} %get-tuple-element.117), channel_id=1, source_target_pairs={{0,6},{1,7},{2,0},{3,1},{4,2},{5,3},{6,4},{7,5},{8,14},{9,15},{10,... | collective-permute-start | bytes 884744 | tf_op jit(solution)/shard_map/ppermute | solution.py:444
  78.3 9.8 %collective-permute-start.12 = (bf16[256,576]{1,0:T(8,128)(2,1)S(1)}, bf16[256,576]{1,0:T(8,128)(2,1)S(1)}, u32[]{:S(2)}, u32[]{:S(2)}) collective-permute-start(bf16[256,576]{1,0:T(8,128)(2,1)S(1)} %get-tuple-element.127), channel_id=1, source_target_pairs={{0,2},{1,3},{2,4},{3,5},{4,6},{5,7},{6,0},{7,1},{8,10},{9,11},{10,... | collective-permute-start | bytes 884744 | tf_op jit(solution)/shard_map/ppermute | solution.py:444
  89.8 16.1 %all-to-all-start.1 = ((bf16[16,2,16,576]{3,2,1,0:T(8,128)(2,1)}), bf16[16,2,16,576]{3,2,1,0:T(8,128)(2,1)S(1)}, u32[]{:S(2)}, u32[]{:S(2)}) async-start(bf16[16,2,16,576]{3,2,1,0:T(8,128)(2,1)} %bitcast.36), calls=%async_computation.1 | async-start | bytes 1310720 | tf_op jit(solution)/shard_map/all_to_all | solution.py:548

commit v7 on v6

--- a/solution.py
+++ b/solution.py
@@ -131,21 +131,15 @@
         gt_ref[:, here] = g_ref[part].reshape(256, LAT).T
 
 
-def two_body(near_ref, far_ref, low_ref, high_ref):
-    half = low_ref.shape[0]
+def two_body(near_ref, far_ref, out_ref):
+    out_ref[...] = (near_ref[...].astype(f32) + far_ref[...].astype(f32)).astype(bf16)
+
+
+def one_body(near_ref, far_ref, two_ref, a_ref, b_ref):
+    size = a_ref.shape[0]
     total = near_ref[...].astype(f32) + far_ref[...].astype(f32)
-    low_ref[...] = total[:half].astype(bf16)
-    high_ref[...] = total[half:].astype(bf16)
-
-
-def one_body(near_ref, far_ref, low_ref, high_ref, left_ref, right_ref):
-    size = left_ref.shape[0]
-    half = size // 2
-    total = near_ref[...].astype(f32) + far_ref[...].astype(f32)
-    left_ref[:half] = total[:half].astype(bf16)
-    left_ref[half:] = (total[half:size] + high_ref[...].astype(f32)).astype(bf16)
-    right_ref[:half] = (total[size : size + half] + low_ref[...].astype(f32)).astype(bf16)
-    right_ref[half:] = total[size + half :].astype(bf16)
+    a_ref[...] = total[:size].astype(bf16)
+    b_ref[...] = (total[size:] + two_ref[...].astype(f32)).astype(bf16)
 
 
 ONCHIP = pl.BlockSpec(memory_space=pltpu.VMEM)
@@ -159,8 +153,7 @@
     ]
     scalars = [pltpu.with_memory_space_constraint(a, pltpu.HBM) for a in scalars]
     shapes = [
-        o if i in smem_out else (pltpu.HBM if i in direct else pltpu.VMEM)(o.shape, o.dtype)
-        for i, o in enumerate(outs)
+        (pltpu.HBM if i in direct or i in smem_out else pltpu.VMEM)(o.shape, o.dtype) for i, o in enumerate(outs)
     ]
     small = pl.BlockSpec(memory_space=pltpu.SMEM)
     return pl.pallas_call(
@@ -176,24 +169,10 @@
     )(*scalars, *args)
 
 
-def forward_body(nkeys, chunk, off, n, block, *refs):
-    refs = list(refs)
-    last = chunk == 2
-    key_refs = [refs.pop(0) for _ in range(nkeys)]
+def forward_body(nkeys, chunk, kept, off, n, block, *refs):
+    key_refs, refs = refs[:nkeys], refs[nkeys:]
     bias, q_ref, g_ref = refs[:3]
-    refs = refs[3 + (4 if chunk else 0) :]
-    turned = []
-    if last:
-        (qt_in, gt_in), refs = refs[:2], refs[2:]
-    (e_out, p_out, k_out, st_out), refs = refs[:4], refs[4:]
-    if last:
-        qt_out, gt_out, sems = refs
-        turned = [
-            pltpu.make_async_copy(qt_in, qt_out, sems.at[0]),
-            pltpu.make_async_copy(gt_in, gt_out, sems.at[1]),
-        ]
-    for copy in turned:
-        copy.start()
+    e_out, p_out, k_out, st_out = refs[3 + kept : 7 + kept]
     at = off
     for ref in key_refs:
         k_out[at : at + ref.shape[0]] = ref[...]
@@ -216,24 +195,20 @@
         return carry
 
     lax.fori_loop(0, q_ref.shape[0] * 16 // block, rows, 0)
-    for copy in turned:
-        copy.wait()
-
-
-def forward(chunk, off, n, total_keys, key_parts, bias, q, g, state=(), turned=(), block=768):
+
+
+def forward(chunk, off, n, total_keys, key_parts, bias, q, g, state=(), block=768):
     rows = q.shape[0] * 16
     side = jax.ShapeDtypeStruct((rows, total_keys), bf16)
     outs = [side, side, jax.ShapeDtypeStruct((total_keys, WIDE), bf16), jax.ShapeDtypeStruct((9, rows, 128), f32)]
-    outs += [jax.ShapeDtypeStruct(t.shape, t.dtype) for t in turned]
-    arrays = [*key_parts, bias, q, g, *state, *turned]
+    if state:
+        outs = [jax.ShapeDtypeStruct(a.shape, a.dtype) for a in state]
     start = len(key_parts) + 3
     return call(
-        functools.partial(forward_body, len(key_parts), chunk, off, n, block),
+        functools.partial(forward_body, len(key_parts), chunk, len(state), off, n, block),
         outs,
         (),
-        arrays,
-        scratch=[pltpu.SemaphoreType.DMA((2,))] if turned else [],
-        direct_in=range(len(arrays) - len(turned), len(arrays)),
+        [*key_parts, bias, q, g, *state],
         alias={start + i: i for i in range(len(state))},
         flops=2 * rows * n * (WIDE + LAT),
     )
@@ -439,8 +414,7 @@
     head = lax.axis_index("head")
     chip, core = head // 2, head % 2
     tokens = latents.shape[1]
-    shift = lambda d: [(x * 2 + c, ((x + d) % 4) * 2 + c) for x in range(4) for c in range(2)]
-    right, left, sibling = shift(1), shift(-1), [(h, h ^ 1) for h in range(8)]
+    pair_a, pair_b, sibling = [[(h, h ^ d) for h in range(8)] for d in (2, 6, 1)]
     send = lambda a, perm: lax.ppermute(a, "head", perm)
     scalars = (list_blocks, list_counts, me.reshape(1).astype(jnp.int32))
 
@@ -474,16 +448,14 @@
     filled = jnp.where(jnp.arange(MAXL, dtype=jnp.int32) < my_count, filled, 0)
     filled = jnp.repeat(filled, tokens)[None, :]
     offset = jnp.tile(jnp.arange(tokens, dtype=jnp.int32), MAXL)[None, :]
-    at = lambda d, c: ((chip + d) % 4) * 2 + c
+    at = lambda d, c: (chip ^ d) * 2 + c
     other = 1 - core
-    places = [at(0, core), at(0, other), at(3, core), at(1, core), at(3, other), at(1, other), at(2, core), at(2, other)]
+    places = [at(0, core), at(0, other), at(1, core), at(3, core), at(1, other), at(3, other), at(2, core), at(2, other)]
     first_token = jnp.stack(places)[:, None] * tokens
     bias = jnp.where(first_token + offset < filled, 0.0, BIG).astype(f32)
     bias0, bias1, bias2 = [bias[i:j].reshape(1, -1) for i, j in ((0, 2), (2, 6), (6, 8))]
 
-    flat = lambda a: jax.ShapeDtypeStruct((a.shape[2], a.shape[0] * a.shape[1]), bf16)
-    qt, gt = call(turn_body, (flat(queries), flat(out_grad)), (), (queries, out_grad))
-    arrived, qt, gt, bias0, bias1, bias2 = lax.optimization_barrier((arrived, qt, gt, bias0, bias1, bias2))
+    arrived, bias0, bias1, bias2 = lax.optimization_barrier((arrived, bias0, bias1, bias2))
 
     (share,) = call(
         take_body,
@@ -496,19 +468,21 @@
     after = lambda a, *others: lax.optimization_barrier((a, *others))[0]
     q, g = queries, out_grad
     every = 8 * keys
-    r1 = send(share, right)
-    l1 = send(share, left)
+    from_b = send(share, pair_b)
+    from_a = send(share, pair_a)
     s0 = send(share, sibling)
     state = forward(0, 0, 2 * keys, every, [share, s0], bias0, q, g)
-    r1 = after(r1, state[3])
-    l1 = after(l1, state[3])
-    r2 = send(r1, right)
-    s1 = send(r1, sibling)
-    s2 = send(l1, sibling)
-    state = forward(1, 2 * keys, 4 * keys, every, [r1, l1, s1, s2], bias1, q, g, state)
+    flat = lambda a: jax.ShapeDtypeStruct((a.shape[2], a.shape[0] * a.shape[1]), bf16)
+    qt, gt = call(turn_body, (flat(queries), flat(out_grad)), (), (q, after(g, state[3])))
+    from_b = after(from_b, gt)
+    from_a = after(from_a, gt)
+    r2 = send(from_b, pair_a)
+    sa = send(from_a, sibling)
+    sb = send(from_b, sibling)
+    state = forward(1, 2 * keys, 4 * keys, every, [from_a, from_b, sa, sb], bias1, q, g, (*state, qt, gt))
     r2 = after(r2, state[3])
     s3 = send(r2, sibling)
-    e, p, k, row, qt, gt = forward(2, 6 * keys, 2 * keys, every, [r2, s3], bias2, q, g, state, (qt, gt))
+    e, p, k, row, qt, gt = forward(2, 6 * keys, 2 * keys, every, [r2, s3], bias2, q, g, state)
 
     fold = lambda a: a.reshape(-1, tokens, WIDE)
     unfold = lambda a: a.reshape(-1, WIDE)
@@ -517,23 +491,22 @@
     far2, near2, e, p, row, k, sg2 = back(2, (7 * keys, 6 * keys), keys, e=e, p=p, row=row, k=k, lead=True)
     mate2 = send(far2, sibling)
     far0, near0, e, p, row, k, sg0, k_saved = back(0, (keys, 0), keys, e=e, p=p, row=row, k=k, final=True)
-    low, high = call(two_body, (share_of(keys // 2),) * 2, (), (after(near2, near0), mate2))
-    from_left = send(low, right)
-    from_right = send(high, left)
-    far1, e, p, row, k, sg1f = back(1, (4 * keys,), 2 * keys, e=e, p=p, row=after(row, low), k=k)
+    (two,) = call(two_body, (share_of(keys),), (), (after(near2, near0), mate2))
+    got_two = send(two, pair_a)
+    far1, e, p, row, k, sg1f = back(1, (4 * keys,), 2 * keys, e=e, p=p, row=after(row, two), k=k)
     mate1 = unfold(send(fold(far1), sibling))
     near1, e, p, row, k, sg1n = back(1, (2 * keys,), 2 * keys, e=e, p=p, row=row, k=k)
     mate0 = send(far0, sibling)
-    to_left, to_right = call(one_body, (share_of(keys),) * 2, (), (near1, mate1, from_left, from_right))
-    got_left = send(to_right, right)
-    got_right = send(to_left, left)
-    attended, query_grad = value_side(e, p, after(k, to_left), early)
+    to_a, to_b = call(one_body, (share_of(keys),) * 2, (), (near1, mate1, got_two))
+    got_b = send(to_b, pair_b)
+    got_a = send(to_a, pair_a)
+    attended, query_grad = value_side(e, p, after(k, to_a), early)
     near0 = after(near0, attended)
     (slot_grads,) = call(
         put_body,
         (slots,),
         scalars,
-        (near0, mate0, got_left, got_right),
+        (near0, mate0, got_a, got_b),
         scratch=[smem(MAXL), smem(16), pltpu.VMEM((keys, WIDE), bf16), dma(MAXL)],
         direct=(0,),
     )

time: 108 us -> 103 us (0.954)
  starting transfers between devices: 23.9 us -> 19.4 us
  local copies, waits for them, and re-layouts: 8.15 us -> 5.24 us
  waiting for transfers between devices: 24.8 us -> 27.4 us
    all_to_all x1, waiting for transfers between devices: 2.23 us -> 8.94 us  [per_device(): lax.all_to_all(outgoing.reshape(16, CAP, tokens, WIDE), 'req', 0, 0, tile...]
    ppermute x14 -> x13, waiting for transfers between devices: 20.1 us -> 15.8 us  [per_device(): send = lambda a, perm: lax.ppermute(a, 'head', perm)]
    ppermute x14 -> x13, starting transfers between devices: 10.7 us -> 7.45 us  [per_device(): send = lambda a, perm: lax.ppermute(a, 'head', perm)]
    unnamed x19 -> x13, local copies, waits for them, and re-layouts: 5.9 us -> 2.99 us
  transfers between devices with their start and end apart: 16 -> 15, of which waited for: 11 -> 9; matrix products, arithmetic and copies ran while one was open for 4% -> 4% of each run, Pallas kernels for 29% -> 30%
where the time goes in v7:
time: 103 us
  Pallas kernels  47.8 us (46%)
  waiting for transfers between devices  27.4 us (27%)
  starting transfers between devices  19.4 us (19%)
  local copies, waits for them, and re-layouts  5.24 us (5%)
  other arithmetic  1.59 us (2%)
  between operations  1.07 us (1%)
    pallas_call x16, Pallas kernels, call(): pl.pallas_call(body, in_specs=[small] * len(scalars) + [INPLACE if i in d...  47.8 us
    ppermute x13, waiting for transfers between devices, per_device(): send = lambda a, perm: lax.ppermute(a, 'head', perm)  15.8 us
    all_to_all x1, waiting for transfers between devices, per_device(): lax.all_to_all(outgoing.reshape(16, CAP, tokens, WIDE), 'req', 0, 0, tile...  8.94 us
    all_to_all x1, starting transfers between devices, per_device(): lax.all_to_all(outgoing.reshape(16, CAP, tokens, WIDE), 'req', 0, 0, tile...  8.17 us
    ppermute x13, starting transfers between devices, per_device(): send = lambda a, perm: lax.ppermute(a, 'head', perm)  7.45 us
    all_to_all x1, starting transfers between devices, per_device(): lax.all_to_all(slot_grads.reshape(16, CAP, tokens, WIDE), 'req', 0, 0, ti...  3.83 us
    unnamed x13, local copies, waits for them, and re-layouts  2.99 us
    all_to_all x1, waiting for transfers between devices, per_device(): lax.all_to_all(slot_grads.reshape(16, CAP, tokens, WIDE), 'req', 0, 0, ti...  2.66 us
  transfers between devices with their start and end apart: 15, of which 9 were waited for; matrix products, arithmetic and copies ran while one was open for 4% of the time, Pallas kernels for 30%

profile of v7, /device:TPU:0, one launch (start us, length us, event | category | flops | bytes accessed | tf_op | source)
XLA Modules:
  0.0 102.6 jit_solution(3218932739983478490)
XLA Ops:
  0.6 3.2 %shard_map.85 = (bf16[32,16,576]{2,1,0:T(8,128)(2,1)}, s32[33]{0:T(128)}) custom-call(s32[16,16]{1,0:T(8,128)} %lists.5, s32[16]{0:T(128)} %counts.5, s32[1]{0:T(128)} %bitcast.me, bf16[16,16,576]{2,1,0:T(8,128)(2,1)} %lat_ref.1), custom_call_target="tpu_custom_call" | custom-call | tf_op jit(solution)/shard_map/pallas_call | solution.py:159
  3.8 8.2 %all-to-all-start = ((bf16[16,2,16,576]{3,2,1,0:T(8,128)(2,1)}), bf16[16,2,16,576]{3,2,1,0:T(8,128)(2,1)S(1)}, u32[]{:S(2)}, u32[]{:S(2)}) async-start(bf16[16,2,16,576]{3,2,1,0:T(8,128)(2,1)} %bitcast.38), calls=%async_computation | async-start | bytes 1310720 | tf_op jit(solution)/shard_map/all_to_all | solution.py:442
  12.0 0.7 dynamic-slice_bitcast_fusion
  12.7 1.2 %dynamic_slice.8 = s32[1]{0:T(128)} dynamic-slice(s32[16]{0:T(128)} %counts.5, s32[]{:T(128)S(6)} %select_n.31), dynamic_slice_sizes={1} | dynamic-slice | bytes 12 | tf_op jit(solution)/shard_map/jit(dynamic_index_in_dim)/dynamic_slice | solution.py:445
  14.0 0.1 stack.35
  14.1 0.9 select_reduce_fusion
  14.9 0.7 compare_select_fusion
  15.6 0.1 broadcast_in_dim.34
  15.7 0.1 lt.32
  15.7 0.1 add.60
  15.8 0.1 fusion
  16.0 8.9 %all-to-all-done = bf16[16,2,16,576]{3,2,1,0:T(8,128)(2,1)S(1)} async-done(((bf16[16,2,16,576]{3,2,1,0:T(8,128)(2,1)}), bf16[16,2,16,576]{3,2,1,0:T(8,128)(2,1)S(1)}, u32[]{:S(2)}, u32[]{:S(2)}) %all-to-all-start) | async-done | bytes 589856 | tf_op jit(solution)/shard_map/all_to_all | solution.py:442
  24.9 1.1 %shard_map.86.refs_0_ = bf16[256,576]{1,0:T(8,128)(2,1)S(1)} custom-call(s32[16,16]{1,0:T(8,128)} %lists.5, s32[16]{0:T(128)} %counts.5, s32[1]{0:T(128)} %bitcast.me, bf16[32,16,576]{2,1,0:T(8,128)(2,1)S(1)} %bitcast.30), custom_call_target="tpu_custom_call" | custom-call | tf_op jit(solution)/shard_map/pallas_call | solution.py:159
  26.0 0.1 collective-permute-start.1
  26.1 1.6 %collective-permute-start.3 = (bf16[256,576]{1,0:T(8,128)(2,1)S(1)}, bf16[256,576]{1,0:T(8,128)(2,1)S(1)}, u32[]{:S(2)}, u32[]{:S(2)}) collective-permute-start(bf16[256,576]{1,0:T(8,128)(2,1)S(1)} %shard_map.86.refs_0_), channel_id=1, source_target_pairs={{0,2},{1,3},{2,0},{3,1},{4,6},{5,7},{6,4},{7,5},{8,10},{9,11},{10,... | collective-permute-start | bytes 884744 | tf_op jit(solution)/shard_map/ppermute | solution.py:418
  27.7 2.1 %collective-permute-start = (bf16[256,576]{1,0:T(8,128)(2,1)S(1)}, bf16[256,576]{1,0:T(8,128)(2,1)S(1)}, u32[]{:S(2)}, u32[]{:S(2)}) collective-permute-start(bf16[256,576]{1,0:T(8,128)(2,1)S(1)} %shard_map.86.refs_0_), channel_id=1, source_target_pairs={{0,6},{1,7},{2,4},{3,5},{4,2},{5,3},{6,0},{7,1},{8,14},{9,15},{10,... | collective-permute-start | bytes 884744 | tf_op jit(solution)/shard_map/ppermute | solution.py:418
  29.8 0.0 collective-permute-done.1.refs_1_
  29.8 0.0 copy-start
  29.8 1.5 %copy-done = bf16[96,16,576]{2,1,0:T(8,128)(2,1)S(1)} copy-done((bf16[96,16,576]{2,1,0:T(8,128)(2,1)S(1)}, bf16[96,16,576]{2,1,0:T(8,128)(2,1)}, u32[]{:S(2)}) %copy-start) | copy-done | bytes 1769496
  31.3 0.0 copy-start.2
  31.3 1.4 %copy-done.2 = bf16[96,16,512]{2,1,0:T(8,128)(2,1)S(1)} copy-done((bf16[96,16,512]{2,1,0:T(8,128)(2,1)S(1)}, bf16[96,16,512]{2,1,0:T(8,128)(2,1)}, u32[]{:S(2)}) %copy-start.2) | copy-done | bytes 1572888
  32.7 0.0 copy-start.1
  32.7 0.0 copy-start.3
  32.7 2.8 %shard_map.87 = (bf16[1536,2048]{1,0:T(8,128)(2,1)S(1)}, bf16[1536,2048]{1,0:T(8,128)(2,1)S(1)}, bf16[2048,576]{1,0:T(8,128)(2,1)S(1)}, f32[9,1536,128]{2,1,0:T(8,128)S(1)}) custom-call(bf16[256,576]{1,0:T(8,128)(2,1)S(1)} %shard_map.86.refs_0_, bf16[256,576]{1,0:T(8,128)(2,1)S(1)} %collective-permute-done.1.refs_1_, f32[1,512]{1,0:T(1,128)S(1)} %bitcast.35, ...), custom_call_target="tpu_custom_call" | custom-call | flops 1711276032 | tf_op jit(solution)/shard_map/pallas_call | solution.py:159
  35.5 0.0 copy-done.1
  35.5 0.0 copy-done.3
  35.5 1.4 %shard_map.88 = (bf16[576,1536]{1,0:T(8,128)(2,1)S(1)}, bf16[512,1536]{1,0:T(8,128)(2,1)S(1)}) custom-call(bf16[96,16,576]{2,1,0:T(8,128)(2,1)S(1)} %copy-done.1, bf16[96,16,512]{2,1,0:T(8,128)(2,1)S(1)} %copy-done.3), custom_call_target="tpu_custom_call" | custom-call | tf_op jit(solution)/shard_map/pallas_call | solution.py:159
  36.9 0.0 collective-permute-done.3.refs_0_
  36.9 0.1 collective-permute-start.4
  37.0 1.6 %collective-permute-done.refs_1_ = bf16[256,576]{1,0:T(8,128)(2,1)S(1)} collective-permute-done((bf16[256,576]{1,0:T(8,128)(2,1)S(1)}, bf16[256,576]{1,0:T(8,128)(2,1)S(1)}, u32[]{:S(2)}, u32[]{:S(2)}) %collective-permute-start) | collective-permute-done | bytes 294944 | tf_op jit(solution)/shard_map/ppermute | solution.py:418
  38.6 0.0 collective-permute-start.5
  38.6 0.0 collective-permute-start.2
  38.6 0.0 collective-permute-done.4.refs_2_
  38.6 1.6 %collective-permute-done.5.refs_3_ = bf16[256,576]{1,0:T(8,128)(2,1)S(1)} collective-permute-done((bf16[256,576]{1,0:T(8,128)(2,1)S(1)}, bf16[256,576]{1,0:T(8,128)(2,1)S(1)}, u32[]{:S(2)}, u32[]{:S(2)}) %collective-permute-start.5) | collective-permute-done | bytes 294944 | tf_op jit(solution)/shard_map/ppermute | solution.py:418
  40.2 5.5 %shard_map.89 = (bf16[1536,2048]{1,0:T(8,128)(2,1)S(1)}, bf16[1536,2048]{1,0:T(8,128)(2,1)S(1)}, bf16[2048,576]{1,0:T(8,128)(2,1)S(1)}, f32[9,1536,128]{2,1,0:T(...) custom-call(bf16[256,576]{1,0:T(8,128)(2,1)S(1)} %collective-permute, ...), custom_call_target="tpu_custom_call", output_to_operand_aliasing={{0}: (7, {}), {1}: (8, {}), {2}: (9, {}), {3}: (10, {}), {4... | custom-call | flops 3422552064 | tf_op jit(solution)/shard_map/pallas_call | solution.py:159
  45.7 3.0 %collective-permute-done.2.refs_0_ = bf16[256,576]{1,0:T(8,128)(2,1)S(1)} collective-permute-done((bf16[256,576]{1,0:T(8,128)(2,1)S(1)}, bf16[256,576]{1,0:T(8,128)(2,1)S(1)}, u32[]{:S(2)}, u32[]{:S(2)}) %collective-permute-start.2) | collective-permute-done | bytes 294944 | tf_op jit(solution)/shard_map/ppermute | solution.py:418
  48.7 0.0 collective-permute-start.6
  48.7 1.6 %collective-permute-done.6.refs_1_ = bf16[256,576]{1,0:T(8,128)(2,1)S(1)} collective-permute-done((bf16[256,576]{1,0:T(8,128)(2,1)S(1)}, bf16[256,576]{1,0:T(8,128)(2,1)S(1)}, u32[]{:S(2)}, u32[]{:S(2)}) %collective-permute-start.6) | collective-permute-done | bytes 294944 | tf_op jit(solution)/shard_map/ppermute | solution.py:418
  50.4 2.8 %shard_map.90 = (bf16[1536,2048]{1,0:T(8,128)(2,1)S(1)}, bf16[1536,2048]{1,0:T(8,128)(2,1)S(1)}, bf16[2048,576]{1,0:T(8,128)(2,1)S(1)}, f32[9,1536,128]{2,1,0:T(...) custom-call(bf16[256,576]{1,0:T(8,128)(2,1)S(1)} %collective-permute, ...), custom_call_target="tpu_custom_call", output_to_operand_aliasing={{0}: (5, {}), {1}: (6, {}), {2}: (7, {}), {3}: (8, {}), {4}... | custom-call | flops 1711276032 | tf_op jit(solution)/shard_map/pallas_call | solution.py:159
  53.1 3.6 %shard_map.91 = (bf16[256,576]{1,0:T(8,128)(2,1)S(1)}, bf16[256,576]{1,0:T(8,128)(2,1)S(1)}, bf16[1536,2048]{1,0:T(8,128)(2,1)S(1)}, bf16[1536,2048]{1,0:T(8,128...) custom-call(bf16[576,1536]{1,0:T(8,128)(2,1)S(1)} %get-tuple-element, ...), custom_call_target="tpu_custom_call", output_to_operand_aliasing={{2}: (2, {}), {3}: (3, {}), {5}: (5, {})} | custom-call | flops 1711276032 | tf_op jit(solution)/shard_map/pallas_call | solution.py:159
  56.8 0.4 collective-permute-start.7
  57.1 3.0 %shard_map.92 = (bf16[256,576]{1,0:T(8,128)(2,1)S(1)}, bf16[256,576]{1,0:T(8,128)(2,1)S(1)}, bf16[1536,2048]{1,0:T(8,128)(2,1)S(1)}, bf16[1536,2048]{1,0:T(8,128...) custom-call(bf16[576,1536]{1,0:T(8,128)(2,1)S(1)} %get-tuple-element, ...), custom_call_target="tpu_custom_call", output_to_operand_aliasing={{2}: (2, {}), {3}: (3, {}), {5}: (5, {}), {4}: (4, {})} | custom-call | flops 1711276032 | tf_op jit(solution)/shard_map/pallas_call | solution.py:159
  60.1 0.0 collective-permute-done.7.far_ref
  60.1 0.1 shard_map.93
  60.2 2.9 %shard_map.94 = (bf16[512,576]{1,0:T(8,128)(2,1)S(1)}, bf16[1536,2048]{1,0:T(8,128)(2,1)S(1)}, bf16[1536,2048]{1,0:T(8,128)(2,1)S(1)}, f32[4,1536,128]{2,1,0:T(8...) custom-call(bf16[576,1536]{1,0:T(8,128)(2,1)S(1)} %get-tuple-element, ...), custom_call_target="tpu_custom_call", output_to_operand_aliasing={{1}: (2, {}), {2}: (3, {}), {4}: (5, {}), {3}: (4, {})} | custom-call | flops 1711276032 | tf_op jit(solution)/shard_map/pallas_call | solution.py:159
  63.1 0.5 collective-permute-start.8
  63.6 0.3 collective-permute-start.9
  63.9 0.0 collective-permute-start.10
  63.9 2.9 %shard_map.95 = (bf16[512,576]{1,0:T(8,128)(2,1)S(1)}, bf16[1536,2048]{1,0:T(8,128)(2,1)S(1)}, bf16[1536,2048]{1,0:T(8,128)(2,1)S(1)}, f32[4,1536,128]{2,1,0:T(8...) custom-call(bf16[576,1536]{1,0:T(8,128)(2,1)S(1)} %get-tuple-element, ...), custom_call_target="tpu_custom_call", output_to_operand_aliasing={{1}: (2, {}), {2}: (3, {}), {4}: (5, {}), {3}: (4, {})} | custom-call | flops 1711276032 | tf_op jit(solution)/shard_map/pallas_call | solution.py:159
  66.8 6.5 %collective-permute-done.9.two_ref = bf16[256,576]{1,0:T(8,128)(2,1)S(1)} collective-permute-done((bf16[256,576]{1,0:T(8,128)(2,1)S(1)}, bf16[256,576]{1,0:T(8,128)(2,1)S(1)}, u32[]{:S(2)}, u32[]{:S(2)}) %collective-permute-start.9) | collective-permute-done | bytes 294944 | tf_op jit(solution)/shard_map/ppermute | solution.py:418
  73.3 0.0 collective-permute-done.8
  73.3 0.2 shard_map.96
  73.6 0.4 collective-permute-start.11
  73.9 2.1 %collective-permute-start.12 = (bf16[256,576]{1,0:T(8,128)(2,1)S(1)}, bf16[256,576]{1,0:T(8,128)(2,1)S(1)}, u32[]{:S(2)}, u32[]{:S(2)}) collective-permute-start(bf16[256,576]{1,0:T(8,128)(2,1)S(1)} %get-tuple-element.125), channel_id=1, source_target_pairs={{0,6},{1,7},{2,4},{3,5},{4,2},{5,3},{6,0},{7,1},{8,14},{9,15},{10,... | collective-permute-start | bytes 884744 | tf_op jit(solution)/shard_map/ppermute | solution.py:418
  76.0 6.4 %shard_map.97 = (bf16[96,16,512]{2,1,0:T(8,128)(2,1)}, bf16[96,16,576]{2,1,0:T(8,128)(2,1)}) custom-call(bf16[1536,2048]{1,0:T(8,128)(2,1)S(1)} %get-tuple-element.110.w_ref, bf16[1536,2048]{1,0:T(8,128)(2,1)S(1)} %get-tuple-element.111.s_ref, bf16[2048,576]{1,0:T(8,128)(2,1)S(1)} %get-tuple-element.116.k_ref), custom_call_target="tpu_custom_call" | custom-call | flops 4429185024 | tf_op jit(solution)/shard_map/pallas_call | solution.py:159
  82.4 0.0 collective-permute-done.10.b_ref
  82.4 0.1 collective-permute-done.11.c_ref
  82.5 1.3 %collective-permute-done.12.d_ref = bf16[256,576]{1,0:T(8,128)(2,1)S(1)} collective-permute-done((bf16[256,576]{1,0:T(8,128)(2,1)S(1)}, bf16[256,576]{1,0:T(8,128)(2,1)S(1)}, u32[]{:S(2)}, u32[]{:S(2)}) %collective-permute-start.12) | collective-permute-done | bytes 294944 | tf_op jit(solution)/shard_map/ppermute | solution.py:418
  83.8 1.7 %shard_map.98 = bf16[32,16,576]{2,1,0:T(8,128)(2,1)} custom-call(s32[16,16]{1,0:T(8,128)} %lists.5, s32[16]{0:T(128)} %counts.5, s32[1]{0:T(128)} %bitcast.me, bf16[256,576]{1,0:T(8,128)(2,1)S(1)} %get-tuple-element.123.a_ref, bf16[256,576]{1,0:T(8,128)(2,1)S(1)} %collective-permute-done.10.b_ref, bf16[256,576]{1,0:T(8,128)(2,1)S(1)} %collective-permute-done.11.c_ref, ...), custom_call_target="tpu_custom_call" | custom-call | tf_op jit(solution)/shard_map/pallas_call | solution.py:159
  85.5 3.8 %all-to-all-start.1 = ((bf16[16,2,16,576]{3,2,1,0:T(8,128)(2,1)}), bf16[16,2,16,576]{3,2,1,0:T(8,128)(2,1)S(1)}, u32[]{:S(2)}, u32[]{:S(2)}) async-start(bf16[16,2,16,576]{3,2,1,0:T(8,128)(2,1)} %bitcast.37), calls=%async_computation.1 | async-start | bytes 1310720 | tf_op jit(solution)/shard_map/all_to_all | solution.py:521
  89.3 8.6 %shard_map.99 = bf16[96,16,576]{2,1,0:T(8,128)(2,1)} custom-call(bf16[2,1024,256]{2,1,0:T(8,128)(2,1)} %get-tuple-element.118.refs_0_, bf16[2,1024,256]{2,1,0:T(8,128)(2,1)} %get-tuple-element.119.refs_1_, bf16[2,1024,256]{2,1,0:T(8,128)(2,1)} %get-tuple-element.120.refs_2_, ...), custom_call_target="tpu_custom_call", output_to_operand_aliasing={{}: (5, {})} | custom-call | flops 2415919104 | tf_op jit(solution)/shard_map/pallas_call | solution.py:159
  97.9 2.7 %all-to-all-done.1 = bf16[16,2,16,576]{3,2,1,0:T(8,128)(2,1)S(1)} async-done(((bf16[16,2,16,576]{3,2,1,0:T(8,128)(2,1)}), bf16[16,2,16,576]{3,2,1,0:T(8,128)(2,1)S(1)}, u32[]{:S(2)}, u32[]{:S(2)}) %all-to-all-start.1) | async-done | bytes 589856 | tf_op jit(solution)/shard_map/all_to_all | solution.py:521
  100.6 1.8 %shard_map.100 = f32[16,16,576]{2,1,0:T(8,128)} custom-call(s32[33]{0:T(128)} %get-tuple-element.128.table, bf16[32,16,576]{2,1,0:T(8,128)(2,1)S(1)} %bitcast.31), custom_call_target="tpu_custom_call" | custom-call | tf_op jit(solution)/shard_map/pallas_call | solution.py:159
  (7 shorter events, 0.0 us)
Async XLA Ops:
  3.8 21.1 %all-to-all-start = ((bf16[16,2,16,576]{3,2,1,0:T(8,128)(2,1)}), bf16[16,2,16,576]{3,2,1,0:T(8,128)(2,1)S(1)}, u32[]{:S(2)}, u32[]{:S(2)}) async-start(bf16[16,2,16,576]{3,2,1,0:T(8,128)(2,1)} %bitcast.38), calls=%async_computation | async-start | bytes 1310720 | tf_op jit(solution)/shard_map/all_to_all | solution.py:442
  26.0 3.8 %collective-permute-start.1 = (bf16[256,576]{1,0:T(8,128)(2,1)S(1)}, bf16[256,576]{1,0:T(8,128)(2,1)S(1)}, u32[]{:S(2)}, u32[]{:S(2)}) collective-permute-start(bf16[256,576]{1,0:T(8,128)(2,1)S(1)} %shard_map.86.refs_0_), channel_id=1, source_target_pairs={{0,1},{1,0},{2,3},{3,2},{4,5},{5,4},{6,7},{7,6},{8,9},{9,8},{10,11... | collective-permute-start | bytes 884744 | tf_op jit(solution)/shard_map/ppermute | solution.py:418
  26.1 10.8 %collective-permute-start.3 = (bf16[256,576]{1,0:T(8,128)(2,1)S(1)}, bf16[256,576]{1,0:T(8,128)(2,1)S(1)}, u32[]{:S(2)}, u32[]{:S(2)}) collective-permute-start(bf16[256,576]{1,0:T(8,128)(2,1)S(1)} %shard_map.86.refs_0_), channel_id=1, source_target_pairs={{0,2},{1,3},{2,0},{3,1},{4,6},{5,7},{6,4},{7,5},{8,10},{9,11},{10,... | collective-permute-start | bytes 884744 | tf_op jit(solution)/shard_map/ppermute | solution.py:418
  27.7 11.0 %collective-permute-start = (bf16[256,576]{1,0:T(8,128)(2,1)S(1)}, bf16[256,576]{1,0:T(8,128)(2,1)S(1)}, u32[]{:S(2)}, u32[]{:S(2)}) collective-permute-start(bf16[256,576]{1,0:T(8,128)(2,1)S(1)} %shard_map.86.refs_0_), channel_id=1, source_target_pairs={{0,6},{1,7},{2,4},{3,5},{4,2},{5,3},{6,0},{7,1},{8,14},{9,15},{10,... | collective-permute-start | bytes 884744 | tf_op jit(solution)/shard_map/ppermute | solution.py:418
  29.8 1.5 %copy-start = (bf16[96,16,576]{2,1,0:T(8,128)(2,1)S(1)}, bf16[96,16,576]{2,1,0:T(8,128)(2,1)}, u32[]{:S(2)}) copy-start(bf16[96,16,576]{2,1,0:T(8,128)(2,1)} %refs_3_.3) | copy-start | bytes 5308420
  31.3 1.4 %copy-start.2 = (bf16[96,16,512]{2,1,0:T(8,128)(2,1)S(1)}, bf16[96,16,512]{2,1,0:T(8,128)(2,1)}, u32[]{:S(2)}) copy-start(bf16[96,16,512]{2,1,0:T(8,128)(2,1)} %refs_4_.3) | copy-start | bytes 4718596
  32.7 2.8 %copy-start.1 = (bf16[96,16,576]{2,1,0:T(8,128)(2,1)S(1)}, bf16[96,16,576]{2,1,0:T(8,128)(2,1)}, u32[]{:S(2)}) copy-start(bf16[96,16,576]{2,1,0:T(8,128)(2,1)} %refs_3_.3) | copy-start | bytes 5308420
  32.7 2.8 %copy-start.3 = (bf16[96,16,512]{2,1,0:T(8,128)(2,1)S(1)}, bf16[96,16,512]{2,1,0:T(8,128)(2,1)}, u32[]{:S(2)}) copy-start(bf16[96,16,512]{2,1,0:T(8,128)(2,1)} %refs_4_.3) | copy-start | bytes 4718596
  36.9 1.7 %collective-permute-start.4 = (bf16[256,576]{1,0:T(8,128)(2,1)S(1)}, bf16[256,576]{1,0:T(8,128)(2,1)S(1)}, u32[]{:S(2)}, u32[]{:S(2)}) collective-permute-start(bf16[256,576]{1,0:T(8,128)(2,1)S(1)} %collective-permute-done.3.refs_0_), channel_id=1, source_target_pairs={{0,1},{1,0},{2,3},{3,2},{4,5},{5,4},{6,7},{7,6},{8,9},{9,8},{10,11... | collective-permute-start | bytes 884744 | tf_op jit(solution)/shard_map/ppermute | solution.py:418
  38.6 1.6 %collective-permute-start.5 = (bf16[256,576]{1,0:T(8,128)(2,1)S(1)}, bf16[256,576]{1,0:T(8,128)(2,1)S(1)}, u32[]{:S(2)}, u32[]{:S(2)}) collective-permute-start(bf16[256,576]{1,0:T(8,128)(2,1)S(1)} %collective-permute-done.refs_1_), channel_id=1, source_target_pairs={{0,1},{1,0},{2,3},{3,2},{4,5},{5,4},{6,7},{7,6},{8,9},{9,8},{10,11... | collective-permute-start | bytes 884744 | tf_op jit(solution)/shard_map/ppermute | solution.py:418
  38.6 10.1 %collective-permute-start.2 = (bf16[256,576]{1,0:T(8,128)(2,1)S(1)}, bf16[256,576]{1,0:T(8,128)(2,1)S(1)}, u32[]{:S(2)}, u32[]{:S(2)}) collective-permute-start(bf16[256,576]{1,0:T(8,128)(2,1)S(1)} %collective-permute-done.refs_1_), channel_id=1, source_target_pairs={{0,2},{1,3},{2,0},{3,1},{4,6},{5,7},{6,4},{7,5},{8,10},{9,11},{10,... | collective-permute-start | bytes 884744 | tf_op jit(solution)/shard_map/ppermute | solution.py:418
  48.7 1.6 %collective-permute-start.6 = (bf16[256,576]{1,0:T(8,128)(2,1)S(1)}, bf16[256,576]{1,0:T(8,128)(2,1)S(1)}, u32[]{:S(2)}, u32[]{:S(2)}) collective-permute-start(bf16[256,576]{1,0:T(8,128)(2,1)S(1)} %collective-permute-done.2.refs_0_), channel_id=1, source_target_pairs={{0,1},{1,0},{2,3},{3,2},{4,5},{5,4},{6,7},{7,6},{8,9},{9,8},{10,11... | collective-permute-start | bytes 884744 | tf_op jit(solution)/shard_map/ppermute | solution.py:418
  56.8 3.4 %collective-permute-start.7 = (bf16[256,576]{1,0:T(8,128)(2,1)S(1)}, bf16[256,576]{1,0:T(8,128)(2,1)S(1)}, u32[]{:S(2)}, u32[]{:S(2)}) collective-permute-start(bf16[256,576]{1,0:T(8,128)(2,1)S(1)} %get-tuple-element.103), channel_id=1, source_target_pairs={{0,1},{1,0},{2,3},{3,2},{4,5},{5,4},{6,7},{7,6},{8,9},{9,8},{10,11... | collective-permute-start | bytes 884744 | tf_op jit(solution)/shard_map/ppermute | solution.py:418
  63.1 10.2 %collective-permute-start.8 = (bf16[32,16,576]{2,1,0:T(8,128)(2,1)S(1)}, bf16[32,16,576]{2,1,0:T(8,128)(2,1)S(1)}, u32[]{:S(2)}, u32[]{:S(2)}) collective-permute-start(bf16[32,16,576]{2,1,0:T(8,128)(2,1)S(1)} %bitcast.36), channel_id=1, source_target_pairs={{0,1},{1,0},{2,3},{3,2},{4,5},{5,4},{6,7},{7,6},{8,9},{9,8},{10,11... | collective-permute-start | bytes 1769480 | tf_op jit(solution)/shard_map/ppermute | solution.py:418
  63.6 9.7 %collective-permute-start.9 = (bf16[256,576]{1,0:T(8,128)(2,1)S(1)}, bf16[256,576]{1,0:T(8,128)(2,1)S(1)}, u32[]{:S(2)}, u32[]{:S(2)}) collective-permute-start(bf16[256,576]{1,0:T(8,128)(2,1)S(1)} %shard_map.93), channel_id=1, source_target_pairs={{0,2},{1,3},{2,0},{3,1},{4,6},{5,7},{6,4},{7,5},{8,10},{9,11},{10,... | collective-permute-start | bytes 884744 | tf_op jit(solution)/shard_map/ppermute | solution.py:418
  63.9 18.5 %collective-permute-start.10 = (bf16[256,576]{1,0:T(8,128)(2,1)S(1)}, bf16[256,576]{1,0:T(8,128)(2,1)S(1)}, u32[]{:S(2)}, u32[]{:S(2)}) collective-permute-start(bf16[256,576]{1,0:T(8,128)(2,1)S(1)} %get-tuple-element.124), channel_id=1, source_target_pairs={{0,1},{1,0},{2,3},{3,2},{4,5},{5,4},{6,7},{7,6},{8,9},{9,8},{10,11... | collective-permute-start | bytes 884744 | tf_op jit(solution)/shard_map/ppermute | solution.py:418
  73.6 9.0 %collective-permute-start.11 = (bf16[256,576]{1,0:T(8,128)(2,1)S(1)}, bf16[256,576]{1,0:T(8,128)(2,1)S(1)}, u32[]{:S(2)}, u32[]{:S(2)}) collective-permute-start(bf16[256,576]{1,0:T(8,128)(2,1)S(1)} %get-tuple-element.115), channel_id=1, source_target_pairs={{0,2},{1,3},{2,0},{3,1},{4,6},{5,7},{6,4},{7,5},{8,10},{9,11},{10,... | collective-permute-start | bytes 884744 | tf_op jit(solution)/shard_map/ppermute | solution.py:418
  73.9 9.9 %collective-permute-start.12 = (bf16[256,576]{1,0:T(8,128)(2,1)S(1)}, bf16[256,576]{1,0:T(8,128)(2,1)S(1)}, u32[]{:S(2)}, u32[]{:S(2)}) collective-permute-start(bf16[256,576]{1,0:T(8,128)(2,1)S(1)} %get-tuple-element.125), channel_id=1, source_target_pairs={{0,6},{1,7},{2,4},{3,5},{4,2},{5,3},{6,0},{7,1},{8,14},{9,15},{10,... | collective-permute-start | bytes 884744 | tf_op jit(solution)/shard_map/ppermute | solution.py:418
  85.5 15.1 %all-to-all-start.1 = ((bf16[16,2,16,576]{3,2,1,0:T(8,128)(2,1)}), bf16[16,2,16,576]{3,2,1,0:T(8,128)(2,1)S(1)}, u32[]{:S(2)}, u32[]{:S(2)}) async-start(bf16[16,2,16,576]{3,2,1,0:T(8,128)(2,1)} %bitcast.37), calls=%async_computation.1 | async-start | bytes 1310720 | tf_op jit(solution)/shard_map/all_to_all | solution.py:521

commit v8 on v7

--- a/solution.py
+++ b/solution.py
@@ -169,10 +169,29 @@
     )(*scalars, *args)
 
 
-def forward_body(nkeys, chunk, kept, off, n, block, *refs):
-    key_refs, refs = refs[:nkeys], refs[nkeys:]
-    bias, q_ref, g_ref = refs[:3]
-    e_out, p_out, k_out, st_out = refs[3 + kept : 7 + kept]
+def forward_body(nkeys, chunk, off, n, block, *refs):
+    refs = list(refs)
+    first = chunk == 0
+    key_refs, bias, refs = refs[:nkeys], refs[nkeys], refs[nkeys + 1 :]
+    if first:
+        (q_in, g_in), refs = refs[:2], refs[2:]
+        sems, refs = refs[-1], refs[:-1]
+    else:
+        refs = refs[len(refs) // 2 :]
+    e_out, p_out, k_out, st_out, q_ref, g_ref = refs
+    steps = q_ref.shape[0] * 16 // block
+
+    def loads(i):
+        part = pl.ds(i * (block // 16), block // 16)
+        return (
+            pltpu.make_async_copy(q_in.at[part], q_ref.at[part], sems.at[2 * i]),
+            pltpu.make_async_copy(g_in.at[part], g_ref.at[part], sems.at[2 * i + 1]),
+        )
+
+    if first:
+        for i in range(steps):
+            for copy in loads(i):
+                copy.start()
     at = off
     for ref in key_refs:
         k_out[at : at + ref.shape[0]] = ref[...]
@@ -182,6 +201,9 @@
     def rows(i, carry):
         here = pl.ds(pl.multiple_of(i * block, block), block)
         part = pl.ds(i * (block // 16), block // 16)
+        if first:
+            for copy in loads(i):
+                copy.wait()
         scores = dot(q_ref[part].reshape(block, WIDE), k_out[mine], NT) + bias[...]
         top = jnp.max(scores, axis=1, keepdims=True)
         expo = jnp.exp2((scores - top) * EXPC)
@@ -194,22 +216,28 @@
         st_out[6 + chunk, here] = wide(jnp.sum(expo * grads, axis=1, keepdims=True))
         return carry
 
-    lax.fori_loop(0, q_ref.shape[0] * 16 // block, rows, 0)
-
-
-def forward(chunk, off, n, total_keys, key_parts, bias, q, g, state=(), block=768):
-    rows = q.shape[0] * 16
-    side = jax.ShapeDtypeStruct((rows, total_keys), bf16)
-    outs = [side, side, jax.ShapeDtypeStruct((total_keys, WIDE), bf16), jax.ShapeDtypeStruct((9, rows, 128), f32)]
-    if state:
-        outs = [jax.ShapeDtypeStruct(a.shape, a.dtype) for a in state]
-    start = len(key_parts) + 3
+    lax.fori_loop(0, steps, rows, 0)
+
+
+def forward(chunk, off, n, total_keys, key_parts, bias, state):
+    first = chunk == 0
+    block = 384 if first else 768
+    if first:
+        rows = state[0].shape[0] * 16
+        side = jax.ShapeDtypeStruct((rows, total_keys), bf16)
+        outs = [side, side, jax.ShapeDtypeStruct((total_keys, WIDE), bf16), jax.ShapeDtypeStruct((9, rows, 128), f32)]
+    else:
+        rows, outs = state[0].shape[0], []
+    outs += [jax.ShapeDtypeStruct(a.shape, a.dtype) for a in state]
+    start = len(key_parts) + 1
     return call(
-        functools.partial(forward_body, len(key_parts), chunk, len(state), off, n, block),
+        functools.partial(forward_body, len(key_parts), chunk, off, n, block),
         outs,
         (),
-        [*key_parts, bias, q, g, *state],
-        alias={start + i: i for i in range(len(state))},
+        [*key_parts, bias, *state],
+        direct_in=(start, start + 1) if first else (),
+        scratch=[pltpu.SemaphoreType.DMA((2 * rows // block,))] if first else [],
+        alias={} if first else {start + i: i for i in range(len(state))},
         flops=2 * rows * n * (WIDE + LAT),
     )
 
@@ -466,37 +494,40 @@
     )
 
     after = lambda a, *others: lax.optimization_barrier((a, *others))[0]
-    q, g = queries, out_grad
     every = 8 * keys
     from_b = send(share, pair_b)
     from_a = send(share, pair_a)
     s0 = send(share, sibling)
-    state = forward(0, 0, 2 * keys, every, [share, s0], bias0, q, g)
-    flat = lambda a: jax.ShapeDtypeStruct((a.shape[2], a.shape[0] * a.shape[1]), bf16)
-    qt, gt = call(turn_body, (flat(queries), flat(out_grad)), (), (q, after(g, state[3])))
-    from_b = after(from_b, gt)
-    from_a = after(from_a, gt)
+    state = forward(0, 0, 2 * keys, every, [share, s0], bias0, (queries, out_grad))
+    from_b = after(from_b, state[3])
+    from_a = after(from_a, state[3])
     r2 = send(from_b, pair_a)
     sa = send(from_a, sibling)
     sb = send(from_b, sibling)
-    state = forward(1, 2 * keys, 4 * keys, every, [from_a, from_b, sa, sb], bias1, q, g, (*state, qt, gt))
+    state = forward(1, 2 * keys, 4 * keys, every, [from_a, from_b, sa, sb], bias1, state)
     r2 = after(r2, state[3])
     s3 = send(r2, sibling)
-    e, p, k, row, qt, gt = forward(2, 6 * keys, 2 * keys, every, [r2, s3], bias2, q, g, state)
+    flat = lambda a: jax.ShapeDtypeStruct((a.shape[2], a.shape[0] * a.shape[1]), bf16)
+    e, p, k, row, q, g = state
+    qt, gt = call(turn_body, (flat(queries), flat(out_grad)), (), (q, after(g, r2)))
+    e, p, k, row, q, g = forward(2, 6 * keys, 2 * keys, every, [r2, s3], bias2, (e, p, k, after(row, gt), q, g))
 
     fold = lambda a: a.reshape(-1, tokens, WIDE)
     unfold = lambda a: a.reshape(-1, WIDE)
     early = 512
     back = functools.partial(backward, early=early, qt=qt, gt=gt)
-    far2, near2, e, p, row, k, sg2 = back(2, (7 * keys, 6 * keys), keys, e=e, p=p, row=row, k=k, lead=True)
+    far2, e, p, row, k, sg2f = back(2, (7 * keys,), keys, e=e, p=p, row=row, k=k, lead=True)
     mate2 = send(far2, sibling)
-    far0, near0, e, p, row, k, sg0, k_saved = back(0, (keys, 0), keys, e=e, p=p, row=row, k=k, final=True)
-    (two,) = call(two_body, (share_of(keys),), (), (after(near2, near0), mate2))
+    near2, e, p, row, k, sg2n = back(2, (6 * keys,), keys, e=e, p=p, row=row, k=k)
+    far0, e, p, row, k, sg0f = back(0, (keys,), keys, e=e, p=p, row=row, k=k)
+    (two,) = call(two_body, (share_of(keys),), (), (after(near2, far0), mate2))
     got_two = send(two, pair_a)
     far1, e, p, row, k, sg1f = back(1, (4 * keys,), 2 * keys, e=e, p=p, row=after(row, two), k=k)
     mate1 = unfold(send(fold(far1), sibling))
     near1, e, p, row, k, sg1n = back(1, (2 * keys,), 2 * keys, e=e, p=p, row=row, k=k)
     mate0 = send(far0, sibling)
+    near0, e, p, row, k, sg0n, k_saved = back(0, (0,), keys, e=e, p=p, row=row, k=k, final=True)
+    near1 = after(near1, near0)
     to_a, to_b = call(one_body, (share_of(keys),) * 2, (), (near1, mate1, got_two))
     got_b = send(to_b, pair_b)
     got_a = send(to_a, pair_a)
@@ -512,8 +543,8 @@
     )
     k_saved = after(k_saved, slot_grads)
     query_grad = query_side(
-        (sg2, sg0, sg1f, sg1n),
-        ((7 * keys, 6 * keys), (keys, 0), (4 * keys, 5 * keys), (2 * keys, 3 * keys)),
+        (sg2f, sg2n, sg0f, sg0n, sg1f, sg1n),
+        ((7 * keys,), (6 * keys,), (keys,), (0,), (4 * keys, 5 * keys), (2 * keys, 3 * keys)),
         early,
         k_saved,
         query_grad,

time: 103 us -> 103 us (level)
  Pallas kernels: 47.8 us -> 50.9 us
  local copies, waits for them, and re-layouts: 5.24 us -> 2.28 us
    pallas_call x16 -> x18, Pallas kernels: 47.8 us -> 50.9 us  [call(): pl.pallas_call(body, in_specs=[small] * len(scalars) + [INPLACE if i in d...]
    unnamed x13 -> x5, local copies, waits for them, and re-layouts: 2.99 us -> 0.03 us
  transfers between devices with their start and end apart: 15 -> 15, of which waited for: 9 -> 10; matrix products, arithmetic and copies ran while one was open for 4% -> 4% of each run, Pallas kernels for 30% -> 34%
where the time goes in v8:
time: 103 us; the launch traced here: 102 us
  Pallas kernels  50.9 us (49%)
  waiting for transfers between devices  27.5 us (27%)
  starting transfers between devices  19 us (18%)
  local copies, waits for them, and re-layouts  2.28 us (2%)
  other arithmetic  1.59 us (2%)
  between operations  1.05 us (1%)
    pallas_call x18, Pallas kernels, call(): pl.pallas_call(body, in_specs=[small] * len(scalars) + [INPLACE if i in d...  50.9 us
    ppermute x13, waiting for transfers between devices, per_device(): send = lambda a, perm: lax.ppermute(a, 'head', perm)  15.7 us
    all_to_all x1, waiting for transfers between devices, per_device(): lax.all_to_all(outgoing.reshape(16, CAP, tokens, WIDE), 'req', 0, 0, tile...  8.95 us
    all_to_all x1, starting transfers between devices, per_device(): lax.all_to_all(outgoing.reshape(16, CAP, tokens, WIDE), 'req', 0, 0, tile...  8.17 us
    ppermute x13, starting transfers between devices, per_device(): send = lambda a, perm: lax.ppermute(a, 'head', perm)  6.96 us
    all_to_all x1, starting transfers between devices, per_device(): lax.all_to_all(slot_grads.reshape(16, CAP, tokens, WIDE), 'req', 0, 0, ti...  3.83 us
    all_to_all x1, waiting for transfers between devices, per_device(): lax.all_to_all(slot_grads.reshape(16, CAP, tokens, WIDE), 'req', 0, 0, ti...  2.85 us
  transfers between devices with their start and end apart: 15, of which 10 were waited for; matrix products, arithmetic and copies ran while one was open for 4% of the time, Pallas kernels for 34%

profile of v8, /device:TPU:0, one launch (start us, length us, event | category | flops | bytes accessed | tf_op | source)
XLA Modules:
  0.0 102.2 jit_solution(18242746091156147607)
XLA Ops:
  0.6 3.2 %shard_map.85 = (bf16[32,16,576]{2,1,0:T(8,128)(2,1)}, s32[33]{0:T(128)}) custom-call(s32[16,16]{1,0:T(8,128)} %lists.5, s32[16]{0:T(128)} %counts.5, s32[1]{0:T(128)} %bitcast.me, bf16[16,16,576]{2,1,0:T(8,128)(2,1)} %lat_ref.1), custom_call_target="tpu_custom_call" | custom-call | tf_op jit(solution)/shard_map/pallas_call | solution.py:159
  3.8 8.2 %all-to-all-start = ((bf16[16,2,16,576]{3,2,1,0:T(8,128)(2,1)}), bf16[16,2,16,576]{3,2,1,0:T(8,128)(2,1)S(1)}, u32[]{:S(2)}, u32[]{:S(2)}) async-start(bf16[16,2,16,576]{3,2,1,0:T(8,128)(2,1)} %bitcast.38), calls=%async_computation | async-start | bytes 1310720 | tf_op jit(solution)/shard_map/all_to_all | solution.py:470
  12.0 1.2 %dynamic_slice.8 = s32[1]{0:T(128)} dynamic-slice(s32[16]{0:T(128)} %counts.5, s32[]{:T(128)S(6)} %select_n.31), dynamic_slice_sizes={1} | dynamic-slice | bytes 12 | tf_op jit(solution)/shard_map/jit(dynamic_index_in_dim)/dynamic_slice | solution.py:473
  13.3 0.7 dynamic-slice_bitcast_fusion
  14.0 0.1 stack.35
  14.1 0.9 select_reduce_fusion
  14.9 0.7 compare_select_fusion
  15.6 0.1 broadcast_in_dim.34
  15.7 0.1 lt.32
  15.7 0.1 add.60
  15.8 0.1 fusion
  15.9 9.0 %all-to-all-done = bf16[16,2,16,576]{3,2,1,0:T(8,128)(2,1)S(1)} async-done(((bf16[16,2,16,576]{3,2,1,0:T(8,128)(2,1)}), bf16[16,2,16,576]{3,2,1,0:T(8,128)(2,1)S(1)}, u32[]{:S(2)}, u32[]{:S(2)}) %all-to-all-start) | async-done | bytes 589856 | tf_op jit(solution)/shard_map/all_to_all | solution.py:470
  24.9 1.1 %shard_map.86.refs_0_ = bf16[256,576]{1,0:T(8,128)(2,1)S(1)} custom-call(s32[16,16]{1,0:T(8,128)} %lists.5, s32[16]{0:T(128)} %counts.5, s32[1]{0:T(128)} %bitcast.me, bf16[32,16,576]{2,1,0:T(8,128)(2,1)S(1)} %bitcast.30), custom_call_target="tpu_custom_call" | custom-call | tf_op jit(solution)/shard_map/pallas_call | solution.py:159
  26.0 0.1 collective-permute-start.1
  26.1 2.8 %collective-permute-start.2 = (bf16[256,576]{1,0:T(8,128)(2,1)S(1)}, bf16[256,576]{1,0:T(8,128)(2,1)S(1)}, u32[]{:S(2)}, u32[]{:S(2)}) collective-permute-start(bf16[256,576]{1,0:T(8,128)(2,1)S(1)} %shard_map.86.refs_0_), channel_id=1, source_target_pairs={{0,6},{1,7},{2,4},{3,5},{4,2},{5,3},{6,0},{7,1},{8,14},{9,15},{10,... | collective-permute-start | bytes 884744 | tf_op jit(solution)/shard_map/ppermute | solution.py:446
  28.9 0.2 collective-permute-start
  29.1 0.0 collective-permute-done.1.refs_1_
  29.1 4.4 %shard_map.87 = (bf16[1536,2048]{1,0:T(8,128)(2,1)S(1)}, bf16[1536,2048]{1,0:T(8,128)(2,1)S(1)}, bf16[2048,576]{1,0:T(8,128)(2,1)S(1)}, f32[9,1536,128]{2,1,0:T(...) custom-call(bf16[256,576]{1,0:T(8,128)(2,1)S(1)} %shard_map.86.refs_0_, ...), custom_call_target="tpu_custom_call" | custom-call | flops 1711276032 | tf_op jit(solution)/shard_map/pallas_call | solution.py:159
  33.5 3.9 %collective-permute-done.2.refs_1_ = bf16[256,576]{1,0:T(8,128)(2,1)S(1)} collective-permute-done((bf16[256,576]{1,0:T(8,128)(2,1)S(1)}, bf16[256,576]{1,0:T(8,128)(2,1)S(1)}, u32[]{:S(2)}, u32[]{:S(2)}) %collective-permute-start.2) | collective-permute-done | bytes 294944 | tf_op jit(solution)/shard_map/ppermute | solution.py:446
  37.4 1.3 %collective-permute-done.refs_0_ = bf16[256,576]{1,0:T(8,128)(2,1)S(1)} collective-permute-done((bf16[256,576]{1,0:T(8,128)(2,1)S(1)}, bf16[256,576]{1,0:T(8,128)(2,1)S(1)}, u32[]{:S(2)}, u32[]{:S(2)}) %collective-permute-start) | collective-permute-done | bytes 294944 | tf_op jit(solution)/shard_map/ppermute | solution.py:446
  38.7 0.0 collective-permute-start.3
  38.7 0.5 collective-permute-start.4
  39.2 0.3 collective-permute-start.5
  39.5 0.8 collective-permute-done.3.refs_2_
  40.3 0.5 collective-permute-done.4.refs_3_
  40.8 5.5 %shard_map.88 = (bf16[1536,2048]{1,0:T(8,128)(2,1)S(1)}, bf16[1536,2048]{1,0:T(8,128)(2,1)S(1)}, bf16[2048,576]{1,0:T(8,128)(2,1)S(1)}, f32[9,1536,128]{2,1,0:T(...) custom-call(bf16[256,576]{1,0:T(8,128)(2,1)S(1)} %collective-permute, ...), custom_call_target="tpu_custom_call", output_to_operand_aliasing={{0}: (5, {}), {1}: (6, {}), {2}: (7, {}), {3}: (8, {}), {4}... | custom-call | flops 3422552064 | tf_op jit(solution)/shard_map/pallas_call | solution.py:159
  46.3 2.5 %collective-permute-done.5.refs_0_ = bf16[256,576]{1,0:T(8,128)(2,1)S(1)} collective-permute-done((bf16[256,576]{1,0:T(8,128)(2,1)S(1)}, bf16[256,576]{1,0:T(8,128)(2,1)S(1)}, u32[]{:S(2)}, u32[]{:S(2)}) %collective-permute-start.5) | collective-permute-done | bytes 294944 | tf_op jit(solution)/shard_map/ppermute | solution.py:446
  48.8 0.0 collective-permute-start.6
  48.8 1.4 %shard_map.89 = (bf16[576,1536]{1,0:T(8,128)(2,1)S(1)}, bf16[512,1536]{1,0:T(8,128)(2,1)S(1)}) custom-call(bf16[96,16,576]{2,1,0:T(8,128)(2,1)S(1)} %get-tuple-element.90.q_ref.refs_7_, bf16[96,16,512]{2,1,0:T(8,128)(2,1)S(1)} %get-tuple-element.94.g_ref.refs_8_), custom_call_target="tpu_custom_call" | custom-call | tf_op jit(solution)/shard_map/pallas_call | solution.py:159
  50.2 0.2 collective-permute-done.6.refs_1_
  50.4 2.8 %shard_map.90 = (bf16[1536,2048]{1,0:T(8,128)(2,1)S(1)}, bf16[1536,2048]{1,0:T(8,128)(2,1)S(1)}, bf16[2048,576]{1,0:T(8,128)(2,1)S(1)}, f32[9,1536,128]{2,1,0:T(...) custom-call(bf16[256,576]{1,0:T(8,128)(2,1)S(1)} %collective-permute, ...), custom_call_target="tpu_custom_call", output_to_operand_aliasing={{0}: (3, {}), {1}: (4, {}), {2}: (5, {}), {3}: (6, {}), {4}... | custom-call | flops 1711276032 | tf_op jit(solution)/shard_map/pallas_call | solution.py:159
  53.2 2.2 %shard_map.91 = (bf16[256,576]{1,0:T(8,128)(2,1)S(1)}, bf16[1536,2048]{1,0:T(8,128)(2,1)S(1)}, bf16[1536,2048]{1,0:T(8,128)(2,1)S(1)}, f32[4,1536,128]{2,1,0:T(8...) custom-call(bf16[576,1536]{1,0:T(8,128)(2,1)S(1)} %get-tuple-element, ...), custom_call_target="tpu_custom_call", output_to_operand_aliasing={{1}: (2, {}), {2}: (3, {}), {4}: (5, {})} | custom-call | flops 855638016 | tf_op jit(solution)/shard_map/pallas_call | solution.py:159
  55.4 0.6 collective-permute-start.7
  56.0 1.7 %shard_map.92 = (bf16[256,576]{1,0:T(8,128)(2,1)S(1)}, bf16[1536,2048]{1,0:T(8,128)(2,1)S(1)}, bf16[1536,2048]{1,0:T(8,128)(2,1)S(1)}, f32[4,1536,128]{2,1,0:T(8...) custom-call(bf16[576,1536]{1,0:T(8,128)(2,1)S(1)} %get-tuple-element, ...), custom_call_target="tpu_custom_call", output_to_operand_aliasing={{1}: (2, {}), {2}: (3, {}), {4}: (5, {}), {3}: (4, {})} | custom-call | flops 855638016 | tf_op jit(solution)/shard_map/pallas_call | solution.py:159
  57.7 1.7 %shard_map.93 = (bf16[256,576]{1,0:T(8,128)(2,1)S(1)}, bf16[1536,2048]{1,0:T(8,128)(2,1)S(1)}, bf16[1536,2048]{1,0:T(8,128)(2,1)S(1)}, f32[4,1536,128]{2,1,0:T(8...) custom-call(bf16[576,1536]{1,0:T(8,128)(2,1)S(1)} %get-tuple-element, ...), custom_call_target="tpu_custom_call", output_to_operand_aliasing={{1}: (2, {}), {2}: (3, {}), {4}: (5, {}), {3}: (4, {})} | custom-call | flops 855638016 | tf_op jit(solution)/shard_map/pallas_call | solution.py:159
  59.4 0.0 collective-permute-done.7.far_ref
  59.4 0.1 shard_map.94
  59.5 2.9 %shard_map.95 = (bf16[512,576]{1,0:T(8,128)(2,1)S(1)}, bf16[1536,2048]{1,0:T(8,128)(2,1)S(1)}, bf16[1536,2048]{1,0:T(8,128)(2,1)S(1)}, f32[4,1536,128]{2,1,0:T(8...) custom-call(bf16[576,1536]{1,0:T(8,128)(2,1)S(1)} %get-tuple-element, ...), custom_call_target="tpu_custom_call", output_to_operand_aliasing={{1}: (2, {}), {2}: (3, {}), {4}: (5, {}), {3}: (4, {})} | custom-call | flops 1711276032 | tf_op jit(solution)/shard_map/pallas_call | solution.py:159
  62.4 0.3 collective-permute-start.8
  62.7 0.3 collective-permute-start.9
  63.0 0.0 collective-permute-start.10
  63.0 2.9 %shard_map.96 = (bf16[512,576]{1,0:T(8,128)(2,1)S(1)}, bf16[1536,2048]{1,0:T(8,128)(2,1)S(1)}, bf16[1536,2048]{1,0:T(8,128)(2,1)S(1)}, f32[4,1536,128]{2,1,0:T(8...) custom-call(bf16[576,1536]{1,0:T(8,128)(2,1)S(1)} %get-tuple-element, ...), custom_call_target="tpu_custom_call", output_to_operand_aliasing={{1}: (2, {}), {2}: (3, {}), {4}: (5, {}), {3}: (4, {})} | custom-call | flops 1711276032 | tf_op jit(solution)/shard_map/pallas_call | solution.py:159
  66.0 2.4 %shard_map.97 = (bf16[256,576]{1,0:T(8,128)(2,1)S(1)}, bf16[1536,2048]{1,0:T(8,128)(2,1)S(1)}, bf16[1536,2048]{1,0:T(8,128)(2,1)S(1)}, f32[4,1536,128]{2,1,0:T(8...) custom-call(bf16[576,1536]{1,0:T(8,128)(2,1)S(1)} %get-tuple-element, ...), custom_call_target="tpu_custom_call", output_to_operand_aliasing={{1}: (2, {}), {2}: (3, {}), {4}: (5, {}), {3}: (4, {})} | custom-call | flops 855638016 | tf_op jit(solution)/shard_map/pallas_call | solution.py:159
  68.4 4.3 %collective-permute-done.9.two_ref = bf16[256,576]{1,0:T(8,128)(2,1)S(1)} collective-permute-done((bf16[256,576]{1,0:T(8,128)(2,1)S(1)}, bf16[256,576]{1,0:T(8,128)(2,1)S(1)}, u32[]{:S(2)}, u32[]{:S(2)}) %collective-permute-start.9) | collective-permute-done | bytes 294944 | tf_op jit(solution)/shard_map/ppermute | solution.py:446
  72.6 0.0 collective-permute-done.8
  72.6 0.2 shard_map.98
  72.8 0.4 collective-permute-start.11
  73.2 1.5 %collective-permute-start.12 = (bf16[256,576]{1,0:T(8,128)(2,1)S(1)}, bf16[256,576]{1,0:T(8,128)(2,1)S(1)}, u32[]{:S(2)}, u32[]{:S(2)}) collective-permute-start(bf16[256,576]{1,0:T(8,128)(2,1)S(1)} %get-tuple-element.149), channel_id=1, source_target_pairs={{0,6},{1,7},{2,4},{3,5},{4,2},{5,3},{6,0},{7,1},{8,14},{9,15},{10,... | collective-permute-start | bytes 884744 | tf_op jit(solution)/shard_map/ppermute | solution.py:446
  74.7 6.4 %shard_map.99 = (bf16[96,16,512]{2,1,0:T(8,128)(2,1)}, bf16[96,16,576]{2,1,0:T(8,128)(2,1)}) custom-call(bf16[1536,2048]{1,0:T(8,128)(2,1)S(1)} %get-tuple-element.131.w_ref, bf16[1536,2048]{1,0:T(8,128)(2,1)S(1)} %get-tuple-element.132.s_ref, bf16[2048,576]{1,0:T(8,128)(2,1)S(1)} %get-tuple-element.139.k_ref), custom_call_target="tpu_custom_call" | custom-call | flops 4429185024 | tf_op jit(solution)/shard_map/pallas_call | solution.py:159
  81.1 0.0 collective-permute-done.10.b_ref
  81.1 2.2 %collective-permute-done.12.d_ref = bf16[256,576]{1,0:T(8,128)(2,1)S(1)} collective-permute-done((bf16[256,576]{1,0:T(8,128)(2,1)S(1)}, bf16[256,576]{1,0:T(8,128)(2,1)S(1)}, u32[]{:S(2)}, u32[]{:S(2)}) %collective-permute-start.12) | collective-permute-done | bytes 294944 | tf_op jit(solution)/shard_map/ppermute | solution.py:446
  83.3 0.0 collective-permute-done.11.c_ref
  83.3 1.7 %shard_map.100 = bf16[32,16,576]{2,1,0:T(8,128)(2,1)} custom-call(s32[16,16]{1,0:T(8,128)} %lists.5, s32[16]{0:T(128)} %counts.5, s32[1]{0:T(128)} %bitcast.me, bf16[256,576]{1,0:T(8,128)(2,1)S(1)} %get-tuple-element.148.a_ref, bf16[256,576]{1,0:T(8,128)(2,1)S(1)} %collective-permute-done.10.b_ref, bf16[256,576]{1,0:T(8,128)(2,1)S(1)} %collective-permute-done.11.c_ref, ...), custom_call_target="tpu_custom_call" | custom-call | tf_op jit(solution)/shard_map/pallas_call | solution.py:159
  85.0 3.8 %all-to-all-start.1 = ((bf16[16,2,16,576]{3,2,1,0:T(8,128)(2,1)}), bf16[16,2,16,576]{3,2,1,0:T(8,128)(2,1)S(1)}, u32[]{:S(2)}, u32[]{:S(2)}) async-start(bf16[16,2,16,576]{3,2,1,0:T(8,128)(2,1)} %bitcast.37), calls=%async_computation.1 | async-start | bytes 1310720 | tf_op jit(solution)/shard_map/all_to_all | solution.py:552
  88.8 8.6 %shard_map.101 = bf16[96,16,576]{2,1,0:T(8,128)(2,1)} custom-call(bf16[1,1024,256]{2,1,0:T(8,128)(2,1)} %get-tuple-element.141.refs_0_, bf16[1,1024,256]{2,1,0:T(8,128)(2,1)} %get-tuple-element.142.refs_1_, bf16[1,1024,256]{2,1,0:T(8,128)(2,1)} %get-tuple-element.143.refs_2_, ...), custom_call_target="tpu_custom_call", output_to_operand_aliasing={{}: (7, {})} | custom-call | flops 2415919104 | tf_op jit(solution)/shard_map/pallas_call | solution.py:159
  97.4 2.8 %all-to-all-done.1 = bf16[16,2,16,576]{3,2,1,0:T(8,128)(2,1)S(1)} async-done(((bf16[16,2,16,576]{3,2,1,0:T(8,128)(2,1)}), bf16[16,2,16,576]{3,2,1,0:T(8,128)(2,1)S(1)}, u32[]{:S(2)}, u32[]{:S(2)}) %all-to-all-start.1) | async-done | bytes 589856 | tf_op jit(solution)/shard_map/all_to_all | solution.py:552
  100.3 1.8 %shard_map.102 = f32[16,16,576]{2,1,0:T(8,128)} custom-call(s32[33]{0:T(128)} %get-tuple-element.152.table, bf16[32,16,576]{2,1,0:T(8,128)(2,1)S(1)} %bitcast.31), custom_call_target="tpu_custom_call" | custom-call | tf_op jit(solution)/shard_map/pallas_call | solution.py:159
  (7 shorter events, 0.0 us)
Async XLA Ops:
  3.8 21.1 %all-to-all-start = ((bf16[16,2,16,576]{3,2,1,0:T(8,128)(2,1)}), bf16[16,2,16,576]{3,2,1,0:T(8,128)(2,1)S(1)}, u32[]{:S(2)}, u32[]{:S(2)}) async-start(bf16[16,2,16,576]{3,2,1,0:T(8,128)(2,1)} %bitcast.38), calls=%async_computation | async-start | bytes 1310720 | tf_op jit(solution)/shard_map/all_to_all | solution.py:470
  26.0 3.2 %collective-permute-start.1 = (bf16[256,576]{1,0:T(8,128)(2,1)S(1)}, bf16[256,576]{1,0:T(8,128)(2,1)S(1)}, u32[]{:S(2)}, u32[]{:S(2)}) collective-permute-start(bf16[256,576]{1,0:T(8,128)(2,1)S(1)} %shard_map.86.refs_0_), channel_id=1, source_target_pairs={{0,1},{1,0},{2,3},{3,2},{4,5},{5,4},{6,7},{7,6},{8,9},{9,8},{10,11... | collective-permute-start | bytes 884744 | tf_op jit(solution)/shard_map/ppermute | solution.py:446
  26.1 11.3 %collective-permute-start.2 = (bf16[256,576]{1,0:T(8,128)(2,1)S(1)}, bf16[256,576]{1,0:T(8,128)(2,1)S(1)}, u32[]{:S(2)}, u32[]{:S(2)}) collective-permute-start(bf16[256,576]{1,0:T(8,128)(2,1)S(1)} %shard_map.86.refs_0_), channel_id=1, source_target_pairs={{0,6},{1,7},{2,4},{3,5},{4,2},{5,3},{6,0},{7,1},{8,14},{9,15},{10,... | collective-permute-start | bytes 884744 | tf_op jit(solution)/shard_map/ppermute | solution.py:446
  28.9 9.8 %collective-permute-start = (bf16[256,576]{1,0:T(8,128)(2,1)S(1)}, bf16[256,576]{1,0:T(8,128)(2,1)S(1)}, u32[]{:S(2)}, u32[]{:S(2)}) collective-permute-start(bf16[256,576]{1,0:T(8,128)(2,1)S(1)} %shard_map.86.refs_0_), channel_id=1, source_target_pairs={{0,2},{1,3},{2,0},{3,1},{4,6},{5,7},{6,4},{7,5},{8,10},{9,11},{10,... | collective-permute-start | bytes 884744 | tf_op jit(solution)/shard_map/ppermute | solution.py:446
  38.7 1.6 %collective-permute-start.3 = (bf16[256,576]{1,0:T(8,128)(2,1)S(1)}, bf16[256,576]{1,0:T(8,128)(2,1)S(1)}, u32[]{:S(2)}, u32[]{:S(2)}) collective-permute-start(bf16[256,576]{1,0:T(8,128)(2,1)S(1)} %collective-permute-done.refs_0_), channel_id=1, source_target_pairs={{0,1},{1,0},{2,3},{3,2},{4,5},{5,4},{6,7},{7,6},{8,9},{9,8},{10,11... | collective-permute-start | bytes 884744 | tf_op jit(solution)/shard_map/ppermute | solution.py:446
  38.7 2.1 %collective-permute-start.4 = (bf16[256,576]{1,0:T(8,128)(2,1)S(1)}, bf16[256,576]{1,0:T(8,128)(2,1)S(1)}, u32[]{:S(2)}, u32[]{:S(2)}) collective-permute-start(bf16[256,576]{1,0:T(8,128)(2,1)S(1)} %collective-permute-done.2.refs_1_), channel_id=1, source_target_pairs={{0,1},{1,0},{2,3},{3,2},{4,5},{5,4},{6,7},{7,6},{8,9},{9,8},{10,11... | collective-permute-start | bytes 884744 | tf_op jit(solution)/shard_map/ppermute | solution.py:446
  39.2 9.6 %collective-permute-start.5 = (bf16[256,576]{1,0:T(8,128)(2,1)S(1)}, bf16[256,576]{1,0:T(8,128)(2,1)S(1)}, u32[]{:S(2)}, u32[]{:S(2)}) collective-permute-start(bf16[256,576]{1,0:T(8,128)(2,1)S(1)} %collective-permute-done.2.refs_1_), channel_id=1, source_target_pairs={{0,2},{1,3},{2,0},{3,1},{4,6},{5,7},{6,4},{7,5},{8,10},{9,11},{10,... | collective-permute-start | bytes 884744 | tf_op jit(solution)/shard_map/ppermute | solution.py:446
  48.8 1.6 %collective-permute-start.6 = (bf16[256,576]{1,0:T(8,128)(2,1)S(1)}, bf16[256,576]{1,0:T(8,128)(2,1)S(1)}, u32[]{:S(2)}, u32[]{:S(2)}) collective-permute-start(bf16[256,576]{1,0:T(8,128)(2,1)S(1)} %collective-permute-done.5.refs_0_), channel_id=1, source_target_pairs={{0,1},{1,0},{2,3},{3,2},{4,5},{5,4},{6,7},{7,6},{8,9},{9,8},{10,11... | collective-permute-start | bytes 884744 | tf_op jit(solution)/shard_map/ppermute | solution.py:446
  55.4 4.0 %collective-permute-start.7 = (bf16[256,576]{1,0:T(8,128)(2,1)S(1)}, bf16[256,576]{1,0:T(8,128)(2,1)S(1)}, u32[]{:S(2)}, u32[]{:S(2)}) collective-permute-start(bf16[256,576]{1,0:T(8,128)(2,1)S(1)} %get-tuple-element.120), channel_id=1, source_target_pairs={{0,1},{1,0},{2,3},{3,2},{4,5},{5,4},{6,7},{7,6},{8,9},{9,8},{10,11... | collective-permute-start | bytes 884744 | tf_op jit(solution)/shard_map/ppermute | solution.py:446
  62.4 10.2 %collective-permute-start.8 = (bf16[32,16,576]{2,1,0:T(8,128)(2,1)S(1)}, bf16[32,16,576]{2,1,0:T(8,128)(2,1)S(1)}, u32[]{:S(2)}, u32[]{:S(2)}) collective-permute-start(bf16[32,16,576]{2,1,0:T(8,128)(2,1)S(1)} %bitcast.36), channel_id=1, source_target_pairs={{0,1},{1,0},{2,3},{3,2},{4,5},{5,4},{6,7},{7,6},{8,9},{9,8},{10,11... | collective-permute-start | bytes 1769480 | tf_op jit(solution)/shard_map/ppermute | solution.py:446
  62.7 9.9 %collective-permute-start.9 = (bf16[256,576]{1,0:T(8,128)(2,1)S(1)}, bf16[256,576]{1,0:T(8,128)(2,1)S(1)}, u32[]{:S(2)}, u32[]{:S(2)}) collective-permute-start(bf16[256,576]{1,0:T(8,128)(2,1)S(1)} %shard_map.94), channel_id=1, source_target_pairs={{0,2},{1,3},{2,0},{3,1},{4,6},{5,7},{6,4},{7,5},{8,10},{9,11},{10,... | collective-permute-start | bytes 884744 | tf_op jit(solution)/shard_map/ppermute | solution.py:446
  63.0 18.1 %collective-permute-start.10 = (bf16[256,576]{1,0:T(8,128)(2,1)S(1)}, bf16[256,576]{1,0:T(8,128)(2,1)S(1)}, u32[]{:S(2)}, u32[]{:S(2)}) collective-permute-start(bf16[256,576]{1,0:T(8,128)(2,1)S(1)} %get-tuple-element.118), channel_id=1, source_target_pairs={{0,1},{1,0},{2,3},{3,2},{4,5},{5,4},{6,7},{7,6},{8,9},{9,8},{10,11... | collective-permute-start | bytes 884744 | tf_op jit(solution)/shard_map/ppermute | solution.py:446
  72.8 10.4 %collective-permute-start.11 = (bf16[256,576]{1,0:T(8,128)(2,1)S(1)}, bf16[256,576]{1,0:T(8,128)(2,1)S(1)}, u32[]{:S(2)}, u32[]{:S(2)}) collective-permute-start(bf16[256,576]{1,0:T(8,128)(2,1)S(1)} %get-tuple-element.138), channel_id=1, source_target_pairs={{0,2},{1,3},{2,0},{3,1},{4,6},{5,7},{6,4},{7,5},{8,10},{9,11},{10,... | collective-permute-start | bytes 884744 | tf_op jit(solution)/shard_map/ppermute | solution.py:446
  73.2 10.1 %collective-permute-start.12 = (bf16[256,576]{1,0:T(8,128)(2,1)S(1)}, bf16[256,576]{1,0:T(8,128)(2,1)S(1)}, u32[]{:S(2)}, u32[]{:S(2)}) collective-permute-start(bf16[256,576]{1,0:T(8,128)(2,1)S(1)} %get-tuple-element.149), channel_id=1, source_target_pairs={{0,6},{1,7},{2,4},{3,5},{4,2},{5,3},{6,0},{7,1},{8,14},{9,15},{10,... | collective-permute-start | bytes 884744 | tf_op jit(solution)/shard_map/ppermute | solution.py:446
  85.0 15.3 %all-to-all-start.1 = ((bf16[16,2,16,576]{3,2,1,0:T(8,128)(2,1)}), bf16[16,2,16,576]{3,2,1,0:T(8,128)(2,1)S(1)}, u32[]{:S(2)}, u32[]{:S(2)}) async-start(bf16[16,2,16,576]{3,2,1,0:T(8,128)(2,1)} %bitcast.37), calls=%async_computation.1 | async-start | bytes 1310720 | tf_op jit(solution)/shard_map/all_to_all | solution.py:552

commit v9 on v8

--- a/solution.py
+++ b/solution.py
@@ -135,11 +135,15 @@
     out_ref[...] = (near_ref[...].astype(f32) + far_ref[...].astype(f32)).astype(bf16)
 
 
-def one_body(near_ref, far_ref, two_ref, a_ref, b_ref):
-    size = a_ref.shape[0]
-    total = near_ref[...].astype(f32) + far_ref[...].astype(f32)
-    a_ref[...] = total[:size].astype(bf16)
-    b_ref[...] = (total[size:] + two_ref[...].astype(f32)).astype(bf16)
+def wrap_body(near_ref, far_ref, out_ref):
+    size = out_ref.shape[0]
+    out_ref[...] = (near_ref[size:].astype(f32) + far_ref[size:].astype(f32)).astype(bf16)
+
+
+def next_body(near_ref, far_ref, two_ref, out_ref):
+    size = out_ref.shape[0]
+    total = near_ref[:size].astype(f32) + far_ref[:size].astype(f32)
+    out_ref[...] = (total + two_ref[...].astype(f32)).astype(bf16)
 
 
 ONCHIP = pl.BlockSpec(memory_space=pltpu.VMEM)
@@ -521,15 +525,15 @@
     near2, e, p, row, k, sg2n = back(2, (6 * keys,), keys, e=e, p=p, row=row, k=k)
     far0, e, p, row, k, sg0f = back(0, (keys,), keys, e=e, p=p, row=row, k=k)
     (two,) = call(two_body, (share_of(keys),), (), (after(near2, far0), mate2))
-    got_two = send(two, pair_a)
-    far1, e, p, row, k, sg1f = back(1, (4 * keys,), 2 * keys, e=e, p=p, row=after(row, two), k=k)
+    got_two = send(two, pair_b)
+    far1, e, p, row, k, sg1f, k_saved = back(1, (4 * keys,), 2 * keys, e=e, p=p, row=after(row, two), k=k, final=True)
     mate1 = unfold(send(fold(far1), sibling))
     near1, e, p, row, k, sg1n = back(1, (2 * keys,), 2 * keys, e=e, p=p, row=row, k=k)
     mate0 = send(far0, sibling)
-    near0, e, p, row, k, sg0n, k_saved = back(0, (0,), keys, e=e, p=p, row=row, k=k, final=True)
-    near1 = after(near1, near0)
-    to_a, to_b = call(one_body, (share_of(keys),) * 2, (), (near1, mate1, got_two))
+    (to_b,) = call(wrap_body, (share_of(keys),), (), (near1, mate1))
     got_b = send(to_b, pair_b)
+    near0, e, p, row, k, sg0n = back(0, (0,), keys, e=e, p=p, row=after(row, to_b), k=k)
+    (to_a,) = call(next_body, (share_of(keys),), (), (after(near1, near0), mate1, got_two))
     got_a = send(to_a, pair_a)
     attended, query_grad = value_side(e, p, after(k, to_a), early)
     near0 = after(near0, attended)

time: 103 us -> 102 us (level)
  starting transfers between devices: 19 us -> 20.2 us
  waiting for transfers between devices: 27.5 us -> 26.3 us
    ppermute x13, starting transfers between devices: 6.96 us -> 8.22 us  [per_device(): send = lambda a, perm: lax.ppermute(a, 'head', perm)]
    pallas_call x18 -> x19, Pallas kernels: 50.9 us -> 50.1 us  [call(): pl.pallas_call(body, in_specs=[small] * len(scalars) + [INPLACE if i in d...]
where the time goes in v9:
time: 102 us
  Pallas kernels  50.1 us (49%)
  waiting for transfers between devices  26.3 us (26%)
  starting transfers between devices  20.2 us (20%)
  local copies, waits for them, and re-layouts  2.28 us (2%)
  other arithmetic  1.59 us (2%)
  between operations  1.07 us (1%)
    pallas_call x19, Pallas kernels, call(): pl.pallas_call(body, in_specs=[small] * len(scalars) + [INPLACE if i in d...  50.1 us
    ppermute x13, waiting for transfers between devices, per_device(): send = lambda a, perm: lax.ppermute(a, 'head', perm)  14.9 us
    all_to_all x1, waiting for transfers between devices, per_device(): lax.all_to_all(outgoing.reshape(16, CAP, tokens, WIDE), 'req', 0, 0, tile...  8.95 us
    ppermute x13, starting transfers between devices, per_device(): send = lambda a, perm: lax.ppermute(a, 'head', perm)  8.22 us
    all_to_all x1, starting transfers between devices, per_device(): lax.all_to_all(outgoing.reshape(16, CAP, tokens, WIDE), 'req', 0, 0, tile...  8.17 us
    all_to_all x1, starting transfers between devices, per_device(): lax.all_to_all(slot_grads.reshape(16, CAP, tokens, WIDE), 'req', 0, 0, ti...  3.83 us
    all_to_all x1, waiting for transfers between devices, per_device(): lax.all_to_all(slot_grads.reshape(16, CAP, tokens, WIDE), 'req', 0, 0, ti...  2.39 us
  transfers between devices with their start and end apart: 15, of which 10 were waited for; matrix products, arithmetic and copies ran while one was open for 4% of the time, Pallas kernels for 34%

profile of v9, /device:TPU:0, one launch (start us, length us, event | category | flops | bytes accessed | tf_op | source)
XLA Modules:
  0.0 101.6 jit_solution(11088784202329447148)
XLA Ops:
  0.6 3.2 %shard_map.85 = (bf16[32,16,576]{2,1,0:T(8,128)(2,1)}, s32[33]{0:T(128)}) custom-call(s32[16,16]{1,0:T(8,128)} %lists.5, s32[16]{0:T(128)} %counts.5, s32[1]{0:T(128)} %bitcast.me, bf16[16,16,576]{2,1,0:T(8,128)(2,1)} %lat_ref.1), custom_call_target="tpu_custom_call" | custom-call | tf_op jit(solution)/shard_map/pallas_call | solution.py:163
  3.8 8.2 %all-to-all-start = ((bf16[16,2,16,576]{3,2,1,0:T(8,128)(2,1)}), bf16[16,2,16,576]{3,2,1,0:T(8,128)(2,1)S(1)}, u32[]{:S(2)}, u32[]{:S(2)}) async-start(bf16[16,2,16,576]{3,2,1,0:T(8,128)(2,1)} %bitcast.39), calls=%async_computation | async-start | bytes 1310720 | tf_op jit(solution)/shard_map/all_to_all | solution.py:474
  12.0 1.2 %dynamic_slice.8 = s32[1]{0:T(128)} dynamic-slice(s32[16]{0:T(128)} %counts.5, s32[]{:T(128)S(6)} %select_n.31), dynamic_slice_sizes={1} | dynamic-slice | bytes 12 | tf_op jit(solution)/shard_map/jit(dynamic_index_in_dim)/dynamic_slice | solution.py:477
  13.3 0.7 dynamic-slice_bitcast_fusion
  14.0 0.1 stack.35
  14.1 0.9 select_reduce_fusion
  14.9 0.7 compare_select_fusion
  15.6 0.1 broadcast_in_dim.34
  15.7 0.1 lt.32
  15.7 0.1 add.60
  15.8 0.1 fusion
  15.9 9.0 %all-to-all-done = bf16[16,2,16,576]{3,2,1,0:T(8,128)(2,1)S(1)} async-done(((bf16[16,2,16,576]{3,2,1,0:T(8,128)(2,1)}), bf16[16,2,16,576]{3,2,1,0:T(8,128)(2,1)S(1)}, u32[]{:S(2)}, u32[]{:S(2)}) %all-to-all-start) | async-done | bytes 589856 | tf_op jit(solution)/shard_map/all_to_all | solution.py:474
  24.9 1.1 %shard_map.86.refs_0_ = bf16[256,576]{1,0:T(8,128)(2,1)S(1)} custom-call(s32[16,16]{1,0:T(8,128)} %lists.5, s32[16]{0:T(128)} %counts.5, s32[1]{0:T(128)} %bitcast.me, bf16[32,16,576]{2,1,0:T(8,128)(2,1)S(1)} %bitcast.30), custom_call_target="tpu_custom_call" | custom-call | tf_op jit(solution)/shard_map/pallas_call | solution.py:163
  26.0 0.1 collective-permute-start.1
  26.1 2.8 %collective-permute-start.2 = (bf16[256,576]{1,0:T(8,128)(2,1)S(1)}, bf16[256,576]{1,0:T(8,128)(2,1)S(1)}, u32[]{:S(2)}, u32[]{:S(2)}) collective-permute-start(bf16[256,576]{1,0:T(8,128)(2,1)S(1)} %shard_map.86.refs_0_), channel_id=1, source_target_pairs={{0,6},{1,7},{2,4},{3,5},{4,2},{5,3},{6,0},{7,1},{8,14},{9,15},{10,... | collective-permute-start | bytes 884744 | tf_op jit(solution)/shard_map/ppermute | solution.py:450
  28.9 0.2 collective-permute-start
  29.1 0.0 collective-permute-done.1.refs_1_
  29.1 4.4 %shard_map.87 = (bf16[1536,2048]{1,0:T(8,128)(2,1)S(1)}, bf16[1536,2048]{1,0:T(8,128)(2,1)S(1)}, bf16[2048,576]{1,0:T(8,128)(2,1)S(1)}, f32[9,1536,128]{2,1,0:T(...) custom-call(bf16[256,576]{1,0:T(8,128)(2,1)S(1)} %shard_map.86.refs_0_, ...), custom_call_target="tpu_custom_call" | custom-call | flops 1711276032 | tf_op jit(solution)/shard_map/pallas_call | solution.py:163
  33.5 3.9 %collective-permute-done.2.refs_1_ = bf16[256,576]{1,0:T(8,128)(2,1)S(1)} collective-permute-done((bf16[256,576]{1,0:T(8,128)(2,1)S(1)}, bf16[256,576]{1,0:T(8,128)(2,1)S(1)}, u32[]{:S(2)}, u32[]{:S(2)}) %collective-permute-start.2) | collective-permute-done | bytes 294944 | tf_op jit(solution)/shard_map/ppermute | solution.py:450
  37.4 1.3 %collective-permute-done.refs_0_ = bf16[256,576]{1,0:T(8,128)(2,1)S(1)} collective-permute-done((bf16[256,576]{1,0:T(8,128)(2,1)S(1)}, bf16[256,576]{1,0:T(8,128)(2,1)S(1)}, u32[]{:S(2)}, u32[]{:S(2)}) %collective-permute-start) | collective-permute-done | bytes 294944 | tf_op jit(solution)/shard_map/ppermute | solution.py:450
  38.7 0.0 collective-permute-start.3
  38.7 0.5 collective-permute-start.4
  39.2 0.3 collective-permute-start.5
  39.5 0.8 collective-permute-done.3.refs_2_
  40.3 0.5 collective-permute-done.4.refs_3_
  40.8 5.5 %shard_map.88 = (bf16[1536,2048]{1,0:T(8,128)(2,1)S(1)}, bf16[1536,2048]{1,0:T(8,128)(2,1)S(1)}, bf16[2048,576]{1,0:T(8,128)(2,1)S(1)}, f32[9,1536,128]{2,1,0:T(...) custom-call(bf16[256,576]{1,0:T(8,128)(2,1)S(1)} %collective-permute, ...), custom_call_target="tpu_custom_call", output_to_operand_aliasing={{0}: (5, {}), {1}: (6, {}), {2}: (7, {}), {3}: (8, {}), {4}... | custom-call | flops 3422552064 | tf_op jit(solution)/shard_map/pallas_call | solution.py:163
  46.3 2.5 %collective-permute-done.5.refs_0_ = bf16[256,576]{1,0:T(8,128)(2,1)S(1)} collective-permute-done((bf16[256,576]{1,0:T(8,128)(2,1)S(1)}, bf16[256,576]{1,0:T(8,128)(2,1)S(1)}, u32[]{:S(2)}, u32[]{:S(2)}) %collective-permute-start.5) | collective-permute-done | bytes 294944 | tf_op jit(solution)/shard_map/ppermute | solution.py:450
  48.8 0.0 collective-permute-start.6
  48.8 1.4 %shard_map.89 = (bf16[576,1536]{1,0:T(8,128)(2,1)S(1)}, bf16[512,1536]{1,0:T(8,128)(2,1)S(1)}) custom-call(bf16[96,16,576]{2,1,0:T(8,128)(2,1)S(1)} %get-tuple-element.89.q_ref.refs_7_, bf16[96,16,512]{2,1,0:T(8,128)(2,1)S(1)} %get-tuple-element.93.g_ref.refs_8_), custom_call_target="tpu_custom_call" | custom-call | tf_op jit(solution)/shard_map/pallas_call | solution.py:163
  50.2 0.2 collective-permute-done.6.refs_1_
  50.4 2.8 %shard_map.90 = (bf16[1536,2048]{1,0:T(8,128)(2,1)S(1)}, bf16[1536,2048]{1,0:T(8,128)(2,1)S(1)}, bf16[2048,576]{1,0:T(8,128)(2,1)S(1)}, f32[9,1536,128]{2,1,0:T(...) custom-call(bf16[256,576]{1,0:T(8,128)(2,1)S(1)} %collective-permute, ...), custom_call_target="tpu_custom_call", output_to_operand_aliasing={{0}: (3, {}), {1}: (4, {}), {2}: (5, {}), {3}: (6, {}), {4}... | custom-call | flops 1711276032 | tf_op jit(solution)/shard_map/pallas_call | solution.py:163
  53.2 2.2 %shard_map.91 = (bf16[256,576]{1,0:T(8,128)(2,1)S(1)}, bf16[1536,2048]{1,0:T(8,128)(2,1)S(1)}, bf16[1536,2048]{1,0:T(8,128)(2,1)S(1)}, f32[4,1536,128]{2,1,0:T(8...) custom-call(bf16[576,1536]{1,0:T(8,128)(2,1)S(1)} %get-tuple-element, ...), custom_call_target="tpu_custom_call", output_to_operand_aliasing={{1}: (2, {}), {2}: (3, {}), {4}: (5, {})} | custom-call | flops 855638016 | tf_op jit(solution)/shard_map/pallas_call | solution.py:163
  55.4 0.6 collective-permute-start.7
  56.0 1.7 %shard_map.92 = (bf16[256,576]{1,0:T(8,128)(2,1)S(1)}, bf16[1536,2048]{1,0:T(8,128)(2,1)S(1)}, bf16[1536,2048]{1,0:T(8,128)(2,1)S(1)}, f32[4,1536,128]{2,1,0:T(8...) custom-call(bf16[576,1536]{1,0:T(8,128)(2,1)S(1)} %get-tuple-element, ...), custom_call_target="tpu_custom_call", output_to_operand_aliasing={{1}: (2, {}), {2}: (3, {}), {4}: (5, {}), {3}: (4, {})} | custom-call | flops 855638016 | tf_op jit(solution)/shard_map/pallas_call | solution.py:163
  57.7 1.7 %shard_map.93 = (bf16[256,576]{1,0:T(8,128)(2,1)S(1)}, bf16[1536,2048]{1,0:T(8,128)(2,1)S(1)}, bf16[1536,2048]{1,0:T(8,128)(2,1)S(1)}, f32[4,1536,128]{2,1,0:T(8...) custom-call(bf16[576,1536]{1,0:T(8,128)(2,1)S(1)} %get-tuple-element, ...), custom_call_target="tpu_custom_call", output_to_operand_aliasing={{1}: (2, {}), {2}: (3, {}), {4}: (5, {}), {3}: (4, {})} | custom-call | flops 855638016 | tf_op jit(solution)/shard_map/pallas_call | solution.py:163
  59.4 0.0 collective-permute-done.7.far_ref
  59.4 0.1 shard_map.94
  59.5 2.9 %shard_map.95 = (bf16[512,576]{1,0:T(8,128)(2,1)S(1)}, bf16[1536,2048]{1,0:T(8,128)(2,1)S(1)}, bf16[1536,2048]{1,0:T(8,128)(2,1)S(1)}, f32[4,1536,128]{2,1,0:T(8...) custom-call(bf16[576,1536]{1,0:T(8,128)(2,1)S(1)} %get-tuple-element, ...), custom_call_target="tpu_custom_call", output_to_operand_aliasing={{1}: (2, {}), {2}: (3, {}), {4}: (5, {}), {3}: (4, {})} | custom-call | flops 1711276032 | tf_op jit(solution)/shard_map/pallas_call | solution.py:163
  62.4 0.3 collective-permute-start.8
  62.7 1.5 %collective-permute-start.9 = (bf16[256,576]{1,0:T(8,128)(2,1)S(1)}, bf16[256,576]{1,0:T(8,128)(2,1)S(1)}, u32[]{:S(2)}, u32[]{:S(2)}) collective-permute-start(bf16[256,576]{1,0:T(8,128)(2,1)S(1)} %shard_map.94), channel_id=1, source_target_pairs={{0,6},{1,7},{2,4},{3,5},{4,2},{5,3},{6,0},{7,1},{8,14},{9,15},{10,... | collective-permute-start | bytes 884744 | tf_op jit(solution)/shard_map/ppermute | solution.py:450
  64.2 0.0 collective-permute-start.10
  64.2 2.9 %shard_map.96 = (bf16[512,576]{1,0:T(8,128)(2,1)S(1)}, bf16[1536,2048]{1,0:T(8,128)(2,1)S(1)}, bf16[1536,2048]{1,0:T(8,128)(2,1)S(1)}, f32[4,1536,128]{2,1,0:T(8...) custom-call(bf16[576,1536]{1,0:T(8,128)(2,1)S(1)} %get-tuple-element, ...), custom_call_target="tpu_custom_call", output_to_operand_aliasing={{1}: (2, {}), {2}: (3, {}), {4}: (5, {}), {3}: (4, {})} | custom-call | flops 1711276032 | tf_op jit(solution)/shard_map/pallas_call | solution.py:163
  67.1 0.0 collective-permute-done.8
  67.2 0.1 shard_map.97
  67.2 1.8 %collective-permute-start.12 = (bf16[256,576]{1,0:T(8,128)(2,1)S(1)}, bf16[256,576]{1,0:T(8,128)(2,1)S(1)}, u32[]{:S(2)}, u32[]{:S(2)}) collective-permute-start(bf16[256,576]{1,0:T(8,128)(2,1)S(1)} %shard_map.97), channel_id=1, source_target_pairs={{0,6},{1,7},{2,4},{3,5},{4,2},{5,3},{6,0},{7,1},{8,14},{9,15},{10,... | collective-permute-start | bytes 884744 | tf_op jit(solution)/shard_map/ppermute | solution.py:450
  69.1 1.7 %shard_map.98 = (bf16[256,576]{1,0:T(8,128)(2,1)S(1)}, bf16[1536,2048]{1,0:T(8,128)(2,1)S(1)}, bf16[1536,2048]{1,0:T(8,128)(2,1)S(1)}, f32[4,1536,128]{2,1,0:T(8...) custom-call(bf16[576,1536]{1,0:T(8,128)(2,1)S(1)} %get-tuple-element, ...), custom_call_target="tpu_custom_call", output_to_operand_aliasing={{1}: (2, {}), {2}: (3, {}), {4}: (5, {}), {3}: (4, {})} | custom-call | flops 855638016 | tf_op jit(solution)/shard_map/pallas_call | solution.py:163
  70.8 3.7 %collective-permute-done.9.two_ref = bf16[256,576]{1,0:T(8,128)(2,1)S(1)} collective-permute-done((bf16[256,576]{1,0:T(8,128)(2,1)S(1)}, bf16[256,576]{1,0:T(8,128)(2,1)S(1)}, u32[]{:S(2)}, u32[]{:S(2)}) %collective-permute-start.9) | collective-permute-done | bytes 294944 | tf_op jit(solution)/shard_map/ppermute | solution.py:450
  74.5 0.1 shard_map.99
  74.6 0.1 collective-permute-start.11
  74.7 6.4 %shard_map.100 = (bf16[96,16,512]{2,1,0:T(8,128)(2,1)}, bf16[96,16,576]{2,1,0:T(8,128)(2,1)}) custom-call(bf16[1536,2048]{1,0:T(8,128)(2,1)S(1)} %get-tuple-element.133.w_ref, bf16[1536,2048]{1,0:T(8,128)(2,1)S(1)} %get-tuple-element.134.s_ref, bf16[2048,576]{1,0:T(8,128)(2,1)S(1)} %get-tuple-element.138.k_ref), custom_call_target="tpu_custom_call" | custom-call | flops 4429185024 | tf_op jit(solution)/shard_map/pallas_call | solution.py:163
  81.1 0.0 collective-permute-done.10.b_ref
  81.1 2.0 %collective-permute-done.11.c_ref = bf16[256,576]{1,0:T(8,128)(2,1)S(1)} collective-permute-done((bf16[256,576]{1,0:T(8,128)(2,1)S(1)}, bf16[256,576]{1,0:T(8,128)(2,1)S(1)}, u32[]{:S(2)}, u32[]{:S(2)}) %collective-permute-start.11) | collective-permute-done | bytes 294944 | tf_op jit(solution)/shard_map/ppermute | solution.py:450
  83.1 0.0 collective-permute-done.12.d_ref
  83.1 1.7 %shard_map.101 = bf16[32,16,576]{2,1,0:T(8,128)(2,1)} custom-call(s32[16,16]{1,0:T(8,128)} %lists.5, s32[16]{0:T(128)} %counts.5, s32[1]{0:T(128)} %bitcast.me, bf16[256,576]{1,0:T(8,128)(2,1)S(1)} %get-tuple-element.147.a_ref, bf16[256,576]{1,0:T(8,128)(2,1)S(1)} %collective-permute-done.10.b_ref, bf16[256,576]{1,0:T(8,128)(2,1)S(1)} %collective-permute-done.11.c_ref, ...), custom_call_target="tpu_custom_call" | custom-call | tf_op jit(solution)/shard_map/pallas_call | solution.py:163
  84.8 3.8 %all-to-all-start.1 = ((bf16[16,2,16,576]{3,2,1,0:T(8,128)(2,1)}), bf16[16,2,16,576]{3,2,1,0:T(8,128)(2,1)S(1)}, u32[]{:S(2)}, u32[]{:S(2)}) async-start(bf16[16,2,16,576]{3,2,1,0:T(8,128)(2,1)} %bitcast.38), calls=%async_computation.1 | async-start | bytes 1310720 | tf_op jit(solution)/shard_map/all_to_all | solution.py:556
  88.6 8.6 %shard_map.102 = bf16[96,16,576]{2,1,0:T(8,128)(2,1)} custom-call(bf16[1,1024,256]{2,1,0:T(8,128)(2,1)} %get-tuple-element.140.refs_0_, bf16[1,1024,256]{2,1,0:T(8,128)(2,1)} %get-tuple-element.141.refs_1_, bf16[1,1024,256]{2,1,0:T(8,128)(2,1)} %get-tuple-element.142.refs_2_, ...), custom_call_target="tpu_custom_call", output_to_operand_aliasing={{}: (7, {})} | custom-call | flops 2415919104 | tf_op jit(solution)/shard_map/pallas_call | solution.py:163
  97.2 2.4 %all-to-all-done.1 = bf16[16,2,16,576]{3,2,1,0:T(8,128)(2,1)S(1)} async-done(((bf16[16,2,16,576]{3,2,1,0:T(8,128)(2,1)}), bf16[16,2,16,576]{3,2,1,0:T(8,128)(2,1)S(1)}, u32[]{:S(2)}, u32[]{:S(2)}) %all-to-all-start.1) | async-done | bytes 589856 | tf_op jit(solution)/shard_map/all_to_all | solution.py:556
  99.6 1.8 %shard_map.103 = f32[16,16,576]{2,1,0:T(8,128)} custom-call(s32[33]{0:T(128)} %get-tuple-element.150.table, bf16[32,16,576]{2,1,0:T(8,128)(2,1)S(1)} %bitcast.33), custom_call_target="tpu_custom_call" | custom-call | tf_op jit(solution)/shard_map/pallas_call | solution.py:163
  (7 shorter events, 0.0 us)
Async XLA Ops:
  3.8 21.1 %all-to-all-start = ((bf16[16,2,16,576]{3,2,1,0:T(8,128)(2,1)}), bf16[16,2,16,576]{3,2,1,0:T(8,128)(2,1)S(1)}, u32[]{:S(2)}, u32[]{:S(2)}) async-start(bf16[16,2,16,576]{3,2,1,0:T(8,128)(2,1)} %bitcast.39), calls=%async_computation | async-start | bytes 1310720 | tf_op jit(solution)/shard_map/all_to_all | solution.py:474
  26.0 3.2 %collective-permute-start.1 = (bf16[256,576]{1,0:T(8,128)(2,1)S(1)}, bf16[256,576]{1,0:T(8,128)(2,1)S(1)}, u32[]{:S(2)}, u32[]{:S(2)}) collective-permute-start(bf16[256,576]{1,0:T(8,128)(2,1)S(1)} %shard_map.86.refs_0_), channel_id=1, source_target_pairs={{0,1},{1,0},{2,3},{3,2},{4,5},{5,4},{6,7},{7,6},{8,9},{9,8},{10,11... | collective-permute-start | bytes 884744 | tf_op jit(solution)/shard_map/ppermute | solution.py:450
  26.1 11.3 %collective-permute-start.2 = (bf16[256,576]{1,0:T(8,128)(2,1)S(1)}, bf16[256,576]{1,0:T(8,128)(2,1)S(1)}, u32[]{:S(2)}, u32[]{:S(2)}) collective-permute-start(bf16[256,576]{1,0:T(8,128)(2,1)S(1)} %shard_map.86.refs_0_), channel_id=1, source_target_pairs={{0,6},{1,7},{2,4},{3,5},{4,2},{5,3},{6,0},{7,1},{8,14},{9,15},{10,... | collective-permute-start | bytes 884744 | tf_op jit(solution)/shard_map/ppermute | solution.py:450
  28.9 9.8 %collective-permute-start = (bf16[256,576]{1,0:T(8,128)(2,1)S(1)}, bf16[256,576]{1,0:T(8,128)(2,1)S(1)}, u32[]{:S(2)}, u32[]{:S(2)}) collective-permute-start(bf16[256,576]{1,0:T(8,128)(2,1)S(1)} %shard_map.86.refs_0_), channel_id=1, source_target_pairs={{0,2},{1,3},{2,0},{3,1},{4,6},{5,7},{6,4},{7,5},{8,10},{9,11},{10,... | collective-permute-start | bytes 884744 | tf_op jit(solution)/shard_map/ppermute | solution.py:450
  38.7 1.6 %collective-permute-start.3 = (bf16[256,576]{1,0:T(8,128)(2,1)S(1)}, bf16[256,576]{1,0:T(8,128)(2,1)S(1)}, u32[]{:S(2)}, u32[]{:S(2)}) collective-permute-start(bf16[256,576]{1,0:T(8,128)(2,1)S(1)} %collective-permute-done.refs_0_), channel_id=1, source_target_pairs={{0,1},{1,0},{2,3},{3,2},{4,5},{5,4},{6,7},{7,6},{8,9},{9,8},{10,11... | collective-permute-start | bytes 884744 | tf_op jit(solution)/shard_map/ppermute | solution.py:450
  38.7 2.1 %collective-permute-start.4 = (bf16[256,576]{1,0:T(8,128)(2,1)S(1)}, bf16[256,576]{1,0:T(8,128)(2,1)S(1)}, u32[]{:S(2)}, u32[]{:S(2)}) collective-permute-start(bf16[256,576]{1,0:T(8,128)(2,1)S(1)} %collective-permute-done.2.refs_1_), channel_id=1, source_target_pairs={{0,1},{1,0},{2,3},{3,2},{4,5},{5,4},{6,7},{7,6},{8,9},{9,8},{10,11... | collective-permute-start | bytes 884744 | tf_op jit(solution)/shard_map/ppermute | solution.py:450
  39.2 9.6 %collective-permute-start.5 = (bf16[256,576]{1,0:T(8,128)(2,1)S(1)}, bf16[256,576]{1,0:T(8,128)(2,1)S(1)}, u32[]{:S(2)}, u32[]{:S(2)}) collective-permute-start(bf16[256,576]{1,0:T(8,128)(2,1)S(1)} %collective-permute-done.2.refs_1_), channel_id=1, source_target_pairs={{0,2},{1,3},{2,0},{3,1},{4,6},{5,7},{6,4},{7,5},{8,10},{9,11},{10,... | collective-permute-start | bytes 884744 | tf_op jit(solution)/shard_map/ppermute | solution.py:450
  48.8 1.6 %collective-permute-start.6 = (bf16[256,576]{1,0:T(8,128)(2,1)S(1)}, bf16[256,576]{1,0:T(8,128)(2,1)S(1)}, u32[]{:S(2)}, u32[]{:S(2)}) collective-permute-start(bf16[256,576]{1,0:T(8,128)(2,1)S(1)} %collective-permute-done.5.refs_0_), channel_id=1, source_target_pairs={{0,1},{1,0},{2,3},{3,2},{4,5},{5,4},{6,7},{7,6},{8,9},{9,8},{10,11... | collective-permute-start | bytes 884744 | tf_op jit(solution)/shard_map/ppermute | solution.py:450
  55.4 4.0 %collective-permute-start.7 = (bf16[256,576]{1,0:T(8,128)(2,1)S(1)}, bf16[256,576]{1,0:T(8,128)(2,1)S(1)}, u32[]{:S(2)}, u32[]{:S(2)}) collective-permute-start(bf16[256,576]{1,0:T(8,128)(2,1)S(1)} %get-tuple-element.119), channel_id=1, source_target_pairs={{0,1},{1,0},{2,3},{3,2},{4,5},{5,4},{6,7},{7,6},{8,9},{9,8},{10,11... | collective-permute-start | bytes 884744 | tf_op jit(solution)/shard_map/ppermute | solution.py:450
  62.4 4.7 %collective-permute-start.8 = (bf16[32,16,576]{2,1,0:T(8,128)(2,1)S(1)}, bf16[32,16,576]{2,1,0:T(8,128)(2,1)S(1)}, u32[]{:S(2)}, u32[]{:S(2)}) collective-permute-start(bf16[32,16,576]{2,1,0:T(8,128)(2,1)S(1)} %bitcast.37), channel_id=1, source_target_pairs={{0,1},{1,0},{2,3},{3,2},{4,5},{5,4},{6,7},{7,6},{8,9},{9,8},{10,11... | collective-permute-start | bytes 1769480 | tf_op jit(solution)/shard_map/ppermute | solution.py:450
  62.7 11.8 %collective-permute-start.9 = (bf16[256,576]{1,0:T(8,128)(2,1)S(1)}, bf16[256,576]{1,0:T(8,128)(2,1)S(1)}, u32[]{:S(2)}, u32[]{:S(2)}) collective-permute-start(bf16[256,576]{1,0:T(8,128)(2,1)S(1)} %shard_map.94), channel_id=1, source_target_pairs={{0,6},{1,7},{2,4},{3,5},{4,2},{5,3},{6,0},{7,1},{8,14},{9,15},{10,... | collective-permute-start | bytes 884744 | tf_op jit(solution)/shard_map/ppermute | solution.py:450
  64.2 16.9 %collective-permute-start.10 = (bf16[256,576]{1,0:T(8,128)(2,1)S(1)}, bf16[256,576]{1,0:T(8,128)(2,1)S(1)}, u32[]{:S(2)}, u32[]{:S(2)}) collective-permute-start(bf16[256,576]{1,0:T(8,128)(2,1)S(1)} %get-tuple-element.117), channel_id=1, source_target_pairs={{0,1},{1,0},{2,3},{3,2},{4,5},{5,4},{6,7},{7,6},{8,9},{9,8},{10,11... | collective-permute-start | bytes 884744 | tf_op jit(solution)/shard_map/ppermute | solution.py:450
  67.2 15.9 %collective-permute-start.12 = (bf16[256,576]{1,0:T(8,128)(2,1)S(1)}, bf16[256,576]{1,0:T(8,128)(2,1)S(1)}, u32[]{:S(2)}, u32[]{:S(2)}) collective-permute-start(bf16[256,576]{1,0:T(8,128)(2,1)S(1)} %shard_map.97), channel_id=1, source_target_pairs={{0,6},{1,7},{2,4},{3,5},{4,2},{5,3},{6,0},{7,1},{8,14},{9,15},{10,... | collective-permute-start | bytes 884744 | tf_op jit(solution)/shard_map/ppermute | solution.py:450
  74.6 8.5 %collective-permute-start.11 = (bf16[256,576]{1,0:T(8,128)(2,1)S(1)}, bf16[256,576]{1,0:T(8,128)(2,1)S(1)}, u32[]{:S(2)}, u32[]{:S(2)}) collective-permute-start(bf16[256,576]{1,0:T(8,128)(2,1)S(1)} %shard_map.99), channel_id=1, source_target_pairs={{0,2},{1,3},{2,0},{3,1},{4,6},{5,7},{6,4},{7,5},{8,10},{9,11},{10,... | collective-permute-start | bytes 884744 | tf_op jit(solution)/shard_map/ppermute | solution.py:450
  84.8 14.9 %all-to-all-start.1 = ((bf16[16,2,16,576]{3,2,1,0:T(8,128)(2,1)}), bf16[16,2,16,576]{3,2,1,0:T(8,128)(2,1)S(1)}, u32[]{:S(2)}, u32[]{:S(2)}) async-start(bf16[16,2,16,576]{3,2,1,0:T(8,128)(2,1)} %bitcast.38), calls=%async_computation.1 | async-start | bytes 1310720 | tf_op jit(solution)/shard_map/all_to_all | solution.py:556

commit v10 on v9

--- a/solution.py
+++ b/solution.py
@@ -27,7 +27,7 @@
     return lax.dot_general(a, b, dims, preferred_element_type=f32)
 
 
-def owner_table(lists, counts, own, table, empty):
+def owner_table(lists, counts, own, table, empty, low=0, high=16):
     def group(g, carry):
         table[g * CAP] = empty
         table[g * CAP + 1] = empty
@@ -39,7 +39,7 @@
             rank = jnp.where(mine, jnp.minimum(rank + 1, CAP - 1), rank)
         return carry
 
-    lax.fori_loop(0, 16, group, 0)
+    lax.fori_loop(low, high, group, 0)
 
 
 def slot_table(lists, own, table, seen):
@@ -55,15 +55,16 @@
 def pick_body(lists, counts, me, lat_ref, out_ref, table, lat, held, sem, sems):
     load = pltpu.make_async_copy(lat_ref, lat, sem.at[0])
     load.start()
-    owner_table(lists, counts, me[0], table, 16)
-    load.wait()
     step = SLOTS // 4
     parts = [slice(i * step, i * step + step) for i in range(4)]
     copies = [pltpu.make_async_copy(held.at[p], out_ref.at[p], sems.at[i]) for i, p in enumerate(parts)]
-    for s in range(SLOTS):
-        held[s] = lat[table[s] & 15]
-        if s % step == step - 1:
-            copies[s // step].start()
+    for i, copy in enumerate(copies):
+        owner_table(lists, counts, me[0], table, 16, 4 * i, 4 * i + 4)
+        if i == 0:
+            load.wait()
+        for s in range(i * step, i * step + step):
+            held[s] = lat[table[s] & 15]
+        copy.start()
     for copy in copies:
         copy.wait()
 
@@ -206,11 +207,12 @@
         here = pl.ds(pl.multiple_of(i * block, block), block)
         part = pl.ds(i * (block // 16), block // 16)
         if first:
-            for copy in loads(i):
-                copy.wait()
+            loads(i)[0].wait()
         scores = dot(q_ref[part].reshape(block, WIDE), k_out[mine], NT) + bias[...]
         top = jnp.max(scores, axis=1, keepdims=True)
         expo = jnp.exp2((scores - top) * EXPC)
+        if first:
+            loads(i)[1].wait()
         grads = dot(g_ref[part].reshape(block, LAT), k_out[mine, :LAT], NT)
         e_out[here, mine] = expo.astype(bf16)
         p_out[here, mine] = grads.astype(bf16)
@@ -532,9 +534,9 @@
     mate0 = send(far0, sibling)
     (to_b,) = call(wrap_body, (share_of(keys),), (), (near1, mate1))
     got_b = send(to_b, pair_b)
-    near0, e, p, row, k, sg0n = back(0, (0,), keys, e=e, p=p, row=after(row, to_b), k=k)
-    (to_a,) = call(next_body, (share_of(keys),), (), (after(near1, near0), mate1, got_two))
+    (to_a,) = call(next_body, (share_of(keys),), (), (after(near1, to_b), mate1, got_two))
     got_a = send(to_a, pair_a)
+    near0, e, p, row, k, sg0n = back(0, (0,), keys, e=e, p=p, row=after(row, to_a), k=k)
     attended, query_grad = value_side(e, p, after(k, to_a), early)
     near0 = after(near0, attended)
     (slot_grads,) = call(

time: 102 us -> 103 us (level)
  Pallas kernels: 50.1 us -> 51.8 us
    pallas_call x19, Pallas kernels: 50.1 us -> 51.8 us  [call(): pl.pallas_call(body, in_specs=[small] * len(scalars) + [INPLACE if i in d...]
    ppermute x13, waiting for transfers between devices: 14.9 us -> 13.9 us  [per_device(): send = lambda a, perm: lax.ppermute(a, 'head', perm)]
  transfers between devices with their start and end apart: 15 -> 15, of which waited for: 10 -> 10; matrix products, arithmetic and copies ran while one was open for 4% -> 4% of each run, Pallas kernels for 34% -> 35%
where the time goes in v10:
time: 103 us
  Pallas kernels  51.8 us (50%)
  waiting for transfers between devices  25.8 us (25%)
  starting transfers between devices  20.2 us (20%)
  local copies, waits for them, and re-layouts  2.28 us (2%)
  other arithmetic  1.59 us (2%)
  between operations  1.07 us (1%)
    pallas_call x19, Pallas kernels, call(): pl.pallas_call(body, in_specs=[small] * len(scalars) + [INPLACE if i in d...  51.8 us
    ppermute x13, waiting for transfers between devices, per_device(): send = lambda a, perm: lax.ppermute(a, 'head', perm)  13.9 us
    all_to_all x1, waiting for transfers between devices, per_device(): lax.all_to_all(outgoing.reshape(16, CAP, tokens, WIDE), 'req', 0, 0, tile...  8.95 us
    ppermute x13, starting transfers between devices, per_device(): send = lambda a, perm: lax.ppermute(a, 'head', perm)  8.22 us
    all_to_all x1, starting transfers between devices, per_device(): lax.all_to_all(outgoing.reshape(16, CAP, tokens, WIDE), 'req', 0, 0, tile...  8.17 us
    all_to_all x1, starting transfers between devices, per_device(): lax.all_to_all(slot_grads.reshape(16, CAP, tokens, WIDE), 'req', 0, 0, ti...  3.83 us
    all_to_all x1, waiting for transfers between devices, per_device(): lax.all_to_all(slot_grads.reshape(16, CAP, tokens, WIDE), 'req', 0, 0, ti...  2.96 us
  transfers between devices with their start and end apart: 15, of which 10 were waited for; matrix products, arithmetic and copies ran while one was open for 4% of the time, Pallas kernels for 35%

profile of v10, /device:TPU:0, one launch (start us, length us, event | category | flops | bytes accessed | tf_op | source)
XLA Modules:
  0.0 102.8 jit_solution(16044523221466335078)
XLA Ops:
  0.6 3.8 %shard_map.85 = (bf16[32,16,576]{2,1,0:T(8,128)(2,1)}, s32[33]{0:T(128)}) custom-call(s32[16,16]{1,0:T(8,128)} %lists.5, s32[16]{0:T(128)} %counts.5, s32[1]{0:T(128)} %bitcast.me, bf16[16,16,576]{2,1,0:T(8,128)(2,1)} %lat_ref.1), custom_call_target="tpu_custom_call" | custom-call | tf_op jit(solution)/shard_map/pallas_call | solution.py:164
  4.4 8.2 %all-to-all-start = ((bf16[16,2,16,576]{3,2,1,0:T(8,128)(2,1)}), bf16[16,2,16,576]{3,2,1,0:T(8,128)(2,1)S(1)}, u32[]{:S(2)}, u32[]{:S(2)}) async-start(bf16[16,2,16,576]{3,2,1,0:T(8,128)(2,1)} %bitcast.39), calls=%async_computation | async-start | bytes 1310720 | tf_op jit(solution)/shard_map/all_to_all | solution.py:476
  12.7 1.2 %dynamic_slice.8 = s32[1]{0:T(128)} dynamic-slice(s32[16]{0:T(128)} %counts.5, s32[]{:T(128)S(6)} %select_n.31), dynamic_slice_sizes={1} | dynamic-slice | bytes 12 | tf_op jit(solution)/shard_map/jit(dynamic_index_in_dim)/dynamic_slice | solution.py:479
  13.9 0.7 dynamic-slice_bitcast_fusion
  14.6 0.1 stack.35
  14.7 0.9 select_reduce_fusion
  15.5 0.7 compare_select_fusion
  16.2 0.1 broadcast_in_dim.34
  16.3 0.1 lt.32
  16.4 0.1 add.60
  16.4 0.1 fusion
  16.6 9.0 %all-to-all-done = bf16[16,2,16,576]{3,2,1,0:T(8,128)(2,1)S(1)} async-done(((bf16[16,2,16,576]{3,2,1,0:T(8,128)(2,1)}), bf16[16,2,16,576]{3,2,1,0:T(8,128)(2,1)S(1)}, u32[]{:S(2)}, u32[]{:S(2)}) %all-to-all-start) | async-done | bytes 589856 | tf_op jit(solution)/shard_map/all_to_all | solution.py:476
  25.5 1.1 %shard_map.86.refs_0_ = bf16[256,576]{1,0:T(8,128)(2,1)S(1)} custom-call(s32[16,16]{1,0:T(8,128)} %lists.5, s32[16]{0:T(128)} %counts.5, s32[1]{0:T(128)} %bitcast.me, bf16[32,16,576]{2,1,0:T(8,128)(2,1)S(1)} %bitcast.30), custom_call_target="tpu_custom_call" | custom-call | tf_op jit(solution)/shard_map/pallas_call | solution.py:164
  26.6 0.1 collective-permute-start.1
  26.7 2.8 %collective-permute-start.2 = (bf16[256,576]{1,0:T(8,128)(2,1)S(1)}, bf16[256,576]{1,0:T(8,128)(2,1)S(1)}, u32[]{:S(2)}, u32[]{:S(2)}) collective-permute-start(bf16[256,576]{1,0:T(8,128)(2,1)S(1)} %shard_map.86.refs_0_), channel_id=1, source_target_pairs={{0,6},{1,7},{2,4},{3,5},{4,2},{5,3},{6,0},{7,1},{8,14},{9,15},{10,... | collective-permute-start | bytes 884744 | tf_op jit(solution)/shard_map/ppermute | solution.py:452
  29.5 0.2 collective-permute-start
  29.8 0.0 collective-permute-done.1.refs_1_
  29.8 5.4 %shard_map.87 = (bf16[1536,2048]{1,0:T(8,128)(2,1)S(1)}, bf16[1536,2048]{1,0:T(8,128)(2,1)S(1)}, bf16[2048,576]{1,0:T(8,128)(2,1)S(1)}, f32[9,1536,128]{2,1,0:T(...) custom-call(bf16[256,576]{1,0:T(8,128)(2,1)S(1)} %shard_map.86.refs_0_, ...), custom_call_target="tpu_custom_call" | custom-call | flops 1711276032 | tf_op jit(solution)/shard_map/pallas_call | solution.py:164
  35.2 2.8 %collective-permute-done.2.refs_1_ = bf16[256,576]{1,0:T(8,128)(2,1)S(1)} collective-permute-done((bf16[256,576]{1,0:T(8,128)(2,1)S(1)}, bf16[256,576]{1,0:T(8,128)(2,1)S(1)}, u32[]{:S(2)}, u32[]{:S(2)}) %collective-permute-start.2) | collective-permute-done | bytes 294944 | tf_op jit(solution)/shard_map/ppermute | solution.py:452
  38.0 1.3 %collective-permute-done.refs_0_ = bf16[256,576]{1,0:T(8,128)(2,1)S(1)} collective-permute-done((bf16[256,576]{1,0:T(8,128)(2,1)S(1)}, bf16[256,576]{1,0:T(8,128)(2,1)S(1)}, u32[]{:S(2)}, u32[]{:S(2)}) %collective-permute-start) | collective-permute-done | bytes 294944 | tf_op jit(solution)/shard_map/ppermute | solution.py:452
  39.3 0.0 collective-permute-start.3
  39.3 0.5 collective-permute-start.4
  39.8 0.3 collective-permute-start.5
  40.1 0.8 collective-permute-done.3.refs_2_
  40.9 0.5 collective-permute-done.4.refs_3_
  41.4 5.5 %shard_map.88 = (bf16[1536,2048]{1,0:T(8,128)(2,1)S(1)}, bf16[1536,2048]{1,0:T(8,128)(2,1)S(1)}, bf16[2048,576]{1,0:T(8,128)(2,1)S(1)}, f32[9,1536,128]{2,1,0:T(...) custom-call(bf16[256,576]{1,0:T(8,128)(2,1)S(1)} %collective-permute, ...), custom_call_target="tpu_custom_call", output_to_operand_aliasing={{0}: (5, {}), {1}: (6, {}), {2}: (7, {}), {3}: (8, {}), {4}... | custom-call | flops 3422552064 | tf_op jit(solution)/shard_map/pallas_call | solution.py:164
  46.9 2.5 %collective-permute-done.5.refs_0_ = bf16[256,576]{1,0:T(8,128)(2,1)S(1)} collective-permute-done((bf16[256,576]{1,0:T(8,128)(2,1)S(1)}, bf16[256,576]{1,0:T(8,128)(2,1)S(1)}, u32[]{:S(2)}, u32[]{:S(2)}) %collective-permute-start.5) | collective-permute-done | bytes 294944 | tf_op jit(solution)/shard_map/ppermute | solution.py:452
  49.4 0.0 collective-permute-start.6
  49.4 1.4 %shard_map.89 = (bf16[576,1536]{1,0:T(8,128)(2,1)S(1)}, bf16[512,1536]{1,0:T(8,128)(2,1)S(1)}) custom-call(bf16[96,16,576]{2,1,0:T(8,128)(2,1)S(1)} %get-tuple-element.89.q_ref.refs_7_, bf16[96,16,512]{2,1,0:T(8,128)(2,1)S(1)} %get-tuple-element.93.g_ref.refs_8_), custom_call_target="tpu_custom_call" | custom-call | tf_op jit(solution)/shard_map/pallas_call | solution.py:164
  50.8 0.2 collective-permute-done.6.refs_1_
  51.1 2.8 %shard_map.90 = (bf16[1536,2048]{1,0:T(8,128)(2,1)S(1)}, bf16[1536,2048]{1,0:T(8,128)(2,1)S(1)}, bf16[2048,576]{1,0:T(8,128)(2,1)S(1)}, f32[9,1536,128]{2,1,0:T(...) custom-call(bf16[256,576]{1,0:T(8,128)(2,1)S(1)} %collective-permute, ...), custom_call_target="tpu_custom_call", output_to_operand_aliasing={{0}: (3, {}), {1}: (4, {}), {2}: (5, {}), {3}: (6, {}), {4}... | custom-call | flops 1711276032 | tf_op jit(solution)/shard_map/pallas_call | solution.py:164
  53.8 2.2 %shard_map.91 = (bf16[256,576]{1,0:T(8,128)(2,1)S(1)}, bf16[1536,2048]{1,0:T(8,128)(2,1)S(1)}, bf16[1536,2048]{1,0:T(8,128)(2,1)S(1)}, f32[4,1536,128]{2,1,0:T(8...) custom-call(bf16[576,1536]{1,0:T(8,128)(2,1)S(1)} %get-tuple-element, ...), custom_call_target="tpu_custom_call", output_to_operand_aliasing={{1}: (2, {}), {2}: (3, {}), {4}: (5, {})} | custom-call | flops 855638016 | tf_op jit(solution)/shard_map/pallas_call | solution.py:164
  56.0 0.6 collective-permute-start.7
  56.6 1.7 %shard_map.92 = (bf16[256,576]{1,0:T(8,128)(2,1)S(1)}, bf16[1536,2048]{1,0:T(8,128)(2,1)S(1)}, bf16[1536,2048]{1,0:T(8,128)(2,1)S(1)}, f32[4,1536,128]{2,1,0:T(8...) custom-call(bf16[576,1536]{1,0:T(8,128)(2,1)S(1)} %get-tuple-element, ...), custom_call_target="tpu_custom_call", output_to_operand_aliasing={{1}: (2, {}), {2}: (3, {}), {4}: (5, {}), {3}: (4, {})} | custom-call | flops 855638016 | tf_op jit(solution)/shard_map/pallas_call | solution.py:164
  58.3 1.7 %shard_map.93 = (bf16[256,576]{1,0:T(8,128)(2,1)S(1)}, bf16[1536,2048]{1,0:T(8,128)(2,1)S(1)}, bf16[1536,2048]{1,0:T(8,128)(2,1)S(1)}, f32[4,1536,128]{2,1,0:T(8...) custom-call(bf16[576,1536]{1,0:T(8,128)(2,1)S(1)} %get-tuple-element, ...), custom_call_target="tpu_custom_call", output_to_operand_aliasing={{1}: (2, {}), {2}: (3, {}), {4}: (5, {}), {3}: (4, {})} | custom-call | flops 855638016 | tf_op jit(solution)/shard_map/pallas_call | solution.py:164
  60.0 0.0 collective-permute-done.7.far_ref
  60.0 0.1 shard_map.94
  60.1 2.9 %shard_map.95 = (bf16[512,576]{1,0:T(8,128)(2,1)S(1)}, bf16[1536,2048]{1,0:T(8,128)(2,1)S(1)}, bf16[1536,2048]{1,0:T(8,128)(2,1)S(1)}, f32[4,1536,128]{2,1,0:T(8...) custom-call(bf16[576,1536]{1,0:T(8,128)(2,1)S(1)} %get-tuple-element, ...), custom_call_target="tpu_custom_call", output_to_operand_aliasing={{1}: (2, {}), {2}: (3, {}), {4}: (5, {}), {3}: (4, {})} | custom-call | flops 1711276032 | tf_op jit(solution)/shard_map/pallas_call | solution.py:164
  63.0 0.3 collective-permute-start.8
  63.3 1.5 %collective-permute-start.9 = (bf16[256,576]{1,0:T(8,128)(2,1)S(1)}, bf16[256,576]{1,0:T(8,128)(2,1)S(1)}, u32[]{:S(2)}, u32[]{:S(2)}) collective-permute-start(bf16[256,576]{1,0:T(8,128)(2,1)S(1)} %shard_map.94), channel_id=1, source_target_pairs={{0,6},{1,7},{2,4},{3,5},{4,2},{5,3},{6,0},{7,1},{8,14},{9,15},{10,... | collective-permute-start | bytes 884744 | tf_op jit(solution)/shard_map/ppermute | solution.py:452
  64.8 0.0 collective-permute-start.10
  64.8 2.9 %shard_map.96 = (bf16[512,576]{1,0:T(8,128)(2,1)S(1)}, bf16[1536,2048]{1,0:T(8,128)(2,1)S(1)}, bf16[1536,2048]{1,0:T(8,128)(2,1)S(1)}, f32[4,1536,128]{2,1,0:T(8...) custom-call(bf16[576,1536]{1,0:T(8,128)(2,1)S(1)} %get-tuple-element, ...), custom_call_target="tpu_custom_call", output_to_operand_aliasing={{1}: (2, {}), {2}: (3, {}), {4}: (5, {}), {3}: (4, {})} | custom-call | flops 1711276032 | tf_op jit(solution)/shard_map/pallas_call | solution.py:164
  67.8 0.0 collective-permute-done.8
  67.8 0.1 shard_map.97
  67.9 1.8 %collective-permute-start.12 = (bf16[256,576]{1,0:T(8,128)(2,1)S(1)}, bf16[256,576]{1,0:T(8,128)(2,1)S(1)}, u32[]{:S(2)}, u32[]{:S(2)}) collective-permute-start(bf16[256,576]{1,0:T(8,128)(2,1)S(1)} %shard_map.97), channel_id=1, source_target_pairs={{0,6},{1,7},{2,4},{3,5},{4,2},{5,3},{6,0},{7,1},{8,14},{9,15},{10,... | collective-permute-start | bytes 884744 | tf_op jit(solution)/shard_map/ppermute | solution.py:452
  69.7 5.4 %collective-permute-done.9.two_ref = bf16[256,576]{1,0:T(8,128)(2,1)S(1)} collective-permute-done((bf16[256,576]{1,0:T(8,128)(2,1)S(1)}, bf16[256,576]{1,0:T(8,128)(2,1)S(1)}, u32[]{:S(2)}, u32[]{:S(2)}) %collective-permute-start.9) | collective-permute-done | bytes 294944 | tf_op jit(solution)/shard_map/ppermute | solution.py:452
  75.1 0.1 shard_map.98
  75.2 0.1 collective-permute-start.11
  75.3 1.7 %shard_map.99 = (bf16[256,576]{1,0:T(8,128)(2,1)S(1)}, bf16[1536,2048]{1,0:T(8,128)(2,1)S(1)}, bf16[1536,2048]{1,0:T(8,128)(2,1)S(1)}, f32[4,1536,128]{2,1,0:T(8...) custom-call(bf16[576,1536]{1,0:T(8,128)(2,1)S(1)} %get-tuple-element, ...), custom_call_target="tpu_custom_call", output_to_operand_aliasing={{1}: (2, {}), {2}: (3, {}), {4}: (5, {}), {3}: (4, {})} | custom-call | flops 855638016 | tf_op jit(solution)/shard_map/pallas_call | solution.py:164
  77.0 6.4 %shard_map.100 = (bf16[96,16,512]{2,1,0:T(8,128)(2,1)}, bf16[96,16,576]{2,1,0:T(8,128)(2,1)}) custom-call(bf16[1536,2048]{1,0:T(8,128)(2,1)S(1)} %get-tuple-element.134.w_ref, bf16[1536,2048]{1,0:T(8,128)(2,1)S(1)} %get-tuple-element.135.s_ref, bf16[2048,576]{1,0:T(8,128)(2,1)S(1)} %get-tuple-element.137.k_ref), custom_call_target="tpu_custom_call" | custom-call | flops 4429185024 | tf_op jit(solution)/shard_map/pallas_call | solution.py:164
  83.4 0.0 collective-permute-done.10.b_ref
  83.4 0.3 collective-permute-done.11.c_ref
  83.7 0.0 collective-permute-done.12.d_ref
  83.7 1.7 %shard_map.101 = bf16[32,16,576]{2,1,0:T(8,128)(2,1)} custom-call(s32[16,16]{1,0:T(8,128)} %lists.5, s32[16]{0:T(128)} %counts.5, s32[1]{0:T(128)} %bitcast.me, bf16[256,576]{1,0:T(8,128)(2,1)S(1)} %get-tuple-element.147.a_ref, bf16[256,576]{1,0:T(8,128)(2,1)S(1)} %collective-permute-done.10.b_ref, bf16[256,576]{1,0:T(8,128)(2,1)S(1)} %collective-permute-done.11.c_ref, ...), custom_call_target="tpu_custom_call" | custom-call | tf_op jit(solution)/shard_map/pallas_call | solution.py:164
  85.4 3.8 %all-to-all-start.1 = ((bf16[16,2,16,576]{3,2,1,0:T(8,128)(2,1)}), bf16[16,2,16,576]{3,2,1,0:T(8,128)(2,1)S(1)}, u32[]{:S(2)}, u32[]{:S(2)}) async-start(bf16[16,2,16,576]{3,2,1,0:T(8,128)(2,1)} %bitcast.38), calls=%async_computation.1 | async-start | bytes 1310720 | tf_op jit(solution)/shard_map/all_to_all | solution.py:558
  89.2 8.6 %shard_map.102 = bf16[96,16,576]{2,1,0:T(8,128)(2,1)} custom-call(bf16[1,1024,256]{2,1,0:T(8,128)(2,1)} %get-tuple-element.139.refs_0_, bf16[1,1024,256]{2,1,0:T(8,128)(2,1)} %get-tuple-element.140.refs_1_, bf16[1,1024,256]{2,1,0:T(8,128)(2,1)} %get-tuple-element.141.refs_2_, ...), custom_call_target="tpu_custom_call", output_to_operand_aliasing={{}: (7, {})} | custom-call | flops 2415919104 | tf_op jit(solution)/shard_map/pallas_call | solution.py:164
  97.8 3.0 %all-to-all-done.1 = bf16[16,2,16,576]{3,2,1,0:T(8,128)(2,1)S(1)} async-done(((bf16[16,2,16,576]{3,2,1,0:T(8,128)(2,1)}), bf16[16,2,16,576]{3,2,1,0:T(8,128)(2,1)S(1)}, u32[]{:S(2)}, u32[]{:S(2)}) %all-to-all-start.1) | async-done | bytes 589856 | tf_op jit(solution)/shard_map/all_to_all | solution.py:558
  100.8 1.8 %shard_map.103 = f32[16,16,576]{2,1,0:T(8,128)} custom-call(s32[33]{0:T(128)} %get-tuple-element.150.table, bf16[32,16,576]{2,1,0:T(8,128)(2,1)S(1)} %bitcast.33), custom_call_target="tpu_custom_call" | custom-call | tf_op jit(solution)/shard_map/pallas_call | solution.py:164
  (7 shorter events, 0.0 us)
Async XLA Ops:
  4.4 21.1 %all-to-all-start = ((bf16[16,2,16,576]{3,2,1,0:T(8,128)(2,1)}), bf16[16,2,16,576]{3,2,1,0:T(8,128)(2,1)S(1)}, u32[]{:S(2)}, u32[]{:S(2)}) async-start(bf16[16,2,16,576]{3,2,1,0:T(8,128)(2,1)} %bitcast.39), calls=%async_computation | async-start | bytes 1310720 | tf_op jit(solution)/shard_map/all_to_all | solution.py:476
  26.6 3.2 %collective-permute-start.1 = (bf16[256,576]{1,0:T(8,128)(2,1)S(1)}, bf16[256,576]{1,0:T(8,128)(2,1)S(1)}, u32[]{:S(2)}, u32[]{:S(2)}) collective-permute-start(bf16[256,576]{1,0:T(8,128)(2,1)S(1)} %shard_map.86.refs_0_), channel_id=1, source_target_pairs={{0,1},{1,0},{2,3},{3,2},{4,5},{5,4},{6,7},{7,6},{8,9},{9,8},{10,11... | collective-permute-start | bytes 884744 | tf_op jit(solution)/shard_map/ppermute | solution.py:452
  26.7 11.3 %collective-permute-start.2 = (bf16[256,576]{1,0:T(8,128)(2,1)S(1)}, bf16[256,576]{1,0:T(8,128)(2,1)S(1)}, u32[]{:S(2)}, u32[]{:S(2)}) collective-permute-start(bf16[256,576]{1,0:T(8,128)(2,1)S(1)} %shard_map.86.refs_0_), channel_id=1, source_target_pairs={{0,6},{1,7},{2,4},{3,5},{4,2},{5,3},{6,0},{7,1},{8,14},{9,15},{10,... | collective-permute-start | bytes 884744 | tf_op jit(solution)/shard_map/ppermute | solution.py:452
  29.5 9.8 %collective-permute-start = (bf16[256,576]{1,0:T(8,128)(2,1)S(1)}, bf16[256,576]{1,0:T(8,128)(2,1)S(1)}, u32[]{:S(2)}, u32[]{:S(2)}) collective-permute-start(bf16[256,576]{1,0:T(8,128)(2,1)S(1)} %shard_map.86.refs_0_), channel_id=1, source_target_pairs={{0,2},{1,3},{2,0},{3,1},{4,6},{5,7},{6,4},{7,5},{8,10},{9,11},{10,... | collective-permute-start | bytes 884744 | tf_op jit(solution)/shard_map/ppermute | solution.py:452
  39.3 1.6 %collective-permute-start.3 = (bf16[256,576]{1,0:T(8,128)(2,1)S(1)}, bf16[256,576]{1,0:T(8,128)(2,1)S(1)}, u32[]{:S(2)}, u32[]{:S(2)}) collective-permute-start(bf16[256,576]{1,0:T(8,128)(2,1)S(1)} %collective-permute-done.refs_0_), channel_id=1, source_target_pairs={{0,1},{1,0},{2,3},{3,2},{4,5},{5,4},{6,7},{7,6},{8,9},{9,8},{10,11... | collective-permute-start | bytes 884744 | tf_op jit(solution)/shard_map/ppermute | solution.py:452
  39.3 2.1 %collective-permute-start.4 = (bf16[256,576]{1,0:T(8,128)(2,1)S(1)}, bf16[256,576]{1,0:T(8,128)(2,1)S(1)}, u32[]{:S(2)}, u32[]{:S(2)}) collective-permute-start(bf16[256,576]{1,0:T(8,128)(2,1)S(1)} %collective-permute-done.2.refs_1_), channel_id=1, source_target_pairs={{0,1},{1,0},{2,3},{3,2},{4,5},{5,4},{6,7},{7,6},{8,9},{9,8},{10,11... | collective-permute-start | bytes 884744 | tf_op jit(solution)/shard_map/ppermute | solution.py:452
  39.8 9.6 %collective-permute-start.5 = (bf16[256,576]{1,0:T(8,128)(2,1)S(1)}, bf16[256,576]{1,0:T(8,128)(2,1)S(1)}, u32[]{:S(2)}, u32[]{:S(2)}) collective-permute-start(bf16[256,576]{1,0:T(8,128)(2,1)S(1)} %collective-permute-done.2.refs_1_), channel_id=1, source_target_pairs={{0,2},{1,3},{2,0},{3,1},{4,6},{5,7},{6,4},{7,5},{8,10},{9,11},{10,... | collective-permute-start | bytes 884744 | tf_op jit(solution)/shard_map/ppermute | solution.py:452
  49.4 1.6 %collective-permute-start.6 = (bf16[256,576]{1,0:T(8,128)(2,1)S(1)}, bf16[256,576]{1,0:T(8,128)(2,1)S(1)}, u32[]{:S(2)}, u32[]{:S(2)}) collective-permute-start(bf16[256,576]{1,0:T(8,128)(2,1)S(1)} %collective-permute-done.5.refs_0_), channel_id=1, source_target_pairs={{0,1},{1,0},{2,3},{3,2},{4,5},{5,4},{6,7},{7,6},{8,9},{9,8},{10,11... | collective-permute-start | bytes 884744 | tf_op jit(solution)/shard_map/ppermute | solution.py:452
  56.0 4.0 %collective-permute-start.7 = (bf16[256,576]{1,0:T(8,128)(2,1)S(1)}, bf16[256,576]{1,0:T(8,128)(2,1)S(1)}, u32[]{:S(2)}, u32[]{:S(2)}) collective-permute-start(bf16[256,576]{1,0:T(8,128)(2,1)S(1)} %get-tuple-element.119), channel_id=1, source_target_pairs={{0,1},{1,0},{2,3},{3,2},{4,5},{5,4},{6,7},{7,6},{8,9},{9,8},{10,11... | collective-permute-start | bytes 884744 | tf_op jit(solution)/shard_map/ppermute | solution.py:452
  63.0 4.7 %collective-permute-start.8 = (bf16[32,16,576]{2,1,0:T(8,128)(2,1)S(1)}, bf16[32,16,576]{2,1,0:T(8,128)(2,1)S(1)}, u32[]{:S(2)}, u32[]{:S(2)}) collective-permute-start(bf16[32,16,576]{2,1,0:T(8,128)(2,1)S(1)} %bitcast.37), channel_id=1, source_target_pairs={{0,1},{1,0},{2,3},{3,2},{4,5},{5,4},{6,7},{7,6},{8,9},{9,8},{10,11... | collective-permute-start | bytes 1769480 | tf_op jit(solution)/shard_map/ppermute | solution.py:452
  63.3 11.8 %collective-permute-start.9 = (bf16[256,576]{1,0:T(8,128)(2,1)S(1)}, bf16[256,576]{1,0:T(8,128)(2,1)S(1)}, u32[]{:S(2)}, u32[]{:S(2)}) collective-permute-start(bf16[256,576]{1,0:T(8,128)(2,1)S(1)} %shard_map.94), channel_id=1, source_target_pairs={{0,6},{1,7},{2,4},{3,5},{4,2},{5,3},{6,0},{7,1},{8,14},{9,15},{10,... | collective-permute-start | bytes 884744 | tf_op jit(solution)/shard_map/ppermute | solution.py:452
  64.8 18.6 %collective-permute-start.10 = (bf16[256,576]{1,0:T(8,128)(2,1)S(1)}, bf16[256,576]{1,0:T(8,128)(2,1)S(1)}, u32[]{:S(2)}, u32[]{:S(2)}) collective-permute-start(bf16[256,576]{1,0:T(8,128)(2,1)S(1)} %get-tuple-element.117), channel_id=1, source_target_pairs={{0,1},{1,0},{2,3},{3,2},{4,5},{5,4},{6,7},{7,6},{8,9},{9,8},{10,11... | collective-permute-start | bytes 884744 | tf_op jit(solution)/shard_map/ppermute | solution.py:452
  67.9 15.8 %collective-permute-start.12 = (bf16[256,576]{1,0:T(8,128)(2,1)S(1)}, bf16[256,576]{1,0:T(8,128)(2,1)S(1)}, u32[]{:S(2)}, u32[]{:S(2)}) collective-permute-start(bf16[256,576]{1,0:T(8,128)(2,1)S(1)} %shard_map.97), channel_id=1, source_target_pairs={{0,6},{1,7},{2,4},{3,5},{4,2},{5,3},{6,0},{7,1},{8,14},{9,15},{10,... | collective-permute-start | bytes 884744 | tf_op jit(solution)/shard_map/ppermute | solution.py:452
  75.2 8.5 %collective-permute-start.11 = (bf16[256,576]{1,0:T(8,128)(2,1)S(1)}, bf16[256,576]{1,0:T(8,128)(2,1)S(1)}, u32[]{:S(2)}, u32[]{:S(2)}) collective-permute-start(bf16[256,576]{1,0:T(8,128)(2,1)S(1)} %shard_map.98), channel_id=1, source_target_pairs={{0,2},{1,3},{2,0},{3,1},{4,6},{5,7},{6,4},{7,5},{8,10},{9,11},{10,... | collective-permute-start | bytes 884744 | tf_op jit(solution)/shard_map/ppermute | solution.py:452
  85.4 15.4 %all-to-all-start.1 = ((bf16[16,2,16,576]{3,2,1,0:T(8,128)(2,1)}), bf16[16,2,16,576]{3,2,1,0:T(8,128)(2,1)S(1)}, u32[]{:S(2)}, u32[]{:S(2)}) async-start(bf16[16,2,16,576]{3,2,1,0:T(8,128)(2,1)} %bitcast.38), calls=%async_computation.1 | async-start | bytes 1310720 | tf_op jit(solution)/shard_map/all_to_all | solution.py:558

commit v11 on v9

--- a/solution.py
+++ b/solution.py
@@ -60,10 +60,10 @@
     step = SLOTS // 4
     parts = [slice(i * step, i * step + step) for i in range(4)]
     copies = [pltpu.make_async_copy(held.at[p], out_ref.at[p], sems.at[i]) for i, p in enumerate(parts)]
-    for s in range(SLOTS):
-        held[s] = lat[table[s] & 15]
-        if s % step == step - 1:
-            copies[s // step].start()
+    for i, copy in enumerate(copies):
+        for s in range(i * step, i * step + step):
+            held[s] = lat[table[s] & 15]
+        copy.start()
     for copy in copies:
         copy.wait()
 
@@ -343,11 +343,12 @@
 def value_body(block, early, w_ref, s_ref, k_ref, out_ref, q_ref, held, held_q, sems, sems_q):
     steps = out_ref.shape[0] * 16 // block
     leave = leaving(held, out_ref, sems, block)
-    leave_q = leaving(held_q, q_ref, sems_q, block)
-    for i in range(early // block):
-        here = slice(i * block, i * block + block)
-        part = slice(i * (block // 16), (i + 1) * (block // 16))
-        held_q[part] = dot(s_ref[here], k_ref[...]).astype(bf16).reshape(block // 16, 16, WIDE)
+    small = held_q.shape[0] * 16 // sems_q.shape[0]
+    leave_q = leaving(held_q, q_ref, sems_q, small)
+    for i in range(early // small):
+        here = slice(i * small, i * small + small)
+        part = slice(i * (small // 16), (i + 1) * (small // 16))
+        held_q[part] = dot(s_ref[here], k_ref[...]).astype(bf16).reshape(small // 16, 16, WIDE)
         leave_q(i).start()
 
     def rows(i, carry):
@@ -358,7 +359,7 @@
         return carry
 
     lax.fori_loop(0, steps, rows, 0)
-    for i in range(early // block):
+    for i in range(early // small):
         leave_q(i).wait()
     for i in range(steps):
         leave(i).wait()
@@ -377,7 +378,7 @@
             pltpu.VMEM(shape, bf16),
             pltpu.VMEM((early // 16, 16, WIDE), bf16),
             dma(rows // block),
-            dma(early // block),
+            dma(early // 256),
         ],
         direct=(0, 1),
         flops=2 * k.shape[0] * (rows * LAT + early * WIDE),
@@ -417,7 +418,7 @@
         copy.wait()
 
 
-def query_side(sgs, offs, early, k, out, block=512):
+def query_side(sgs, offs, early, k, out, block=256):
     tile, rows = sgs[0].shape[2], sgs[0].shape[1]
     dma = lambda n: pltpu.SemaphoreType.DMA((n,))
     steps, tiles = rows // block, k.shape[0] // tile
@@ -518,7 +519,7 @@
 
     fold = lambda a: a.reshape(-1, tokens, WIDE)
     unfold = lambda a: a.reshape(-1, WIDE)
-    early = 512
+    early = 256
     back = functools.partial(backward, early=early, qt=qt, gt=gt)
     far2, e, p, row, k, sg2f = back(2, (7 * keys,), keys, e=e, p=p, row=row, k=k, lead=True)
     mate2 = send(far2, sibling)
@@ -532,9 +533,9 @@
     mate0 = send(far0, sibling)
     (to_b,) = call(wrap_body, (share_of(keys),), (), (near1, mate1))
     got_b = send(to_b, pair_b)
-    near0, e, p, row, k, sg0n = back(0, (0,), keys, e=e, p=p, row=after(row, to_b), k=k)
-    (to_a,) = call(next_body, (share_of(keys),), (), (after(near1, near0), mate1, got_two))
+    (to_a,) = call(next_body, (share_of(keys),), (), (after(near1, to_b), mate1, got_two))
     got_a = send(to_a, pair_a)
+    near0, e, p, row, k, sg0n = back(0, (0,), keys, e=e, p=p, row=after(row, to_a), k=k)
     attended, query_grad = value_side(e, p, after(k, to_a), early)
     near0 = after(near0, attended)
     (slot_grads,) = call(

time: 102 us -> 102 us (level)
  no operation moved by 1% of the time
where the time goes in v11:
time: 102 us
  Pallas kernels  50.4 us (49%)
  waiting for transfers between devices  26.1 us (26%)
  starting transfers between devices  20.2 us (20%)
  local copies, waits for them, and re-layouts  2.28 us (2%)
  other arithmetic  1.59 us (2%)
  between operations  1.07 us (1%)
    pallas_call x19, Pallas kernels, call(): pl.pallas_call(body, in_specs=[small] * len(scalars) + [INPLACE if i in d...  50.4 us
    ppermute x13, waiting for transfers between devices, per_device(): send = lambda a, perm: lax.ppermute(a, 'head', perm)  15.7 us
    all_to_all x1, waiting for transfers between devices, per_device(): lax.all_to_all(outgoing.reshape(16, CAP, tokens, WIDE), 'req', 0, 0, tile...  8.95 us
    ppermute x13, starting transfers between devices, per_device(): send = lambda a, perm: lax.ppermute(a, 'head', perm)  8.22 us
    all_to_all x1, starting transfers between devices, per_device(): lax.all_to_all(outgoing.reshape(16, CAP, tokens, WIDE), 'req', 0, 0, tile...  8.17 us
    all_to_all x1, starting transfers between devices, per_device(): lax.all_to_all(slot_grads.reshape(16, CAP, tokens, WIDE), 'req', 0, 0, ti...  3.83 us
  transfers between devices with their start and end apart: 15, of which 10 were waited for; matrix products, arithmetic and copies ran while one was open for 4% of the time, Pallas kernels for 34%

profile of v11, /device:TPU:0, one launch (start us, length us, event | category | flops | bytes accessed | tf_op | source)
XLA Modules:
  0.0 101.7 jit_solution(12823396758685934555)
XLA Ops:
  0.6 3.2 %shard_map.85 = (bf16[32,16,576]{2,1,0:T(8,128)(2,1)}, s32[33]{0:T(128)}) custom-call(s32[16,16]{1,0:T(8,128)} %lists.5, s32[16]{0:T(128)} %counts.5, s32[1]{0:T(128)} %bitcast.me, bf16[16,16,576]{2,1,0:T(8,128)(2,1)} %lat_ref.1), custom_call_target="tpu_custom_call" | custom-call | tf_op jit(solution)/shard_map/pallas_call | solution.py:163
  3.8 8.2 %all-to-all-start = ((bf16[16,2,16,576]{3,2,1,0:T(8,128)(2,1)}), bf16[16,2,16,576]{3,2,1,0:T(8,128)(2,1)S(1)}, u32[]{:S(2)}, u32[]{:S(2)}) async-start(bf16[16,2,16,576]{3,2,1,0:T(8,128)(2,1)} %bitcast.39), calls=%async_computation | async-start | bytes 1310720 | tf_op jit(solution)/shard_map/all_to_all | solution.py:475
  12.0 1.2 %dynamic_slice.8 = s32[1]{0:T(128)} dynamic-slice(s32[16]{0:T(128)} %counts.5, s32[]{:T(128)S(6)} %select_n.31), dynamic_slice_sizes={1} | dynamic-slice | bytes 12 | tf_op jit(solution)/shard_map/jit(dynamic_index_in_dim)/dynamic_slice | solution.py:478
  13.3 0.7 dynamic-slice_bitcast_fusion
  14.0 0.1 stack.35
  14.1 0.9 select_reduce_fusion
  14.9 0.7 compare_select_fusion
  15.6 0.1 broadcast_in_dim.34
  15.7 0.1 lt.32
  15.7 0.1 add.60
  15.8 0.1 fusion
  15.9 9.0 %all-to-all-done = bf16[16,2,16,576]{3,2,1,0:T(8,128)(2,1)S(1)} async-done(((bf16[16,2,16,576]{3,2,1,0:T(8,128)(2,1)}), bf16[16,2,16,576]{3,2,1,0:T(8,128)(2,1)S(1)}, u32[]{:S(2)}, u32[]{:S(2)}) %all-to-all-start) | async-done | bytes 589856 | tf_op jit(solution)/shard_map/all_to_all | solution.py:475
  24.9 1.1 %shard_map.86.refs_0_ = bf16[256,576]{1,0:T(8,128)(2,1)S(1)} custom-call(s32[16,16]{1,0:T(8,128)} %lists.5, s32[16]{0:T(128)} %counts.5, s32[1]{0:T(128)} %bitcast.me, bf16[32,16,576]{2,1,0:T(8,128)(2,1)S(1)} %bitcast.30), custom_call_target="tpu_custom_call" | custom-call | tf_op jit(solution)/shard_map/pallas_call | solution.py:163
  26.0 0.1 collective-permute-start.1
  26.1 2.8 %collective-permute-start.2 = (bf16[256,576]{1,0:T(8,128)(2,1)S(1)}, bf16[256,576]{1,0:T(8,128)(2,1)S(1)}, u32[]{:S(2)}, u32[]{:S(2)}) collective-permute-start(bf16[256,576]{1,0:T(8,128)(2,1)S(1)} %shard_map.86.refs_0_), channel_id=1, source_target_pairs={{0,6},{1,7},{2,4},{3,5},{4,2},{5,3},{6,0},{7,1},{8,14},{9,15},{10,... | collective-permute-start | bytes 884744 | tf_op jit(solution)/shard_map/ppermute | solution.py:451
  28.9 0.2 collective-permute-start
  29.1 0.0 collective-permute-done.1.refs_1_
  29.1 4.4 %shard_map.87 = (bf16[1536,2048]{1,0:T(8,128)(2,1)S(1)}, bf16[1536,2048]{1,0:T(8,128)(2,1)S(1)}, bf16[2048,576]{1,0:T(8,128)(2,1)S(1)}, f32[9,1536,128]{2,1,0:T(...) custom-call(bf16[256,576]{1,0:T(8,128)(2,1)S(1)} %shard_map.86.refs_0_, ...), custom_call_target="tpu_custom_call" | custom-call | flops 1711276032 | tf_op jit(solution)/shard_map/pallas_call | solution.py:163
  33.5 3.9 %collective-permute-done.2.refs_1_ = bf16[256,576]{1,0:T(8,128)(2,1)S(1)} collective-permute-done((bf16[256,576]{1,0:T(8,128)(2,1)S(1)}, bf16[256,576]{1,0:T(8,128)(2,1)S(1)}, u32[]{:S(2)}, u32[]{:S(2)}) %collective-permute-start.2) | collective-permute-done | bytes 294944 | tf_op jit(solution)/shard_map/ppermute | solution.py:451
  37.4 1.3 %collective-permute-done.refs_0_ = bf16[256,576]{1,0:T(8,128)(2,1)S(1)} collective-permute-done((bf16[256,576]{1,0:T(8,128)(2,1)S(1)}, bf16[256,576]{1,0:T(8,128)(2,1)S(1)}, u32[]{:S(2)}, u32[]{:S(2)}) %collective-permute-start) | collective-permute-done | bytes 294944 | tf_op jit(solution)/shard_map/ppermute | solution.py:451
  38.7 0.0 collective-permute-start.3
  38.7 0.5 collective-permute-start.4
  39.2 0.3 collective-permute-start.5
  39.5 0.8 collective-permute-done.3.refs_2_
  40.3 0.5 collective-permute-done.4.refs_3_
  40.8 5.5 %shard_map.88 = (bf16[1536,2048]{1,0:T(8,128)(2,1)S(1)}, bf16[1536,2048]{1,0:T(8,128)(2,1)S(1)}, bf16[2048,576]{1,0:T(8,128)(2,1)S(1)}, f32[9,1536,128]{2,1,0:T(...) custom-call(bf16[256,576]{1,0:T(8,128)(2,1)S(1)} %collective-permute, ...), custom_call_target="tpu_custom_call", output_to_operand_aliasing={{0}: (5, {}), {1}: (6, {}), {2}: (7, {}), {3}: (8, {}), {4}... | custom-call | flops 3422552064 | tf_op jit(solution)/shard_map/pallas_call | solution.py:163
  46.3 2.5 %collective-permute-done.5.refs_0_ = bf16[256,576]{1,0:T(8,128)(2,1)S(1)} collective-permute-done((bf16[256,576]{1,0:T(8,128)(2,1)S(1)}, bf16[256,576]{1,0:T(8,128)(2,1)S(1)}, u32[]{:S(2)}, u32[]{:S(2)}) %collective-permute-start.5) | collective-permute-done | bytes 294944 | tf_op jit(solution)/shard_map/ppermute | solution.py:451
  48.8 0.0 collective-permute-start.6
  48.8 1.4 %shard_map.89 = (bf16[576,1536]{1,0:T(8,128)(2,1)S(1)}, bf16[512,1536]{1,0:T(8,128)(2,1)S(1)}) custom-call(bf16[96,16,576]{2,1,0:T(8,128)(2,1)S(1)} %get-tuple-element.89.q_ref.refs_7_, bf16[96,16,512]{2,1,0:T(8,128)(2,1)S(1)} %get-tuple-element.93.g_ref.refs_8_), custom_call_target="tpu_custom_call" | custom-call | tf_op jit(solution)/shard_map/pallas_call | solution.py:163
  50.2 0.2 collective-permute-done.6.refs_1_
  50.4 2.8 %shard_map.90 = (bf16[1536,2048]{1,0:T(8,128)(2,1)S(1)}, bf16[1536,2048]{1,0:T(8,128)(2,1)S(1)}, bf16[2048,576]{1,0:T(8,128)(2,1)S(1)}, f32[9,1536,128]{2,1,0:T(...) custom-call(bf16[256,576]{1,0:T(8,128)(2,1)S(1)} %collective-permute, ...), custom_call_target="tpu_custom_call", output_to_operand_aliasing={{0}: (3, {}), {1}: (4, {}), {2}: (5, {}), {3}: (6, {}), {4}... | custom-call | flops 1711276032 | tf_op jit(solution)/shard_map/pallas_call | solution.py:163
  53.2 2.2 %shard_map.91 = (bf16[256,576]{1,0:T(8,128)(2,1)S(1)}, bf16[1536,2048]{1,0:T(8,128)(2,1)S(1)}, bf16[1536,2048]{1,0:T(8,128)(2,1)S(1)}, f32[4,1536,128]{2,1,0:T(8...) custom-call(bf16[576,1536]{1,0:T(8,128)(2,1)S(1)} %get-tuple-element, ...), custom_call_target="tpu_custom_call", output_to_operand_aliasing={{1}: (2, {}), {2}: (3, {}), {4}: (5, {})} | custom-call | flops 855638016 | tf_op jit(solution)/shard_map/pallas_call | solution.py:163
  55.4 0.6 collective-permute-start.7
  56.0 1.7 %shard_map.92 = (bf16[256,576]{1,0:T(8,128)(2,1)S(1)}, bf16[1536,2048]{1,0:T(8,128)(2,1)S(1)}, bf16[1536,2048]{1,0:T(8,128)(2,1)S(1)}, f32[4,1536,128]{2,1,0:T(8...) custom-call(bf16[576,1536]{1,0:T(8,128)(2,1)S(1)} %get-tuple-element, ...), custom_call_target="tpu_custom_call", output_to_operand_aliasing={{1}: (2, {}), {2}: (3, {}), {4}: (5, {}), {3}: (4, {})} | custom-call | flops 855638016 | tf_op jit(solution)/shard_map/pallas_call | solution.py:163
  57.7 1.7 %shard_map.93 = (bf16[256,576]{1,0:T(8,128)(2,1)S(1)}, bf16[1536,2048]{1,0:T(8,128)(2,1)S(1)}, bf16[1536,2048]{1,0:T(8,128)(2,1)S(1)}, f32[4,1536,128]{2,1,0:T(8...) custom-call(bf16[576,1536]{1,0:T(8,128)(2,1)S(1)} %get-tuple-element, ...), custom_call_target="tpu_custom_call", output_to_operand_aliasing={{1}: (2, {}), {2}: (3, {}), {4}: (5, {}), {3}: (4, {})} | custom-call | flops 855638016 | tf_op jit(solution)/shard_map/pallas_call | solution.py:163
  59.4 0.0 collective-permute-done.7.far_ref
  59.4 0.1 shard_map.94
  59.5 3.0 %shard_map.95 = (bf16[512,576]{1,0:T(8,128)(2,1)S(1)}, bf16[1536,2048]{1,0:T(8,128)(2,1)S(1)}, bf16[1536,2048]{1,0:T(8,128)(2,1)S(1)}, f32[4,1536,128]{2,1,0:T(8...) custom-call(bf16[576,1536]{1,0:T(8,128)(2,1)S(1)} %get-tuple-element, ...), custom_call_target="tpu_custom_call", output_to_operand_aliasing={{1}: (2, {}), {2}: (3, {}), {4}: (5, {}), {3}: (4, {})} | custom-call | flops 1711276032 | tf_op jit(solution)/shard_map/pallas_call | solution.py:163
  62.5 0.3 collective-permute-start.8
  62.8 1.5 %collective-permute-start.9 = (bf16[256,576]{1,0:T(8,128)(2,1)S(1)}, bf16[256,576]{1,0:T(8,128)(2,1)S(1)}, u32[]{:S(2)}, u32[]{:S(2)}) collective-permute-start(bf16[256,576]{1,0:T(8,128)(2,1)S(1)} %shard_map.94), channel_id=1, source_target_pairs={{0,6},{1,7},{2,4},{3,5},{4,2},{5,3},{6,0},{7,1},{8,14},{9,15},{10,... | collective-permute-start | bytes 884744 | tf_op jit(solution)/shard_map/ppermute | solution.py:451
  64.3 0.0 collective-permute-start.10
  64.3 3.0 %shard_map.96 = (bf16[512,576]{1,0:T(8,128)(2,1)S(1)}, bf16[1536,2048]{1,0:T(8,128)(2,1)S(1)}, bf16[1536,2048]{1,0:T(8,128)(2,1)S(1)}, f32[4,1536,128]{2,1,0:T(8...) custom-call(bf16[576,1536]{1,0:T(8,128)(2,1)S(1)} %get-tuple-element, ...), custom_call_target="tpu_custom_call", output_to_operand_aliasing={{1}: (2, {}), {2}: (3, {}), {4}: (5, {}), {3}: (4, {})} | custom-call | flops 1711276032 | tf_op jit(solution)/shard_map/pallas_call | solution.py:163
  67.3 0.0 collective-permute-done.8
  67.3 0.1 shard_map.97
  67.4 1.8 %collective-permute-start.12 = (bf16[256,576]{1,0:T(8,128)(2,1)S(1)}, bf16[256,576]{1,0:T(8,128)(2,1)S(1)}, u32[]{:S(2)}, u32[]{:S(2)}) collective-permute-start(bf16[256,576]{1,0:T(8,128)(2,1)S(1)} %shard_map.97), channel_id=1, source_target_pairs={{0,6},{1,7},{2,4},{3,5},{4,2},{5,3},{6,0},{7,1},{8,14},{9,15},{10,... | collective-permute-start | bytes 884744 | tf_op jit(solution)/shard_map/ppermute | solution.py:451
  69.2 5.4 %collective-permute-done.9.two_ref = bf16[256,576]{1,0:T(8,128)(2,1)S(1)} collective-permute-done((bf16[256,576]{1,0:T(8,128)(2,1)S(1)}, bf16[256,576]{1,0:T(8,128)(2,1)S(1)}, u32[]{:S(2)}, u32[]{:S(2)}) %collective-permute-start.9) | collective-permute-done | bytes 294944 | tf_op jit(solution)/shard_map/ppermute | solution.py:451
  74.6 0.1 shard_map.98
  74.7 0.1 collective-permute-start.11
  74.8 1.7 %shard_map.99 = (bf16[256,576]{1,0:T(8,128)(2,1)S(1)}, bf16[1536,2048]{1,0:T(8,128)(2,1)S(1)}, bf16[1536,2048]{1,0:T(8,128)(2,1)S(1)}, f32[4,1536,128]{2,1,0:T(8...) custom-call(bf16[576,1536]{1,0:T(8,128)(2,1)S(1)} %get-tuple-element, ...), custom_call_target="tpu_custom_call", output_to_operand_aliasing={{1}: (2, {}), {2}: (3, {}), {4}: (5, {}), {3}: (4, {})} | custom-call | flops 855638016 | tf_op jit(solution)/shard_map/pallas_call | solution.py:163
  76.5 5.6 %shard_map.100 = (bf16[96,16,512]{2,1,0:T(8,128)(2,1)}, bf16[96,16,576]{2,1,0:T(8,128)(2,1)}) custom-call(bf16[1536,2048]{1,0:T(8,128)(2,1)S(1)} %get-tuple-element.134.w_ref, bf16[1536,2048]{1,0:T(8,128)(2,1)S(1)} %get-tuple-element.135.s_ref, bf16[2048,576]{1,0:T(8,128)(2,1)S(1)} %get-tuple-element.137.k_ref), custom_call_target="tpu_custom_call" | custom-call | flops 3825205248 | tf_op jit(solution)/shard_map/pallas_call | solution.py:163
  82.1 0.0 collective-permute-done.10.b_ref
  82.1 1.1 %collective-permute-done.11.c_ref = bf16[256,576]{1,0:T(8,128)(2,1)S(1)} collective-permute-done((bf16[256,576]{1,0:T(8,128)(2,1)S(1)}, bf16[256,576]{1,0:T(8,128)(2,1)S(1)}, u32[]{:S(2)}, u32[]{:S(2)}) %collective-permute-start.11) | collective-permute-done | bytes 294944 | tf_op jit(solution)/shard_map/ppermute | solution.py:451
  83.2 0.0 collective-permute-done.12.d_ref
  83.2 1.7 %shard_map.101 = bf16[32,16,576]{2,1,0:T(8,128)(2,1)} custom-call(s32[16,16]{1,0:T(8,128)} %lists.5, s32[16]{0:T(128)} %counts.5, s32[1]{0:T(128)} %bitcast.me, bf16[256,576]{1,0:T(8,128)(2,1)S(1)} %get-tuple-element.147.a_ref, bf16[256,576]{1,0:T(8,128)(2,1)S(1)} %collective-permute-done.10.b_ref, bf16[256,576]{1,0:T(8,128)(2,1)S(1)} %collective-permute-done.11.c_ref, ...), custom_call_target="tpu_custom_call" | custom-call | tf_op jit(solution)/shard_map/pallas_call | solution.py:163
  84.9 3.8 %all-to-all-start.1 = ((bf16[16,2,16,576]{3,2,1,0:T(8,128)(2,1)}), bf16[16,2,16,576]{3,2,1,0:T(8,128)(2,1)S(1)}, u32[]{:S(2)}, u32[]{:S(2)}) async-start(bf16[16,2,16,576]{3,2,1,0:T(8,128)(2,1)} %bitcast.38), calls=%async_computation.1 | async-start | bytes 1310720 | tf_op jit(solution)/shard_map/all_to_all | solution.py:557
  88.7 9.5 %shard_map.102 = bf16[96,16,576]{2,1,0:T(8,128)(2,1)} custom-call(bf16[1,1280,256]{2,1,0:T(8,128)(2,1)} %get-tuple-element.139.refs_0_, bf16[1,1280,256]{2,1,0:T(8,128)(2,1)} %get-tuple-element.140.refs_1_, bf16[1,1280,256]{2,1,0:T(8,128)(2,1)} %get-tuple-element.141.refs_2_, ...), custom_call_target="tpu_custom_call", output_to_operand_aliasing={{}: (7, {})} | custom-call | flops 3019898880 | tf_op jit(solution)/shard_map/pallas_call | solution.py:163
  98.2 1.5 %all-to-all-done.1 = bf16[16,2,16,576]{3,2,1,0:T(8,128)(2,1)S(1)} async-done(((bf16[16,2,16,576]{3,2,1,0:T(8,128)(2,1)}), bf16[16,2,16,576]{3,2,1,0:T(8,128)(2,1)S(1)}, u32[]{:S(2)}, u32[]{:S(2)}) %all-to-all-start.1) | async-done | bytes 589856 | tf_op jit(solution)/shard_map/all_to_all | solution.py:557
  99.7 1.8 %shard_map.103 = f32[16,16,576]{2,1,0:T(8,128)} custom-call(s32[33]{0:T(128)} %get-tuple-element.150.table, bf16[32,16,576]{2,1,0:T(8,128)(2,1)S(1)} %bitcast.33), custom_call_target="tpu_custom_call" | custom-call | tf_op jit(solution)/shard_map/pallas_call | solution.py:163
  (7 shorter events, 0.0 us)
Async XLA Ops:
  3.8 21.1 %all-to-all-start = ((bf16[16,2,16,576]{3,2,1,0:T(8,128)(2,1)}), bf16[16,2,16,576]{3,2,1,0:T(8,128)(2,1)S(1)}, u32[]{:S(2)}, u32[]{:S(2)}) async-start(bf16[16,2,16,576]{3,2,1,0:T(8,128)(2,1)} %bitcast.39), calls=%async_computation | async-start | bytes 1310720 | tf_op jit(solution)/shard_map/all_to_all | solution.py:475
  26.0 3.2 %collective-permute-start.1 = (bf16[256,576]{1,0:T(8,128)(2,1)S(1)}, bf16[256,576]{1,0:T(8,128)(2,1)S(1)}, u32[]{:S(2)}, u32[]{:S(2)}) collective-permute-start(bf16[256,576]{1,0:T(8,128)(2,1)S(1)} %shard_map.86.refs_0_), channel_id=1, source_target_pairs={{0,1},{1,0},{2,3},{3,2},{4,5},{5,4},{6,7},{7,6},{8,9},{9,8},{10,11... | collective-permute-start | bytes 884744 | tf_op jit(solution)/shard_map/ppermute | solution.py:451
  26.1 11.3 %collective-permute-start.2 = (bf16[256,576]{1,0:T(8,128)(2,1)S(1)}, bf16[256,576]{1,0:T(8,128)(2,1)S(1)}, u32[]{:S(2)}, u32[]{:S(2)}) collective-permute-start(bf16[256,576]{1,0:T(8,128)(2,1)S(1)} %shard_map.86.refs_0_), channel_id=1, source_target_pairs={{0,6},{1,7},{2,4},{3,5},{4,2},{5,3},{6,0},{7,1},{8,14},{9,15},{10,... | collective-permute-start | bytes 884744 | tf_op jit(solution)/shard_map/ppermute | solution.py:451
  28.9 9.8 %collective-permute-start = (bf16[256,576]{1,0:T(8,128)(2,1)S(1)}, bf16[256,576]{1,0:T(8,128)(2,1)S(1)}, u32[]{:S(2)}, u32[]{:S(2)}) collective-permute-start(bf16[256,576]{1,0:T(8,128)(2,1)S(1)} %shard_map.86.refs_0_), channel_id=1, source_target_pairs={{0,2},{1,3},{2,0},{3,1},{4,6},{5,7},{6,4},{7,5},{8,10},{9,11},{10,... | collective-permute-start | bytes 884744 | tf_op jit(solution)/shard_map/ppermute | solution.py:451
  38.7 1.6 %collective-permute-start.3 = (bf16[256,576]{1,0:T(8,128)(2,1)S(1)}, bf16[256,576]{1,0:T(8,128)(2,1)S(1)}, u32[]{:S(2)}, u32[]{:S(2)}) collective-permute-start(bf16[256,576]{1,0:T(8,128)(2,1)S(1)} %collective-permute-done.refs_0_), channel_id=1, source_target_pairs={{0,1},{1,0},{2,3},{3,2},{4,5},{5,4},{6,7},{7,6},{8,9},{9,8},{10,11... | collective-permute-start | bytes 884744 | tf_op jit(solution)/shard_map/ppermute | solution.py:451
  38.7 2.1 %collective-permute-start.4 = (bf16[256,576]{1,0:T(8,128)(2,1)S(1)}, bf16[256,576]{1,0:T(8,128)(2,1)S(1)}, u32[]{:S(2)}, u32[]{:S(2)}) collective-permute-start(bf16[256,576]{1,0:T(8,128)(2,1)S(1)} %collective-permute-done.2.refs_1_), channel_id=1, source_target_pairs={{0,1},{1,0},{2,3},{3,2},{4,5},{5,4},{6,7},{7,6},{8,9},{9,8},{10,11... | collective-permute-start | bytes 884744 | tf_op jit(solution)/shard_map/ppermute | solution.py:451
  39.2 9.6 %collective-permute-start.5 = (bf16[256,576]{1,0:T(8,128)(2,1)S(1)}, bf16[256,576]{1,0:T(8,128)(2,1)S(1)}, u32[]{:S(2)}, u32[]{:S(2)}) collective-permute-start(bf16[256,576]{1,0:T(8,128)(2,1)S(1)} %collective-permute-done.2.refs_1_), channel_id=1, source_target_pairs={{0,2},{1,3},{2,0},{3,1},{4,6},{5,7},{6,4},{7,5},{8,10},{9,11},{10,... | collective-permute-start | bytes 884744 | tf_op jit(solution)/shard_map/ppermute | solution.py:451
  48.8 1.6 %collective-permute-start.6 = (bf16[256,576]{1,0:T(8,128)(2,1)S(1)}, bf16[256,576]{1,0:T(8,128)(2,1)S(1)}, u32[]{:S(2)}, u32[]{:S(2)}) collective-permute-start(bf16[256,576]{1,0:T(8,128)(2,1)S(1)} %collective-permute-done.5.refs_0_), channel_id=1, source_target_pairs={{0,1},{1,0},{2,3},{3,2},{4,5},{5,4},{6,7},{7,6},{8,9},{9,8},{10,11... | collective-permute-start | bytes 884744 | tf_op jit(solution)/shard_map/ppermute | solution.py:451
  55.4 4.0 %collective-permute-start.7 = (bf16[256,576]{1,0:T(8,128)(2,1)S(1)}, bf16[256,576]{1,0:T(8,128)(2,1)S(1)}, u32[]{:S(2)}, u32[]{:S(2)}) collective-permute-start(bf16[256,576]{1,0:T(8,128)(2,1)S(1)} %get-tuple-element.119), channel_id=1, source_target_pairs={{0,1},{1,0},{2,3},{3,2},{4,5},{5,4},{6,7},{7,6},{8,9},{9,8},{10,11... | collective-permute-start | bytes 884744 | tf_op jit(solution)/shard_map/ppermute | solution.py:451
  62.5 4.8 %collective-permute-start.8 = (bf16[32,16,576]{2,1,0:T(8,128)(2,1)S(1)}, bf16[32,16,576]{2,1,0:T(8,128)(2,1)S(1)}, u32[]{:S(2)}, u32[]{:S(2)}) collective-permute-start(bf16[32,16,576]{2,1,0:T(8,128)(2,1)S(1)} %bitcast.37), channel_id=1, source_target_pairs={{0,1},{1,0},{2,3},{3,2},{4,5},{5,4},{6,7},{7,6},{8,9},{9,8},{10,11... | collective-permute-start | bytes 1769480 | tf_op jit(solution)/shard_map/ppermute | solution.py:451
  62.8 11.8 %collective-permute-start.9 = (bf16[256,576]{1,0:T(8,128)(2,1)S(1)}, bf16[256,576]{1,0:T(8,128)(2,1)S(1)}, u32[]{:S(2)}, u32[]{:S(2)}) collective-permute-start(bf16[256,576]{1,0:T(8,128)(2,1)S(1)} %shard_map.94), channel_id=1, source_target_pairs={{0,6},{1,7},{2,4},{3,5},{4,2},{5,3},{6,0},{7,1},{8,14},{9,15},{10,... | collective-permute-start | bytes 884744 | tf_op jit(solution)/shard_map/ppermute | solution.py:451
  64.3 17.8 %collective-permute-start.10 = (bf16[256,576]{1,0:T(8,128)(2,1)S(1)}, bf16[256,576]{1,0:T(8,128)(2,1)S(1)}, u32[]{:S(2)}, u32[]{:S(2)}) collective-permute-start(bf16[256,576]{1,0:T(8,128)(2,1)S(1)} %get-tuple-element.117), channel_id=1, source_target_pairs={{0,1},{1,0},{2,3},{3,2},{4,5},{5,4},{6,7},{7,6},{8,9},{9,8},{10,11... | collective-permute-start | bytes 884744 | tf_op jit(solution)/shard_map/ppermute | solution.py:451
  67.4 15.8 %collective-permute-start.12 = (bf16[256,576]{1,0:T(8,128)(2,1)S(1)}, bf16[256,576]{1,0:T(8,128)(2,1)S(1)}, u32[]{:S(2)}, u32[]{:S(2)}) collective-permute-start(bf16[256,576]{1,0:T(8,128)(2,1)S(1)} %shard_map.97), channel_id=1, source_target_pairs={{0,6},{1,7},{2,4},{3,5},{4,2},{5,3},{6,0},{7,1},{8,14},{9,15},{10,... | collective-permute-start | bytes 884744 | tf_op jit(solution)/shard_map/ppermute | solution.py:451
  74.7 8.5 %collective-permute-start.11 = (bf16[256,576]{1,0:T(8,128)(2,1)S(1)}, bf16[256,576]{1,0:T(8,128)(2,1)S(1)}, u32[]{:S(2)}, u32[]{:S(2)}) collective-permute-start(bf16[256,576]{1,0:T(8,128)(2,1)S(1)} %shard_map.98), channel_id=1, source_target_pairs={{0,2},{1,3},{2,0},{3,1},{4,6},{5,7},{6,4},{7,5},{8,10},{9,11},{10,... | collective-permute-start | bytes 884744 | tf_op jit(solution)/shard_map/ppermute | solution.py:451
  84.9 14.8 %all-to-all-start.1 = ((bf16[16,2,16,576]{3,2,1,0:T(8,128)(2,1)}), bf16[16,2,16,576]{3,2,1,0:T(8,128)(2,1)S(1)}, u32[]{:S(2)}, u32[]{:S(2)}) async-start(bf16[16,2,16,576]{3,2,1,0:T(8,128)(2,1)} %bitcast.38), calls=%async_computation.1 | async-start | bytes 1310720 | tf_op jit(solution)/shard_map/all_to_all | solution.py:557

commit v12 on v11

--- a/solution.py
+++ b/solution.py
@@ -131,19 +131,25 @@
         gt_ref[:, here] = g_ref[part].reshape(256, LAT).T
 
 
-def two_body(near_ref, far_ref, out_ref):
-    out_ref[...] = (near_ref[...].astype(f32) + far_ref[...].astype(f32)).astype(bf16)
-
-
-def wrap_body(near_ref, far_ref, out_ref):
-    size = out_ref.shape[0]
-    out_ref[...] = (near_ref[size:].astype(f32) + far_ref[size:].astype(f32)).astype(bf16)
-
-
-def next_body(near_ref, far_ref, two_ref, out_ref):
-    size = out_ref.shape[0]
+def two_body(near_ref, far_ref, low_ref, high_ref):
+    half = low_ref.shape[0]
+    total = near_ref[...].astype(f32) + far_ref[...].astype(f32)
+    low_ref[...] = total[:half].astype(bf16)
+    high_ref[...] = total[half:].astype(bf16)
+
+
+def wrap_body(near_ref, far_ref, low_ref, out_ref):
+    size, half = out_ref.shape[0], low_ref.shape[0]
+    total = near_ref[size:].astype(f32) + far_ref[size:].astype(f32)
+    out_ref[:half] = (total[:half] + low_ref[...].astype(f32)).astype(bf16)
+    out_ref[half:] = total[half:].astype(bf16)
+
+
+def next_body(near_ref, far_ref, high_ref, out_ref):
+    size, half = out_ref.shape[0], high_ref.shape[0]
     total = near_ref[:size].astype(f32) + far_ref[:size].astype(f32)
-    out_ref[...] = (total + two_ref[...].astype(f32)).astype(bf16)
+    out_ref[:half] = total[:half].astype(bf16)
+    out_ref[half:] = (total[half:] + high_ref[...].astype(f32)).astype(bf16)
 
 
 ONCHIP = pl.BlockSpec(memory_space=pltpu.VMEM)
@@ -525,15 +531,16 @@
     mate2 = send(far2, sibling)
     near2, e, p, row, k, sg2n = back(2, (6 * keys,), keys, e=e, p=p, row=row, k=k)
     far0, e, p, row, k, sg0f = back(0, (keys,), keys, e=e, p=p, row=row, k=k)
-    (two,) = call(two_body, (share_of(keys),), (), (after(near2, far0), mate2))
-    got_two = send(two, pair_b)
-    far1, e, p, row, k, sg1f, k_saved = back(1, (4 * keys,), 2 * keys, e=e, p=p, row=after(row, two), k=k, final=True)
+    low, high = call(two_body, (share_of(keys // 2),) * 2, (), (after(near2, far0), mate2))
+    got_high = send(high, pair_b)
+    got_low = send(low, pair_a)
+    far1, e, p, row, k, sg1f, k_saved = back(1, (4 * keys,), 2 * keys, e=e, p=p, row=after(row, low), k=k, final=True)
     mate1 = unfold(send(fold(far1), sibling))
     near1, e, p, row, k, sg1n = back(1, (2 * keys,), 2 * keys, e=e, p=p, row=row, k=k)
     mate0 = send(far0, sibling)
-    (to_b,) = call(wrap_body, (share_of(keys),), (), (near1, mate1))
+    (to_b,) = call(wrap_body, (share_of(keys),), (), (near1, mate1, got_low))
     got_b = send(to_b, pair_b)
-    (to_a,) = call(next_body, (share_of(keys),), (), (after(near1, to_b), mate1, got_two))
+    (to_a,) = call(next_body, (share_of(keys),), (), (after(near1, to_b), mate1, got_high))
     got_a = send(to_a, pair_a)
     near0, e, p, row, k, sg0n = back(0, (0,), keys, e=e, p=p, row=after(row, to_a), k=k)
     attended, query_grad = value_side(e, p, after(k, to_a), early)

time: 102 us -> 99.4 us (0.975)
  waiting for transfers between devices: 26.1 us -> 22.9 us
    ppermute x13 -> x14, waiting for transfers between devices: 15.7 us -> 12.1 us  [per_device(): send = lambda a, perm: lax.ppermute(a, 'head', perm)]
    ppermute x13 -> x14, starting transfers between devices: 8.22 us -> 8.59 us  [per_device(): send = lambda a, perm: lax.ppermute(a, 'head', perm)]
  transfers between devices with their start and end apart: 15 -> 16, of which waited for: 10 -> 10; matrix products, arithmetic and copies ran while one was open for 4% -> 4% of each run, Pallas kernels for 34% -> 35%
where the time goes in v12:
time: 99.4 us; the launch traced here: 98.8 us
  Pallas kernels  50.4 us (51%)
  waiting for transfers between devices  22.9 us (23%)
  starting transfers between devices  20.6 us (21%)
  local copies, waits for them, and re-layouts  2.28 us (2%)
  other arithmetic  1.59 us (2%)
  between operations  1.05 us (1%)
    pallas_call x19, Pallas kernels, call(): pl.pallas_call(body, in_specs=[small] * len(scalars) + [INPLACE if i in d...  50.4 us
    ppermute x14, waiting for transfers between devices, per_device(): send = lambda a, perm: lax.ppermute(a, 'head', perm)  12.1 us
    all_to_all x1, waiting for transfers between devices, per_device(): lax.all_to_all(outgoing.reshape(16, CAP, tokens, WIDE), 'req', 0, 0, tile...  8.95 us
    ppermute x14, starting transfers between devices, per_device(): send = lambda a, perm: lax.ppermute(a, 'head', perm)  8.59 us
    all_to_all x1, starting transfers between devices, per_device(): lax.all_to_all(outgoing.reshape(16, CAP, tokens, WIDE), 'req', 0, 0, tile...  8.17 us
    all_to_all x1, starting transfers between devices, per_device(): lax.all_to_all(slot_grads.reshape(16, CAP, tokens, WIDE), 'req', 0, 0, ti...  3.83 us
  transfers between devices with their start and end apart: 16, of which 10 were waited for; matrix products, arithmetic and copies ran while one was open for 4% of the time, Pallas kernels for 35%

profile of v12, /device:TPU:0, one launch (start us, length us, event | category | flops | bytes accessed | tf_op | source)
XLA Modules:
  0.0 98.8 jit_solution(10023672841356629000)
XLA Ops:
  0.6 3.2 %shard_map.85 = (bf16[32,16,576]{2,1,0:T(8,128)(2,1)}, s32[33]{0:T(128)}) custom-call(s32[16,16]{1,0:T(8,128)} %lists.5, s32[16]{0:T(128)} %counts.5, s32[1]{0:T(128)} %bitcast.me, bf16[16,16,576]{2,1,0:T(8,128)(2,1)} %lat_ref.1), custom_call_target="tpu_custom_call" | custom-call | tf_op jit(solution)/shard_map/pallas_call | solution.py:169
  3.8 8.2 %all-to-all-start = ((bf16[16,2,16,576]{3,2,1,0:T(8,128)(2,1)}), bf16[16,2,16,576]{3,2,1,0:T(8,128)(2,1)S(1)}, u32[]{:S(2)}, u32[]{:S(2)}) async-start(bf16[16,2,16,576]{3,2,1,0:T(8,128)(2,1)} %bitcast.39), calls=%async_computation | async-start | bytes 1310720 | tf_op jit(solution)/shard_map/all_to_all | solution.py:481
  12.0 1.2 %dynamic_slice.8 = s32[1]{0:T(128)} dynamic-slice(s32[16]{0:T(128)} %counts.5, s32[]{:T(128)S(6)} %select_n.31), dynamic_slice_sizes={1} | dynamic-slice | bytes 12 | tf_op jit(solution)/shard_map/jit(dynamic_index_in_dim)/dynamic_slice | solution.py:484
  13.3 0.7 dynamic-slice_bitcast_fusion
  14.0 0.1 stack.35
  14.1 0.9 select_reduce_fusion
  14.9 0.7 compare_select_fusion
  15.6 0.1 broadcast_in_dim.34
  15.7 0.1 lt.32
  15.7 0.1 add.60
  15.8 0.1 fusion
  15.9 9.0 %all-to-all-done = bf16[16,2,16,576]{3,2,1,0:T(8,128)(2,1)S(1)} async-done(((bf16[16,2,16,576]{3,2,1,0:T(8,128)(2,1)}), bf16[16,2,16,576]{3,2,1,0:T(8,128)(2,1)S(1)}, u32[]{:S(2)}, u32[]{:S(2)}) %all-to-all-start) | async-done | bytes 589856 | tf_op jit(solution)/shard_map/all_to_all | solution.py:481
  24.9 1.1 %shard_map.86.refs_0_ = bf16[256,576]{1,0:T(8,128)(2,1)S(1)} custom-call(s32[16,16]{1,0:T(8,128)} %lists.5, s32[16]{0:T(128)} %counts.5, s32[1]{0:T(128)} %bitcast.me, bf16[32,16,576]{2,1,0:T(8,128)(2,1)S(1)} %bitcast.32), custom_call_target="tpu_custom_call" | custom-call | tf_op jit(solution)/shard_map/pallas_call | solution.py:169
  26.0 0.1 collective-permute-start.1
  26.1 2.8 %collective-permute-start.2 = (bf16[256,576]{1,0:T(8,128)(2,1)S(1)}, bf16[256,576]{1,0:T(8,128)(2,1)S(1)}, u32[]{:S(2)}, u32[]{:S(2)}) collective-permute-start(bf16[256,576]{1,0:T(8,128)(2,1)S(1)} %shard_map.86.refs_0_), channel_id=1, source_target_pairs={{0,6},{1,7},{2,4},{3,5},{4,2},{5,3},{6,0},{7,1},{8,14},{9,15},{10,... | collective-permute-start | bytes 884744 | tf_op jit(solution)/shard_map/ppermute | solution.py:457
  28.9 0.2 collective-permute-start
  29.1 0.0 collective-permute-done.1.refs_1_
  29.1 4.4 %shard_map.87 = (bf16[1536,2048]{1,0:T(8,128)(2,1)S(1)}, bf16[1536,2048]{1,0:T(8,128)(2,1)S(1)}, bf16[2048,576]{1,0:T(8,128)(2,1)S(1)}, f32[9,1536,128]{2,1,0:T(...) custom-call(bf16[256,576]{1,0:T(8,128)(2,1)S(1)} %shard_map.86.refs_0_, ...), custom_call_target="tpu_custom_call" | custom-call | flops 1711276032 | tf_op jit(solution)/shard_map/pallas_call | solution.py:169
  33.5 3.9 %collective-permute-done.2.refs_1_ = bf16[256,576]{1,0:T(8,128)(2,1)S(1)} collective-permute-done((bf16[256,576]{1,0:T(8,128)(2,1)S(1)}, bf16[256,576]{1,0:T(8,128)(2,1)S(1)}, u32[]{:S(2)}, u32[]{:S(2)}) %collective-permute-start.2) | collective-permute-done | bytes 294944 | tf_op jit(solution)/shard_map/ppermute | solution.py:457
  37.4 1.3 %collective-permute-done.refs_0_ = bf16[256,576]{1,0:T(8,128)(2,1)S(1)} collective-permute-done((bf16[256,576]{1,0:T(8,128)(2,1)S(1)}, bf16[256,576]{1,0:T(8,128)(2,1)S(1)}, u32[]{:S(2)}, u32[]{:S(2)}) %collective-permute-start) | collective-permute-done | bytes 294944 | tf_op jit(solution)/shard_map/ppermute | solution.py:457
  38.7 0.0 collective-permute-start.3
  38.7 0.5 collective-permute-start.4
  39.2 0.3 collective-permute-start.5
  39.5 0.8 collective-permute-done.3.refs_2_
  40.3 0.5 collective-permute-done.4.refs_3_
  40.8 5.5 %shard_map.88 = (bf16[1536,2048]{1,0:T(8,128)(2,1)S(1)}, bf16[1536,2048]{1,0:T(8,128)(2,1)S(1)}, bf16[2048,576]{1,0:T(8,128)(2,1)S(1)}, f32[9,1536,128]{2,1,0:T(...) custom-call(bf16[256,576]{1,0:T(8,128)(2,1)S(1)} %collective-permute, ...), custom_call_target="tpu_custom_call", output_to_operand_aliasing={{0}: (5, {}), {1}: (6, {}), {2}: (7, {}), {3}: (8, {}), {4}... | custom-call | flops 3422552064 | tf_op jit(solution)/shard_map/pallas_call | solution.py:169
  46.3 2.5 %collective-permute-done.5.refs_0_ = bf16[256,576]{1,0:T(8,128)(2,1)S(1)} collective-permute-done((bf16[256,576]{1,0:T(8,128)(2,1)S(1)}, bf16[256,576]{1,0:T(8,128)(2,1)S(1)}, u32[]{:S(2)}, u32[]{:S(2)}) %collective-permute-start.5) | collective-permute-done | bytes 294944 | tf_op jit(solution)/shard_map/ppermute | solution.py:457
  48.8 0.0 collective-permute-start.6
  48.8 1.4 %shard_map.89 = (bf16[576,1536]{1,0:T(8,128)(2,1)S(1)}, bf16[512,1536]{1,0:T(8,128)(2,1)S(1)}) custom-call(bf16[96,16,576]{2,1,0:T(8,128)(2,1)S(1)} %get-tuple-element.91.q_ref.refs_7_, bf16[96,16,512]{2,1,0:T(8,128)(2,1)S(1)} %get-tuple-element.95.g_ref.refs_8_), custom_call_target="tpu_custom_call" | custom-call | tf_op jit(solution)/shard_map/pallas_call | solution.py:169
  50.2 0.2 collective-permute-done.6.refs_1_
  50.4 2.8 %shard_map.90 = (bf16[1536,2048]{1,0:T(8,128)(2,1)S(1)}, bf16[1536,2048]{1,0:T(8,128)(2,1)S(1)}, bf16[2048,576]{1,0:T(8,128)(2,1)S(1)}, f32[9,1536,128]{2,1,0:T(...) custom-call(bf16[256,576]{1,0:T(8,128)(2,1)S(1)} %collective-permute, ...), custom_call_target="tpu_custom_call", output_to_operand_aliasing={{0}: (3, {}), {1}: (4, {}), {2}: (5, {}), {3}: (6, {}), {4}... | custom-call | flops 1711276032 | tf_op jit(solution)/shard_map/pallas_call | solution.py:169
  53.2 2.2 %shard_map.91 = (bf16[256,576]{1,0:T(8,128)(2,1)S(1)}, bf16[1536,2048]{1,0:T(8,128)(2,1)S(1)}, bf16[1536,2048]{1,0:T(8,128)(2,1)S(1)}, f32[4,1536,128]{2,1,0:T(8...) custom-call(bf16[576,1536]{1,0:T(8,128)(2,1)S(1)} %get-tuple-element, ...), custom_call_target="tpu_custom_call", output_to_operand_aliasing={{1}: (2, {}), {2}: (3, {}), {4}: (5, {})} | custom-call | flops 855638016 | tf_op jit(solution)/shard_map/pallas_call | solution.py:169
  55.4 0.6 collective-permute-start.7
  56.0 1.7 %shard_map.92 = (bf16[256,576]{1,0:T(8,128)(2,1)S(1)}, bf16[1536,2048]{1,0:T(8,128)(2,1)S(1)}, bf16[1536,2048]{1,0:T(8,128)(2,1)S(1)}, f32[4,1536,128]{2,1,0:T(8...) custom-call(bf16[576,1536]{1,0:T(8,128)(2,1)S(1)} %get-tuple-element, ...), custom_call_target="tpu_custom_call", output_to_operand_aliasing={{1}: (2, {}), {2}: (3, {}), {4}: (5, {}), {3}: (4, {})} | custom-call | flops 855638016 | tf_op jit(solution)/shard_map/pallas_call | solution.py:169
  57.7 1.7 %shard_map.93 = (bf16[256,576]{1,0:T(8,128)(2,1)S(1)}, bf16[1536,2048]{1,0:T(8,128)(2,1)S(1)}, bf16[1536,2048]{1,0:T(8,128)(2,1)S(1)}, f32[4,1536,128]{2,1,0:T(8...) custom-call(bf16[576,1536]{1,0:T(8,128)(2,1)S(1)} %get-tuple-element, ...), custom_call_target="tpu_custom_call", output_to_operand_aliasing={{1}: (2, {}), {2}: (3, {}), {4}: (5, {}), {3}: (4, {})} | custom-call | flops 855638016 | tf_op jit(solution)/shard_map/pallas_call | solution.py:169
  59.4 0.0 collective-permute-done.7.far_ref
  59.4 0.1 shard_map.94
  59.5 3.0 %shard_map.95 = (bf16[512,576]{1,0:T(8,128)(2,1)S(1)}, bf16[1536,2048]{1,0:T(8,128)(2,1)S(1)}, bf16[1536,2048]{1,0:T(8,128)(2,1)S(1)}, f32[4,1536,128]{2,1,0:T(8...) custom-call(bf16[576,1536]{1,0:T(8,128)(2,1)S(1)} %get-tuple-element, ...), custom_call_target="tpu_custom_call", output_to_operand_aliasing={{1}: (2, {}), {2}: (3, {}), {4}: (5, {}), {3}: (4, {})} | custom-call | flops 1711276032 | tf_op jit(solution)/shard_map/pallas_call | solution.py:169
  62.5 0.3 collective-permute-start.8
  62.8 0.3 collective-permute-start.11
  63.1 0.3 collective-permute-start.9
  63.4 1.5 %collective-permute-start.10 = (bf16[128,576]{1,0:T(8,128)(2,1)S(1)}, bf16[128,576]{1,0:T(8,128)(2,1)S(1)}, u32[]{:S(2)}, u32[]{:S(2)}) collective-permute-start(bf16[128,576]{1,0:T(8,128)(2,1)S(1)} %get-tuple-element.135), channel_id=1, source_target_pairs={{0,6},{1,7},{2,4},{3,5},{4,2},{5,3},{6,0},{7,1},{8,14},{9,15},{10,... | collective-permute-start | bytes 442376 | tf_op jit(solution)/shard_map/ppermute | solution.py:457
  64.9 3.0 %shard_map.96 = (bf16[512,576]{1,0:T(8,128)(2,1)S(1)}, bf16[1536,2048]{1,0:T(8,128)(2,1)S(1)}, bf16[1536,2048]{1,0:T(8,128)(2,1)S(1)}, f32[4,1536,128]{2,1,0:T(8...) custom-call(bf16[576,1536]{1,0:T(8,128)(2,1)S(1)} %get-tuple-element, ...), custom_call_target="tpu_custom_call", output_to_operand_aliasing={{1}: (2, {}), {2}: (3, {}), {4}: (5, {}), {3}: (4, {})} | custom-call | flops 1711276032 | tf_op jit(solution)/shard_map/pallas_call | solution.py:169
  67.8 1.6 %collective-permute-done.9.low_ref = bf16[128,576]{1,0:T(8,128)(2,1)S(1)} collective-permute-done((bf16[128,576]{1,0:T(8,128)(2,1)S(1)}, bf16[128,576]{1,0:T(8,128)(2,1)S(1)}, u32[]{:S(2)}, u32[]{:S(2)}) %collective-permute-start.9) | collective-permute-done | bytes 147488 | tf_op jit(solution)/shard_map/ppermute | solution.py:457
  69.4 0.0 collective-permute-done.8
  69.4 0.1 shard_map.97
  69.5 1.6 %collective-permute-start.13 = (bf16[256,576]{1,0:T(8,128)(2,1)S(1)}, bf16[256,576]{1,0:T(8,128)(2,1)S(1)}, u32[]{:S(2)}, u32[]{:S(2)}) collective-permute-start(bf16[256,576]{1,0:T(8,128)(2,1)S(1)} %shard_map.97), channel_id=1, source_target_pairs={{0,6},{1,7},{2,4},{3,5},{4,2},{5,3},{6,0},{7,1},{8,14},{9,15},{10,... | collective-permute-start | bytes 884744 | tf_op jit(solution)/shard_map/ppermute | solution.py:457
  71.1 0.0 collective-permute-done.10.high_ref
  71.1 0.1 shard_map.98
  71.2 0.1 collective-permute-start.12
  71.3 1.7 %shard_map.99 = (bf16[256,576]{1,0:T(8,128)(2,1)S(1)}, bf16[1536,2048]{1,0:T(8,128)(2,1)S(1)}, bf16[1536,2048]{1,0:T(8,128)(2,1)S(1)}, f32[4,1536,128]{2,1,0:T(8...) custom-call(bf16[576,1536]{1,0:T(8,128)(2,1)S(1)} %get-tuple-element, ...), custom_call_target="tpu_custom_call", output_to_operand_aliasing={{1}: (2, {}), {2}: (3, {}), {4}: (5, {}), {3}: (4, {})} | custom-call | flops 855638016 | tf_op jit(solution)/shard_map/pallas_call | solution.py:169
  73.0 5.6 %shard_map.100 = (bf16[96,16,512]{2,1,0:T(8,128)(2,1)}, bf16[96,16,576]{2,1,0:T(8,128)(2,1)}) custom-call(bf16[1536,2048]{1,0:T(8,128)(2,1)S(1)} %get-tuple-element.138.w_ref, bf16[1536,2048]{1,0:T(8,128)(2,1)S(1)} %get-tuple-element.139.s_ref, bf16[2048,576]{1,0:T(8,128)(2,1)S(1)} %get-tuple-element.141.k_ref), custom_call_target="tpu_custom_call" | custom-call | flops 3825205248 | tf_op jit(solution)/shard_map/pallas_call | solution.py:169
  78.6 0.0 collective-permute-done.11.b_ref
  78.6 1.3 %collective-permute-done.12.c_ref = bf16[256,576]{1,0:T(8,128)(2,1)S(1)} collective-permute-done((bf16[256,576]{1,0:T(8,128)(2,1)S(1)}, bf16[256,576]{1,0:T(8,128)(2,1)S(1)}, u32[]{:S(2)}, u32[]{:S(2)}) %collective-permute-start.12) | collective-permute-done | bytes 294944 | tf_op jit(solution)/shard_map/ppermute | solution.py:457
  80.0 0.0 collective-permute-done.13.d_ref
  80.0 1.7 %shard_map.101 = bf16[32,16,576]{2,1,0:T(8,128)(2,1)} custom-call(s32[16,16]{1,0:T(8,128)} %lists.5, s32[16]{0:T(128)} %counts.5, s32[1]{0:T(128)} %bitcast.me, bf16[256,576]{1,0:T(8,128)(2,1)S(1)} %get-tuple-element.151.a_ref, bf16[256,576]{1,0:T(8,128)(2,1)S(1)} %collective-permute-done.11.b_ref, bf16[256,576]{1,0:T(8,128)(2,1)S(1)} %collective-permute-done.12.c_ref, ...), custom_call_target="tpu_custom_call" | custom-call | tf_op jit(solution)/shard_map/pallas_call | solution.py:169
  81.7 3.8 %all-to-all-start.1 = ((bf16[16,2,16,576]{3,2,1,0:T(8,128)(2,1)}), bf16[16,2,16,576]{3,2,1,0:T(8,128)(2,1)S(1)}, u32[]{:S(2)}, u32[]{:S(2)}) async-start(bf16[16,2,16,576]{3,2,1,0:T(8,128)(2,1)} %bitcast.38), calls=%async_computation.1 | async-start | bytes 1310720 | tf_op jit(solution)/shard_map/all_to_all | solution.py:564
  85.5 9.5 %shard_map.102 = bf16[96,16,576]{2,1,0:T(8,128)(2,1)} custom-call(bf16[1,1280,256]{2,1,0:T(8,128)(2,1)} %get-tuple-element.143.refs_0_, bf16[1,1280,256]{2,1,0:T(8,128)(2,1)} %get-tuple-element.144.refs_1_, bf16[1,1280,256]{2,1,0:T(8,128)(2,1)} %get-tuple-element.145.refs_2_, ...), custom_call_target="tpu_custom_call", output_to_operand_aliasing={{}: (7, {})} | custom-call | flops 3019898880 | tf_op jit(solution)/shard_map/pallas_call | solution.py:169
  95.0 1.9 %all-to-all-done.1 = bf16[16,2,16,576]{3,2,1,0:T(8,128)(2,1)S(1)} async-done(((bf16[16,2,16,576]{3,2,1,0:T(8,128)(2,1)}), bf16[16,2,16,576]{3,2,1,0:T(8,128)(2,1)S(1)}, u32[]{:S(2)}, u32[]{:S(2)}) %all-to-all-start.1) | async-done | bytes 589856 | tf_op jit(solution)/shard_map/all_to_all | solution.py:564
  96.9 1.8 %shard_map.103 = f32[16,16,576]{2,1,0:T(8,128)} custom-call(s32[33]{0:T(128)} %get-tuple-element.154.table, bf16[32,16,576]{2,1,0:T(8,128)(2,1)S(1)} %bitcast.33), custom_call_target="tpu_custom_call" | custom-call | tf_op jit(solution)/shard_map/pallas_call | solution.py:169
  (7 shorter events, 0.0 us)
Async XLA Ops:
  3.8 21.1 %all-to-all-start = ((bf16[16,2,16,576]{3,2,1,0:T(8,128)(2,1)}), bf16[16,2,16,576]{3,2,1,0:T(8,128)(2,1)S(1)}, u32[]{:S(2)}, u32[]{:S(2)}) async-start(bf16[16,2,16,576]{3,2,1,0:T(8,128)(2,1)} %bitcast.39), calls=%async_computation | async-start | bytes 1310720 | tf_op jit(solution)/shard_map/all_to_all | solution.py:481
  26.0 3.2 %collective-permute-start.1 = (bf16[256,576]{1,0:T(8,128)(2,1)S(1)}, bf16[256,576]{1,0:T(8,128)(2,1)S(1)}, u32[]{:S(2)}, u32[]{:S(2)}) collective-permute-start(bf16[256,576]{1,0:T(8,128)(2,1)S(1)} %shard_map.86.refs_0_), channel_id=1, source_target_pairs={{0,1},{1,0},{2,3},{3,2},{4,5},{5,4},{6,7},{7,6},{8,9},{9,8},{10,11... | collective-permute-start | bytes 884744 | tf_op jit(solution)/shard_map/ppermute | solution.py:457
  26.1 11.3 %collective-permute-start.2 = (bf16[256,576]{1,0:T(8,128)(2,1)S(1)}, bf16[256,576]{1,0:T(8,128)(2,1)S(1)}, u32[]{:S(2)}, u32[]{:S(2)}) collective-permute-start(bf16[256,576]{1,0:T(8,128)(2,1)S(1)} %shard_map.86.refs_0_), channel_id=1, source_target_pairs={{0,6},{1,7},{2,4},{3,5},{4,2},{5,3},{6,0},{7,1},{8,14},{9,15},{10,... | collective-permute-start | bytes 884744 | tf_op jit(solution)/shard_map/ppermute | solution.py:457
  28.9 9.8 %collective-permute-start = (bf16[256,576]{1,0:T(8,128)(2,1)S(1)}, bf16[256,576]{1,0:T(8,128)(2,1)S(1)}, u32[]{:S(2)}, u32[]{:S(2)}) collective-permute-start(bf16[256,576]{1,0:T(8,128)(2,1)S(1)} %shard_map.86.refs_0_), channel_id=1, source_target_pairs={{0,2},{1,3},{2,0},{3,1},{4,6},{5,7},{6,4},{7,5},{8,10},{9,11},{10,... | collective-permute-start | bytes 884744 | tf_op jit(solution)/shard_map/ppermute | solution.py:457
  38.7 1.6 %collective-permute-start.3 = (bf16[256,576]{1,0:T(8,128)(2,1)S(1)}, bf16[256,576]{1,0:T(8,128)(2,1)S(1)}, u32[]{:S(2)}, u32[]{:S(2)}) collective-permute-start(bf16[256,576]{1,0:T(8,128)(2,1)S(1)} %collective-permute-done.refs_0_), channel_id=1, source_target_pairs={{0,1},{1,0},{2,3},{3,2},{4,5},{5,4},{6,7},{7,6},{8,9},{9,8},{10,11... | collective-permute-start | bytes 884744 | tf_op jit(solution)/shard_map/ppermute | solution.py:457
  38.7 2.1 %collective-permute-start.4 = (bf16[256,576]{1,0:T(8,128)(2,1)S(1)}, bf16[256,576]{1,0:T(8,128)(2,1)S(1)}, u32[]{:S(2)}, u32[]{:S(2)}) collective-permute-start(bf16[256,576]{1,0:T(8,128)(2,1)S(1)} %collective-permute-done.2.refs_1_), channel_id=1, source_target_pairs={{0,1},{1,0},{2,3},{3,2},{4,5},{5,4},{6,7},{7,6},{8,9},{9,8},{10,11... | collective-permute-start | bytes 884744 | tf_op jit(solution)/shard_map/ppermute | solution.py:457
  39.2 9.6 %collective-permute-start.5 = (bf16[256,576]{1,0:T(8,128)(2,1)S(1)}, bf16[256,576]{1,0:T(8,128)(2,1)S(1)}, u32[]{:S(2)}, u32[]{:S(2)}) collective-permute-start(bf16[256,576]{1,0:T(8,128)(2,1)S(1)} %collective-permute-done.2.refs_1_), channel_id=1, source_target_pairs={{0,2},{1,3},{2,0},{3,1},{4,6},{5,7},{6,4},{7,5},{8,10},{9,11},{10,... | collective-permute-start | bytes 884744 | tf_op jit(solution)/shard_map/ppermute | solution.py:457
  48.8 1.6 %collective-permute-start.6 = (bf16[256,576]{1,0:T(8,128)(2,1)S(1)}, bf16[256,576]{1,0:T(8,128)(2,1)S(1)}, u32[]{:S(2)}, u32[]{:S(2)}) collective-permute-start(bf16[256,576]{1,0:T(8,128)(2,1)S(1)} %collective-permute-done.5.refs_0_), channel_id=1, source_target_pairs={{0,1},{1,0},{2,3},{3,2},{4,5},{5,4},{6,7},{7,6},{8,9},{9,8},{10,11... | collective-permute-start | bytes 884744 | tf_op jit(solution)/shard_map/ppermute | solution.py:457
  55.4 4.0 %collective-permute-start.7 = (bf16[256,576]{1,0:T(8,128)(2,1)S(1)}, bf16[256,576]{1,0:T(8,128)(2,1)S(1)}, u32[]{:S(2)}, u32[]{:S(2)}) collective-permute-start(bf16[256,576]{1,0:T(8,128)(2,1)S(1)} %get-tuple-element.121), channel_id=1, source_target_pairs={{0,1},{1,0},{2,3},{3,2},{4,5},{5,4},{6,7},{7,6},{8,9},{9,8},{10,11... | collective-permute-start | bytes 884744 | tf_op jit(solution)/shard_map/ppermute | solution.py:457
  62.5 6.9 %collective-permute-start.8 = (bf16[32,16,576]{2,1,0:T(8,128)(2,1)S(1)}, bf16[32,16,576]{2,1,0:T(8,128)(2,1)S(1)}, u32[]{:S(2)}, u32[]{:S(2)}) collective-permute-start(bf16[32,16,576]{2,1,0:T(8,128)(2,1)S(1)} %bitcast.37), channel_id=1, source_target_pairs={{0,1},{1,0},{2,3},{3,2},{4,5},{5,4},{6,7},{7,6},{8,9},{9,8},{10,11... | collective-permute-start | bytes 1769480 | tf_op jit(solution)/shard_map/ppermute | solution.py:457
  62.8 15.8 %collective-permute-start.11 = (bf16[256,576]{1,0:T(8,128)(2,1)S(1)}, bf16[256,576]{1,0:T(8,128)(2,1)S(1)}, u32[]{:S(2)}, u32[]{:S(2)}) collective-permute-start(bf16[256,576]{1,0:T(8,128)(2,1)S(1)} %get-tuple-element.119), channel_id=1, source_target_pairs={{0,1},{1,0},{2,3},{3,2},{4,5},{5,4},{6,7},{7,6},{8,9},{9,8},{10,11... | collective-permute-start | bytes 884744 | tf_op jit(solution)/shard_map/ppermute | solution.py:457
  63.1 6.3 %collective-permute-start.9 = (bf16[128,576]{1,0:T(8,128)(2,1)S(1)}, bf16[128,576]{1,0:T(8,128)(2,1)S(1)}, u32[]{:S(2)}, u32[]{:S(2)}) collective-permute-start(bf16[128,576]{1,0:T(8,128)(2,1)S(1)} %get-tuple-element.122), channel_id=1, source_target_pairs={{0,2},{1,3},{2,0},{3,1},{4,6},{5,7},{6,4},{7,5},{8,10},{9,11},{10,... | collective-permute-start | bytes 442376 | tf_op jit(solution)/shard_map/ppermute | solution.py:457
  63.4 7.7 %collective-permute-start.10 = (bf16[128,576]{1,0:T(8,128)(2,1)S(1)}, bf16[128,576]{1,0:T(8,128)(2,1)S(1)}, u32[]{:S(2)}, u32[]{:S(2)}) collective-permute-start(bf16[128,576]{1,0:T(8,128)(2,1)S(1)} %get-tuple-element.135), channel_id=1, source_target_pairs={{0,6},{1,7},{2,4},{3,5},{4,2},{5,3},{6,0},{7,1},{8,14},{9,15},{10,... | collective-permute-start | bytes 442376 | tf_op jit(solution)/shard_map/ppermute | solution.py:457
  69.5 10.5 %collective-permute-start.13 = (bf16[256,576]{1,0:T(8,128)(2,1)S(1)}, bf16[256,576]{1,0:T(8,128)(2,1)S(1)}, u32[]{:S(2)}, u32[]{:S(2)}) collective-permute-start(bf16[256,576]{1,0:T(8,128)(2,1)S(1)} %shard_map.97), channel_id=1, source_target_pairs={{0,6},{1,7},{2,4},{3,5},{4,2},{5,3},{6,0},{7,1},{8,14},{9,15},{10,... | collective-permute-start | bytes 884744 | tf_op jit(solution)/shard_map/ppermute | solution.py:457
  71.2 8.8 %collective-permute-start.12 = (bf16[256,576]{1,0:T(8,128)(2,1)S(1)}, bf16[256,576]{1,0:T(8,128)(2,1)S(1)}, u32[]{:S(2)}, u32[]{:S(2)}) collective-permute-start(bf16[256,576]{1,0:T(8,128)(2,1)S(1)} %shard_map.98), channel_id=1, source_target_pairs={{0,2},{1,3},{2,0},{3,1},{4,6},{5,7},{6,4},{7,5},{8,10},{9,11},{10,... | collective-permute-start | bytes 884744 | tf_op jit(solution)/shard_map/ppermute | solution.py:457
  81.7 15.2 %all-to-all-start.1 = ((bf16[16,2,16,576]{3,2,1,0:T(8,128)(2,1)}), bf16[16,2,16,576]{3,2,1,0:T(8,128)(2,1)S(1)}, u32[]{:S(2)}, u32[]{:S(2)}) async-start(bf16[16,2,16,576]{3,2,1,0:T(8,128)(2,1)} %bitcast.38), calls=%async_computation.1 | async-start | bytes 1310720 | tf_op jit(solution)/shard_map/all_to_all | solution.py:564
